TPU v7x, 32 devices: a whole 2x2x4 slice. The times are simulated.
32 devices in a mesh: dp: 8 (over z, y), tm: 4 (over x, core).
Axes of the slice: x: 2, y: 2, z: 4, core: 2. Of those that a mesh axis runs over, the one named last changes fastest.
Arguments:
- clip_frames: bfloat16 [8, 8, 4, 32, 128], P('dp', 'tm'), may hold values from -6 to 6
- out_grad: bfloat16 [8, 8, 4, 32, 128], P('dp', 'tm'), may hold values from -6 to 6
- conv_kernel: bfloat16 [3, 3, 3, 128, 128], replicated, may hold values from -0.109375 to 0.109375
- proj_weight: bfloat16 [128, 128], replicated, may hold values from -0.5 to 0.5
Outputs:
- mixed: bfloat16 [8, 8, 4, 32, 128], P('dp', 'tm')
- input_grad: bfloat16 [8, 8, 4, 32, 128], P('dp', 'tm')
- kernel_grad: float32 [3, 3, 3, 128, 128], replicated
- proj_grad: float32 [128, 128], replicated
All inputs are finite; a program needn't handle non-finite values.
Results may differ from a plain program's by a relative error of at most 0.0034.
Values may be sent and summed in bfloat16 or wider, within the bound.
No kernel may reach another device: no remote copies, remote signals or barrier semaphores. Data moves between devices by JAX's collectives and lax.ppermute only.
A program may use at most 64 MiB of HBM per device.

v0:
```python
import math

import jax
import jax.numpy as jnp
from jax import lax
from jax.sharding import PartitionSpec as P


def passed_along(shard, axis, by):
    size = lax.axis_size(axis)
    pairs = [(i, i + by) for i in range(size) if 0 <= i + by < size]
    return lax.ppermute(shard, axis, pairs)


def patches_of(stack):
    height = stack.shape[1]
    width = stack.shape[2]
    padded = jnp.pad(stack, ((0, 0), (1, 1), (1, 1), (0, 0)))
    return jnp.concatenate(
        [padded[:, row : row + height, col : col + width] for row in range(3) for col in range(3)],
        axis=-1,
    )


def contract_rows(left, right):
    return lax.dot_general(
        left, right, (((0,), (0,)), ((), ())), preferred_element_type=jnp.float32
    )


def shards(clip_frames, out_grad, conv_kernel, proj_weight):
    frames = clip_frames[0]
    grads = out_grad[0]
    n_frames, height, width, chans = frames.shape
    rows = n_frames * height * width
    kern = conv_kernel.reshape(3, 9 * chans, chans)
    kern_flip = jnp.swapaxes(conv_kernel[:, ::-1, ::-1], 3, 4).reshape(3, 9 * chans, chans)
    cache = passed_along(frames, "tm", 1)
    patches = patches_of(jnp.concatenate([cache, frames], axis=0))
    pre = jnp.zeros((rows, chans), jnp.float32)
    for offset in range(3):
        pre = pre + jnp.dot(
            patches[offset : offset + n_frames].reshape(rows, 9 * chans),
            kern[offset],
            preferred_element_type=jnp.float32,
        )
    sig = jax.nn.sigmoid(pre)
    hidden = (pre * sig).astype(jnp.bfloat16)
    flat_grads = grads.reshape(rows, chans)
    mixed = (
        frames.reshape(rows, chans).astype(jnp.float32)
        + jnp.dot(hidden, proj_weight, preferred_element_type=jnp.float32)
    ).astype(jnp.bfloat16)
    proj_part = contract_rows(hidden, flat_grads)
    hidden_grad = lax.dot_general(
        flat_grads, proj_weight, (((1,), (1,)), ((), ())), preferred_element_type=jnp.float32
    )
    pre_grad = (hidden_grad * sig * (1.0 + pre * (1.0 - sig))).astype(jnp.bfloat16)
    kern_part = jnp.stack(
        [
            contract_rows(patches[offset : offset + n_frames].reshape(rows, 9 * chans), pre_grad)
            for offset in range(3)
        ]
    )
    grad_maps = pre_grad.reshape(n_frames, height, width, chans)
    extended = jnp.pad(grad_maps, ((2, 2), (0, 0), (0, 0), (0, 0)))
    ext_rows = (n_frames + 2) * height * width
    total = jnp.zeros((ext_rows, chans), jnp.float32)
    for offset in range(3):
        piece = patches_of(extended[2 - offset : 2 - offset + n_frames + 2]).reshape(
            ext_rows, 9 * chans
        )
        total = total + jnp.dot(piece, kern_flip[offset], preferred_element_type=jnp.float32)
    total = total.reshape(n_frames + 2, height, width, chans)
    arrived = passed_along(total[:2], "tm", -1)
    back = total[2:] + jnp.concatenate(
        [jnp.zeros((n_frames - 2, height, width, chans), jnp.float32), arrived], axis=0
    )
    back = back.reshape(rows, chans)
    input_grad = (flat_grads.astype(jnp.float32) + back).astype(jnp.bfloat16)
    kern_sum, proj_sum = lax.psum((kern_part, proj_part), ("dp", "tm"))
    total_pixels = (
        clip_frames.shape[0] * lax.axis_size("dp") * n_frames * lax.axis_size("tm") * height * width
    )
    scale = 1.0 / math.sqrt(total_pixels)
    kernel_grad = (kern_sum * scale).reshape(3, 3, 3, chans, chans)
    proj_grad = proj_sum * scale
    return (
        mixed.reshape(clip_frames.shape),
        input_grad.reshape(clip_frames.shape),
        kernel_grad,
        proj_grad,
    )


def solution(mesh):
    placed = (P("dp", "tm", None, None, None), P("dp", "tm", None, None, None), P(), P())
    return jax.shard_map(
        shards,
        mesh=mesh,
        in_specs=placed,
        out_specs=(P("dp", "tm", None, None, None), P("dp", "tm", None, None, None), P(), P()),
        check_vma=False,
    )
```

profile of v0, /device:TPU:1, one launch (start us, length us, event | category | flops | bytes accessed | tf_op | source)
XLA Modules:
  0.0 171.1 jit_solution(1182897407177018026)
XLA Ops:
  7.2 0.0 copy-start
  7.2 0.0 copy-start.1
  7.2 0.0 all-reduce.8.cloned.1.call-start
  7.2 4.6 %collective-permute-start = (bf16[2,4,32,128]{3,2,1,0:T(8,128)(2,1)}, bf16[2,4,32,128]{3,2,1,0:T(8,128)(2,1)S(1)}, u32[]{:S(2)}, u32[]{:S(2)}) collective-permute-start(bf16[2,4,32,128]{3,2,1,0:T(8,128)(2,1)} %bitcast.73), channel_id=1, source_target_pairs={{0,1},{1,2},{2,3},{4,5},{5,6},{6,7},{8,9},{9,10},{10,11},{12,13},{... | collective-permute-start | bytes 196616 | tf_op jit(solution)/shard_map/ppermute | solution.py:12
  11.9 1.9 %fusion.38 = (bf16[1,3,3,128,128]{4,3,2,1,0:T(8,128)(2,1)}, bf16[1,3,3,128,128]{4,3,2,1,0:T(8,128)(2,1)S(1)}, bf16[1,3,3,128,128]{4,3,2,1,0:T(8,128)(2,1)S(1)}) fusion(bf16[3,3,3,128,128]{4,3,2,1,0:T(8,128)(2,1)} %param.6), kind=kLoop, calls=%fused_computation.94 | loop fusion | bytes 1769472 | tf_op jit(solution)/shard_map/slice | solution.py:44
  13.8 0.0 copy-done.1
  13.8 1.4 copy.8
  15.2 0.1 reverse_bitcast_fusion
  15.3 0.0 copy-start.2
  15.3 0.1 fusion.37
  15.4 0.0 collective-permute-done
  15.4 0.7 copy-done.2
  16.2 0.1 fusion.5
  16.3 0.1 fusion.6
  16.4 0.1 fusion.7
  16.5 0.1 fusion.8
  16.5 0.1 fusion.10
  16.6 0.2 fusion.36
  16.8 0.0 copy-start.3
  16.8 0.3 fusion.40
  17.1 0.0 copy-start.4
  17.1 0.3 convolution_add_fusion.3
  17.4 0.3 copy-done.3
  17.7 0.3 multiply_convert_fusion
  18.1 0.0 copy-done
  18.1 0.0 copy-done.4
  18.1 0.2 fusion.1
  18.3 0.4 convolution_bitcast_fusion
  18.6 0.4 convolution_bitcast_fusion.1
  19.0 0.4 convolution_bitcast_fusion.2
  19.4 0.8 fusion.42
  20.2 0.1 pad_slice_fusion.32
  20.3 0.7 fusion.11
  21.0 0.7 fusion.12
  21.7 0.7 fusion.13
  22.4 0.7 fusion.14
  23.2 0.1 fusion.21
  23.2 0.1 fusion.22
  23.4 0.1 fusion.29
  23.4 0.1 fusion.30
  23.5 0.8 constant_dynamic-update-slice_fusion.3
  24.3 0.1 fusion.31
  24.3 0.1 fusion.32
  24.4 0.1 fusion.34
  24.5 0.1 fusion.23
  24.5 0.1 fusion.24
  24.6 0.1 fusion.26
  24.7 0.7 fusion.15
  25.4 0.7 fusion.16
  26.1 0.7 fusion.17
  26.8 0.7 fusion.18
  27.5 1.3 pad_maximum_fusion
  28.8 0.0 all-reduce.8.cloned.1.call-update
  28.8 1.7 %fusion.41 = f32[512,128]{1,0:T(8,128)S(1)} fusion(bf16[512,1152]{1,0:T(8,128)(2,1)} %bitcast.11, bf16[1152,128]{1,0:T(8,128)(2,1)S(1)} %bitcast.71), kind=kOutput, calls=%fused_computation.97 | convolution fusion | flops 150994944 | bytes 1736704 | tf_op jit(solution)/shard_map/dot_general | solution.py:73
  30.6 0.5 convolution_add_fusion.1
  31.1 0.5 convolution_add_fusion
  31.6 1.9 %collective-permute-start.1 = (f32[2,4,32,128]{3,2,1,0:T(8,128)S(1)}, f32[2,4,32,128]{3,2,1,0:T(8,128)S(1)}, u32[]{:S(2)}, u32[]{:S(2)}) collective-permute-start(f32[2,4,32,128]{3,2,1,0:T(8,128)S(1)} %bitcast.81), channel_id=1, source_target_pairs={{1,0},{2,1},{3,2},{5,4},{6,5},{7,6},{9,8},{10,9},{11,10},{13,12},{... | collective-permute-start | bytes 393224 | tf_op jit(solution)/shard_map/ppermute | solution.py:12
  33.5 0.8 fusion.2
  34.3 4.6 %collective-permute-done.1 = f32[2,4,32,128]{3,2,1,0:T(8,128)S(1)} collective-permute-done((f32[2,4,32,128]{3,2,1,0:T(8,128)S(1)}, f32[2,4,32,128]{3,2,1,0:T(8,128)S(1)}, u32[]{:S(2)}, u32[]{:S(2)}) %collective-permute-start.1) | collective-permute-done | bytes 131104 | tf_op jit(solution)/shard_map/ppermute | solution.py:12
  38.9 0.7 fusion.35
  39.5 121.3 %all-reduce.8.cloned.1.call-done = (f32[3,1152,128]{2,1,0:T(8,128)}, f32[128,128]{1,0:T(8,128)}) async-done(((f32[3,1152,128]{2,1,0:T(8,128)}, f32[128,128]{1,0:T(8,128)}), (f32[3,1152,128]{2,1,0:T(8,128)}, f32[128,128]{1,0:T(8,128)})) %all-reduce.8.cloned.1.call-update) | async-done | bytes 1835024 | tf_op jit(solution)/shard_map/psum | solution.py:81
  160.8 2.9 %broadcast_multiply_fusion = f32[3,1152,128]{2,1,0:T(8,128)} fusion(f32[3,1152,128]{2,1,0:T(8,128)} %get-tuple-element.4), kind=kLoop, calls=%fused_computation.13 | loop fusion | flops 442368 | bytes 3538944 | tf_op jit(solution)/shard_map/mul | solution.py:86
  163.7 0.0 copy-done.5
  163.7 0.6 broadcast_multiply_fusion.1
  (12 shorter events, 0.3 us)
Async XLA Ops:
  7.2 10.9 %copy-start = (bf16[128,128]{1,0:T(8,128)(2,1)S(1)}, bf16[128,128]{1,0:T(8,128)(2,1)}, u32[]{:S(2)}) copy-start(bf16[128,128]{1,0:T(8,128)(2,1)} %param.7) | copy-start | bytes 98308
  7.2 6.6 %copy-start.1 = (bf16[3,3,3,128,128]{4,3,2,1,0:T(8,128)(2,1)S(1)}, bf16[3,3,3,128,128]{4,3,2,1,0:T(8,128)(2,1)}, u32[]{:S(2)}) copy-start(bf16[3,3,3,128,128]{4,3,2,1,0:T(8,128)(2,1)} %param.6) | copy-start | bytes 2654212
  7.2 153.6 %all-reduce.8.cloned.1.call-start = ((), (), s32[]{:S(2)}) async-start(), calls=%async_computation | async-start | bytes 3670016 | tf_op jit(solution)/shard_map/psum | solution.py:81
  7.2 8.2 %collective-permute-start = (bf16[2,4,32,128]{3,2,1,0:T(8,128)(2,1)}, bf16[2,4,32,128]{3,2,1,0:T(8,128)(2,1)S(1)}, u32[]{:S(2)}, u32[]{:S(2)}) collective-permute-start(bf16[2,4,32,128]{3,2,1,0:T(8,128)(2,1)} %bitcast.73), channel_id=1, source_target_pairs={{0,1},{1,2},{2,3},{4,5},{5,6},{6,7},{8,9},{9,10},{10,11},{12,13},{... | collective-permute-start | bytes 196616 | tf_op jit(solution)/shard_map/ppermute | solution.py:12
  15.3 0.8 copy-start.2
  16.8 1.0 copy-start.3
  17.1 1.0 copy-start.4
  31.6 7.3 %collective-permute-start.1 = (f32[2,4,32,128]{3,2,1,0:T(8,128)S(1)}, f32[2,4,32,128]{3,2,1,0:T(8,128)S(1)}, u32[]{:S(2)}, u32[]{:S(2)}) collective-permute-start(f32[2,4,32,128]{3,2,1,0:T(8,128)S(1)} %bitcast.81), channel_id=1, source_target_pairs={{1,0},{2,1},{3,2},{5,4},{6,5},{7,6},{9,8},{10,9},{11,10},{13,12},{... | collective-permute-start | bytes 393224 | tf_op jit(solution)/shard_map/ppermute | solution.py:12
  160.8 2.9 %copy-start.5 = (f32[128,128]{1,0:T(8,128)S(1)}, f32[128,128]{1,0:T(8,128)}, u32[]{:S(2)}) copy-start(f32[128,128]{1,0:T(8,128)} %get-tuple-element.5) | copy-start | bytes 196612
Sparse Core Ops, SparseCore 0:
  28.9 131.7 all-reduce.7
where the time goes:
time: 173 us; the launch traced here: 171 us
  waiting for transfers between devices  126 us (73%)
  between operations  14.3 us (8%)
  local copies, waits for them, and re-layouts  12.3 us (7%)
  starting transfers between devices  6.6 us (4%)
  matrix products  6.55 us (4%)
  other arithmetic  5.52 us (3%)
    psum x1, waiting for transfers between devices, shards(): kern_sum, proj_sum = lax.psum((kern_part, proj_part), ('dp', 'tm'))  121 us
    unnamed x41, local copies, waits for them, and re-layouts  9.07 us
    ppermute x2, starting transfers between devices, passed_along(): return lax.ppermute(shard, axis, pairs)  6.56 us
    ppermute x2, waiting for transfers between devices, passed_along(): return lax.ppermute(shard, axis, pairs)  4.59 us
  transfers between devices with their start and end apart: 3, of which 2 were waited for; matrix products, arithmetic and copies ran while one was open for 4% of the time, Pallas kernels for 0%

commit v1 on v0

--- a/solution.py
+++ b/solution.py
@@ -1,9 +1,16 @@
+import functools
 import math
 
 import jax
 import jax.numpy as jnp
 from jax import lax
+from jax.experimental import pallas as pl
+from jax.experimental.pallas import tpu as pltpu
 from jax.sharding import PartitionSpec as P
+
+AXES = ("dp", "tm")
+HALVINGS = 4
+ORDERS = ((1, 2, 3), (2, 3, 1))
 
 
 def passed_along(shard, axis, by):
@@ -26,6 +33,106 @@
     return lax.dot_general(
         left, right, (((0,), (0,)), ((), ())), preferred_element_type=jnp.float32
     )
+
+
+def device_number():
+    return lax.axis_index("dp") * lax.axis_size("tm") + lax.axis_index("tm")
+
+
+def swapped(array, bits):
+    count = lax.axis_size("dp") * lax.axis_size("tm")
+    return lax.ppermute(array, AXES, [(i, i ^ (1 << bits[i & 1])) for i in range(count)])
+
+
+def bit(number, place):
+    return (number >> place) & 1
+
+
+def place_of(offset, orders):
+    return (
+        4 * bit(offset, orders[0]) + 2 * bit(offset, orders[1]) + bit(offset, orders[2])
+    )
+
+
+def pack_kernel(me_ref, kern_ref, proj_ref, keep_ref, send_ref):
+    me = me_ref[0] & 15
+    core = me & 1
+    taps = kern_ref.shape[0]
+    for pair in range(8):
+        places = []
+        for c in range(2):
+            places.append(place_of((2 * pair) ^ (me & 14), ORDERS[c]))
+        mine = jnp.where(core == 0, places[0], places[1])
+        other = jnp.where(core == 0, places[1], places[0])
+        mine_rows = pl.ds(pl.multiple_of(16 * pair + 8 * core, 8), 8)
+        other_rows = pl.ds(pl.multiple_of(16 * pair + 8 * (1 - core), 8), 8)
+        keep_ref[mine, :taps] = kern_ref[:, mine_rows, :]
+        keep_ref[mine, taps] = proj_ref[mine_rows, :]
+        send_ref[other, :taps] = kern_ref[:, other_rows, :]
+        send_ref[other, taps] = proj_ref[other_rows, :]
+
+
+def unpack_kernel(scale, me_ref, mine_ref, other_ref, kern_ref, proj_ref):
+    me = me_ref[0] & 15
+    core = me & 1
+    taps = kern_ref.shape[0]
+    for pair in range(8):
+        places = []
+        for c in range(2):
+            places.append(place_of((2 * pair) ^ (me & 14), ORDERS[c]))
+        mine = jnp.where(core == 0, places[0], places[1])
+        other = jnp.where(core == 0, places[1], places[0])
+        mine_rows = pl.ds(pl.multiple_of(16 * pair + 8 * core, 8), 8)
+        other_rows = pl.ds(pl.multiple_of(16 * pair + 8 * (1 - core), 8), 8)
+        kern_ref[:, mine_rows, :] = mine_ref[mine, :taps].astype(jnp.float32) * scale
+        proj_ref[mine_rows, :] = mine_ref[mine, taps].astype(jnp.float32) * scale
+        kern_ref[:, other_rows, :] = other_ref[other, :taps].astype(jnp.float32) * scale
+        proj_ref[other_rows, :] = other_ref[other, taps].astype(jnp.float32) * scale
+
+
+def in_vmem(count):
+    return [pl.BlockSpec(memory_space=pltpu.VMEM) for _ in range(count)]
+
+
+def summed(kern_part, proj_part, scale):
+    taps, chans, _ = kern_part.shape
+    me = device_number().astype(jnp.int32).reshape(1)
+    half = (8, taps + 1, 8, chans)
+    keep, send = pl.pallas_call(
+        pack_kernel,
+        out_shape=(
+            jax.ShapeDtypeStruct(half, jnp.float32),
+            jax.ShapeDtypeStruct(half, jnp.float32),
+        ),
+        in_specs=[pl.BlockSpec(memory_space=pltpu.SMEM)] + in_vmem(2),
+        out_specs=tuple(in_vmem(2)),
+        name="pack",
+    )(me, kern_part, proj_part)
+    rounds = [tuple(order[k] for order in ORDERS) for k in range(3)]
+    total = keep + swapped(send, (0, 0))
+    for bits, link_type in zip(rounds, (jnp.bfloat16, jnp.bfloat16, jnp.float32)):
+        rest = total.shape[0] // 2
+        came = swapped(total[rest:].astype(link_type), bits)
+        total = total[:rest] + came.astype(jnp.float32)
+    count = lax.axis_size("dp") * lax.axis_size("tm")
+    place = HALVINGS
+    while (1 << place) < count:
+        total = total + swapped(total, (place, place))
+        place += 1
+    total = total.astype(jnp.bfloat16)
+    for bits in reversed(rounds):
+        total = jnp.concatenate([total, swapped(total, bits)], axis=0)
+    other = swapped(total, (0, 0))
+    return pl.pallas_call(
+        functools.partial(unpack_kernel, scale),
+        out_shape=(
+            jax.ShapeDtypeStruct(kern_part.shape, jnp.float32),
+            jax.ShapeDtypeStruct(proj_part.shape, jnp.float32),
+        ),
+        in_specs=[pl.BlockSpec(memory_space=pltpu.SMEM)] + in_vmem(2),
+        out_specs=tuple(in_vmem(2)),
+        name="unpack",
+    )(me, total, other)
 
 
 def shards(clip_frames, out_grad, conv_kernel, proj_weight):
@@ -78,17 +185,17 @@
     )
     back = back.reshape(rows, chans)
     input_grad = (flat_grads.astype(jnp.float32) + back).astype(jnp.bfloat16)
-    kern_sum, proj_sum = lax.psum((kern_part, proj_part), ("dp", "tm"))
     total_pixels = (
         clip_frames.shape[0] * lax.axis_size("dp") * n_frames * lax.axis_size("tm") * height * width
     )
     scale = 1.0 / math.sqrt(total_pixels)
-    kernel_grad = (kern_sum * scale).reshape(3, 3, 3, chans, chans)
-    proj_grad = proj_sum * scale
+    kernel_grad, proj_grad = summed(
+        kern_part.reshape(27, chans, chans), proj_part, scale
+    )
     return (
         mixed.reshape(clip_frames.shape),
         input_grad.reshape(clip_frames.shape),
-        kernel_grad,
+        kernel_grad.reshape(3, 3, 3, chans, chans),
         proj_grad,
     )
 

time: 173 us -> 63.7 us (0.37)
  waiting for transfers between devices: 126 us -> 17.4 us
  starting transfers between devices: 6.6 us -> 25.1 us
  between operations: 14.3 us -> 1.05 us
  local copies, waits for them, and re-layouts: 12.3 us -> 6.37 us
  Pallas kernels: 0 us -> 5.48 us
  other arithmetic: 5.52 us -> 2.3 us
    psum x1 -> x0, waiting for transfers between devices: 121 us -> none  [shards(): kern_sum, proj_sum = lax.psum((kern_part, proj_part), ('dp', 'tm'))]
    ppermute x0 -> x9, waiting for transfers between devices: none -> 17.4 us  [swapped(): lax.ppermute(array, AXES, [(i, i ^ 1 << bits[i & 1]) for i in range(count)])]
    ppermute x0 -> x9, starting transfers between devices: none -> 11.9 us  [swapped(): lax.ppermute(array, AXES, [(i, i ^ 1 << bits[i & 1]) for i in range(count)])]
    ppermute x2, starting transfers between devices: 6.56 us -> 13.3 us  [passed_along(): return lax.ppermute(shard, axis, pairs)]
    pallas_call x0 -> x2, Pallas kernels: none -> 5.48 us  [the longest x1 2.87 us: summed(): pl.pallas_call(pack_kernel, out_shape=(jax.ShapeDtypeStruct(half, jnp.flo...]
    ppermute x2, waiting for transfers between devices: 4.59 us -> 0.01 us  [passed_along(): return lax.ppermute(shard, axis, pairs)]
    unnamed x41 -> x43, local copies, waits for them, and re-layouts: 9.07 us -> 4.5 us
    mul x2 -> x0, other arithmetic: 3.5 us -> none  [the longest x1 2.87 us: shards(): kernel_grad = (kern_sum * scale).reshape(3, 3, 3, chans, chans)]
  transfers between devices with their start and end apart: 3 -> 11, of which waited for: 2 -> 7; matrix products, arithmetic and copies ran while one was open for 4% -> 11% of each run, Pallas kernels for 0% -> 0%
where the time goes in v1:
time: 63.7 us; the launch traced here: 63.1 us
  starting transfers between devices  25.1 us (39%)
  waiting for transfers between devices  17.4 us (27%)
  local copies, waits for them, and re-layouts  6.37 us (10%)
  Pallas kernels  5.48 us (9%)
  matrix products  5.29 us (8%)
  other arithmetic  2.3 us (4%)
  between operations  1.05 us (2%)
    ppermute x9, waiting for transfers between devices, swapped(): lax.ppermute(array, AXES, [(i, i ^ 1 << bits[i & 1]) for i in range(count)])  17.4 us
    ppermute x2, starting transfers between devices, passed_along(): return lax.ppermute(shard, axis, pairs)  13.3 us
    ppermute x9, starting transfers between devices, swapped(): lax.ppermute(array, AXES, [(i, i ^ 1 << bits[i & 1]) for i in range(count)])  11.9 us
    unnamed x43, local copies, waits for them, and re-layouts  4.5 us
    pallas_call x1, Pallas kernels, summed(): pl.pallas_call(pack_kernel, out_shape=(jax.ShapeDtypeStruct(half, jnp.flo...  2.87 us
    pallas_call x1, Pallas kernels, summed(): pl.pallas_call(functools.partial(unpack_kernel, scale), out_shape=(jax.Sh...  2.6 us
    dot_general x4, matrix products, contract_rows(): lax.dot_general(left, right, (((0,), (0,)), ((), ())), preferred_element_...  1.95 us
    dot_general x3, matrix products, shards(): jnp.dot(piece, kern_flip[offset], preferred_element_type=jnp.float32)  1.44 us
  transfers between devices with their start and end apart: 11, of which 7 were waited for; matrix products, arithmetic and copies ran while one was open for 11% of the time, Pallas kernels for 0%

profile of v1, /device:TPU:1, one launch (start us, length us, event | category | flops | bytes accessed | tf_op | source)
XLA Modules:
  0.0 63.1 jit_solution(6327232207754974349)
XLA Ops:
  0.7 4.6 %collective-permute-start = (bf16[2,4,32,128]{3,2,1,0:T(8,128)(2,1)}, bf16[2,4,32,128]{3,2,1,0:T(8,128)(2,1)S(1)}, u32[]{:S(2)}, u32[]{:S(2)}) collective-permute-start(bf16[2,4,32,128]{3,2,1,0:T(8,128)(2,1)} %bitcast.76), channel_id=1, source_target_pairs={{0,1},{1,2},{2,3},{4,5},{5,6},{6,7},{8,9},{9,10},{10,11},{12,13},{... | collective-permute-start | bytes 196616 | tf_op jit(solution)/shard_map/ppermute | solution.py:19
  5.3 1.2 %fusion.38 = (bf16[1,3,3,128,128]{4,3,2,1,0:T(8,128)(2,1)S(1)}, bf16[1,3,3,128,128]{4,3,2,1,0:T(8,128)(2,1)S(1)}, bf16[1,3,3,128,128]{4,3,2,1,0:T(8,128)(2,1)S(1)}) fusion(bf16[3,3,3,128,128]{4,3,2,1,0:T(8,128)(2,1)} %param.6), kind=kLoop, calls=%fused_computation.101 | loop fusion | bytes 1769472 | tf_op jit(solution)/shard_map/slice | solution.py:151
  6.5 1.4 %copy.8 = bf16[3,3,3,128,128]{3,4,2,1,0:T(8,128)(2,1)S(1)} copy(bf16[3,3,3,128,128]{4,3,2,1,0:T(8,128)(2,1)S(1)} %copy-done.1) | data formatting | bytes 1769472 | tf_op args[2]
  7.9 0.1 reverse_bitcast_fusion
  8.0 0.1 fusion.37
  8.1 0.7 %copy-done.4 = bf16[1,2,4,32,128]{4,3,2,1,0:T(8,128)(2,1)S(1)} copy-done((bf16[1,2,4,32,128]{4,3,2,1,0:T(8,128)(2,1)S(1)}, bf16[1,2,4,32,128]{4,3,2,1,0:T(8,128)(2,1)}, u32[]{:S(2)}) %copy-start.4) | copy-done | bytes 65560
  8.9 0.1 fusion.5
  9.0 0.1 fusion.6
  9.1 0.1 fusion.7
  9.2 0.1 fusion.8
  9.3 0.1 fusion.10
  9.3 0.2 fusion.36
  9.5 0.3 fusion.40
  9.8 0.3 convolution_add_fusion.3
  10.1 0.3 multiply_convert_fusion
  10.5 0.2 copy-done.6
  10.7 0.2 fusion.1
  10.8 0.4 convolution_bitcast_fusion
  11.2 0.4 convolution_bitcast_fusion.1
  11.6 0.4 convolution_bitcast_fusion.2
  12.0 0.8 %fusion.42.proj_ref = f32[128,128]{1,0:T(8,128)} fusion(bf16[256,128]{1,0:T(8,128)(2,1)S(1)} %get-tuple-element.29, bf16[256,128]{1,0:T(8,128)(2,1)S(1)} %bitcast.83), kind=kOutput, calls=%fused_computation.105 | convolution fusion | flops 8388608 | bytes 196608 | tf_op jit(solution)/shard_map/dot_general | solution.py:33
  12.8 1.3 %pad_maximum_fusion = f32[3,1152,128]{2,1,0:T(8,128)} fusion(f32[1,1152,128]{2,1,0:T(8,128)S(1)} %convolution_bitcast_fusion, f32[1,1152,128]{2,1,0:T(8,128)S(1)} %convolution_bitcast_fusion.1, f32[1,1152,128]{2,1,0:T(8,128)S(1)} %convolution_bitcast_fusion.2), kind=kLoop, calls=%fused_computation.3 | loop fusion | flops 884736 | bytes 3538944 | tf_op jit(solution)/shard_map/stack | solution.py:166
  14.1 2.9 %pack.1 = (f32[8,28,8,128]{3,2,1,0:T(8,128)}, f32[8,28,8,128]{3,2,1,0:T(8,128)}) custom-call(s32[1]{0:T(128)} %bitcast.21.me_ref, f32[27,128,128]{2,1,0:T(8,128)} %bitcast.59, f32[128,128]{1,0:T(8,128)} %fusion.42.proj_ref), custom_call_target="tpu_custom_call" | custom-call | tf_op jit(solution)/shard_map/pack/pallas_call | solution.py:101
  17.0 0.1 pad_slice_fusion.32
  17.0 0.1 fusion.11
  17.1 0.1 fusion.13
  17.2 0.1 fusion.14
  17.3 0.1 fusion.21
  17.4 0.1 fusion.22
  17.5 0.1 fusion.29
  17.6 0.1 fusion.30
  17.6 0.1 constant_dynamic-update-slice_fusion.3
  17.8 0.1 fusion.23
  17.8 0.1 fusion.24
  17.9 0.1 fusion.26
  18.0 0.1 fusion.15
  18.1 0.1 fusion.16
  18.2 0.1 fusion.18
  18.2 0.5 fusion.41
  18.7 1.0 %collective-permute-done.2 = f32[8,28,8,128]{3,2,1,0:T(8,128)S(1)} collective-permute-done((f32[8,28,8,128]{3,2,1,0:T(8,128)}, f32[8,28,8,128]{3,2,1,0:T(8,128)S(1)}, u32[]{:S(2)}, u32[]{:S(2)}) %collective-permute-start.2) | collective-permute-done | bytes 917536 | tf_op jit(solution)/shard_map/ppermute | solution.py:44
  19.7 0.1 add.66
  19.8 1.3 %collective-permute-start.3 = (bf16[4,28,8,128]{3,2,1,0:T(8,128)(2,1)S(1)}, bf16[4,28,8,128]{3,2,1,0:T(8,128)(2,1)S(1)}, u32[]{:S(2)}, u32[]{:S(2)}) collective-permute-start(bf16[4,28,8,128]{3,2,1,0:T(8,128)(2,1)S(1)} %slice.355), channel_id=1, source_target_pairs={{0,2},{1,5},{2,0},{3,7},{4,6},{5,1},{6,4},{7,3},{8,10},{9,13},{10,... | collective-permute-start | bytes 688136 | tf_op jit(solution)/shard_map/ppermute | solution.py:44
  21.1 0.5 convolution_add_fusion.1
  21.6 3.4 %collective-permute-done.3 = bf16[4,28,8,128]{3,2,1,0:T(8,128)(2,1)S(1)} collective-permute-done((bf16[4,28,8,128]{3,2,1,0:T(8,128)(2,1)S(1)}, bf16[4,28,8,128]{3,2,1,0:T(8,128)(2,1)S(1)}, u32[]{:S(2)}, u32[]{:S(2)}) %collective-permute-start.3) | collective-permute-done | bytes 229408 | tf_op jit(solution)/shard_map/ppermute | solution.py:44
  25.1 1.4 %collective-permute-start.4 = (bf16[2,28,8,128]{3,2,1,0:T(8,128)(2,1)S(1)}, bf16[2,28,8,128]{3,2,1,0:T(8,128)(2,1)S(1)}, u32[]{:S(2)}, u32[]{:S(2)}) collective-permute-start(bf16[2,28,8,128]{3,2,1,0:T(8,128)(2,1)S(1)} %slice.356), channel_id=1, source_target_pairs={{0,4},{1,9},{2,6},{3,11},{4,0},{5,13},{6,2},{7,15},{8,12},{9,1},{1... | collective-permute-start | bytes 344072 | tf_op jit(solution)/shard_map/ppermute | solution.py:44
  26.5 0.1 fusion.31
  26.5 2.3 %collective-permute-done.4 = bf16[2,28,8,128]{3,2,1,0:T(8,128)(2,1)S(1)} collective-permute-done((bf16[2,28,8,128]{3,2,1,0:T(8,128)(2,1)S(1)}, bf16[2,28,8,128]{3,2,1,0:T(8,128)(2,1)S(1)}, u32[]{:S(2)}, u32[]{:S(2)}) %collective-permute-start.4) | collective-permute-done | bytes 114720 | tf_op jit(solution)/shard_map/ppermute | solution.py:44
  28.9 0.1 collective-permute-start.5
  29.0 0.1 fusion.32
  29.1 3.5 %collective-permute-done.5 = f32[1,28,8,128]{3,2,1,0:T(8,128)S(1)} collective-permute-done((f32[1,28,8,128]{3,2,1,0:T(8,128)S(1)}, f32[1,28,8,128]{3,2,1,0:T(8,128)S(1)}, u32[]{:S(2)}, u32[]{:S(2)}) %collective-permute-start.5) | collective-permute-done | bytes 114720 | tf_op jit(solution)/shard_map/ppermute | solution.py:44
  32.6 2.4 %collective-permute-start.6 = (f32[1,28,8,128]{3,2,1,0:T(8,128)S(1)}, f32[1,28,8,128]{3,2,1,0:T(8,128)S(1)}, u32[]{:S(2)}, u32[]{:S(2)}) collective-permute-start(f32[1,28,8,128]{3,2,1,0:T(8,128)S(1)} %slice_add_fusion.2), channel_id=1, source_target_pairs={{0,16},{1,17},{2,18},{3,19},{4,20},{5,21},{6,22},{7,23},{8,24},{9,... | collective-permute-start | bytes 344072 | tf_op jit(solution)/shard_map/ppermute | solution.py:44
  35.0 2.4 %collective-permute-done.6 = f32[1,28,8,128]{3,2,1,0:T(8,128)S(1)} collective-permute-done((f32[1,28,8,128]{3,2,1,0:T(8,128)S(1)}, f32[1,28,8,128]{3,2,1,0:T(8,128)S(1)}, u32[]{:S(2)}, u32[]{:S(2)}) %collective-permute-start.6) | collective-permute-done | bytes 114720 | tf_op jit(solution)/shard_map/ppermute | solution.py:44
  37.4 0.2 collective-permute-start.7
  37.7 3.1 %collective-permute-done.7 = bf16[1,28,8,128]{3,2,1,0:T(8,128)(2,1)S(1)} collective-permute-done((bf16[1,28,8,128]{3,2,1,0:T(8,128)(2,1)S(1)}, bf16[1,28,8,128]{3,2,1,0:T(8,128)(2,1)S(1)}, u32[]{:S(2)}, u32[]{:S(2)}) %collective-permute-start.7) | collective-permute-done | bytes 57376 | tf_op jit(solution)/shard_map/ppermute | solution.py:44
  40.8 1.8 %collective-permute-start.8 = (bf16[2,28,8,128]{3,2,1,0:T(8,128)(2,1)S(1)}, bf16[2,28,8,128]{3,2,1,0:T(8,128)(2,1)S(1)}, u32[]{:S(2)}, u32[]{:S(2)}) collective-permute-start(bf16[2,28,8,128]{3,2,1,0:T(8,128)(2,1)S(1)} %pad_maximum_fusion.4), channel_id=1, source_target_pairs={{0,4},{1,9},{2,6},{3,11},{4,0},{5,13},{6,2},{7,15},{8,12},{9,1},{1... | collective-permute-start | bytes 344072 | tf_op jit(solution)/shard_map/ppermute | solution.py:44
  42.6 0.5 convolution_add_fusion
  43.1 1.7 %collective-permute-done.8 = bf16[2,28,8,128]{3,2,1,0:T(8,128)(2,1)S(1)} collective-permute-done((bf16[2,28,8,128]{3,2,1,0:T(8,128)(2,1)S(1)}, bf16[2,28,8,128]{3,2,1,0:T(8,128)(2,1)S(1)}, u32[]{:S(2)}, u32[]{:S(2)}) %collective-permute-start.8) | collective-permute-done | bytes 114720 | tf_op jit(solution)/shard_map/ppermute | solution.py:44
  44.8 1.3 %collective-permute-start.9 = (bf16[4,28,8,128]{3,2,1,0:T(8,128)(2,1)S(1)}, bf16[4,28,8,128]{3,2,1,0:T(8,128)(2,1)S(1)}, u32[]{:S(2)}, u32[]{:S(2)}) collective-permute-start(bf16[4,28,8,128]{3,2,1,0:T(8,128)(2,1)S(1)} %pad_maximum_fusion.2), channel_id=1, source_target_pairs={{0,2},{1,5},{2,0},{3,7},{4,6},{5,1},{6,4},{7,3},{8,10},{9,13},{10,... | collective-permute-start | bytes 688136 | tf_op jit(solution)/shard_map/ppermute | solution.py:44
  46.1 8.6 %collective-permute-start.1 = (f32[2,4,32,128]{3,2,1,0:T(8,128)S(1)}, f32[2,4,32,128]{3,2,1,0:T(8,128)S(1)}, u32[]{:S(2)}, u32[]{:S(2)}) collective-permute-start(f32[2,4,32,128]{3,2,1,0:T(8,128)S(1)} %bitcast.84), channel_id=1, source_target_pairs={{1,0},{2,1},{3,2},{5,4},{6,5},{7,6},{9,8},{10,9},{11,10},{13,12},{... | collective-permute-start | bytes 393224 | tf_op jit(solution)/shard_map/ppermute | solution.py:19
  54.9 3.4 %collective-permute-start.10 = (bf16[8,28,8,128]{3,2,1,0:T(8,128)(2,1)S(1)}, bf16[8,28,8,128]{3,2,1,0:T(8,128)(2,1)S(1)}, u32[]{:S(2)}, u32[]{:S(2)}) collective-permute-start(bf16[8,28,8,128]{3,2,1,0:T(8,128)(2,1)S(1)} %pad_maximum_fusion.1.mine_ref), channel_id=1, source_target_pairs={{0,1},{1,0},{2,3},{3,2},{4,5},{5,4},{6,7},{7,6},{8,9},{9,8},{10,11... | collective-permute-start | bytes 1376264 | tf_op jit(solution)/shard_map/ppermute | solution.py:44
  58.2 0.8 %fusion.2 = bf16[256,128]{1,0:T(8,128)(2,1)} fusion(bf16[256,128]{1,0:T(8,128)(2,1)S(1)} %get-tuple-element.29, bf16[128,128]{1,0:T(8,128)(2,1)S(1)} %copy-done, bf16[256,128]{1,0:T(8,128)(2,1)S(1)} %bitcast.79), kind=kOutput, calls=%fused_computation.12 | convolution fusion | flops 8486912 | bytes 229376 | tf_op jit(solution)/shard_map/dot_general | solution.py:159
  59.0 0.7 %fusion.35 = bf16[1,2,4,32,128]{4,3,2,1,0:T(8,128)(2,1)} fusion(f32[2,4,32,128]{3,2,1,0:T(8,128)S(1)} %bitcast.80, f32[2,4,32,128]{3,2,1,0:T(8,128)S(1)} %collective-permute-done.1, bf16[1,2,4,32,128]{4,3,2,1,0:T(8,128)(2,1)S(1)} %copy-done.6), kind=kLoop, calls=%fused_computation.89 | loop fusion | flops 131072 | bytes 393216 | tf_op jit(solution)/shard_map/convert_element_type | solution.py:187
  59.7 0.8 %copy-done.5 = bf16[8,28,8,128]{3,2,1,0:T(8,128)(2,1)} copy-done((bf16[8,28,8,128]{3,2,1,0:T(8,128)(2,1)}, bf16[8,28,8,128]{3,2,1,0:T(8,128)(2,1)S(1)}, u32[]{:S(2)}) %copy-start.5) | copy-done | bytes 458776
  60.5 2.6 %unpack.1 = (f32[27,128,128]{2,1,0:T(8,128)}, f32[128,128]{1,0:T(8,128)}) custom-call(s32[1]{0:T(128)} %bitcast.21.me_ref, bf16[8,28,8,128]{3,2,1,0:T(8,128)(2,1)} %copy-done.2, bf16[8,28,8,128]{3,2,1,0:T(8,128)(2,1)} %copy-done.5), custom_call_target="tpu_custom_call" | custom-call | tf_op jit(solution)/shard_map/unpack/pallas_call | solution.py:126
  (40 shorter events, 0.7 us)
Async XLA Ops:
  0.6 9.9 %copy-start = (bf16[128,128]{1,0:T(8,128)(2,1)S(1)}, bf16[128,128]{1,0:T(8,128)(2,1)}, u32[]{:S(2)}) copy-start(bf16[128,128]{1,0:T(8,128)(2,1)} %param.7) | copy-start | bytes 98308
  0.6 5.9 %copy-start.1 = (bf16[3,3,3,128,128]{4,3,2,1,0:T(8,128)(2,1)S(1)}, bf16[3,3,3,128,128]{4,3,2,1,0:T(8,128)(2,1)}, u32[]{:S(2)}) copy-start(bf16[3,3,3,128,128]{4,3,2,1,0:T(8,128)(2,1)} %param.6) | copy-start | bytes 2654212
  0.7 7.5 %collective-permute-start = (bf16[2,4,32,128]{3,2,1,0:T(8,128)(2,1)}, bf16[2,4,32,128]{3,2,1,0:T(8,128)(2,1)S(1)}, u32[]{:S(2)}, u32[]{:S(2)}) collective-permute-start(bf16[2,4,32,128]{3,2,1,0:T(8,128)(2,1)} %bitcast.76), channel_id=1, source_target_pairs={{0,1},{1,2},{2,3},{4,5},{5,6},{6,7},{8,9},{9,10},{10,11},{12,13},{... | collective-permute-start | bytes 196616 | tf_op jit(solution)/shard_map/ppermute | solution.py:19
  8.0 0.8 %copy-start.4 = (bf16[1,2,4,32,128]{4,3,2,1,0:T(8,128)(2,1)S(1)}, bf16[1,2,4,32,128]{4,3,2,1,0:T(8,128)(2,1)}, u32[]{:S(2)}) copy-start(bf16[1,2,4,32,128]{4,3,2,1,0:T(8,128)(2,1)} %param.4) | copy-start | bytes 196612
  9.8 0.8 %copy-start.6 = (bf16[1,2,4,32,128]{4,3,2,1,0:T(8,128)(2,1)S(1)}, bf16[1,2,4,32,128]{4,3,2,1,0:T(8,128)(2,1)}, u32[]{:S(2)}) copy-start(bf16[1,2,4,32,128]{4,3,2,1,0:T(8,128)(2,1)} %param.5) | copy-start | bytes 196612
  17.0 2.7 %collective-permute-start.2 = (f32[8,28,8,128]{3,2,1,0:T(8,128)}, f32[8,28,8,128]{3,2,1,0:T(8,128)S(1)}, u32[]{:S(2)}, u32[]{:S(2)}) collective-permute-start(f32[8,28,8,128]{3,2,1,0:T(8,128)} %get-tuple-element.9), channel_id=1, source_target_pairs={{0,1},{1,0},{2,3},{3,2},{4,5},{5,4},{6,7},{7,6},{8,9},{9,8},{10,11... | collective-permute-start | bytes 2752520 | tf_op jit(solution)/shard_map/ppermute | solution.py:44
  18.1 1.6 %copy-start.3 = (f32[8,28,8,128]{3,2,1,0:T(8,128)S(1)}, f32[8,28,8,128]{3,2,1,0:T(8,128)}, u32[]{:S(2)}) copy-start(f32[8,28,8,128]{3,2,1,0:T(8,128)} %get-tuple-element.8) | copy-start | bytes 2752516
  19.8 5.2 %collective-permute-start.3 = (bf16[4,28,8,128]{3,2,1,0:T(8,128)(2,1)S(1)}, bf16[4,28,8,128]{3,2,1,0:T(8,128)(2,1)S(1)}, u32[]{:S(2)}, u32[]{:S(2)}) collective-permute-start(bf16[4,28,8,128]{3,2,1,0:T(8,128)(2,1)S(1)} %slice.355), channel_id=1, source_target_pairs={{0,2},{1,5},{2,0},{3,7},{4,6},{5,1},{6,4},{7,3},{8,10},{9,13},{10,... | collective-permute-start | bytes 688136 | tf_op jit(solution)/shard_map/ppermute | solution.py:44
  25.1 3.7 %collective-permute-start.4 = (bf16[2,28,8,128]{3,2,1,0:T(8,128)(2,1)S(1)}, bf16[2,28,8,128]{3,2,1,0:T(8,128)(2,1)S(1)}, u32[]{:S(2)}, u32[]{:S(2)}) collective-permute-start(bf16[2,28,8,128]{3,2,1,0:T(8,128)(2,1)S(1)} %slice.356), channel_id=1, source_target_pairs={{0,4},{1,9},{2,6},{3,11},{4,0},{5,13},{6,2},{7,15},{8,12},{9,1},{1... | collective-permute-start | bytes 344072 | tf_op jit(solution)/shard_map/ppermute | solution.py:44
  28.9 3.7 %collective-permute-start.5 = (f32[1,28,8,128]{3,2,1,0:T(8,128)S(1)}, f32[1,28,8,128]{3,2,1,0:T(8,128)S(1)}, u32[]{:S(2)}, u32[]{:S(2)}) collective-permute-start(f32[1,28,8,128]{3,2,1,0:T(8,128)S(1)} %slice.244), channel_id=1, source_target_pairs={{0,8},{1,3},{2,10},{3,1},{4,12},{5,7},{6,14},{7,5},{8,0},{9,11},{1... | collective-permute-start | bytes 344072 | tf_op jit(solution)/shard_map/ppermute | solution.py:44
  32.6 4.8 %collective-permute-start.6 = (f32[1,28,8,128]{3,2,1,0:T(8,128)S(1)}, f32[1,28,8,128]{3,2,1,0:T(8,128)S(1)}, u32[]{:S(2)}, u32[]{:S(2)}) collective-permute-start(f32[1,28,8,128]{3,2,1,0:T(8,128)S(1)} %slice_add_fusion.2), channel_id=1, source_target_pairs={{0,16},{1,17},{2,18},{3,19},{4,20},{5,21},{6,22},{7,23},{8,24},{9,... | collective-permute-start | bytes 344072 | tf_op jit(solution)/shard_map/ppermute | solution.py:44
  37.4 3.4 %collective-permute-start.7 = (bf16[1,28,8,128]{3,2,1,0:T(8,128)(2,1)S(1)}, bf16[1,28,8,128]{3,2,1,0:T(8,128)(2,1)S(1)}, u32[]{:S(2)}, u32[]{:S(2)}) collective-permute-start(bf16[1,28,8,128]{3,2,1,0:T(8,128)(2,1)S(1)} %add_convert_fusion), channel_id=1, source_target_pairs={{0,8},{1,3},{2,10},{3,1},{4,12},{5,7},{6,14},{7,5},{8,0},{9,11},{1... | collective-permute-start | bytes 172040 | tf_op jit(solution)/shard_map/ppermute | solution.py:44
  40.8 4.0 %collective-permute-start.8 = (bf16[2,28,8,128]{3,2,1,0:T(8,128)(2,1)S(1)}, bf16[2,28,8,128]{3,2,1,0:T(8,128)(2,1)S(1)}, u32[]{:S(2)}, u32[]{:S(2)}) collective-permute-start(bf16[2,28,8,128]{3,2,1,0:T(8,128)(2,1)S(1)} %pad_maximum_fusion.4), channel_id=1, source_target_pairs={{0,4},{1,9},{2,6},{3,11},{4,0},{5,13},{6,2},{7,15},{8,12},{9,1},{1... | collective-permute-start | bytes 344072 | tf_op jit(solution)/shard_map/ppermute | solution.py:44
  44.8 10.0 %collective-permute-start.9 = (bf16[4,28,8,128]{3,2,1,0:T(8,128)(2,1)S(1)}, bf16[4,28,8,128]{3,2,1,0:T(8,128)(2,1)S(1)}, u32[]{:S(2)}, u32[]{:S(2)}) collective-permute-start(bf16[4,28,8,128]{3,2,1,0:T(8,128)(2,1)S(1)} %pad_maximum_fusion.2), channel_id=1, source_target_pairs={{0,2},{1,5},{2,0},{3,7},{4,6},{5,1},{6,4},{7,3},{8,10},{9,13},{10,... | collective-permute-start | bytes 688136 | tf_op jit(solution)/shard_map/ppermute | solution.py:44
  46.1 12.9 %collective-permute-start.1 = (f32[2,4,32,128]{3,2,1,0:T(8,128)S(1)}, f32[2,4,32,128]{3,2,1,0:T(8,128)S(1)}, u32[]{:S(2)}, u32[]{:S(2)}) collective-permute-start(f32[2,4,32,128]{3,2,1,0:T(8,128)S(1)} %bitcast.84), channel_id=1, source_target_pairs={{1,0},{2,1},{3,2},{5,4},{6,5},{7,6},{9,8},{10,9},{11,10},{13,12},{... | collective-permute-start | bytes 393224 | tf_op jit(solution)/shard_map/ppermute | solution.py:19
  54.9 4.8 %copy-start.2 = (bf16[8,28,8,128]{3,2,1,0:T(8,128)(2,1)}, bf16[8,28,8,128]{3,2,1,0:T(8,128)(2,1)S(1)}, u32[]{:S(2)}) copy-start(bf16[8,28,8,128]{3,2,1,0:T(8,128)(2,1)S(1)} %pad_maximum_fusion.1.mine_ref) | copy-start | bytes 1376260
  54.9 4.8 %collective-permute-start.10 = (bf16[8,28,8,128]{3,2,1,0:T(8,128)(2,1)S(1)}, bf16[8,28,8,128]{3,2,1,0:T(8,128)(2,1)S(1)}, u32[]{:S(2)}, u32[]{:S(2)}) collective-permute-start(bf16[8,28,8,128]{3,2,1,0:T(8,128)(2,1)S(1)} %pad_maximum_fusion.1.mine_ref), channel_id=1, source_target_pairs={{0,1},{1,0},{2,3},{3,2},{4,5},{5,4},{6,7},{7,6},{8,9},{9,8},{10,11... | collective-permute-start | bytes 1376264 | tf_op jit(solution)/shard_map/ppermute | solution.py:44
  59.7 0.8 %copy-start.5 = (bf16[8,28,8,128]{3,2,1,0:T(8,128)(2,1)}, bf16[8,28,8,128]{3,2,1,0:T(8,128)(2,1)S(1)}, u32[]{:S(2)}) copy-start(bf16[8,28,8,128]{3,2,1,0:T(8,128)(2,1)S(1)} %collective-permute-done.10.other_ref) | copy-start | bytes 1376260

commit v2 on v0

v2 whole, which is shorter than its diff:
```python
import functools
import math

import jax
import jax.numpy as jnp
from jax import lax
from jax.experimental import pallas as pl
from jax.experimental.pallas import tpu as pltpu
from jax.sharding import PartitionSpec as P

AXES = ("dp", "tm")
HALVINGS = 4
ORDERS = ((1, 2, 3), (2, 3, 1))
UNPACK_CHUNK = 7
LIMIT = pltpu.CompilerParams(vmem_limit_bytes=16 * 1024 * 1024)
SCALAR = pl.BlockSpec(memory_space=pltpu.SMEM)
VECTOR = pl.BlockSpec(memory_space=pltpu.VMEM)
ANYWHERE = pl.BlockSpec(memory_space=pl.ANY)


def passed_along(shard, axis, by):
    size = lax.axis_size(axis)
    pairs = [(i, i + by) for i in range(size) if 0 <= i + by < size]
    return lax.ppermute(shard, axis, pairs)


def device_number():
    return lax.axis_index("dp") * lax.axis_size("tm") + lax.axis_index("tm")


def swapped(array, bits):
    count = lax.axis_size("dp") * lax.axis_size("tm")
    return lax.ppermute(array, AXES, [(i, i ^ (1 << bits[i & 1])) for i in range(count)])


def bit(number, place):
    return (number >> place) & 1


def places_of(me, pair):
    offset = (2 * pair) ^ (me & 14)
    first, second = (
        4 * bit(offset, order[0]) + 2 * bit(offset, order[1]) + bit(offset, order[2])
        for order in ORDERS
    )
    core = me & 1
    return jnp.where(core == 0, first, second), jnp.where(core == 0, second, first)


def beside(flat, width):
    rows = flat.shape[0]
    wide = flat.astype(jnp.float32)
    column = lax.broadcasted_iota(jnp.int32, flat.shape, 0) % width
    before = jnp.where(column == 0, 0.0, pltpu.roll(wide, 1, 0)).astype(flat.dtype)
    after = jnp.where(column == width - 1, 0.0, pltpu.roll(wide, rows - 1, 0)).astype(flat.dtype)
    return before, after


def moved_rows(flat, map_rows, width, by):
    zero = jnp.zeros((width, flat.shape[1]), flat.dtype)
    pieces = []
    for start in range(0, flat.shape[0], map_rows):
        whole = flat[start : start + map_rows]
        pieces += [zero, whole[:-width]] if by == 1 else [whole[width:], zero]
    return jnp.concatenate(pieces, axis=0)


def dot(left, right, contract):
    return lax.dot_general(
        left, right, ((contract[:1], contract[1:]), ((), ())), preferred_element_type=jnp.float32
    )


def forward_kernel(
    shape, me_ref, halo_ref, frames_ref, grads_ref, kern_ref, proj_ref,
    keep_ref, send_ref, hidden_ref, pre_grad_ref, wide_ref,
):
    _, height, width, chans = shape
    map_rows = height * width
    rows = shape[0] * map_rows
    halo_rows = 2 * map_rows
    for ref, start in ((halo_ref, 0), (frames_ref, halo_rows)):
        flat = ref[...]
        before, after = beside(flat, width)
        here = slice(start, start + flat.shape[0])
        wide_ref[here, :chans] = before
        wide_ref[here, chans : 2 * chans] = flat
        wide_ref[here, 2 * chans :] = after
    sums = None
    for tau in range(3):
        weights = jnp.concatenate(
            [kern_ref[tau, row].reshape(3 * chans, chans) for row in range(3)], axis=1
        )
        term = dot(wide_ref[tau * map_rows : tau * map_rows + rows], weights, (1, 0))
        sums = term if sums is None else sums + term
    pre = (
        moved_rows(sums[:, :chans], map_rows, width, 1)
        + sums[:, chans : 2 * chans]
        + moved_rows(sums[:, 2 * chans :], map_rows, width, -1)
    )
    sig = jax.nn.sigmoid(pre)
    hidden = (pre * sig).astype(jnp.bfloat16)
    grads = grads_ref[...]
    hidden_grad = dot(grads, proj_ref[...], (1, 1))
    pre_grad = (hidden_grad * sig * (1.0 + pre * (1.0 - sig))).astype(jnp.bfloat16)
    hidden_ref[...] = hidden
    pre_grad_ref[...] = pre_grad
    me = me_ref[0]
    core = me & 1
    places = [places_of(me, pair) for pair in range(8)]

    def put(tap, value):
        for pair in range(8):
            even = value[16 * pair : 16 * pair + 8]
            odd = value[16 * pair + 8 : 16 * pair + 16]
            mine, other = places[pair]
            keep_ref[mine, tap] = jnp.where(core == 0, even, odd)
            send_ref[other, tap] = jnp.where(core == 0, odd, even).astype(send_ref.dtype)

    put(27, dot(hidden, grads, (0, 0)))
    grad_rows = jnp.concatenate(
        [
            moved_rows(pre_grad, map_rows, width, -1),
            pre_grad,
            moved_rows(pre_grad, map_rows, width, 1),
        ],
        axis=1,
    )
    for tau in range(3):
        part = dot(wide_ref[tau * map_rows : tau * map_rows + rows], grad_rows, (0, 0))
        for row in range(3):
            for col in range(3):
                put(
                    tau * 9 + row * 3 + col,
                    part[col * chans : (col + 1) * chans, row * chans : (row + 1) * chans],
                )


def backward_kernel(
    shape, pre_grad_ref, next_ref, hidden_ref, frames_ref, grads_ref, kern_ref, proj_ref,
    mixed_ref, input_grad_ref, wide_ref,
):
    _, height, width, chans = shape
    map_rows = height * width
    rows = shape[0] * map_rows
    for ref, start in ((pre_grad_ref, 0), (next_ref, rows)):
        flat = ref[...]
        before, after = beside(flat, width)
        here = slice(start, start + flat.shape[0])
        wide_ref[here, :chans] = after
        wide_ref[here, chans : 2 * chans] = flat
        wide_ref[here, 2 * chans :] = before
    sums = None
    for tau in range(3):
        weights = jnp.concatenate(
            [kern_ref[tau, :, col].reshape(3 * chans, chans) for col in range(3)], axis=1
        )
        start = (2 - tau) * map_rows
        term = dot(wide_ref[start : start + rows], weights, (1, 1))
        sums = term if sums is None else sums + term
    back = (
        moved_rows(sums[:, :chans], map_rows, width, -1)
        + sums[:, chans : 2 * chans]
        + moved_rows(sums[:, 2 * chans :], map_rows, width, 1)
    )
    input_grad_ref[...] = (grads_ref[...].astype(jnp.float32) + back).astype(jnp.bfloat16)
    mixed_ref[...] = (
        frames_ref[...].astype(jnp.float32) + dot(hidden_ref[...], proj_ref[...], (1, 0))
    ).astype(jnp.bfloat16)


def unpack_kernel(scale, me_ref, mine_ref, other_ref, kern_ref, proj_ref, out_ref, sems):
    me = me_ref[0]
    core = me & 1
    taps = kern_ref.shape[0]
    copies = []
    for first in range(0, taps + 1, UNPACK_CHUNK):
        last = min(first + UNPACK_CHUNK, taps + 1)
        for pair in range(8):
            mine, other = places_of(me, pair)
            mine_rows = pl.ds(pl.multiple_of(16 * pair + 8 * core, 8), 8)
            other_rows = pl.ds(pl.multiple_of(16 * pair + 8 * (1 - core), 8), 8)
            out_ref[first:last, mine_rows, :] = (
                mine_ref[mine, first:last].astype(jnp.float32) * scale
            )
            out_ref[first:last, other_rows, :] = (
                other_ref[other, first:last].astype(jnp.float32) * scale
            )
        inside = min(last, taps)
        copies.append(
            pltpu.make_async_copy(
                out_ref.at[first:inside], kern_ref.at[first:inside], sems.at[len(copies)]
            )
        )
        copies[-1].start()
    copies.append(pltpu.make_async_copy(out_ref.at[taps], proj_ref, sems.at[len(copies)]))
    copies[-1].start()
    for copy in copies:
        copy.wait()


def summed(me, keep, send, scale):
    taps, chans = keep.shape[1] - 1, keep.shape[3]
    rounds = [tuple(order[k] for order in ORDERS) for k in range(3)]
    total = keep + swapped(send, (0, 0)).astype(jnp.float32)
    for bits, link_type in zip(rounds, (jnp.bfloat16, jnp.bfloat16, jnp.float32)):
        rest = total.shape[0] // 2
        came = swapped(total[rest:].astype(link_type), bits)
        total = total[:rest] + came.astype(jnp.float32)
    count = lax.axis_size("dp") * lax.axis_size("tm")
    place = HALVINGS
    while (1 << place) < count:
        total = total + swapped(total, (place, place))
        place += 1
    total = total.astype(jnp.bfloat16)
    for bits in reversed(rounds):
        total = jnp.concatenate([total, swapped(total, bits)], axis=0)
    other = swapped(total, (0, 0))
    return pl.pallas_call(
        functools.partial(unpack_kernel, scale),
        out_shape=(
            jax.ShapeDtypeStruct((taps, chans, chans), jnp.float32),
            jax.ShapeDtypeStruct((chans, chans), jnp.float32),
        ),
        in_specs=[SCALAR, VECTOR, VECTOR],
        out_specs=(ANYWHERE, ANYWHERE),
        scratch_shapes=[
            pltpu.VMEM((taps + 1, chans, chans), jnp.float32),
            pltpu.SemaphoreType.DMA((pl.cdiv(taps + 1, UNPACK_CHUNK) + 1,)),
        ],
        compiler_params=LIMIT,
        name="unpack",
    )(me, total, other)


def forward(shape, me, halo, frames, grads, conv_kernel, proj_weight):
    n_frames, height, width, chans = shape
    rows = n_frames * height * width
    half = (8, 28, 8, chans)
    return pl.pallas_call(
        functools.partial(forward_kernel, shape),
        out_shape=(
            jax.ShapeDtypeStruct(half, jnp.float32),
            jax.ShapeDtypeStruct(half, jnp.float32),
            jax.ShapeDtypeStruct((rows, chans), jnp.bfloat16),
            jax.ShapeDtypeStruct((rows, chans), jnp.bfloat16),
        ),
        in_specs=[SCALAR] + [VECTOR] * 5,
        out_specs=(VECTOR,) * 4,
        scratch_shapes=[pltpu.VMEM((rows + 2 * height * width, 3 * chans), jnp.bfloat16)],
        compiler_params=LIMIT,
        name="forward",
    )(me, halo, frames, grads, conv_kernel, proj_weight)


def backward(shape, pre_grad, following, hidden, frames, grads, conv_kernel, proj_weight):
    n_frames, height, width, chans = shape
    rows = n_frames * height * width
    flops = 2 * rows * 28 * chans * chans
    return pl.pallas_call(
        functools.partial(backward_kernel, shape),
        out_shape=(jax.ShapeDtypeStruct((rows, chans), jnp.bfloat16),) * 2,
        in_specs=[VECTOR] * 7,
        out_specs=(VECTOR,) * 2,
        scratch_shapes=[pltpu.VMEM((rows + 2 * height * width, 3 * chans), jnp.bfloat16)],
        compiler_params=LIMIT,
        cost_estimate=pl.CostEstimate(flops=flops, bytes_accessed=1 << 20, transcendentals=0),
        name="backward",
    )(pre_grad, following, hidden, frames, grads, conv_kernel, proj_weight)


def shards(clip_frames, out_grad, conv_kernel, proj_weight):
    shape = clip_frames.shape[1:]
    n_frames, height, width, chans = shape
    rows = n_frames * height * width
    halo_rows = 2 * height * width
    frames = clip_frames.reshape(rows, chans)
    grads = out_grad.reshape(rows, chans)
    me = device_number().astype(jnp.int32).reshape(1)
    halo = passed_along(frames[rows - halo_rows :], "tm", 1)
    keep, send, hidden, pre_grad = forward(
        shape, me, halo, frames, grads, conv_kernel, proj_weight
    )
    following = passed_along(pre_grad[:halo_rows], "tm", -1)
    mixed, input_grad = backward(
        shape, pre_grad, following, hidden, frames, grads, conv_kernel, proj_weight
    )
    total_pixels = lax.axis_size("dp") * lax.axis_size("tm") * rows
    kernel_grad, proj_grad = summed(me, keep, send, 1.0 / math.sqrt(total_pixels))
    return (
        mixed.reshape(clip_frames.shape),
        input_grad.reshape(clip_frames.shape),
        kernel_grad.reshape(conv_kernel.shape),
        proj_grad,
    )


def solution(mesh):
    placed = (P("dp", "tm", None, None, None), P("dp", "tm", None, None, None), P(), P())
    return jax.shard_map(
        shards,
        mesh=mesh,
        in_specs=placed,
        out_specs=(P("dp", "tm", None, None, None), P("dp", "tm", None, None, None), P(), P()),
        check_vma=False,
    )
```

time: 173 us -> 61.8 us (0.36)
  waiting for transfers between devices: 126 us -> 26.3 us
  starting transfers between devices: 6.6 us -> 26.8 us
  between operations: 14.3 us -> 0.77 us
  local copies, waits for them, and re-layouts: 12.3 us -> 3.69 us
  matrix products: 6.55 us -> 0 us
  other arithmetic: 5.52 us -> 0.32 us
  Pallas kernels: 0 us -> 3.6 us
    psum x1 -> x0, waiting for transfers between devices: 121 us -> none  [shards(): kern_sum, proj_sum = lax.psum((kern_part, proj_part), ('dp', 'tm'))]
    ppermute x0 -> x9, waiting for transfers between devices: none -> 21 us  [swapped(): lax.ppermute(array, AXES, [(i, i ^ 1 << bits[i & 1]) for i in range(count)])]
    ppermute x0 -> x9, starting transfers between devices: none -> 20.3 us  [swapped(): lax.ppermute(array, AXES, [(i, i ^ 1 << bits[i & 1]) for i in range(count)])]
    dot_general x12 -> x0, matrix products: 6.55 us -> none  [the longest x3 2.7 us: shards(): jnp.dot(piece, kern_flip[offset], preferred_element_type=jnp.float32)]
    unnamed x41 -> x16, local copies, waits for them, and re-layouts: 9.07 us -> 3.63 us
    pallas_call x0 -> x3, Pallas kernels: none -> 3.6 us  [the longest x1 1.33 us: summed(): pl.pallas_call(functools.partial(unpack_kernel, scale), out_shape=(jax.Sh...]
    mul x2 -> x0, other arithmetic: 3.5 us -> none  [the longest x1 2.87 us: shards(): kernel_grad = (kern_sum * scale).reshape(3, 3, 3, chans, chans)]
    slice x5 -> x3, local copies, waits for them, and re-layouts: 2.25 us -> 0.06 us  [summed(): came = swapped(total[rest:].astype(link_type), bits)]
  transfers between devices with their start and end apart: 3 -> 11, of which waited for: 2 -> 10; matrix products, arithmetic and copies ran while one was open for 4% -> 0% of each run, Pallas kernels for 0% -> 2%
where the time goes in v2:
time: 61.8 us; the launch traced here: 61.4 us
  starting transfers between devices  26.8 us (43%)
  waiting for transfers between devices  26.3 us (43%)
  local copies, waits for them, and re-layouts  3.69 us (6%)
  Pallas kernels  3.6 us (6%)
  between operations  0.77 us (1%)
    ppermute x9, waiting for transfers between devices, swapped(): lax.ppermute(array, AXES, [(i, i ^ 1 << bits[i & 1]) for i in range(count)])  21 us
    ppermute x9, starting transfers between devices, swapped(): lax.ppermute(array, AXES, [(i, i ^ 1 << bits[i & 1]) for i in range(count)])  20.3 us
    ppermute x2, starting transfers between devices, passed_along(): return lax.ppermute(shard, axis, pairs)  6.43 us
    ppermute x2, waiting for transfers between devices, passed_along(): return lax.ppermute(shard, axis, pairs)  5.26 us
    unnamed x16, local copies, waits for them, and re-layouts  3.63 us
    pallas_call x1, Pallas kernels, summed(): pl.pallas_call(functools.partial(unpack_kernel, scale), out_shape=(jax.Sh...  1.33 us
  transfers between devices with their start and end apart: 11, of which 10 were waited for; matrix products, arithmetic and copies ran while one was open for 0% of the time, Pallas kernels for 2%

profile of v2, /device:TPU:1, one launch (start us, length us, event | category | flops | bytes accessed | tf_op | source)
XLA Modules:
  0.0 61.4 jit_solution(7832677272146825507)
XLA Ops:
  0.6 4.5 %collective-permute-start = (bf16[256,128]{1,0:T(8,128)(2,1)}, bf16[256,128]{1,0:T(8,128)(2,1)S(1)}, u32[]{:S(2)}, u32[]{:S(2)}) collective-permute-start(bf16[256,128]{1,0:T(8,128)(2,1)} %bitcast.6), channel_id=1, source_target_pairs={{0,1},{1,2},{2,3},{4,5},{5,6},{6,7},{8,9},{9,10},{10,11},{12,13},{... | collective-permute-start | bytes 196616 | tf_op jit(solution)/shard_map/ppermute | solution.py:24
  5.2 1.6 %collective-permute-done.halo_ref = bf16[256,128]{1,0:T(8,128)(2,1)S(1)} collective-permute-done((bf16[256,128]{1,0:T(8,128)(2,1)}, bf16[256,128]{1,0:T(8,128)(2,1)S(1)}, u32[]{:S(2)}, u32[]{:S(2)}) %collective-permute-start) | collective-permute-done | bytes 65568 | tf_op jit(solution)/shard_map/ppermute | solution.py:24
  6.8 0.0 copy-start
  6.8 1.2 %copy-done = bf16[3,3,3,128,128]{4,3,2,1,0:T(8,128)(2,1)S(1)} copy-done((bf16[3,3,3,128,128]{4,3,2,1,0:T(8,128)(2,1)S(1)}, bf16[3,3,3,128,128]{4,3,2,1,0:T(8,128)(2,1)}, u32[]{:S(2)}) %copy-start) | copy-done | bytes 884760
  7.9 0.0 copy-start.2
  7.9 0.8 %copy-done.2 = bf16[1,2,4,32,128]{4,3,2,1,0:T(8,128)(2,1)S(1)} copy-done((bf16[1,2,4,32,128]{4,3,2,1,0:T(8,128)(2,1)S(1)}, bf16[1,2,4,32,128]{4,3,2,1,0:T(8,128)(2,1)}, u32[]{:S(2)}) %copy-start.2) | copy-done | bytes 65560
  8.8 0.0 copy-start.4
  8.8 0.8 %copy-done.4 = bf16[1,2,4,32,128]{4,3,2,1,0:T(8,128)(2,1)S(1)} copy-done((bf16[1,2,4,32,128]{4,3,2,1,0:T(8,128)(2,1)S(1)}, bf16[1,2,4,32,128]{4,3,2,1,0:T(8,128)(2,1)}, u32[]{:S(2)}) %copy-start.4) | copy-done | bytes 65560
  9.6 0.0 copy-start.6
  9.6 0.8 %copy-done.6 = bf16[128,128]{1,0:T(8,128)(2,1)S(1)} copy-done((bf16[128,128]{1,0:T(8,128)(2,1)S(1)}, bf16[128,128]{1,0:T(8,128)(2,1)}, u32[]{:S(2)}) %copy-start.6) | copy-done | bytes 32792
  10.4 1.1 %forward.1 = (f32[8,28,8,128]{3,2,1,0:T(8,128)S(1)}, f32[8,28,8,128]{3,2,1,0:T(8,128)S(1)}, bf16[256,128]{1,0:T(8,128)(2,1)S(1)}, bf16[256,128]{1,0:T(8,128)(2,1)S(1)}) custom-call(s32[1]{0:T(128)} %bitcast.me_ref, bf16[256,128]{1,0:T(8,128)(2,1)S(1)} %collective-permute-done.halo_ref, bf16[256,128]{1,0:T(8,128)(2,1)S(1)} %bitcast.7, ...), custom_call_target="tpu_custom_call" | custom-call | tf_op jit(solution)/shard_map/forward/pallas_call | solution.py:240
  11.5 0.1 collective-permute-start.2
  11.5 2.5 %collective-permute-done.2 = f32[8,28,8,128]{3,2,1,0:T(8,128)S(1)} collective-permute-done((f32[8,28,8,128]{3,2,1,0:T(8,128)S(1)}, f32[8,28,8,128]{3,2,1,0:T(8,128)S(1)}, u32[]{:S(2)}, u32[]{:S(2)}) %collective-permute-start.2) | collective-permute-done | bytes 917536 | tf_op jit(solution)/shard_map/ppermute | solution.py:33
  14.0 0.1 add.19
  14.2 1.3 %collective-permute-start.3 = (bf16[4,28,8,128]{3,2,1,0:T(8,128)(2,1)S(1)}, bf16[4,28,8,128]{3,2,1,0:T(8,128)(2,1)S(1)}, u32[]{:S(2)}, u32[]{:S(2)}) collective-permute-start(bf16[4,28,8,128]{3,2,1,0:T(8,128)(2,1)S(1)} %slice.37), channel_id=1, source_target_pairs={{0,2},{1,5},{2,0},{3,7},{4,6},{5,1},{6,4},{7,3},{8,10},{9,13},{10,... | collective-permute-start | bytes 688136 | tf_op jit(solution)/shard_map/ppermute | solution.py:33
  15.5 3.9 %collective-permute-done.3 = bf16[4,28,8,128]{3,2,1,0:T(8,128)(2,1)S(1)} collective-permute-done((bf16[4,28,8,128]{3,2,1,0:T(8,128)(2,1)S(1)}, bf16[4,28,8,128]{3,2,1,0:T(8,128)(2,1)S(1)}, u32[]{:S(2)}, u32[]{:S(2)}) %collective-permute-start.3) | collective-permute-done | bytes 229408 | tf_op jit(solution)/shard_map/ppermute | solution.py:33
  19.4 0.1 slice_add_fusion
  19.4 0.0 copy-start.1
  19.5 0.0 copy-start.3
  19.5 0.0 copy-start.5
  19.5 0.0 copy-start.7
  19.5 1.4 %collective-permute-start.4 = (bf16[2,28,8,128]{3,2,1,0:T(8,128)(2,1)S(1)}, bf16[2,28,8,128]{3,2,1,0:T(8,128)(2,1)S(1)}, u32[]{:S(2)}, u32[]{:S(2)}) collective-permute-start(bf16[2,28,8,128]{3,2,1,0:T(8,128)(2,1)S(1)} %slice.38), channel_id=1, source_target_pairs={{0,4},{1,9},{2,6},{3,11},{4,0},{5,13},{6,2},{7,15},{8,12},{9,1},{1... | collective-permute-start | bytes 344072 | tf_op jit(solution)/shard_map/ppermute | solution.py:33
  20.9 2.3 %collective-permute-done.4 = bf16[2,28,8,128]{3,2,1,0:T(8,128)(2,1)S(1)} collective-permute-done((bf16[2,28,8,128]{3,2,1,0:T(8,128)(2,1)S(1)}, bf16[2,28,8,128]{3,2,1,0:T(8,128)(2,1)S(1)}, u32[]{:S(2)}, u32[]{:S(2)}) %collective-permute-start.4) | collective-permute-done | bytes 114720 | tf_op jit(solution)/shard_map/ppermute | solution.py:33
  23.3 2.1 %collective-permute-start.5 = (f32[1,28,8,128]{3,2,1,0:T(8,128)S(1)}, f32[1,28,8,128]{3,2,1,0:T(8,128)S(1)}, u32[]{:S(2)}, u32[]{:S(2)}) collective-permute-start(f32[1,28,8,128]{3,2,1,0:T(8,128)S(1)} %slice.31), channel_id=1, source_target_pairs={{0,8},{1,3},{2,10},{3,1},{4,12},{5,7},{6,14},{7,5},{8,0},{9,11},{1... | collective-permute-start | bytes 344072 | tf_op jit(solution)/shard_map/ppermute | solution.py:33
  25.3 2.2 %collective-permute-done.5 = f32[1,28,8,128]{3,2,1,0:T(8,128)S(1)} collective-permute-done((f32[1,28,8,128]{3,2,1,0:T(8,128)S(1)}, f32[1,28,8,128]{3,2,1,0:T(8,128)S(1)}, u32[]{:S(2)}, u32[]{:S(2)}) %collective-permute-start.5) | collective-permute-done | bytes 114720 | tf_op jit(solution)/shard_map/ppermute | solution.py:33
  27.5 2.4 %collective-permute-start.6 = (f32[1,28,8,128]{3,2,1,0:T(8,128)S(1)}, f32[1,28,8,128]{3,2,1,0:T(8,128)S(1)}, u32[]{:S(2)}, u32[]{:S(2)}) collective-permute-start(f32[1,28,8,128]{3,2,1,0:T(8,128)S(1)} %slice_add_fusion.2), channel_id=1, source_target_pairs={{0,16},{1,17},{2,18},{3,19},{4,20},{5,21},{6,22},{7,23},{8,24},{9,... | collective-permute-start | bytes 344072 | tf_op jit(solution)/shard_map/ppermute | solution.py:33
  29.9 2.4 %collective-permute-done.6 = f32[1,28,8,128]{3,2,1,0:T(8,128)S(1)} collective-permute-done((f32[1,28,8,128]{3,2,1,0:T(8,128)S(1)}, f32[1,28,8,128]{3,2,1,0:T(8,128)S(1)}, u32[]{:S(2)}, u32[]{:S(2)}) %collective-permute-start.6) | collective-permute-done | bytes 114720 | tf_op jit(solution)/shard_map/ppermute | solution.py:33
  32.3 1.6 %collective-permute-start.7 = (bf16[1,28,8,128]{3,2,1,0:T(8,128)(2,1)S(1)}, bf16[1,28,8,128]{3,2,1,0:T(8,128)(2,1)S(1)}, u32[]{:S(2)}, u32[]{:S(2)}) collective-permute-start(bf16[1,28,8,128]{3,2,1,0:T(8,128)(2,1)S(1)} %add_convert_fusion), channel_id=1, source_target_pairs={{0,8},{1,3},{2,10},{3,1},{4,12},{5,7},{6,14},{7,5},{8,0},{9,11},{1... | collective-permute-start | bytes 172040 | tf_op jit(solution)/shard_map/ppermute | solution.py:33
  33.9 1.9 %collective-permute-done.7 = bf16[1,28,8,128]{3,2,1,0:T(8,128)(2,1)S(1)} collective-permute-done((bf16[1,28,8,128]{3,2,1,0:T(8,128)(2,1)S(1)}, bf16[1,28,8,128]{3,2,1,0:T(8,128)(2,1)S(1)}, u32[]{:S(2)}, u32[]{:S(2)}) %collective-permute-start.7) | collective-permute-done | bytes 57376 | tf_op jit(solution)/shard_map/ppermute | solution.py:33
  35.8 1.7 %collective-permute-start.8 = (bf16[2,28,8,128]{3,2,1,0:T(8,128)(2,1)S(1)}, bf16[2,28,8,128]{3,2,1,0:T(8,128)(2,1)S(1)}, u32[]{:S(2)}, u32[]{:S(2)}) collective-permute-start(bf16[2,28,8,128]{3,2,1,0:T(8,128)(2,1)S(1)} %pad_maximum_fusion.2), channel_id=1, source_target_pairs={{0,4},{1,9},{2,6},{3,11},{4,0},{5,13},{6,2},{7,15},{8,12},{9,1},{1... | collective-permute-start | bytes 344072 | tf_op jit(solution)/shard_map/ppermute | solution.py:33
  37.5 2.2 %collective-permute-done.8 = bf16[2,28,8,128]{3,2,1,0:T(8,128)(2,1)S(1)} collective-permute-done((bf16[2,28,8,128]{3,2,1,0:T(8,128)(2,1)S(1)}, bf16[2,28,8,128]{3,2,1,0:T(8,128)(2,1)S(1)}, u32[]{:S(2)}, u32[]{:S(2)}) %collective-permute-start.8) | collective-permute-done | bytes 114720 | tf_op jit(solution)/shard_map/ppermute | solution.py:33
  39.8 1.3 %collective-permute-start.9 = (bf16[4,28,8,128]{3,2,1,0:T(8,128)(2,1)S(1)}, bf16[4,28,8,128]{3,2,1,0:T(8,128)(2,1)S(1)}, u32[]{:S(2)}, u32[]{:S(2)}) collective-permute-start(bf16[4,28,8,128]{3,2,1,0:T(8,128)(2,1)S(1)} %pad_maximum_fusion.1), channel_id=1, source_target_pairs={{0,2},{1,5},{2,0},{3,7},{4,6},{5,1},{6,4},{7,3},{8,10},{9,13},{10,... | collective-permute-start | bytes 688136 | tf_op jit(solution)/shard_map/ppermute | solution.py:33
  41.1 3.6 %collective-permute-done.9 = bf16[4,28,8,128]{3,2,1,0:T(8,128)(2,1)S(1)} collective-permute-done((bf16[4,28,8,128]{3,2,1,0:T(8,128)(2,1)S(1)}, bf16[4,28,8,128]{3,2,1,0:T(8,128)(2,1)S(1)}, u32[]{:S(2)}, u32[]{:S(2)}) %collective-permute-start.9) | collective-permute-done | bytes 229408 | tf_op jit(solution)/shard_map/ppermute | solution.py:33
  44.7 8.5 %collective-permute-start.10 = (bf16[8,28,8,128]{3,2,1,0:T(8,128)(2,1)S(1)}, bf16[8,28,8,128]{3,2,1,0:T(8,128)(2,1)S(1)}, u32[]{:S(2)}, u32[]{:S(2)}) collective-permute-start(bf16[8,28,8,128]{3,2,1,0:T(8,128)(2,1)S(1)} %pad_maximum_fusion.mine_ref), channel_id=1, source_target_pairs={{0,1},{1,0},{2,3},{3,2},{4,5},{5,4},{6,7},{7,6},{8,9},{9,8},{10,11... | collective-permute-start | bytes 1376264 | tf_op jit(solution)/shard_map/ppermute | solution.py:33
  53.3 1.9 %collective-permute-start.1 = (bf16[256,128]{1,0:T(8,128)(2,1)S(1)}, bf16[256,128]{1,0:T(8,128)(2,1)S(1)}, u32[]{:S(2)}, u32[]{:S(2)}) collective-permute-start(bf16[256,128]{1,0:T(8,128)(2,1)S(1)} %get-tuple-element.12.pre_grad_ref), channel_id=1, source_target_pairs={{1,0},{2,1},{3,2},{5,4},{6,5},{7,6},{9,8},{10,9},{11,10},{13,12},{... | collective-permute-start | bytes 196616 | tf_op jit(solution)/shard_map/ppermute | solution.py:24
  55.2 3.6 %collective-permute-done.1.next_ref = bf16[256,128]{1,0:T(8,128)(2,1)S(1)} collective-permute-done((bf16[256,128]{1,0:T(8,128)(2,1)S(1)}, bf16[256,128]{1,0:T(8,128)(2,1)S(1)}, u32[]{:S(2)}, u32[]{:S(2)}) %collective-permute-start.1) | collective-permute-done | bytes 65568 | tf_op jit(solution)/shard_map/ppermute | solution.py:24
  58.9 0.0 copy-done.1
  58.9 0.0 copy-done.3
  58.9 0.0 copy-done.5
  58.9 0.0 copy-done.7
  58.9 1.2 %backward.1 = (bf16[256,128]{1,0:T(8,128)(2,1)}, bf16[256,128]{1,0:T(8,128)(2,1)}) custom-call(bf16[256,128]{1,0:T(8,128)(2,1)S(1)} %get-tuple-element.12.pre_grad_ref, bf16[256,128]{1,0:T(8,128)(2,1)S(1)} %collective-permute-done.1.next_ref, bf16[256,128]{1,0:T(8,128)(2,1)S(1)} %get-tuple-element.13.hidden_ref, bf16[256,128]{1,0:T(8,128)(2,1)S(1)} %bitcast.8, ...), custom_call_target="tpu_custom_call" | custom-call | flops 234881024 | bytes 1048576 | tf_op jit(solution)/shard_map/backward/pallas_call | solution.py:260
  60.1 0.0 collective-permute-done.10.other_ref
  60.1 1.3 %unpack.1 = (f32[27,128,128]{2,1,0:T(8,128)}, f32[128,128]{1,0:T(8,128)}) custom-call(s32[1]{0:T(128)} %bitcast.me_ref, bf16[8,28,8,128]{3,2,1,0:T(8,128)(2,1)S(1)} %pad_maximum_fusion.mine_ref, bf16[8,28,8,128]{3,2,1,0:T(8,128)(2,1)S(1)} %collective-permute-done.10.other_ref), custom_call_target="tpu_custom_call" | custom-call | tf_op jit(solution)/shard_map/unpack/pallas_call | solution.py:219
  (9 shorter events, 0.2 us)
Async XLA Ops:
  0.6 6.1 %collective-permute-start = (bf16[256,128]{1,0:T(8,128)(2,1)}, bf16[256,128]{1,0:T(8,128)(2,1)S(1)}, u32[]{:S(2)}, u32[]{:S(2)}) collective-permute-start(bf16[256,128]{1,0:T(8,128)(2,1)} %bitcast.6), channel_id=1, source_target_pairs={{0,1},{1,2},{2,3},{4,5},{5,6},{6,7},{8,9},{9,10},{10,11},{12,13},{... | collective-permute-start | bytes 196616 | tf_op jit(solution)/shard_map/ppermute | solution.py:24
  6.8 1.2 %copy-start = (bf16[3,3,3,128,128]{4,3,2,1,0:T(8,128)(2,1)S(1)}, bf16[3,3,3,128,128]{4,3,2,1,0:T(8,128)(2,1)}, u32[]{:S(2)}) copy-start(bf16[3,3,3,128,128]{4,3,2,1,0:T(8,128)(2,1)} %kern_ref.3) | copy-start | bytes 2654212
  7.9 0.8 %copy-start.2 = (bf16[1,2,4,32,128]{4,3,2,1,0:T(8,128)(2,1)S(1)}, bf16[1,2,4,32,128]{4,3,2,1,0:T(8,128)(2,1)}, u32[]{:S(2)}) copy-start(bf16[1,2,4,32,128]{4,3,2,1,0:T(8,128)(2,1)} %param.4) | copy-start | bytes 196612
  8.8 0.8 %copy-start.4 = (bf16[1,2,4,32,128]{4,3,2,1,0:T(8,128)(2,1)S(1)}, bf16[1,2,4,32,128]{4,3,2,1,0:T(8,128)(2,1)}, u32[]{:S(2)}) copy-start(bf16[1,2,4,32,128]{4,3,2,1,0:T(8,128)(2,1)} %param.5) | copy-start | bytes 196612
  9.6 0.8 %copy-start.6 = (bf16[128,128]{1,0:T(8,128)(2,1)S(1)}, bf16[128,128]{1,0:T(8,128)(2,1)}, u32[]{:S(2)}) copy-start(bf16[128,128]{1,0:T(8,128)(2,1)} %proj_ref.3) | copy-start | bytes 98308
  11.5 2.5 %collective-permute-start.2 = (f32[8,28,8,128]{3,2,1,0:T(8,128)S(1)}, f32[8,28,8,128]{3,2,1,0:T(8,128)S(1)}, u32[]{:S(2)}, u32[]{:S(2)}) collective-permute-start(f32[8,28,8,128]{3,2,1,0:T(8,128)S(1)} %get-tuple-element.17), channel_id=1, source_target_pairs={{0,1},{1,0},{2,3},{3,2},{4,5},{5,4},{6,7},{7,6},{8,9},{9,8},{10,11... | collective-permute-start | bytes 2752520 | tf_op jit(solution)/shard_map/ppermute | solution.py:33
  14.2 5.2 %collective-permute-start.3 = (bf16[4,28,8,128]{3,2,1,0:T(8,128)(2,1)S(1)}, bf16[4,28,8,128]{3,2,1,0:T(8,128)(2,1)S(1)}, u32[]{:S(2)}, u32[]{:S(2)}) collective-permute-start(bf16[4,28,8,128]{3,2,1,0:T(8,128)(2,1)S(1)} %slice.37), channel_id=1, source_target_pairs={{0,2},{1,5},{2,0},{3,7},{4,6},{5,1},{6,4},{7,3},{8,10},{9,13},{10,... | collective-permute-start | bytes 688136 | tf_op jit(solution)/shard_map/ppermute | solution.py:33
  19.4 39.4 %copy-start.1 = (bf16[3,3,3,128,128]{4,3,2,1,0:T(8,128)(2,1)S(1)}, bf16[3,3,3,128,128]{4,3,2,1,0:T(8,128)(2,1)}, u32[]{:S(2)}) copy-start(bf16[3,3,3,128,128]{4,3,2,1,0:T(8,128)(2,1)} %kern_ref.3) | copy-start | bytes 2654212
  19.5 39.4 %copy-start.3 = (bf16[1,2,4,32,128]{4,3,2,1,0:T(8,128)(2,1)S(1)}, bf16[1,2,4,32,128]{4,3,2,1,0:T(8,128)(2,1)}, u32[]{:S(2)}) copy-start(bf16[1,2,4,32,128]{4,3,2,1,0:T(8,128)(2,1)} %param.4) | copy-start | bytes 196612
  19.5 39.4 %copy-start.5 = (bf16[1,2,4,32,128]{4,3,2,1,0:T(8,128)(2,1)S(1)}, bf16[1,2,4,32,128]{4,3,2,1,0:T(8,128)(2,1)}, u32[]{:S(2)}) copy-start(bf16[1,2,4,32,128]{4,3,2,1,0:T(8,128)(2,1)} %param.5) | copy-start | bytes 196612
  19.5 39.4 %copy-start.7 = (bf16[128,128]{1,0:T(8,128)(2,1)S(1)}, bf16[128,128]{1,0:T(8,128)(2,1)}, u32[]{:S(2)}) copy-start(bf16[128,128]{1,0:T(8,128)(2,1)} %proj_ref.3) | copy-start | bytes 98308
  19.5 3.7 %collective-permute-start.4 = (bf16[2,28,8,128]{3,2,1,0:T(8,128)(2,1)S(1)}, bf16[2,28,8,128]{3,2,1,0:T(8,128)(2,1)S(1)}, u32[]{:S(2)}, u32[]{:S(2)}) collective-permute-start(bf16[2,28,8,128]{3,2,1,0:T(8,128)(2,1)S(1)} %slice.38), channel_id=1, source_target_pairs={{0,4},{1,9},{2,6},{3,11},{4,0},{5,13},{6,2},{7,15},{8,12},{9,1},{1... | collective-permute-start | bytes 344072 | tf_op jit(solution)/shard_map/ppermute | solution.py:33
  23.3 4.2 %collective-permute-start.5 = (f32[1,28,8,128]{3,2,1,0:T(8,128)S(1)}, f32[1,28,8,128]{3,2,1,0:T(8,128)S(1)}, u32[]{:S(2)}, u32[]{:S(2)}) collective-permute-start(f32[1,28,8,128]{3,2,1,0:T(8,128)S(1)} %slice.31), channel_id=1, source_target_pairs={{0,8},{1,3},{2,10},{3,1},{4,12},{5,7},{6,14},{7,5},{8,0},{9,11},{1... | collective-permute-start | bytes 344072 | tf_op jit(solution)/shard_map/ppermute | solution.py:33
  27.5 4.8 %collective-permute-start.6 = (f32[1,28,8,128]{3,2,1,0:T(8,128)S(1)}, f32[1,28,8,128]{3,2,1,0:T(8,128)S(1)}, u32[]{:S(2)}, u32[]{:S(2)}) collective-permute-start(f32[1,28,8,128]{3,2,1,0:T(8,128)S(1)} %slice_add_fusion.2), channel_id=1, source_target_pairs={{0,16},{1,17},{2,18},{3,19},{4,20},{5,21},{6,22},{7,23},{8,24},{9,... | collective-permute-start | bytes 344072 | tf_op jit(solution)/shard_map/ppermute | solution.py:33
  32.3 3.4 %collective-permute-start.7 = (bf16[1,28,8,128]{3,2,1,0:T(8,128)(2,1)S(1)}, bf16[1,28,8,128]{3,2,1,0:T(8,128)(2,1)S(1)}, u32[]{:S(2)}, u32[]{:S(2)}) collective-permute-start(bf16[1,28,8,128]{3,2,1,0:T(8,128)(2,1)S(1)} %add_convert_fusion), channel_id=1, source_target_pairs={{0,8},{1,3},{2,10},{3,1},{4,12},{5,7},{6,14},{7,5},{8,0},{9,11},{1... | collective-permute-start | bytes 172040 | tf_op jit(solution)/shard_map/ppermute | solution.py:33
  35.8 3.9 %collective-permute-start.8 = (bf16[2,28,8,128]{3,2,1,0:T(8,128)(2,1)S(1)}, bf16[2,28,8,128]{3,2,1,0:T(8,128)(2,1)S(1)}, u32[]{:S(2)}, u32[]{:S(2)}) collective-permute-start(bf16[2,28,8,128]{3,2,1,0:T(8,128)(2,1)S(1)} %pad_maximum_fusion.2), channel_id=1, source_target_pairs={{0,4},{1,9},{2,6},{3,11},{4,0},{5,13},{6,2},{7,15},{8,12},{9,1},{1... | collective-permute-start | bytes 344072 | tf_op jit(solution)/shard_map/ppermute | solution.py:33
  39.8 4.9 %collective-permute-start.9 = (bf16[4,28,8,128]{3,2,1,0:T(8,128)(2,1)S(1)}, bf16[4,28,8,128]{3,2,1,0:T(8,128)(2,1)S(1)}, u32[]{:S(2)}, u32[]{:S(2)}) collective-permute-start(bf16[4,28,8,128]{3,2,1,0:T(8,128)(2,1)S(1)} %pad_maximum_fusion.1), channel_id=1, source_target_pairs={{0,2},{1,5},{2,0},{3,7},{4,6},{5,1},{6,4},{7,3},{8,10},{9,13},{10,... | collective-permute-start | bytes 688136 | tf_op jit(solution)/shard_map/ppermute | solution.py:33
  44.7 15.3 %collective-permute-start.10 = (bf16[8,28,8,128]{3,2,1,0:T(8,128)(2,1)S(1)}, bf16[8,28,8,128]{3,2,1,0:T(8,128)(2,1)S(1)}, u32[]{:S(2)}, u32[]{:S(2)}) collective-permute-start(bf16[8,28,8,128]{3,2,1,0:T(8,128)(2,1)S(1)} %pad_maximum_fusion.mine_ref), channel_id=1, source_target_pairs={{0,1},{1,0},{2,3},{3,2},{4,5},{5,4},{6,7},{7,6},{8,9},{9,8},{10,11... | collective-permute-start | bytes 1376264 | tf_op jit(solution)/shard_map/ppermute | solution.py:33
  53.3 5.6 %collective-permute-start.1 = (bf16[256,128]{1,0:T(8,128)(2,1)S(1)}, bf16[256,128]{1,0:T(8,128)(2,1)S(1)}, u32[]{:S(2)}, u32[]{:S(2)}) collective-permute-start(bf16[256,128]{1,0:T(8,128)(2,1)S(1)} %get-tuple-element.12.pre_grad_ref), channel_id=1, source_target_pairs={{1,0},{2,1},{3,2},{5,4},{6,5},{7,6},{9,8},{10,9},{11,10},{13,12},{... | collective-permute-start | bytes 196616 | tf_op jit(solution)/shard_map/ppermute | solution.py:24

commit v3 on v2

--- a/solution.py
+++ b/solution.py
@@ -9,13 +9,12 @@
 from jax.sharding import PartitionSpec as P
 
 AXES = ("dp", "tm")
-HALVINGS = 4
-ORDERS = ((1, 2, 3), (2, 3, 1))
+ORDERS = ((1, 2, 3, 4), (2, 3, 4, 1))
 UNPACK_CHUNK = 7
 LIMIT = pltpu.CompilerParams(vmem_limit_bytes=16 * 1024 * 1024)
 SCALAR = pl.BlockSpec(memory_space=pltpu.SMEM)
 VECTOR = pl.BlockSpec(memory_space=pltpu.VMEM)
-ANYWHERE = pl.BlockSpec(memory_space=pl.ANY)
+OUTSIDE = pl.BlockSpec(memory_space=pltpu.HBM)
 
 
 def passed_along(shard, axis, by):
@@ -33,14 +32,9 @@
     return lax.ppermute(array, AXES, [(i, i ^ (1 << bits[i & 1])) for i in range(count)])
 
 
-def bit(number, place):
-    return (number >> place) & 1
-
-
-def places_of(me, pair):
-    offset = (2 * pair) ^ (me & 14)
+def halves_of(me):
     first, second = (
-        4 * bit(offset, order[0]) + 2 * bit(offset, order[1]) + bit(offset, order[2])
+        4 * ((me >> order[0]) & 1) + 2 * ((me >> order[1]) & 1) + ((me >> order[2]) & 1)
         for order in ORDERS
     )
     core = me & 1
@@ -71,28 +65,65 @@
     )
 
 
+def spread(flat, width, wide_ref, flipped=False):
+    chans = flat.shape[1]
+    before, after = beside(flat, width)
+    wide_ref[:, :chans] = after if flipped else before
+    wide_ref[:, chans : 2 * chans] = flat
+    wide_ref[:, 2 * chans :] = before if flipped else after
+
+
+def weights_of(kern_ref, tau):
+    chans = kern_ref.shape[-1]
+    return jnp.concatenate(
+        [kern_ref[tau, row].reshape(3 * chans, chans) for row in range(3)], axis=1
+    )
+
+
+def prepare_kernel(
+    shape, frames_hbm, grads_hbm, kern_hbm, proj_hbm,
+    frames_ref, grads_ref, kern_ref, proj_ref, wide_ref, sums_ref, hidden_grad_ref, sems,
+):
+    _, height, width, chans = shape
+    map_rows = height * width
+    rows = shape[0] * map_rows
+    pairs = (
+        (frames_hbm, frames_ref), (kern_hbm, kern_ref), (grads_hbm, grads_ref), (proj_hbm, proj_ref)
+    )
+    copies = [pltpu.make_async_copy(*pair, sems.at[i]) for i, pair in enumerate(pairs)]
+    for copy in copies:
+        copy.start()
+    copies[0].wait()
+    spread(frames_ref[...], width, wide_ref)
+    copies[1].wait()
+    sums_ref[...] = dot(wide_ref[...], weights_of(kern_ref, 2), (1, 0))
+    for tau in range(2):
+        skip = (2 - tau) * map_rows
+        if skip < rows:
+            sums_ref[skip:] += dot(wide_ref[: rows - skip], weights_of(kern_ref, tau), (1, 0))
+    copies[2].wait()
+    copies[3].wait()
+    hidden_grad_ref[...] = dot(grads_ref[...], proj_ref[...], (1, 1))
+
+
 def forward_kernel(
-    shape, me_ref, halo_ref, frames_ref, grads_ref, kern_ref, proj_ref,
+    shape, me_ref, halo_ref, grads_ref, kern_ref, own_ref, sums_ref, hidden_grad_ref,
     keep_ref, send_ref, hidden_ref, pre_grad_ref, wide_ref,
 ):
     _, height, width, chans = shape
     map_rows = height * width
     rows = shape[0] * map_rows
-    halo_rows = 2 * map_rows
-    for ref, start in ((halo_ref, 0), (frames_ref, halo_rows)):
-        flat = ref[...]
-        before, after = beside(flat, width)
-        here = slice(start, start + flat.shape[0])
-        wide_ref[here, :chans] = before
-        wide_ref[here, chans : 2 * chans] = flat
-        wide_ref[here, 2 * chans :] = after
-    sums = None
-    for tau in range(3):
-        weights = jnp.concatenate(
-            [kern_ref[tau, row].reshape(3 * chans, chans) for row in range(3)], axis=1
+    spread(halo_ref[...], width, wide_ref)
+    term = dot(wide_ref[...], weights_of(kern_ref, 0), (1, 0))
+    early = dot(wide_ref[map_rows:], weights_of(kern_ref, 1), (1, 0))
+    head = jnp.concatenate([term[:map_rows] + early, term[map_rows:]], axis=0)
+    sums = sums_ref[...]
+    if rows > 2 * map_rows:
+        sums = jnp.concatenate(
+            [sums[: 2 * map_rows] + head, sums[2 * map_rows :]], axis=0
         )
-        term = dot(wide_ref[tau * map_rows : tau * map_rows + rows], weights, (1, 0))
-        sums = term if sums is None else sums + term
+    else:
+        sums = sums + head
     pre = (
         moved_rows(sums[:, :chans], map_rows, width, 1)
         + sums[:, chans : 2 * chans]
@@ -101,21 +132,19 @@
     sig = jax.nn.sigmoid(pre)
     hidden = (pre * sig).astype(jnp.bfloat16)
     grads = grads_ref[...]
-    hidden_grad = dot(grads, proj_ref[...], (1, 1))
-    pre_grad = (hidden_grad * sig * (1.0 + pre * (1.0 - sig))).astype(jnp.bfloat16)
+    pre_grad = (hidden_grad_ref[...] * sig * (1.0 + pre * (1.0 - sig))).astype(jnp.bfloat16)
     hidden_ref[...] = hidden
     pre_grad_ref[...] = pre_grad
     me = me_ref[0]
     core = me & 1
-    places = [places_of(me, pair) for pair in range(8)]
+    mine, other = halves_of(me)
 
     def put(tap, value):
-        for pair in range(8):
-            even = value[16 * pair : 16 * pair + 8]
-            odd = value[16 * pair + 8 : 16 * pair + 16]
-            mine, other = places[pair]
-            keep_ref[mine, tap] = jnp.where(core == 0, even, odd)
-            send_ref[other, tap] = jnp.where(core == 0, odd, even).astype(send_ref.dtype)
+        for block in range(8):
+            even = value[16 * block : 16 * block + 8]
+            odd = value[16 * block + 8 : 16 * block + 16]
+            keep_ref[block ^ mine, tap] = jnp.where(core == 0, even, odd)
+            send_ref[block ^ other, tap] = jnp.where(core == 0, odd, even)
 
     put(27, dot(hidden, grads, (0, 0)))
     grad_rows = jnp.concatenate(
@@ -127,7 +156,11 @@
         axis=1,
     )
     for tau in range(3):
-        part = dot(wide_ref[tau * map_rows : tau * map_rows + rows], grad_rows, (0, 0))
+        skip = (2 - tau) * map_rows
+        part = dot(own_ref[: rows - skip], grad_rows[skip:], (0, 0)) if skip < rows else None
+        if skip:
+            term = dot(wide_ref[tau * map_rows :], grad_rows[:skip], (0, 0))
+            part = term if part is None else part + term
         for row in range(3):
             for col in range(3):
                 put(
@@ -143,13 +176,8 @@
     _, height, width, chans = shape
     map_rows = height * width
     rows = shape[0] * map_rows
-    for ref, start in ((pre_grad_ref, 0), (next_ref, rows)):
-        flat = ref[...]
-        before, after = beside(flat, width)
-        here = slice(start, start + flat.shape[0])
-        wide_ref[here, :chans] = after
-        wide_ref[here, chans : 2 * chans] = flat
-        wide_ref[here, 2 * chans :] = before
+    spread(pre_grad_ref[...], width, wide_ref.at[:rows], flipped=True)
+    spread(next_ref[...], width, wide_ref.at[rows:], flipped=True)
     sums = None
     for tau in range(3):
         weights = jnp.concatenate(
@@ -172,19 +200,19 @@
 def unpack_kernel(scale, me_ref, mine_ref, other_ref, kern_ref, proj_ref, out_ref, sems):
     me = me_ref[0]
     core = me & 1
+    mine, other = halves_of(me)
     taps = kern_ref.shape[0]
     copies = []
     for first in range(0, taps + 1, UNPACK_CHUNK):
         last = min(first + UNPACK_CHUNK, taps + 1)
-        for pair in range(8):
-            mine, other = places_of(me, pair)
-            mine_rows = pl.ds(pl.multiple_of(16 * pair + 8 * core, 8), 8)
-            other_rows = pl.ds(pl.multiple_of(16 * pair + 8 * (1 - core), 8), 8)
+        for block in range(8):
+            mine_rows = pl.ds(pl.multiple_of(16 * block + 8 * core, 8), 8)
+            other_rows = pl.ds(pl.multiple_of(16 * block + 8 * (1 - core), 8), 8)
             out_ref[first:last, mine_rows, :] = (
-                mine_ref[mine, first:last].astype(jnp.float32) * scale
+                mine_ref[block ^ mine, first:last].astype(jnp.float32) * scale
             )
             out_ref[first:last, other_rows, :] = (
-                other_ref[other, first:last].astype(jnp.float32) * scale
+                other_ref[block ^ other, first:last].astype(jnp.float32) * scale
             )
         inside = min(last, taps)
         copies.append(
@@ -199,21 +227,29 @@
         copy.wait()
 
 
-def summed(me, keep, send, scale):
+def summed(me, keep, send, scale, beside_second, beside_third):
     taps, chans = keep.shape[1] - 1, keep.shape[3]
-    rounds = [tuple(order[k] for order in ORDERS) for k in range(3)]
-    total = keep + swapped(send, (0, 0)).astype(jnp.float32)
-    for bits, link_type in zip(rounds, (jnp.bfloat16, jnp.bfloat16, jnp.float32)):
+    rounds = [tuple(order[k] for order in ORDERS) for k in range(4)]
+    total = keep + swapped(send, (0, 0))
+    done = ()
+    for bits, link_type, work in zip(
+        rounds[:3],
+        (jnp.bfloat16, jnp.bfloat16, jnp.float32),
+        (lambda nothing: nothing, beside_second, beside_third),
+    ):
         rest = total.shape[0] // 2
+        done = work(done)
+        total, done = lax.optimization_barrier((total, done))
         came = swapped(total[rest:].astype(link_type), bits)
         total = total[:rest] + came.astype(jnp.float32)
+    total = total + swapped(total, rounds[3])
     count = lax.axis_size("dp") * lax.axis_size("tm")
-    place = HALVINGS
+    place = 1 + len(rounds)
     while (1 << place) < count:
         total = total + swapped(total, (place, place))
         place += 1
     total = total.astype(jnp.bfloat16)
-    for bits in reversed(rounds):
+    for bits in reversed(rounds[:3]):
         total = jnp.concatenate([total, swapped(total, bits)], axis=0)
     other = swapped(total, (0, 0))
     return pl.pallas_call(
@@ -223,17 +259,42 @@
             jax.ShapeDtypeStruct((chans, chans), jnp.float32),
         ),
         in_specs=[SCALAR, VECTOR, VECTOR],
-        out_specs=(ANYWHERE, ANYWHERE),
+        out_specs=(OUTSIDE, OUTSIDE),
         scratch_shapes=[
             pltpu.VMEM((taps + 1, chans, chans), jnp.float32),
             pltpu.SemaphoreType.DMA((pl.cdiv(taps + 1, UNPACK_CHUNK) + 1,)),
         ],
         compiler_params=LIMIT,
         name="unpack",
-    )(me, total, other)
-
-
-def forward(shape, me, halo, frames, grads, conv_kernel, proj_weight):
+    )(me, total, other), done
+
+
+def prepare(shape, frames, grads, conv_kernel, proj_weight):
+    n_frames, height, width, chans = shape
+    rows = n_frames * height * width
+    return pl.pallas_call(
+        functools.partial(prepare_kernel, shape),
+        out_shape=(
+            jax.ShapeDtypeStruct(frames.shape, frames.dtype),
+            jax.ShapeDtypeStruct(grads.shape, grads.dtype),
+            jax.ShapeDtypeStruct(conv_kernel.shape, conv_kernel.dtype),
+            jax.ShapeDtypeStruct(proj_weight.shape, proj_weight.dtype),
+            jax.ShapeDtypeStruct((rows, 3 * chans), jnp.bfloat16),
+            jax.ShapeDtypeStruct((rows, 3 * chans), jnp.float32),
+            jax.ShapeDtypeStruct((rows, chans), jnp.float32),
+        ),
+        in_specs=[OUTSIDE] * 4,
+        out_specs=(VECTOR,) * 7,
+        scratch_shapes=[pltpu.SemaphoreType.DMA((4,))],
+        compiler_params=LIMIT,
+        cost_estimate=pl.CostEstimate(
+            flops=2 * rows * 20 * chans * chans, bytes_accessed=1 << 20, transcendentals=0
+        ),
+        name="prepare",
+    )(*(pltpu.with_memory_space_constraint(x, pltpu.HBM) for x in (frames, grads, conv_kernel, proj_weight)))
+
+
+def forward(shape, me, halo, grads, conv_kernel, own, sums, hidden_grad):
     n_frames, height, width, chans = shape
     rows = n_frames * height * width
     half = (8, 28, 8, chans)
@@ -245,12 +306,12 @@
             jax.ShapeDtypeStruct((rows, chans), jnp.bfloat16),
             jax.ShapeDtypeStruct((rows, chans), jnp.bfloat16),
         ),
-        in_specs=[SCALAR] + [VECTOR] * 5,
+        in_specs=[SCALAR] + [VECTOR] * 6,
         out_specs=(VECTOR,) * 4,
-        scratch_shapes=[pltpu.VMEM((rows + 2 * height * width, 3 * chans), jnp.bfloat16)],
+        scratch_shapes=[pltpu.VMEM((2 * height * width, 3 * chans), jnp.bfloat16)],
         compiler_params=LIMIT,
         name="forward",
-    )(me, halo, frames, grads, conv_kernel, proj_weight)
+    )(me, halo, grads, conv_kernel, own, sums, hidden_grad)
 
 
 def backward(shape, pre_grad, following, hidden, frames, grads, conv_kernel, proj_weight):
@@ -278,15 +339,23 @@
     grads = out_grad.reshape(rows, chans)
     me = device_number().astype(jnp.int32).reshape(1)
     halo = passed_along(frames[rows - halo_rows :], "tm", 1)
+    frames, grads, conv_kernel, proj_weight, own, sums, hidden_grad = prepare(
+        shape, frames, grads, conv_kernel, proj_weight
+    )
     keep, send, hidden, pre_grad = forward(
-        shape, me, halo, frames, grads, conv_kernel, proj_weight
-    )
-    following = passed_along(pre_grad[:halo_rows], "tm", -1)
-    mixed, input_grad = backward(
-        shape, pre_grad, following, hidden, frames, grads, conv_kernel, proj_weight
+        shape, me, halo, grads, conv_kernel, own, sums, hidden_grad
     )
     total_pixels = lax.axis_size("dp") * lax.axis_size("tm") * rows
-    kernel_grad, proj_grad = summed(me, keep, send, 1.0 / math.sqrt(total_pixels))
+    (kernel_grad, proj_grad), (mixed, input_grad) = summed(
+        me,
+        keep,
+        send,
+        1.0 / math.sqrt(total_pixels),
+        lambda _: passed_along(pre_grad[:halo_rows], "tm", -1),
+        lambda following: backward(
+            shape, pre_grad, following, hidden, frames, grads, conv_kernel, proj_weight
+        ),
+    )
     return (
         mixed.reshape(clip_frames.shape),
         input_grad.reshape(clip_frames.shape),

time: 61.8 us -> 54.7 us (0.89)
  local copies, waits for them, and re-layouts: 3.69 us -> 0.06 us
  starting transfers between devices: 26.8 us -> 24 us
  waiting for transfers between devices: 26.3 us -> 23.7 us
  Pallas kernels: 3.6 us -> 5.37 us
    ppermute x9, starting transfers between devices: 20.3 us -> 16.4 us  [swapped(): lax.ppermute(array, AXES, [(i, i ^ 1 << bits[i & 1]) for i in range(count)])]
    ppermute x2, waiting for transfers between devices: 5.26 us -> 1.61 us  [passed_along(): return lax.ppermute(shard, axis, pairs)]
    unnamed x16 -> x0, local copies, waits for them, and re-layouts: 3.63 us -> none
    pallas_call x0 -> x1, Pallas kernels: none -> 1.79 us  [prepare(): pl.pallas_call(functools.partial(prepare_kernel, shape), out_shape=(jax.S...]
    ppermute x2, starting transfers between devices: 6.43 us -> 7.62 us  [passed_along(): return lax.ppermute(shard, axis, pairs)]
    ppermute x9, waiting for transfers between devices: 21 us -> 22.1 us  [swapped(): lax.ppermute(array, AXES, [(i, i ^ 1 << bits[i & 1]) for i in range(count)])]
  transfers between devices with their start and end apart: 11 -> 11, of which waited for: 10 -> 10; matrix products, arithmetic and copies ran while one was open for 0% -> 0% of each run, Pallas kernels for 2% -> 6%
where the time goes in v3:
time: 54.7 us; the launch traced here: 54.2 us
  starting transfers between devices  24 us (44%)
  waiting for transfers between devices  23.7 us (43%)
  Pallas kernels  5.37 us (10%)
  between operations  0.74 us (1%)
    ppermute x9, waiting for transfers between devices, swapped(): lax.ppermute(array, AXES, [(i, i ^ 1 << bits[i & 1]) for i in range(count)])  22.1 us
    ppermute x9, starting transfers between devices, swapped(): lax.ppermute(array, AXES, [(i, i ^ 1 << bits[i & 1]) for i in range(count)])  16.4 us
    ppermute x2, starting transfers between devices, passed_along(): return lax.ppermute(shard, axis, pairs)  7.62 us
    pallas_call x1, Pallas kernels, prepare(): pl.pallas_call(functools.partial(prepare_kernel, shape), out_shape=(jax.S...  1.79 us
    ppermute x2, waiting for transfers between devices, passed_along(): return lax.ppermute(shard, axis, pairs)  1.61 us
    pallas_call x1, Pallas kernels, summed(): pl.pallas_call(functools.partial(unpack_kernel, scale), out_shape=(jax.Sh...  1.3 us
    pallas_call x1, Pallas kernels, backward(): pl.pallas_call(functools.partial(backward_kernel, shape), out_shape=(jax....  1.21 us
  transfers between devices with their start and end apart: 11, of which 10 were waited for; matrix products, arithmetic and copies ran while one was open for 0% of the time, Pallas kernels for 6%

profile of v3, /device:TPU:1, one launch (start us, length us, event | category | flops | bytes accessed | tf_op | source)
XLA Modules:
  0.0 54.2 jit_solution(13570716149727922775)
XLA Ops:
  0.6 4.5 %collective-permute-start = (bf16[256,128]{1,0:T(8,128)(2,1)}, bf16[256,128]{1,0:T(8,128)(2,1)S(1)}, u32[]{:S(2)}, u32[]{:S(2)}) collective-permute-start(bf16[256,128]{1,0:T(8,128)(2,1)} %bitcast.7), channel_id=1, source_target_pairs={{0,1},{1,2},{2,3},{4,5},{5,6},{6,7},{8,9},{9,10},{10,11},{12,13},{... | collective-permute-start | bytes 196616 | tf_op jit(solution)/shard_map/ppermute | solution.py:23
  5.2 1.8 %prepare.1 = (bf16[256,128]{1,0:T(8,128)(2,1)S(1)}, bf16[256,128]{1,0:T(8,128)(2,1)S(1)}, bf16[3,3,3,128,128]{4,3,2,1,0:T(8,128)(2,1)S(1)}, bf16[128,128]{1,0:T(...) custom-call(bf16[256,128]{1,0:T(8,128)(2,1)} %bitcast.8, ...), custom_call_target="tpu_custom_call" | custom-call | flops 167772160 | bytes 1048576 | tf_op jit(solution)/shard_map/prepare/pallas_call | solution.py:275
  7.0 0.0 collective-permute-done.halo_ref
  7.0 1.1 %forward.1 = (f32[8,28,8,128]{3,2,1,0:T(8,128)S(1)}, f32[8,28,8,128]{3,2,1,0:T(8,128)S(1)}, bf16[256,128]{1,0:T(8,128)(2,1)S(1)}, bf16[256,128]{1,0:T(8,128)(2,1)S(1)}) custom-call(s32[1]{0:T(128)} %bitcast.me_ref, bf16[256,128]{1,0:T(8,128)(2,1)S(1)} %collective-permute-done.halo_ref, bf16[256,128]{1,0:T(8,128)(2,1)S(1)} %get-tuple-element.24.grads_ref, ...), custom_call_target="tpu_custom_call" | custom-call | tf_op jit(solution)/shard_map/forward/pallas_call | solution.py:301
  8.0 0.1 collective-permute-start.1
  8.1 2.5 %collective-permute-done.1 = f32[8,28,8,128]{3,2,1,0:T(8,128)S(1)} collective-permute-done((f32[8,28,8,128]{3,2,1,0:T(8,128)S(1)}, f32[8,28,8,128]{3,2,1,0:T(8,128)S(1)}, u32[]{:S(2)}, u32[]{:S(2)}) %collective-permute-start.1) | collective-permute-done | bytes 917536 | tf_op jit(solution)/shard_map/ppermute | solution.py:32
  10.6 0.1 add.19
  10.8 1.3 %collective-permute-start.2 = (bf16[4,28,8,128]{3,2,1,0:T(8,128)(2,1)S(1)}, bf16[4,28,8,128]{3,2,1,0:T(8,128)(2,1)S(1)}, u32[]{:S(2)}, u32[]{:S(2)}) collective-permute-start(bf16[4,28,8,128]{3,2,1,0:T(8,128)(2,1)S(1)} %slice.34), channel_id=1, source_target_pairs={{0,2},{1,5},{2,0},{3,7},{4,6},{5,1},{6,4},{7,3},{8,10},{9,13},{10,... | collective-permute-start | bytes 688136 | tf_op jit(solution)/shard_map/ppermute | solution.py:32
  12.1 3.1 %collective-permute-start.3 = (bf16[256,128]{1,0:T(8,128)(2,1)S(1)}, bf16[256,128]{1,0:T(8,128)(2,1)S(1)}, u32[]{:S(2)}, u32[]{:S(2)}) collective-permute-start(bf16[256,128]{1,0:T(8,128)(2,1)S(1)} %get-tuple-element.31.pre_grad_ref), channel_id=1, source_target_pairs={{1,0},{2,1},{3,2},{5,4},{6,5},{7,6},{9,8},{10,9},{11,10},{13,12},{... | collective-permute-start | bytes 196616 | tf_op jit(solution)/shard_map/ppermute | solution.py:23
  15.2 0.8 %collective-permute-done.2 = bf16[4,28,8,128]{3,2,1,0:T(8,128)(2,1)S(1)} collective-permute-done((bf16[4,28,8,128]{3,2,1,0:T(8,128)(2,1)S(1)}, bf16[4,28,8,128]{3,2,1,0:T(8,128)(2,1)S(1)}, u32[]{:S(2)}, u32[]{:S(2)}) %collective-permute-start.2) | collective-permute-done | bytes 229408 | tf_op jit(solution)/shard_map/ppermute | solution.py:32
  16.0 1.6 %collective-permute-done.3.next_ref = bf16[256,128]{1,0:T(8,128)(2,1)S(1)} collective-permute-done((bf16[256,128]{1,0:T(8,128)(2,1)S(1)}, bf16[256,128]{1,0:T(8,128)(2,1)S(1)}, u32[]{:S(2)}, u32[]{:S(2)}) %collective-permute-start.3) | collective-permute-done | bytes 65568 | tf_op jit(solution)/shard_map/ppermute | solution.py:23
  17.7 1.4 %collective-permute-start.4 = (bf16[2,28,8,128]{3,2,1,0:T(8,128)(2,1)S(1)}, bf16[2,28,8,128]{3,2,1,0:T(8,128)(2,1)S(1)}, u32[]{:S(2)}, u32[]{:S(2)}) collective-permute-start(bf16[2,28,8,128]{3,2,1,0:T(8,128)(2,1)S(1)} %slice.35), channel_id=1, source_target_pairs={{0,4},{1,9},{2,6},{3,11},{4,0},{5,13},{6,2},{7,15},{8,12},{9,1},{1... | collective-permute-start | bytes 344072 | tf_op jit(solution)/shard_map/ppermute | solution.py:32
  19.0 1.2 %backward.1 = (bf16[256,128]{1,0:T(8,128)(2,1)}, bf16[256,128]{1,0:T(8,128)(2,1)}) custom-call(bf16[256,128]{1,0:T(8,128)(2,1)S(1)} %get-tuple-element.31.pre_grad_ref, bf16[256,128]{1,0:T(8,128)(2,1)S(1)} %collective-permute-done.3.next_ref, bf16[256,128]{1,0:T(8,128)(2,1)S(1)} %get-tuple-element.34.hidden_ref, ...), custom_call_target="tpu_custom_call" | custom-call | flops 234881024 | bytes 1048576 | tf_op jit(solution)/shard_map/backward/pallas_call | solution.py:321
  20.2 1.4 %collective-permute-done.4 = bf16[2,28,8,128]{3,2,1,0:T(8,128)(2,1)S(1)} collective-permute-done((bf16[2,28,8,128]{3,2,1,0:T(8,128)(2,1)S(1)}, bf16[2,28,8,128]{3,2,1,0:T(8,128)(2,1)S(1)}, u32[]{:S(2)}, u32[]{:S(2)}) %collective-permute-start.4) | collective-permute-done | bytes 114720 | tf_op jit(solution)/shard_map/ppermute | solution.py:32
  21.7 2.4 %collective-permute-start.5 = (f32[1,28,8,128]{3,2,1,0:T(8,128)S(1)}, f32[1,28,8,128]{3,2,1,0:T(8,128)S(1)}, u32[]{:S(2)}, u32[]{:S(2)}) collective-permute-start(f32[1,28,8,128]{3,2,1,0:T(8,128)S(1)} %slice.25), channel_id=1, source_target_pairs={{0,8},{1,17},{2,10},{3,19},{4,12},{5,21},{6,14},{7,23},{8,0},{9,25... | collective-permute-start | bytes 344072 | tf_op jit(solution)/shard_map/ppermute | solution.py:32
  24.1 3.5 %collective-permute-done.5 = f32[1,28,8,128]{3,2,1,0:T(8,128)S(1)} collective-permute-done((f32[1,28,8,128]{3,2,1,0:T(8,128)S(1)}, f32[1,28,8,128]{3,2,1,0:T(8,128)S(1)}, u32[]{:S(2)}, u32[]{:S(2)}) %collective-permute-start.5) | collective-permute-done | bytes 114720 | tf_op jit(solution)/shard_map/ppermute | solution.py:32
  27.6 0.1 collective-permute-start.6
  27.6 3.6 %collective-permute-done.6 = f32[1,28,8,128]{3,2,1,0:T(8,128)S(1)} collective-permute-done((f32[1,28,8,128]{3,2,1,0:T(8,128)S(1)}, f32[1,28,8,128]{3,2,1,0:T(8,128)S(1)}, u32[]{:S(2)}, u32[]{:S(2)}) %collective-permute-start.6) | collective-permute-done | bytes 114720 | tf_op jit(solution)/shard_map/ppermute | solution.py:32
  31.3 2.7 %collective-permute-start.7 = (bf16[1,28,8,128]{3,2,1,0:T(8,128)(2,1)S(1)}, bf16[1,28,8,128]{3,2,1,0:T(8,128)(2,1)S(1)}, u32[]{:S(2)}, u32[]{:S(2)}) collective-permute-start(bf16[1,28,8,128]{3,2,1,0:T(8,128)(2,1)S(1)} %add_convert_fusion), channel_id=1, source_target_pairs={{0,8},{1,17},{2,10},{3,19},{4,12},{5,21},{6,14},{7,23},{8,0},{9,25... | collective-permute-start | bytes 172040 | tf_op jit(solution)/shard_map/ppermute | solution.py:32
  34.0 1.6 %collective-permute-done.7 = bf16[1,28,8,128]{3,2,1,0:T(8,128)(2,1)S(1)} collective-permute-done((bf16[1,28,8,128]{3,2,1,0:T(8,128)(2,1)S(1)}, bf16[1,28,8,128]{3,2,1,0:T(8,128)(2,1)S(1)}, u32[]{:S(2)}, u32[]{:S(2)}) %collective-permute-start.7) | collective-permute-done | bytes 57376 | tf_op jit(solution)/shard_map/ppermute | solution.py:32
  35.5 1.3 %collective-permute-start.8 = (bf16[2,28,8,128]{3,2,1,0:T(8,128)(2,1)S(1)}, bf16[2,28,8,128]{3,2,1,0:T(8,128)(2,1)S(1)}, u32[]{:S(2)}, u32[]{:S(2)}) collective-permute-start(bf16[2,28,8,128]{3,2,1,0:T(8,128)(2,1)S(1)} %pad_maximum_fusion.2), channel_id=1, source_target_pairs={{0,4},{1,9},{2,6},{3,11},{4,0},{5,13},{6,2},{7,15},{8,12},{9,1},{1... | collective-permute-start | bytes 344072 | tf_op jit(solution)/shard_map/ppermute | solution.py:32
  36.8 2.4 %collective-permute-done.8 = bf16[2,28,8,128]{3,2,1,0:T(8,128)(2,1)S(1)} collective-permute-done((bf16[2,28,8,128]{3,2,1,0:T(8,128)(2,1)S(1)}, bf16[2,28,8,128]{3,2,1,0:T(8,128)(2,1)S(1)}, u32[]{:S(2)}, u32[]{:S(2)}) %collective-permute-start.8) | collective-permute-done | bytes 114720 | tf_op jit(solution)/shard_map/ppermute | solution.py:32
  39.3 0.7 %collective-permute-start.9 = (bf16[4,28,8,128]{3,2,1,0:T(8,128)(2,1)S(1)}, bf16[4,28,8,128]{3,2,1,0:T(8,128)(2,1)S(1)}, u32[]{:S(2)}, u32[]{:S(2)}) collective-permute-start(bf16[4,28,8,128]{3,2,1,0:T(8,128)(2,1)S(1)} %pad_maximum_fusion.1), channel_id=1, source_target_pairs={{0,2},{1,5},{2,0},{3,7},{4,6},{5,1},{6,4},{7,3},{8,10},{9,13},{10,... | collective-permute-start | bytes 688136 | tf_op jit(solution)/shard_map/ppermute | solution.py:32
  40.0 4.9 %collective-permute-done.9 = bf16[4,28,8,128]{3,2,1,0:T(8,128)(2,1)S(1)} collective-permute-done((bf16[4,28,8,128]{3,2,1,0:T(8,128)(2,1)S(1)}, bf16[4,28,8,128]{3,2,1,0:T(8,128)(2,1)S(1)}, u32[]{:S(2)}, u32[]{:S(2)}) %collective-permute-start.9) | collective-permute-done | bytes 229408 | tf_op jit(solution)/shard_map/ppermute | solution.py:32
  44.9 6.5 %collective-permute-start.10 = (bf16[8,28,8,128]{3,2,1,0:T(8,128)(2,1)S(1)}, bf16[8,28,8,128]{3,2,1,0:T(8,128)(2,1)S(1)}, u32[]{:S(2)}, u32[]{:S(2)}) collective-permute-start(bf16[8,28,8,128]{3,2,1,0:T(8,128)(2,1)S(1)} %pad_maximum_fusion.mine_ref), channel_id=1, source_target_pairs={{0,1},{1,0},{2,3},{3,2},{4,5},{5,4},{6,7},{7,6},{8,9},{9,8},{10,11... | collective-permute-start | bytes 1376264 | tf_op jit(solution)/shard_map/ppermute | solution.py:32
  51.5 1.4 %collective-permute-done.10.other_ref = bf16[8,28,8,128]{3,2,1,0:T(8,128)(2,1)S(1)} collective-permute-done((bf16[8,28,8,128]{3,2,1,0:T(8,128)(2,1)S(1)}, bf16[8,28,8,128]{3,2,1,0:T(8,128)(2,1)S(1)}, u32[]{:S(2)}, u32[]{:S(2)}) %collective-permute-start.10) | collective-permute-done | bytes 458784 | tf_op jit(solution)/shard_map/ppermute | solution.py:32
  52.9 1.3 %unpack.1 = (f32[27,128,128]{2,1,0:T(8,128)}, f32[128,128]{1,0:T(8,128)}) custom-call(s32[1]{0:T(128)} %bitcast.me_ref, bf16[8,28,8,128]{3,2,1,0:T(8,128)(2,1)S(1)} %pad_maximum_fusion.mine_ref, bf16[8,28,8,128]{3,2,1,0:T(8,128)(2,1)S(1)} %collective-permute-done.10.other_ref), custom_call_target="tpu_custom_call" | custom-call | tf_op jit(solution)/shard_map/unpack/pallas_call | solution.py:255
  (10 shorter events, 0.2 us)
Async XLA Ops:
  0.6 6.3 %collective-permute-start = (bf16[256,128]{1,0:T(8,128)(2,1)}, bf16[256,128]{1,0:T(8,128)(2,1)S(1)}, u32[]{:S(2)}, u32[]{:S(2)}) collective-permute-start(bf16[256,128]{1,0:T(8,128)(2,1)} %bitcast.7), channel_id=1, source_target_pairs={{0,1},{1,2},{2,3},{4,5},{5,6},{6,7},{8,9},{9,10},{10,11},{12,13},{... | collective-permute-start | bytes 196616 | tf_op jit(solution)/shard_map/ppermute | solution.py:23
  8.0 2.5 %collective-permute-start.1 = (f32[8,28,8,128]{3,2,1,0:T(8,128)S(1)}, f32[8,28,8,128]{3,2,1,0:T(8,128)S(1)}, u32[]{:S(2)}, u32[]{:S(2)}) collective-permute-start(f32[8,28,8,128]{3,2,1,0:T(8,128)S(1)} %get-tuple-element.30), channel_id=1, source_target_pairs={{0,1},{1,0},{2,3},{3,2},{4,5},{5,4},{6,7},{7,6},{8,9},{9,8},{10,11... | collective-permute-start | bytes 2752520 | tf_op jit(solution)/shard_map/ppermute | solution.py:32
  10.8 5.2 %collective-permute-start.2 = (bf16[4,28,8,128]{3,2,1,0:T(8,128)(2,1)S(1)}, bf16[4,28,8,128]{3,2,1,0:T(8,128)(2,1)S(1)}, u32[]{:S(2)}, u32[]{:S(2)}) collective-permute-start(bf16[4,28,8,128]{3,2,1,0:T(8,128)(2,1)S(1)} %slice.34), channel_id=1, source_target_pairs={{0,2},{1,5},{2,0},{3,7},{4,6},{5,1},{6,4},{7,3},{8,10},{9,13},{10,... | collective-permute-start | bytes 688136 | tf_op jit(solution)/shard_map/ppermute | solution.py:32
  12.1 5.6 %collective-permute-start.3 = (bf16[256,128]{1,0:T(8,128)(2,1)S(1)}, bf16[256,128]{1,0:T(8,128)(2,1)S(1)}, u32[]{:S(2)}, u32[]{:S(2)}) collective-permute-start(bf16[256,128]{1,0:T(8,128)(2,1)S(1)} %get-tuple-element.31.pre_grad_ref), channel_id=1, source_target_pairs={{1,0},{2,1},{3,2},{5,4},{6,5},{7,6},{9,8},{10,9},{11,10},{13,12},{... | collective-permute-start | bytes 196616 | tf_op jit(solution)/shard_map/ppermute | solution.py:23
  17.7 4.0 %collective-permute-start.4 = (bf16[2,28,8,128]{3,2,1,0:T(8,128)(2,1)S(1)}, bf16[2,28,8,128]{3,2,1,0:T(8,128)(2,1)S(1)}, u32[]{:S(2)}, u32[]{:S(2)}) collective-permute-start(bf16[2,28,8,128]{3,2,1,0:T(8,128)(2,1)S(1)} %slice.35), channel_id=1, source_target_pairs={{0,4},{1,9},{2,6},{3,11},{4,0},{5,13},{6,2},{7,15},{8,12},{9,1},{1... | collective-permute-start | bytes 344072 | tf_op jit(solution)/shard_map/ppermute | solution.py:32
  21.7 5.8 %collective-permute-start.5 = (f32[1,28,8,128]{3,2,1,0:T(8,128)S(1)}, f32[1,28,8,128]{3,2,1,0:T(8,128)S(1)}, u32[]{:S(2)}, u32[]{:S(2)}) collective-permute-start(f32[1,28,8,128]{3,2,1,0:T(8,128)S(1)} %slice.25), channel_id=1, source_target_pairs={{0,8},{1,17},{2,10},{3,19},{4,12},{5,21},{6,14},{7,23},{8,0},{9,25... | collective-permute-start | bytes 344072 | tf_op jit(solution)/shard_map/ppermute | solution.py:32
  27.6 3.7 %collective-permute-start.6 = (f32[1,28,8,128]{3,2,1,0:T(8,128)S(1)}, f32[1,28,8,128]{3,2,1,0:T(8,128)S(1)}, u32[]{:S(2)}, u32[]{:S(2)}) collective-permute-start(f32[1,28,8,128]{3,2,1,0:T(8,128)S(1)} %slice_add_fusion.1), channel_id=1, source_target_pairs={{0,16},{1,3},{2,18},{3,1},{4,20},{5,7},{6,22},{7,5},{8,24},{9,11},... | collective-permute-start | bytes 344072 | tf_op jit(solution)/shard_map/ppermute | solution.py:32
  31.3 4.2 %collective-permute-start.7 = (bf16[1,28,8,128]{3,2,1,0:T(8,128)(2,1)S(1)}, bf16[1,28,8,128]{3,2,1,0:T(8,128)(2,1)S(1)}, u32[]{:S(2)}, u32[]{:S(2)}) collective-permute-start(bf16[1,28,8,128]{3,2,1,0:T(8,128)(2,1)S(1)} %add_convert_fusion), channel_id=1, source_target_pairs={{0,8},{1,17},{2,10},{3,19},{4,12},{5,21},{6,14},{7,23},{8,0},{9,25... | collective-permute-start | bytes 172040 | tf_op jit(solution)/shard_map/ppermute | solution.py:32
  35.5 3.7 %collective-permute-start.8 = (bf16[2,28,8,128]{3,2,1,0:T(8,128)(2,1)S(1)}, bf16[2,28,8,128]{3,2,1,0:T(8,128)(2,1)S(1)}, u32[]{:S(2)}, u32[]{:S(2)}) collective-permute-start(bf16[2,28,8,128]{3,2,1,0:T(8,128)(2,1)S(1)} %pad_maximum_fusion.2), channel_id=1, source_target_pairs={{0,4},{1,9},{2,6},{3,11},{4,0},{5,13},{6,2},{7,15},{8,12},{9,1},{1... | collective-permute-start | bytes 344072 | tf_op jit(solution)/shard_map/ppermute | solution.py:32
  39.3 5.6 %collective-permute-start.9 = (bf16[4,28,8,128]{3,2,1,0:T(8,128)(2,1)S(1)}, bf16[4,28,8,128]{3,2,1,0:T(8,128)(2,1)S(1)}, u32[]{:S(2)}, u32[]{:S(2)}) collective-permute-start(bf16[4,28,8,128]{3,2,1,0:T(8,128)(2,1)S(1)} %pad_maximum_fusion.1), channel_id=1, source_target_pairs={{0,2},{1,5},{2,0},{3,7},{4,6},{5,1},{6,4},{7,3},{8,10},{9,13},{10,... | collective-permute-start | bytes 688136 | tf_op jit(solution)/shard_map/ppermute | solution.py:32
  44.9 8.0 %collective-permute-start.10 = (bf16[8,28,8,128]{3,2,1,0:T(8,128)(2,1)S(1)}, bf16[8,28,8,128]{3,2,1,0:T(8,128)(2,1)S(1)}, u32[]{:S(2)}, u32[]{:S(2)}) collective-permute-start(bf16[8,28,8,128]{3,2,1,0:T(8,128)(2,1)S(1)} %pad_maximum_fusion.mine_ref), channel_id=1, source_target_pairs={{0,1},{1,0},{2,3},{3,2},{4,5},{5,4},{6,7},{7,6},{8,9},{9,8},{10,11... | collective-permute-start | bytes 1376264 | tf_op jit(solution)/shard_map/ppermute | solution.py:32

commit v4 on v3

--- a/solution.py
+++ b/solution.py
@@ -9,7 +9,7 @@
 from jax.sharding import PartitionSpec as P
 
 AXES = ("dp", "tm")
-ORDERS = ((1, 2, 3, 4), (2, 3, 4, 1))
+PAIRS = (((1, 2), (3, 4)), ((3, 4), (1, 2)))
 UNPACK_CHUNK = 7
 LIMIT = pltpu.CompilerParams(vmem_limit_bytes=16 * 1024 * 1024)
 SCALAR = pl.BlockSpec(memory_space=pltpu.SMEM)
@@ -27,16 +27,19 @@
     return lax.axis_index("dp") * lax.axis_size("tm") + lax.axis_index("tm")
 
 
-def swapped(array, bits):
+def swapped(array, masks):
     count = lax.axis_size("dp") * lax.axis_size("tm")
-    return lax.ppermute(array, AXES, [(i, i ^ (1 << bits[i & 1])) for i in range(count)])
+    return lax.ppermute(array, AXES, [(i, i ^ masks[i & 1]) for i in range(count)])
+
+
+def masks_of(stage, offset):
+    return tuple(
+        (offset >> 1) << pairs[stage][0] | (offset & 1) << pairs[stage][1] for pairs in PAIRS
+    )
 
 
 def halves_of(me):
-    first, second = (
-        4 * ((me >> order[0]) & 1) + 2 * ((me >> order[1]) & 1) + ((me >> order[2]) & 1)
-        for order in ORDERS
-    )
+    first, second = (4 * ((me >> split[0]) & 1) + 2 * ((me >> split[1]) & 1) for split, _ in PAIRS)
     core = me & 1
     return jnp.where(core == 0, first, second), jnp.where(core == 0, second, first)
 
@@ -227,31 +230,36 @@
         copy.wait()
 
 
-def summed(me, keep, send, scale, beside_second, beside_third):
+def summed(me, keep, send, scale, beside_split, beside_exchange):
     taps, chans = keep.shape[1] - 1, keep.shape[3]
-    rounds = [tuple(order[k] for order in ORDERS) for k in range(4)]
-    total = keep + swapped(send, (0, 0))
-    done = ()
-    for bits, link_type, work in zip(
-        rounds[:3],
-        (jnp.bfloat16, jnp.bfloat16, jnp.float32),
-        (lambda nothing: nothing, beside_second, beside_third),
-    ):
-        rest = total.shape[0] // 2
-        done = work(done)
-        total, done = lax.optimization_barrier((total, done))
-        came = swapped(total[rest:].astype(link_type), bits)
-        total = total[:rest] + came.astype(jnp.float32)
-    total = total + swapped(total, rounds[3])
+    total = keep + swapped(send, (1, 1))
+    part = total.shape[0] // 4
+    came = [
+        swapped(total[offset * part : (offset + 1) * part].astype(jnp.bfloat16), masks_of(0, offset))
+        for offset in (3, 2, 1)
+    ]
+    total = total[:part]
+    for piece in came:
+        total = total + piece.astype(jnp.float32)
+    done = beside_split()
+    total, done = lax.optimization_barrier((total, done))
+    total = lax.reduce_precision(total, 8, 7)
+    third, second, first = (
+        swapped(total.astype(jnp.bfloat16), masks_of(1, offset)).astype(jnp.float32)
+        for offset in (3, 2, 1)
+    )
+    total = (total + first) + (second + third)
     count = lax.axis_size("dp") * lax.axis_size("tm")
-    place = 1 + len(rounds)
-    while (1 << place) < count:
-        total = total + swapped(total, (place, place))
-        place += 1
+    mask = 1 << (1 + sum(len(pair) for pair in PAIRS[0]))
+    while mask < count:
+        total = total + swapped(total, (mask, mask))
+        mask *= 2
+    done = beside_exchange(done)
     total = total.astype(jnp.bfloat16)
-    for bits in reversed(rounds[:3]):
-        total = jnp.concatenate([total, swapped(total, bits)], axis=0)
-    other = swapped(total, (0, 0))
+    total, done = lax.optimization_barrier((total, done))
+    third, second, first = (swapped(total, masks_of(0, offset)) for offset in (3, 2, 1))
+    total = jnp.concatenate([total, first, second, third], axis=0)
+    other = swapped(total, (1, 1))
     return pl.pallas_call(
         functools.partial(unpack_kernel, scale),
         out_shape=(
@@ -351,7 +359,7 @@
         keep,
         send,
         1.0 / math.sqrt(total_pixels),
-        lambda _: passed_along(pre_grad[:halo_rows], "tm", -1),
+        lambda: passed_along(pre_grad[:halo_rows], "tm", -1),
         lambda following: backward(
             shape, pre_grad, following, hidden, frames, grads, conv_kernel, proj_weight
         ),

time: 54.7 us -> 42.1 us (0.77)
  waiting for transfers between devices: 23.7 us -> 15.2 us
  starting transfers between devices: 24 us -> 19.9 us
    ppermute x9 -> x11, waiting for transfers between devices: 22.1 us -> 14.1 us  [swapped(): lax.ppermute(array, AXES, [(i, i ^ masks[i & 1]) for i in range(count)])]
    ppermute x9 -> x11, starting transfers between devices: 16.4 us -> 13.1 us  [swapped(): lax.ppermute(array, AXES, [(i, i ^ masks[i & 1]) for i in range(count)])]
    ppermute x2, starting transfers between devices: 7.62 us -> 6.77 us  [passed_along(): return lax.ppermute(shard, axis, pairs)]
  transfers between devices with their start and end apart: 11 -> 13, of which waited for: 10 -> 10; matrix products, arithmetic and copies ran while one was open for 0% -> 0% of each run, Pallas kernels for 6% -> 7%
where the time goes in v4:
time: 42.1 us; the launch traced here: 41.6 us
  starting transfers between devices  19.9 us (47%)
  waiting for transfers between devices  15.2 us (36%)
  Pallas kernels  5.37 us (13%)
  between operations  0.74 us (2%)
    ppermute x11, waiting for transfers between devices, swapped(): lax.ppermute(array, AXES, [(i, i ^ masks[i & 1]) for i in range(count)])  14.1 us
    ppermute x11, starting transfers between devices, swapped(): lax.ppermute(array, AXES, [(i, i ^ masks[i & 1]) for i in range(count)])  13.1 us
    ppermute x2, starting transfers between devices, passed_along(): return lax.ppermute(shard, axis, pairs)  6.77 us
    pallas_call x1, Pallas kernels, prepare(): pl.pallas_call(functools.partial(prepare_kernel, shape), out_shape=(jax.S...  1.79 us
    pallas_call x1, Pallas kernels, summed(): pl.pallas_call(functools.partial(unpack_kernel, scale), out_shape=(jax.Sh...  1.3 us
    pallas_call x1, Pallas kernels, backward(): pl.pallas_call(functools.partial(backward_kernel, shape), out_shape=(jax....  1.2 us
    ppermute x2, waiting for transfers between devices, passed_along(): return lax.ppermute(shard, axis, pairs)  1.13 us
    pallas_call x1, Pallas kernels, forward(): pl.pallas_call(functools.partial(forward_kernel, shape), out_shape=(jax.S...  1.07 us
  transfers between devices with their start and end apart: 13, of which 10 were waited for; matrix products, arithmetic and copies ran while one was open for 0% of the time, Pallas kernels for 7%

profile of v4, /device:TPU:1, one launch (start us, length us, event | category | flops | bytes accessed | tf_op | source)
XLA Modules:
  0.0 41.6 jit_solution(15655860228453696979)
XLA Ops:
  0.6 4.5 %collective-permute-start = (bf16[256,128]{1,0:T(8,128)(2,1)}, bf16[256,128]{1,0:T(8,128)(2,1)S(1)}, u32[]{:S(2)}, u32[]{:S(2)}) collective-permute-start(bf16[256,128]{1,0:T(8,128)(2,1)} %bitcast.7), channel_id=1, source_target_pairs={{0,1},{1,2},{2,3},{4,5},{5,6},{6,7},{8,9},{9,10},{10,11},{12,13},{... | collective-permute-start | bytes 196616 | tf_op jit(solution)/shard_map/ppermute | solution.py:23
  5.2 1.8 %prepare.1 = (bf16[256,128]{1,0:T(8,128)(2,1)S(1)}, bf16[256,128]{1,0:T(8,128)(2,1)S(1)}, bf16[3,3,3,128,128]{4,3,2,1,0:T(8,128)(2,1)S(1)}, bf16[128,128]{1,0:T(...) custom-call(bf16[256,128]{1,0:T(8,128)(2,1)} %bitcast.8, ...), custom_call_target="tpu_custom_call" | custom-call | flops 167772160 | bytes 1048576 | tf_op jit(solution)/shard_map/prepare/pallas_call | solution.py:283
  7.0 0.0 collective-permute-done.halo_ref
  7.0 1.1 %forward.1 = (f32[8,28,8,128]{3,2,1,0:T(8,128)S(1)}, f32[8,28,8,128]{3,2,1,0:T(8,128)S(1)}, bf16[256,128]{1,0:T(8,128)(2,1)S(1)}, bf16[256,128]{1,0:T(8,128)(2,1)S(1)}) custom-call(s32[1]{0:T(128)} %bitcast.me_ref, bf16[256,128]{1,0:T(8,128)(2,1)S(1)} %collective-permute-done.halo_ref, bf16[256,128]{1,0:T(8,128)(2,1)S(1)} %get-tuple-element.24.grads_ref, ...), custom_call_target="tpu_custom_call" | custom-call | tf_op jit(solution)/shard_map/forward/pallas_call | solution.py:309
  8.0 0.1 collective-permute-start.1
  8.1 2.5 %collective-permute-done.1 = f32[8,28,8,128]{3,2,1,0:T(8,128)S(1)} collective-permute-done((f32[8,28,8,128]{3,2,1,0:T(8,128)S(1)}, f32[8,28,8,128]{3,2,1,0:T(8,128)S(1)}, u32[]{:S(2)}, u32[]{:S(2)}) %collective-permute-start.1) | collective-permute-done | bytes 917536 | tf_op jit(solution)/shard_map/ppermute | solution.py:32
  10.6 0.1 fusion.2
  10.8 3.4 %collective-permute-start.2 = (bf16[2,28,8,128]{3,2,1,0:T(8,128)(2,1)S(1)}, bf16[2,28,8,128]{3,2,1,0:T(8,128)(2,1)S(1)}, u32[]{:S(2)}, u32[]{:S(2)}) collective-permute-start(bf16[2,28,8,128]{3,2,1,0:T(8,128)(2,1)S(1)} %get-tuple-element.46), channel_id=1, source_target_pairs={{0,6},{1,25},{2,4},{3,27},{4,2},{5,29},{6,0},{7,31},{8,14},{9,17},... | collective-permute-start | bytes 344072 | tf_op jit(solution)/shard_map/ppermute | solution.py:32
  14.1 0.0 collective-permute-start.3
  14.1 0.4 collective-permute-start.4
  14.5 2.3 %collective-permute-start.5 = (bf16[256,128]{1,0:T(8,128)(2,1)S(1)}, bf16[256,128]{1,0:T(8,128)(2,1)S(1)}, u32[]{:S(2)}, u32[]{:S(2)}) collective-permute-start(bf16[256,128]{1,0:T(8,128)(2,1)S(1)} %get-tuple-element.31.pre_grad_ref), channel_id=1, source_target_pairs={{1,0},{2,1},{3,2},{5,4},{6,5},{7,6},{9,8},{10,9},{11,10},{13,12},{... | collective-permute-start | bytes 196616 | tf_op jit(solution)/shard_map/ppermute | solution.py:23
  16.8 0.0 collective-permute-done.2
  16.8 2.2 %collective-permute-done.3 = bf16[2,28,8,128]{3,2,1,0:T(8,128)(2,1)S(1)} collective-permute-done((bf16[2,28,8,128]{3,2,1,0:T(8,128)(2,1)S(1)}, bf16[2,28,8,128]{3,2,1,0:T(8,128)(2,1)S(1)}, u32[]{:S(2)}, u32[]{:S(2)}) %collective-permute-start.3) | collective-permute-done | bytes 114720 | tf_op jit(solution)/shard_map/ppermute | solution.py:32
  19.0 0.0 collective-permute-done.4
  19.0 0.1 fusion.1
  19.1 1.1 %collective-permute-done.5.next_ref = bf16[256,128]{1,0:T(8,128)(2,1)S(1)} collective-permute-done((bf16[256,128]{1,0:T(8,128)(2,1)S(1)}, bf16[256,128]{1,0:T(8,128)(2,1)S(1)}, u32[]{:S(2)}, u32[]{:S(2)}) %collective-permute-start.5) | collective-permute-done | bytes 65568 | tf_op jit(solution)/shard_map/ppermute | solution.py:23
  20.2 1.3 %collective-permute-start.6 = (bf16[2,28,8,128]{3,2,1,0:T(8,128)(2,1)S(1)}, bf16[2,28,8,128]{3,2,1,0:T(8,128)(2,1)S(1)}, u32[]{:S(2)}, u32[]{:S(2)}) collective-permute-start(bf16[2,28,8,128]{3,2,1,0:T(8,128)(2,1)S(1)} %reduce-precision_convert_fusion), channel_id=1, source_target_pairs={{0,16},{1,5},{2,18},{3,7},{4,20},{5,1},{6,22},{7,3},{8,24},{9,13},... | collective-permute-start | bytes 344072 | tf_op jit(solution)/shard_map/ppermute | solution.py:32
  21.5 0.7 %collective-permute-start.7 = (bf16[2,28,8,128]{3,2,1,0:T(8,128)(2,1)S(1)}, bf16[2,28,8,128]{3,2,1,0:T(8,128)(2,1)S(1)}, u32[]{:S(2)}, u32[]{:S(2)}) collective-permute-start(bf16[2,28,8,128]{3,2,1,0:T(8,128)(2,1)S(1)} %reduce-precision_convert_fusion), channel_id=1, source_target_pairs={{0,8},{1,3},{2,10},{3,1},{4,12},{5,7},{6,14},{7,5},{8,0},{9,11},{1... | collective-permute-start | bytes 344072 | tf_op jit(solution)/shard_map/ppermute | solution.py:32
  22.2 0.7 %collective-permute-start.8 = (bf16[2,28,8,128]{3,2,1,0:T(8,128)(2,1)S(1)}, bf16[2,28,8,128]{3,2,1,0:T(8,128)(2,1)S(1)}, u32[]{:S(2)}, u32[]{:S(2)}) collective-permute-start(bf16[2,28,8,128]{3,2,1,0:T(8,128)(2,1)S(1)} %reduce-precision_convert_fusion), channel_id=1, source_target_pairs={{0,24},{1,7},{2,26},{3,5},{4,28},{5,3},{6,30},{7,1},{8,16},{9,15},... | collective-permute-start | bytes 344072 | tf_op jit(solution)/shard_map/ppermute | solution.py:32
  22.9 1.2 %backward.1 = (bf16[256,128]{1,0:T(8,128)(2,1)}, bf16[256,128]{1,0:T(8,128)(2,1)}) custom-call(bf16[256,128]{1,0:T(8,128)(2,1)S(1)} %get-tuple-element.31.pre_grad_ref, bf16[256,128]{1,0:T(8,128)(2,1)S(1)} %collective-permute-done.5.next_ref, bf16[256,128]{1,0:T(8,128)(2,1)S(1)} %get-tuple-element.34.hidden_ref, ...), custom_call_target="tpu_custom_call" | custom-call | flops 234881024 | bytes 1048576 | tf_op jit(solution)/shard_map/backward/pallas_call | solution.py:329
  24.2 0.1 collective-permute-done.6
  24.2 1.2 %collective-permute-done.7 = bf16[2,28,8,128]{3,2,1,0:T(8,128)(2,1)S(1)} collective-permute-done((bf16[2,28,8,128]{3,2,1,0:T(8,128)(2,1)S(1)}, bf16[2,28,8,128]{3,2,1,0:T(8,128)(2,1)S(1)}, u32[]{:S(2)}, u32[]{:S(2)}) %collective-permute-start.7) | collective-permute-done | bytes 114720 | tf_op jit(solution)/shard_map/ppermute | solution.py:32
  25.5 1.3 %collective-permute-done.8 = bf16[2,28,8,128]{3,2,1,0:T(8,128)(2,1)S(1)} collective-permute-done((bf16[2,28,8,128]{3,2,1,0:T(8,128)(2,1)S(1)}, bf16[2,28,8,128]{3,2,1,0:T(8,128)(2,1)S(1)}, u32[]{:S(2)}, u32[]{:S(2)}) %collective-permute-start.8) | collective-permute-done | bytes 114720 | tf_op jit(solution)/shard_map/ppermute | solution.py:32
  26.8 0.1 add_convert_fusion
  26.8 2.2 %collective-permute-start.9 = (bf16[2,28,8,128]{3,2,1,0:T(8,128)(2,1)S(1)}, bf16[2,28,8,128]{3,2,1,0:T(8,128)(2,1)S(1)}, u32[]{:S(2)}, u32[]{:S(2)}) collective-permute-start(bf16[2,28,8,128]{3,2,1,0:T(8,128)(2,1)S(1)} %add_convert_fusion), channel_id=1, source_target_pairs={{0,4},{1,17},{2,6},{3,19},{4,0},{5,21},{6,2},{7,23},{8,12},{9,25},... | collective-permute-start | bytes 344072 | tf_op jit(solution)/shard_map/ppermute | solution.py:32
  29.0 1.4 %collective-permute-start.10 = (bf16[2,28,8,128]{3,2,1,0:T(8,128)(2,1)S(1)}, bf16[2,28,8,128]{3,2,1,0:T(8,128)(2,1)S(1)}, u32[]{:S(2)}, u32[]{:S(2)}) collective-permute-start(bf16[2,28,8,128]{3,2,1,0:T(8,128)(2,1)S(1)} %add_convert_fusion), channel_id=1, source_target_pairs={{0,2},{1,9},{2,0},{3,11},{4,6},{5,13},{6,4},{7,15},{8,10},{9,1},{1... | collective-permute-start | bytes 344072 | tf_op jit(solution)/shard_map/ppermute | solution.py:32
  30.4 0.1 collective-permute-start.11
  30.5 2.3 %collective-permute-done.9 = bf16[2,28,8,128]{3,2,1,0:T(8,128)(2,1)S(1)} collective-permute-done((bf16[2,28,8,128]{3,2,1,0:T(8,128)(2,1)S(1)}, bf16[2,28,8,128]{3,2,1,0:T(8,128)(2,1)S(1)}, u32[]{:S(2)}, u32[]{:S(2)}) %collective-permute-start.9) | collective-permute-done | bytes 114720 | tf_op jit(solution)/shard_map/ppermute | solution.py:32
  32.8 0.1 collective-permute-done.10
  32.9 3.0 %collective-permute-done.11 = bf16[2,28,8,128]{3,2,1,0:T(8,128)(2,1)S(1)} collective-permute-done((bf16[2,28,8,128]{3,2,1,0:T(8,128)(2,1)S(1)}, bf16[2,28,8,128]{3,2,1,0:T(8,128)(2,1)S(1)}, u32[]{:S(2)}, u32[]{:S(2)}) %collective-permute-start.11) | collective-permute-done | bytes 114720 | tf_op jit(solution)/shard_map/ppermute | solution.py:32
  35.8 3.0 %collective-permute-start.12 = (bf16[8,28,8,128]{3,2,1,0:T(8,128)(2,1)S(1)}, bf16[8,28,8,128]{3,2,1,0:T(8,128)(2,1)S(1)}, u32[]{:S(2)}, u32[]{:S(2)}) collective-permute-start(bf16[8,28,8,128]{3,2,1,0:T(8,128)(2,1)S(1)} %constant_dynamic-update-slice_fusion.mine_ref), channel_id=1, source_target_pairs={{0,1},{1,0},{2,3},{3,2},{4,5},{5,4},{6,7},{7,6},{8,9},{9,8},{10,11... | collective-permute-start | bytes 1376264 | tf_op jit(solution)/shard_map/ppermute | solution.py:32
  38.8 1.4 %collective-permute-done.12.other_ref = bf16[8,28,8,128]{3,2,1,0:T(8,128)(2,1)S(1)} collective-permute-done((bf16[8,28,8,128]{3,2,1,0:T(8,128)(2,1)S(1)}, bf16[8,28,8,128]{3,2,1,0:T(8,128)(2,1)S(1)}, u32[]{:S(2)}, u32[]{:S(2)}) %collective-permute-start.12) | collective-permute-done | bytes 458784 | tf_op jit(solution)/shard_map/ppermute | solution.py:32
  40.3 1.3 %unpack.1 = (f32[27,128,128]{2,1,0:T(8,128)}, f32[128,128]{1,0:T(8,128)}) custom-call(s32[1]{0:T(128)} %bitcast.me_ref, bf16[8,28,8,128]{3,2,1,0:T(8,128)(2,1)S(1)} %constant_dynamic-update-slice_fusion.mine_ref, bf16[8,28,8,128]{3,2,1,0:T(8,128)(2,1)S(1)} %collective-permute-done.12.other_ref), custom_call_target="tpu_custom_call" | custom-call | tf_op jit(solution)/shard_map/unpack/pallas_call | solution.py:263
  (6 shorter events, 0.1 us)
Async XLA Ops:
  0.6 6.3 %collective-permute-start = (bf16[256,128]{1,0:T(8,128)(2,1)}, bf16[256,128]{1,0:T(8,128)(2,1)S(1)}, u32[]{:S(2)}, u32[]{:S(2)}) collective-permute-start(bf16[256,128]{1,0:T(8,128)(2,1)} %bitcast.7), channel_id=1, source_target_pairs={{0,1},{1,2},{2,3},{4,5},{5,6},{6,7},{8,9},{9,10},{10,11},{12,13},{... | collective-permute-start | bytes 196616 | tf_op jit(solution)/shard_map/ppermute | solution.py:23
  8.0 2.5 %collective-permute-start.1 = (f32[8,28,8,128]{3,2,1,0:T(8,128)S(1)}, f32[8,28,8,128]{3,2,1,0:T(8,128)S(1)}, u32[]{:S(2)}, u32[]{:S(2)}) collective-permute-start(f32[8,28,8,128]{3,2,1,0:T(8,128)S(1)} %get-tuple-element.30), channel_id=1, source_target_pairs={{0,1},{1,0},{2,3},{3,2},{4,5},{5,4},{6,7},{7,6},{8,9},{9,8},{10,11... | collective-permute-start | bytes 2752520 | tf_op jit(solution)/shard_map/ppermute | solution.py:32
  10.8 6.0 %collective-permute-start.2 = (bf16[2,28,8,128]{3,2,1,0:T(8,128)(2,1)S(1)}, bf16[2,28,8,128]{3,2,1,0:T(8,128)(2,1)S(1)}, u32[]{:S(2)}, u32[]{:S(2)}) collective-permute-start(bf16[2,28,8,128]{3,2,1,0:T(8,128)(2,1)S(1)} %get-tuple-element.46), channel_id=1, source_target_pairs={{0,6},{1,25},{2,4},{3,27},{4,2},{5,29},{6,0},{7,31},{8,14},{9,17},... | collective-permute-start | bytes 344072 | tf_op jit(solution)/shard_map/ppermute | solution.py:32
  14.1 4.9 %collective-permute-start.3 = (bf16[2,28,8,128]{3,2,1,0:T(8,128)(2,1)S(1)}, bf16[2,28,8,128]{3,2,1,0:T(8,128)(2,1)S(1)}, u32[]{:S(2)}, u32[]{:S(2)}) collective-permute-start(bf16[2,28,8,128]{3,2,1,0:T(8,128)(2,1)S(1)} %get-tuple-element.48), channel_id=1, source_target_pairs={{0,2},{1,9},{2,0},{3,11},{4,6},{5,13},{6,4},{7,15},{8,10},{9,1},{1... | collective-permute-start | bytes 344072 | tf_op jit(solution)/shard_map/ppermute | solution.py:32
  14.1 4.9 %collective-permute-start.4 = (bf16[2,28,8,128]{3,2,1,0:T(8,128)(2,1)S(1)}, bf16[2,28,8,128]{3,2,1,0:T(8,128)(2,1)S(1)}, u32[]{:S(2)}, u32[]{:S(2)}) collective-permute-start(bf16[2,28,8,128]{3,2,1,0:T(8,128)(2,1)S(1)} %get-tuple-element.47), channel_id=1, source_target_pairs={{0,4},{1,17},{2,6},{3,19},{4,0},{5,21},{6,2},{7,23},{8,12},{9,25},... | collective-permute-start | bytes 344072 | tf_op jit(solution)/shard_map/ppermute | solution.py:32
  14.5 5.7 %collective-permute-start.5 = (bf16[256,128]{1,0:T(8,128)(2,1)S(1)}, bf16[256,128]{1,0:T(8,128)(2,1)S(1)}, u32[]{:S(2)}, u32[]{:S(2)}) collective-permute-start(bf16[256,128]{1,0:T(8,128)(2,1)S(1)} %get-tuple-element.31.pre_grad_ref), channel_id=1, source_target_pairs={{1,0},{2,1},{3,2},{5,4},{6,5},{7,6},{9,8},{10,9},{11,10},{13,12},{... | collective-permute-start | bytes 196616 | tf_op jit(solution)/shard_map/ppermute | solution.py:23
  20.2 4.0 %collective-permute-start.6 = (bf16[2,28,8,128]{3,2,1,0:T(8,128)(2,1)S(1)}, bf16[2,28,8,128]{3,2,1,0:T(8,128)(2,1)S(1)}, u32[]{:S(2)}, u32[]{:S(2)}) collective-permute-start(bf16[2,28,8,128]{3,2,1,0:T(8,128)(2,1)S(1)} %reduce-precision_convert_fusion), channel_id=1, source_target_pairs={{0,16},{1,5},{2,18},{3,7},{4,20},{5,1},{6,22},{7,3},{8,24},{9,13},... | collective-permute-start | bytes 344072 | tf_op jit(solution)/shard_map/ppermute | solution.py:32
  21.5 3.9 %collective-permute-start.7 = (bf16[2,28,8,128]{3,2,1,0:T(8,128)(2,1)S(1)}, bf16[2,28,8,128]{3,2,1,0:T(8,128)(2,1)S(1)}, u32[]{:S(2)}, u32[]{:S(2)}) collective-permute-start(bf16[2,28,8,128]{3,2,1,0:T(8,128)(2,1)S(1)} %reduce-precision_convert_fusion), channel_id=1, source_target_pairs={{0,8},{1,3},{2,10},{3,1},{4,12},{5,7},{6,14},{7,5},{8,0},{9,11},{1... | collective-permute-start | bytes 344072 | tf_op jit(solution)/shard_map/ppermute | solution.py:32
  22.2 4.5 %collective-permute-start.8 = (bf16[2,28,8,128]{3,2,1,0:T(8,128)(2,1)S(1)}, bf16[2,28,8,128]{3,2,1,0:T(8,128)(2,1)S(1)}, u32[]{:S(2)}, u32[]{:S(2)}) collective-permute-start(bf16[2,28,8,128]{3,2,1,0:T(8,128)(2,1)S(1)} %reduce-precision_convert_fusion), channel_id=1, source_target_pairs={{0,24},{1,7},{2,26},{3,5},{4,28},{5,3},{6,30},{7,1},{8,16},{9,15},... | collective-permute-start | bytes 344072 | tf_op jit(solution)/shard_map/ppermute | solution.py:32
  26.8 5.9 %collective-permute-start.9 = (bf16[2,28,8,128]{3,2,1,0:T(8,128)(2,1)S(1)}, bf16[2,28,8,128]{3,2,1,0:T(8,128)(2,1)S(1)}, u32[]{:S(2)}, u32[]{:S(2)}) collective-permute-start(bf16[2,28,8,128]{3,2,1,0:T(8,128)(2,1)S(1)} %add_convert_fusion), channel_id=1, source_target_pairs={{0,4},{1,17},{2,6},{3,19},{4,0},{5,21},{6,2},{7,23},{8,12},{9,25},... | collective-permute-start | bytes 344072 | tf_op jit(solution)/shard_map/ppermute | solution.py:32
  29.0 3.8 %collective-permute-start.10 = (bf16[2,28,8,128]{3,2,1,0:T(8,128)(2,1)S(1)}, bf16[2,28,8,128]{3,2,1,0:T(8,128)(2,1)S(1)}, u32[]{:S(2)}, u32[]{:S(2)}) collective-permute-start(bf16[2,28,8,128]{3,2,1,0:T(8,128)(2,1)S(1)} %add_convert_fusion), channel_id=1, source_target_pairs={{0,2},{1,9},{2,0},{3,11},{4,6},{5,13},{6,4},{7,15},{8,10},{9,1},{1... | collective-permute-start | bytes 344072 | tf_op jit(solution)/shard_map/ppermute | solution.py:32
  30.4 5.4 %collective-permute-start.11 = (bf16[2,28,8,128]{3,2,1,0:T(8,128)(2,1)S(1)}, bf16[2,28,8,128]{3,2,1,0:T(8,128)(2,1)S(1)}, u32[]{:S(2)}, u32[]{:S(2)}) collective-permute-start(bf16[2,28,8,128]{3,2,1,0:T(8,128)(2,1)S(1)} %add_convert_fusion), channel_id=1, source_target_pairs={{0,6},{1,25},{2,4},{3,27},{4,2},{5,29},{6,0},{7,31},{8,14},{9,17},... | collective-permute-start | bytes 344072 | tf_op jit(solution)/shard_map/ppermute | solution.py:32
  35.8 4.4 %collective-permute-start.12 = (bf16[8,28,8,128]{3,2,1,0:T(8,128)(2,1)S(1)}, bf16[8,28,8,128]{3,2,1,0:T(8,128)(2,1)S(1)}, u32[]{:S(2)}, u32[]{:S(2)}) collective-permute-start(bf16[8,28,8,128]{3,2,1,0:T(8,128)(2,1)S(1)} %constant_dynamic-update-slice_fusion.mine_ref), channel_id=1, source_target_pairs={{0,1},{1,0},{2,3},{3,2},{4,5},{5,4},{6,7},{7,6},{8,9},{9,8},{10,11... | collective-permute-start | bytes 1376264 | tf_op jit(solution)/shard_map/ppermute | solution.py:32

commit v5 on v4

--- a/solution.py
+++ b/solution.py
@@ -17,10 +17,9 @@
 OUTSIDE = pl.BlockSpec(memory_space=pltpu.HBM)
 
 
-def passed_along(shard, axis, by):
+def passed_round(shard, axis, by):
     size = lax.axis_size(axis)
-    pairs = [(i, i + by) for i in range(size) if 0 <= i + by < size]
-    return lax.ppermute(shard, axis, pairs)
+    return lax.ppermute(shard, axis, [(i, (i + by) % size) for i in range(size)])
 
 
 def device_number():
@@ -76,6 +75,16 @@
     wide_ref[:, 2 * chans :] = before if flipped else after
 
 
+def spread_unless(outside, ref, width, wide_ref, flipped=False):
+    @pl.when(outside)
+    def _():
+        wide_ref[...] = jnp.zeros(wide_ref.shape, wide_ref.dtype)
+
+    @pl.when(jnp.logical_not(outside))
+    def _():
+        spread(ref[...], width, wide_ref, flipped)
+
+
 def weights_of(kern_ref, tau):
     chans = kern_ref.shape[-1]
     return jnp.concatenate(
@@ -90,33 +99,34 @@
     _, height, width, chans = shape
     map_rows = height * width
     rows = shape[0] * map_rows
-    pairs = (
-        (frames_hbm, frames_ref), (kern_hbm, kern_ref), (grads_hbm, grads_ref), (proj_hbm, proj_ref)
-    )
+    pairs = [(frames_hbm, frames_ref)]
+    pairs += [(kern_hbm.at[tau], kern_ref.at[tau]) for tau in (2, 1, 0)]
+    pairs += [(proj_hbm, proj_ref), (grads_hbm, grads_ref)]
     copies = [pltpu.make_async_copy(*pair, sems.at[i]) for i, pair in enumerate(pairs)]
     for copy in copies:
         copy.start()
     copies[0].wait()
     spread(frames_ref[...], width, wide_ref)
-    copies[1].wait()
-    sums_ref[...] = dot(wide_ref[...], weights_of(kern_ref, 2), (1, 0))
-    for tau in range(2):
-        skip = (2 - tau) * map_rows
-        if skip < rows:
+    for place, tau in enumerate((2, 1, 0)):
+        copies[1 + place].wait()
+        skip = place * map_rows
+        if place == 0:
+            sums_ref[...] = dot(wide_ref[...], weights_of(kern_ref, tau), (1, 0))
+        elif skip < rows:
             sums_ref[skip:] += dot(wide_ref[: rows - skip], weights_of(kern_ref, tau), (1, 0))
-    copies[2].wait()
-    copies[3].wait()
+    copies[4].wait()
+    copies[5].wait()
     hidden_grad_ref[...] = dot(grads_ref[...], proj_ref[...], (1, 1))
 
 
 def forward_kernel(
-    shape, me_ref, halo_ref, grads_ref, kern_ref, own_ref, sums_ref, hidden_grad_ref,
+    shape, where_ref, halo_ref, grads_ref, kern_ref, own_ref, sums_ref, hidden_grad_ref,
     keep_ref, send_ref, hidden_ref, pre_grad_ref, wide_ref,
 ):
     _, height, width, chans = shape
     map_rows = height * width
     rows = shape[0] * map_rows
-    spread(halo_ref[...], width, wide_ref)
+    spread_unless((where_ref[0] & 2) != 0, halo_ref, width, wide_ref)
     term = dot(wide_ref[...], weights_of(kern_ref, 0), (1, 0))
     early = dot(wide_ref[map_rows:], weights_of(kern_ref, 1), (1, 0))
     head = jnp.concatenate([term[:map_rows] + early, term[map_rows:]], axis=0)
@@ -138,7 +148,7 @@
     pre_grad = (hidden_grad_ref[...] * sig * (1.0 + pre * (1.0 - sig))).astype(jnp.bfloat16)
     hidden_ref[...] = hidden
     pre_grad_ref[...] = pre_grad
-    me = me_ref[0]
+    me = where_ref[0] >> 2
     core = me & 1
     mine, other = halves_of(me)
 
@@ -173,14 +183,14 @@
 
 
 def backward_kernel(
-    shape, pre_grad_ref, next_ref, hidden_ref, frames_ref, grads_ref, kern_ref, proj_ref,
+    shape, where_ref, pre_grad_ref, next_ref, hidden_ref, frames_ref, grads_ref, kern_ref, proj_ref,
     mixed_ref, input_grad_ref, wide_ref,
 ):
     _, height, width, chans = shape
     map_rows = height * width
     rows = shape[0] * map_rows
     spread(pre_grad_ref[...], width, wide_ref.at[:rows], flipped=True)
-    spread(next_ref[...], width, wide_ref.at[rows:], flipped=True)
+    spread_unless((where_ref[0] & 1) != 0, next_ref, width, wide_ref.at[rows:], flipped=True)
     sums = None
     for tau in range(3):
         weights = jnp.concatenate(
@@ -200,8 +210,8 @@
     ).astype(jnp.bfloat16)
 
 
-def unpack_kernel(scale, me_ref, mine_ref, other_ref, kern_ref, proj_ref, out_ref, sems):
-    me = me_ref[0]
+def unpack_kernel(scale, where_ref, mine_ref, other_ref, kern_ref, proj_ref, out_ref, sems):
+    me = where_ref[0] >> 2
     core = me & 1
     mine, other = halves_of(me)
     taps = kern_ref.shape[0]
@@ -230,7 +240,7 @@
         copy.wait()
 
 
-def summed(me, keep, send, scale, beside_split, beside_exchange):
+def summed(where, keep, send, scale, beside_split, beside_exchange):
     taps, chans = keep.shape[1] - 1, keep.shape[3]
     total = keep + swapped(send, (1, 1))
     part = total.shape[0] // 4
@@ -274,7 +284,7 @@
         ],
         compiler_params=LIMIT,
         name="unpack",
-    )(me, total, other), done
+    )(where, total, other), done
 
 
 def prepare(shape, frames, grads, conv_kernel, proj_weight):
@@ -293,7 +303,7 @@
         ),
         in_specs=[OUTSIDE] * 4,
         out_specs=(VECTOR,) * 7,
-        scratch_shapes=[pltpu.SemaphoreType.DMA((4,))],
+        scratch_shapes=[pltpu.SemaphoreType.DMA((6,))],
         compiler_params=LIMIT,
         cost_estimate=pl.CostEstimate(
             flops=2 * rows * 20 * chans * chans, bytes_accessed=1 << 20, transcendentals=0
@@ -302,7 +312,7 @@
     )(*(pltpu.with_memory_space_constraint(x, pltpu.HBM) for x in (frames, grads, conv_kernel, proj_weight)))
 
 
-def forward(shape, me, halo, grads, conv_kernel, own, sums, hidden_grad):
+def forward(shape, where, halo, grads, conv_kernel, own, sums, hidden_grad):
     n_frames, height, width, chans = shape
     rows = n_frames * height * width
     half = (8, 28, 8, chans)
@@ -319,23 +329,23 @@
         scratch_shapes=[pltpu.VMEM((2 * height * width, 3 * chans), jnp.bfloat16)],
         compiler_params=LIMIT,
         name="forward",
-    )(me, halo, grads, conv_kernel, own, sums, hidden_grad)
-
-
-def backward(shape, pre_grad, following, hidden, frames, grads, conv_kernel, proj_weight):
+    )(where, halo, grads, conv_kernel, own, sums, hidden_grad)
+
+
+def backward(shape, where, pre_grad, following, hidden, frames, grads, conv_kernel, proj_weight):
     n_frames, height, width, chans = shape
     rows = n_frames * height * width
     flops = 2 * rows * 28 * chans * chans
     return pl.pallas_call(
         functools.partial(backward_kernel, shape),
         out_shape=(jax.ShapeDtypeStruct((rows, chans), jnp.bfloat16),) * 2,
-        in_specs=[VECTOR] * 7,
+        in_specs=[SCALAR] + [VECTOR] * 7,
         out_specs=(VECTOR,) * 2,
         scratch_shapes=[pltpu.VMEM((rows + 2 * height * width, 3 * chans), jnp.bfloat16)],
         compiler_params=LIMIT,
         cost_estimate=pl.CostEstimate(flops=flops, bytes_accessed=1 << 20, transcendentals=0),
         name="backward",
-    )(pre_grad, following, hidden, frames, grads, conv_kernel, proj_weight)
+    )(where, pre_grad, following, hidden, frames, grads, conv_kernel, proj_weight)
 
 
 def shards(clip_frames, out_grad, conv_kernel, proj_weight):
@@ -345,23 +355,26 @@
     halo_rows = 2 * height * width
     frames = clip_frames.reshape(rows, chans)
     grads = out_grad.reshape(rows, chans)
-    me = device_number().astype(jnp.int32).reshape(1)
-    halo = passed_along(frames[rows - halo_rows :], "tm", 1)
+    block = lax.axis_index("tm")
+    first = (block == 0).astype(jnp.int32)
+    last = (block == lax.axis_size("tm") - 1).astype(jnp.int32)
+    where = (4 * device_number() + 2 * first + last).astype(jnp.int32).reshape(1)
+    halo = passed_round(frames[rows - halo_rows :], "tm", 1)
     frames, grads, conv_kernel, proj_weight, own, sums, hidden_grad = prepare(
         shape, frames, grads, conv_kernel, proj_weight
     )
     keep, send, hidden, pre_grad = forward(
-        shape, me, halo, grads, conv_kernel, own, sums, hidden_grad
+        shape, where, halo, grads, conv_kernel, own, sums, hidden_grad
     )
     total_pixels = lax.axis_size("dp") * lax.axis_size("tm") * rows
     (kernel_grad, proj_grad), (mixed, input_grad) = summed(
-        me,
+        where,
         keep,
         send,
         1.0 / math.sqrt(total_pixels),
-        lambda: passed_along(pre_grad[:halo_rows], "tm", -1),
+        lambda: passed_round(pre_grad[:halo_rows], "tm", -1),
         lambda following: backward(
-            shape, pre_grad, following, hidden, frames, grads, conv_kernel, proj_weight
+            shape, where, pre_grad, following, hidden, frames, grads, conv_kernel, proj_weight
         ),
     )
     return (

time: 42.1 us -> 40 us (0.950)
  starting transfers between devices: 19.9 us -> 17 us
  waiting for transfers between devices: 15.2 us -> 16 us
    ppermute x2, starting transfers between devices: 6.77 us -> 2.65 us  [passed_round(): lax.ppermute(shard, axis, [(i, (i + by) % size) for i in range(size)])]
    ppermute x11, waiting for transfers between devices: 14.1 us -> 16 us  [swapped(): lax.ppermute(array, AXES, [(i, i ^ masks[i & 1]) for i in range(count)])]
    ppermute x11, starting transfers between devices: 13.1 us -> 14.3 us  [swapped(): lax.ppermute(array, AXES, [(i, i ^ masks[i & 1]) for i in range(count)])]
    ppermute x2, waiting for transfers between devices: 1.13 us -> 0.01 us  [passed_round(): lax.ppermute(shard, axis, [(i, (i + by) % size) for i in range(size)])]
  transfers between devices with their start and end apart: 13 -> 13, of which waited for: 10 -> 9; matrix products, arithmetic and copies ran while one was open for 0% -> 0% of each run, Pallas kernels for 7% -> 8%
where the time goes in v5:
time: 40 us; the launch traced here: 39.5 us
  starting transfers between devices  17 us (42%)
  waiting for transfers between devices  16 us (40%)
  Pallas kernels  5.44 us (14%)
  between operations  0.72 us (2%)
    ppermute x11, waiting for transfers between devices, swapped(): lax.ppermute(array, AXES, [(i, i ^ masks[i & 1]) for i in range(count)])  16 us
    ppermute x11, starting transfers between devices, swapped(): lax.ppermute(array, AXES, [(i, i ^ masks[i & 1]) for i in range(count)])  14.3 us
    ppermute x2, starting transfers between devices, passed_round(): lax.ppermute(shard, axis, [(i, (i + by) % size) for i in range(size)])  2.65 us
    pallas_call x1, Pallas kernels, prepare(): pl.pallas_call(functools.partial(prepare_kernel, shape), out_shape=(jax.S...  1.72 us
    pallas_call x1, Pallas kernels, backward(): pl.pallas_call(functools.partial(backward_kernel, shape), out_shape=(jax....  1.3 us
    pallas_call x1, Pallas kernels, summed(): pl.pallas_call(functools.partial(unpack_kernel, scale), out_shape=(jax.Sh...  1.3 us
    pallas_call x1, Pallas kernels, forward(): pl.pallas_call(functools.partial(forward_kernel, shape), out_shape=(jax.S...  1.12 us
  transfers between devices with their start and end apart: 13, of which 9 were waited for; matrix products, arithmetic and copies ran while one was open for 0% of the time, Pallas kernels for 8%

profile of v5, /device:TPU:1, one launch (start us, length us, event | category | flops | bytes accessed | tf_op | source)
XLA Modules:
  0.0 39.5 jit_solution(1403438609377553822)
XLA Ops:
  0.6 2.7 %collective-permute-start = (bf16[256,128]{1,0:T(8,128)(2,1)}, bf16[256,128]{1,0:T(8,128)(2,1)S(1)}, u32[]{:S(2)}, u32[]{:S(2)}) collective-permute-start(bf16[256,128]{1,0:T(8,128)(2,1)} %bitcast.7), channel_id=1, source_target_pairs={{0,1},{1,2},{2,3},{3,0},{4,5},{5,6},{6,7},{7,4},{8,9},{9,10},{10,1... | collective-permute-start | bytes 196616 | tf_op jit(solution)/shard_map/ppermute | solution.py:22
  3.3 1.7 %prepare.1 = (bf16[256,128]{1,0:T(8,128)(2,1)S(1)}, bf16[256,128]{1,0:T(8,128)(2,1)S(1)}, bf16[3,3,3,128,128]{4,3,2,1,0:T(8,128)(2,1)S(1)}, bf16[128,128]{1,0:T(...) custom-call(bf16[256,128]{1,0:T(8,128)(2,1)} %bitcast.8, ...), custom_call_target="tpu_custom_call" | custom-call | flops 167772160 | bytes 1048576 | tf_op jit(solution)/shard_map/prepare/pallas_call | solution.py:293
  5.0 0.0 collective-permute-done.halo_ref
  5.0 1.1 %forward.1 = (f32[8,28,8,128]{3,2,1,0:T(8,128)S(1)}, f32[8,28,8,128]{3,2,1,0:T(8,128)S(1)}, bf16[256,128]{1,0:T(8,128)(2,1)S(1)}, bf16[256,128]{1,0:T(8,128)(2,1)S(1)}) custom-call(s32[1]{0:T(128)} %bitcast.where_ref, bf16[256,128]{1,0:T(8,128)(2,1)S(1)} %collective-permute-done.halo_ref, bf16[256,128]{1,0:T(8,128)(2,1)S(1)} %get-tuple-element.24.grads_ref, ...), custom_call_target="tpu_custom_call" | custom-call | tf_op jit(solution)/shard_map/forward/pallas_call | solution.py:319
  6.2 0.3 collective-permute-start.1
  6.4 2.3 %collective-permute-done.1 = f32[8,28,8,128]{3,2,1,0:T(8,128)S(1)} collective-permute-done((f32[8,28,8,128]{3,2,1,0:T(8,128)S(1)}, f32[8,28,8,128]{3,2,1,0:T(8,128)S(1)}, u32[]{:S(2)}, u32[]{:S(2)}) %collective-permute-start.1) | collective-permute-done | bytes 917536 | tf_op jit(solution)/shard_map/ppermute | solution.py:31
  8.7 0.1 fusion.2
  8.9 4.0 %collective-permute-start.2 = (bf16[2,28,8,128]{3,2,1,0:T(8,128)(2,1)S(1)}, bf16[2,28,8,128]{3,2,1,0:T(8,128)(2,1)S(1)}, u32[]{:S(2)}, u32[]{:S(2)}) collective-permute-start(bf16[2,28,8,128]{3,2,1,0:T(8,128)(2,1)S(1)} %get-tuple-element.46), channel_id=1, source_target_pairs={{0,6},{1,25},{2,4},{3,27},{4,2},{5,29},{6,0},{7,31},{8,14},{9,17},... | collective-permute-start | bytes 344072 | tf_op jit(solution)/shard_map/ppermute | solution.py:31
  12.9 0.0 collective-permute-start.3
  12.9 0.4 collective-permute-start.4
  13.3 0.0 collective-permute-start.5
  13.3 1.9 %collective-permute-done.2 = bf16[2,28,8,128]{3,2,1,0:T(8,128)(2,1)S(1)} collective-permute-done((bf16[2,28,8,128]{3,2,1,0:T(8,128)(2,1)S(1)}, bf16[2,28,8,128]{3,2,1,0:T(8,128)(2,1)S(1)}, u32[]{:S(2)}, u32[]{:S(2)}) %collective-permute-start.2) | collective-permute-done | bytes 114720 | tf_op jit(solution)/shard_map/ppermute | solution.py:31
  15.2 2.6 %collective-permute-done.3 = bf16[2,28,8,128]{3,2,1,0:T(8,128)(2,1)S(1)} collective-permute-done((bf16[2,28,8,128]{3,2,1,0:T(8,128)(2,1)S(1)}, bf16[2,28,8,128]{3,2,1,0:T(8,128)(2,1)S(1)}, u32[]{:S(2)}, u32[]{:S(2)}) %collective-permute-start.3) | collective-permute-done | bytes 114720 | tf_op jit(solution)/shard_map/ppermute | solution.py:31
  17.8 0.0 collective-permute-done.4
  17.8 0.1 fusion.1
  17.8 0.0 collective-permute-done.5.next_ref
  17.9 1.3 %collective-permute-start.6 = (bf16[2,28,8,128]{3,2,1,0:T(8,128)(2,1)S(1)}, bf16[2,28,8,128]{3,2,1,0:T(8,128)(2,1)S(1)}, u32[]{:S(2)}, u32[]{:S(2)}) collective-permute-start(bf16[2,28,8,128]{3,2,1,0:T(8,128)(2,1)S(1)} %reduce-precision_convert_fusion), channel_id=1, source_target_pairs={{0,16},{1,5},{2,18},{3,7},{4,20},{5,1},{6,22},{7,3},{8,24},{9,13},... | collective-permute-start | bytes 344072 | tf_op jit(solution)/shard_map/ppermute | solution.py:31
  19.2 1.2 %collective-permute-start.7 = (bf16[2,28,8,128]{3,2,1,0:T(8,128)(2,1)S(1)}, bf16[2,28,8,128]{3,2,1,0:T(8,128)(2,1)S(1)}, u32[]{:S(2)}, u32[]{:S(2)}) collective-permute-start(bf16[2,28,8,128]{3,2,1,0:T(8,128)(2,1)S(1)} %reduce-precision_convert_fusion), channel_id=1, source_target_pairs={{0,8},{1,3},{2,10},{3,1},{4,12},{5,7},{6,14},{7,5},{8,0},{9,11},{1... | collective-permute-start | bytes 344072 | tf_op jit(solution)/shard_map/ppermute | solution.py:31
  20.4 0.2 collective-permute-start.8
  20.6 1.3 %backward.1 = (bf16[256,128]{1,0:T(8,128)(2,1)}, bf16[256,128]{1,0:T(8,128)(2,1)}) custom-call(s32[1]{0:T(128)} %bitcast.where_ref, bf16[256,128]{1,0:T(8,128)(2,1)S(1)} %get-tuple-element.31.pre_grad_ref, bf16[256,128]{1,0:T(8,128)(2,1)S(1)} %collective-permute-done.5.next_ref, bf16[256,128]{1,0:T(8,128)(2,1)S(1)} %get-tuple-element.34.hidden_ref, ...), custom_call_target="tpu_custom_call" | custom-call | flops 234881024 | bytes 1048576 | tf_op jit(solution)/shard_map/backward/pallas_call | solution.py:339
  21.9 0.0 collective-permute-done.6
  21.9 1.2 %collective-permute-done.7 = bf16[2,28,8,128]{3,2,1,0:T(8,128)(2,1)S(1)} collective-permute-done((bf16[2,28,8,128]{3,2,1,0:T(8,128)(2,1)S(1)}, bf16[2,28,8,128]{3,2,1,0:T(8,128)(2,1)S(1)}, u32[]{:S(2)}, u32[]{:S(2)}) %collective-permute-start.7) | collective-permute-done | bytes 114720 | tf_op jit(solution)/shard_map/ppermute | solution.py:31
  23.1 1.8 %collective-permute-done.8 = bf16[2,28,8,128]{3,2,1,0:T(8,128)(2,1)S(1)} collective-permute-done((bf16[2,28,8,128]{3,2,1,0:T(8,128)(2,1)S(1)}, bf16[2,28,8,128]{3,2,1,0:T(8,128)(2,1)S(1)}, u32[]{:S(2)}, u32[]{:S(2)}) %collective-permute-start.8) | collective-permute-done | bytes 114720 | tf_op jit(solution)/shard_map/ppermute | solution.py:31
  25.0 0.1 add_convert_fusion
  25.0 2.2 %collective-permute-start.9 = (bf16[2,28,8,128]{3,2,1,0:T(8,128)(2,1)S(1)}, bf16[2,28,8,128]{3,2,1,0:T(8,128)(2,1)S(1)}, u32[]{:S(2)}, u32[]{:S(2)}) collective-permute-start(bf16[2,28,8,128]{3,2,1,0:T(8,128)(2,1)S(1)} %add_convert_fusion), channel_id=1, source_target_pairs={{0,4},{1,17},{2,6},{3,19},{4,0},{5,21},{6,2},{7,23},{8,12},{9,25},... | collective-permute-start | bytes 344072 | tf_op jit(solution)/shard_map/ppermute | solution.py:31
  27.2 0.7 %collective-permute-start.10 = (bf16[2,28,8,128]{3,2,1,0:T(8,128)(2,1)S(1)}, bf16[2,28,8,128]{3,2,1,0:T(8,128)(2,1)S(1)}, u32[]{:S(2)}, u32[]{:S(2)}) collective-permute-start(bf16[2,28,8,128]{3,2,1,0:T(8,128)(2,1)S(1)} %add_convert_fusion), channel_id=1, source_target_pairs={{0,2},{1,9},{2,0},{3,11},{4,6},{5,13},{6,4},{7,15},{8,10},{9,1},{1... | collective-permute-start | bytes 344072 | tf_op jit(solution)/shard_map/ppermute | solution.py:31
  28.0 0.7 %collective-permute-start.11 = (bf16[2,28,8,128]{3,2,1,0:T(8,128)(2,1)S(1)}, bf16[2,28,8,128]{3,2,1,0:T(8,128)(2,1)S(1)}, u32[]{:S(2)}, u32[]{:S(2)}) collective-permute-start(bf16[2,28,8,128]{3,2,1,0:T(8,128)(2,1)S(1)} %add_convert_fusion), channel_id=1, source_target_pairs={{0,6},{1,25},{2,4},{3,27},{4,2},{5,29},{6,0},{7,31},{8,14},{9,17},... | collective-permute-start | bytes 344072 | tf_op jit(solution)/shard_map/ppermute | solution.py:31
  28.7 2.3 %collective-permute-done.9 = bf16[2,28,8,128]{3,2,1,0:T(8,128)(2,1)S(1)} collective-permute-done((bf16[2,28,8,128]{3,2,1,0:T(8,128)(2,1)S(1)}, bf16[2,28,8,128]{3,2,1,0:T(8,128)(2,1)S(1)}, u32[]{:S(2)}, u32[]{:S(2)}) %collective-permute-start.9) | collective-permute-done | bytes 114720 | tf_op jit(solution)/shard_map/ppermute | solution.py:31
  31.0 0.1 collective-permute-done.10
  31.1 2.3 %collective-permute-done.11 = bf16[2,28,8,128]{3,2,1,0:T(8,128)(2,1)S(1)} collective-permute-done((bf16[2,28,8,128]{3,2,1,0:T(8,128)(2,1)S(1)}, bf16[2,28,8,128]{3,2,1,0:T(8,128)(2,1)S(1)}, u32[]{:S(2)}, u32[]{:S(2)}) %collective-permute-start.11) | collective-permute-done | bytes 114720 | tf_op jit(solution)/shard_map/ppermute | solution.py:31
  33.4 3.3 %collective-permute-start.12 = (bf16[8,28,8,128]{3,2,1,0:T(8,128)(2,1)S(1)}, bf16[8,28,8,128]{3,2,1,0:T(8,128)(2,1)S(1)}, u32[]{:S(2)}, u32[]{:S(2)}) collective-permute-start(bf16[8,28,8,128]{3,2,1,0:T(8,128)(2,1)S(1)} %constant_dynamic-update-slice_fusion.mine_ref), channel_id=1, source_target_pairs={{0,1},{1,0},{2,3},{3,2},{4,5},{5,4},{6,7},{7,6},{8,9},{9,8},{10,11... | collective-permute-start | bytes 1376264 | tf_op jit(solution)/shard_map/ppermute | solution.py:31
  36.7 1.4 %collective-permute-done.12.other_ref = bf16[8,28,8,128]{3,2,1,0:T(8,128)(2,1)S(1)} collective-permute-done((bf16[8,28,8,128]{3,2,1,0:T(8,128)(2,1)S(1)}, bf16[8,28,8,128]{3,2,1,0:T(8,128)(2,1)S(1)}, u32[]{:S(2)}, u32[]{:S(2)}) %collective-permute-start.12) | collective-permute-done | bytes 458784 | tf_op jit(solution)/shard_map/ppermute | solution.py:31
  38.2 1.3 %unpack.1 = (f32[27,128,128]{2,1,0:T(8,128)}, f32[128,128]{1,0:T(8,128)}) custom-call(s32[1]{0:T(128)} %bitcast.where_ref, bf16[8,28,8,128]{3,2,1,0:T(8,128)(2,1)S(1)} %constant_dynamic-update-slice_fusion.mine_ref, bf16[8,28,8,128]{3,2,1,0:T(8,128)(2,1)S(1)} %collective-permute-done.12.other_ref), custom_call_target="tpu_custom_call" | custom-call | tf_op jit(solution)/shard_map/unpack/pallas_call | solution.py:273
  (6 shorter events, 0.1 us)
Async XLA Ops:
  0.6 4.4 %collective-permute-start = (bf16[256,128]{1,0:T(8,128)(2,1)}, bf16[256,128]{1,0:T(8,128)(2,1)S(1)}, u32[]{:S(2)}, u32[]{:S(2)}) collective-permute-start(bf16[256,128]{1,0:T(8,128)(2,1)} %bitcast.7), channel_id=1, source_target_pairs={{0,1},{1,2},{2,3},{3,0},{4,5},{5,6},{6,7},{7,4},{8,9},{9,10},{10,1... | collective-permute-start | bytes 196616 | tf_op jit(solution)/shard_map/ppermute | solution.py:22
  6.2 2.5 %collective-permute-start.1 = (f32[8,28,8,128]{3,2,1,0:T(8,128)S(1)}, f32[8,28,8,128]{3,2,1,0:T(8,128)S(1)}, u32[]{:S(2)}, u32[]{:S(2)}) collective-permute-start(f32[8,28,8,128]{3,2,1,0:T(8,128)S(1)} %get-tuple-element.30), channel_id=1, source_target_pairs={{0,1},{1,0},{2,3},{3,2},{4,5},{5,4},{6,7},{7,6},{8,9},{9,8},{10,11... | collective-permute-start | bytes 2752520 | tf_op jit(solution)/shard_map/ppermute | solution.py:31
  8.9 6.3 %collective-permute-start.2 = (bf16[2,28,8,128]{3,2,1,0:T(8,128)(2,1)S(1)}, bf16[2,28,8,128]{3,2,1,0:T(8,128)(2,1)S(1)}, u32[]{:S(2)}, u32[]{:S(2)}) collective-permute-start(bf16[2,28,8,128]{3,2,1,0:T(8,128)(2,1)S(1)} %get-tuple-element.46), channel_id=1, source_target_pairs={{0,6},{1,25},{2,4},{3,27},{4,2},{5,29},{6,0},{7,31},{8,14},{9,17},... | collective-permute-start | bytes 344072 | tf_op jit(solution)/shard_map/ppermute | solution.py:31
  12.9 4.9 %collective-permute-start.3 = (bf16[2,28,8,128]{3,2,1,0:T(8,128)(2,1)S(1)}, bf16[2,28,8,128]{3,2,1,0:T(8,128)(2,1)S(1)}, u32[]{:S(2)}, u32[]{:S(2)}) collective-permute-start(bf16[2,28,8,128]{3,2,1,0:T(8,128)(2,1)S(1)} %get-tuple-element.48), channel_id=1, source_target_pairs={{0,2},{1,9},{2,0},{3,11},{4,6},{5,13},{6,4},{7,15},{8,10},{9,1},{1... | collective-permute-start | bytes 344072 | tf_op jit(solution)/shard_map/ppermute | solution.py:31
  12.9 4.9 %collective-permute-start.4 = (bf16[2,28,8,128]{3,2,1,0:T(8,128)(2,1)S(1)}, bf16[2,28,8,128]{3,2,1,0:T(8,128)(2,1)S(1)}, u32[]{:S(2)}, u32[]{:S(2)}) collective-permute-start(bf16[2,28,8,128]{3,2,1,0:T(8,128)(2,1)S(1)} %get-tuple-element.47), channel_id=1, source_target_pairs={{0,4},{1,17},{2,6},{3,19},{4,0},{5,21},{6,2},{7,23},{8,12},{9,25},... | collective-permute-start | bytes 344072 | tf_op jit(solution)/shard_map/ppermute | solution.py:31
  13.3 4.6 %collective-permute-start.5 = (bf16[256,128]{1,0:T(8,128)(2,1)S(1)}, bf16[256,128]{1,0:T(8,128)(2,1)S(1)}, u32[]{:S(2)}, u32[]{:S(2)}) collective-permute-start(bf16[256,128]{1,0:T(8,128)(2,1)S(1)} %get-tuple-element.31.pre_grad_ref), channel_id=1, source_target_pairs={{0,3},{1,0},{2,1},{3,2},{4,7},{5,4},{6,5},{7,6},{8,11},{9,8},{10,9... | collective-permute-start | bytes 196616 | tf_op jit(solution)/shard_map/ppermute | solution.py:22
  17.9 4.0 %collective-permute-start.6 = (bf16[2,28,8,128]{3,2,1,0:T(8,128)(2,1)S(1)}, bf16[2,28,8,128]{3,2,1,0:T(8,128)(2,1)S(1)}, u32[]{:S(2)}, u32[]{:S(2)}) collective-permute-start(bf16[2,28,8,128]{3,2,1,0:T(8,128)(2,1)S(1)} %reduce-precision_convert_fusion), channel_id=1, source_target_pairs={{0,16},{1,5},{2,18},{3,7},{4,20},{5,1},{6,22},{7,3},{8,24},{9,13},... | collective-permute-start | bytes 344072 | tf_op jit(solution)/shard_map/ppermute | solution.py:31
  19.2 3.9 %collective-permute-start.7 = (bf16[2,28,8,128]{3,2,1,0:T(8,128)(2,1)S(1)}, bf16[2,28,8,128]{3,2,1,0:T(8,128)(2,1)S(1)}, u32[]{:S(2)}, u32[]{:S(2)}) collective-permute-start(bf16[2,28,8,128]{3,2,1,0:T(8,128)(2,1)S(1)} %reduce-precision_convert_fusion), channel_id=1, source_target_pairs={{0,8},{1,3},{2,10},{3,1},{4,12},{5,7},{6,14},{7,5},{8,0},{9,11},{1... | collective-permute-start | bytes 344072 | tf_op jit(solution)/shard_map/ppermute | solution.py:31
  20.4 4.5 %collective-permute-start.8 = (bf16[2,28,8,128]{3,2,1,0:T(8,128)(2,1)S(1)}, bf16[2,28,8,128]{3,2,1,0:T(8,128)(2,1)S(1)}, u32[]{:S(2)}, u32[]{:S(2)}) collective-permute-start(bf16[2,28,8,128]{3,2,1,0:T(8,128)(2,1)S(1)} %reduce-precision_convert_fusion), channel_id=1, source_target_pairs={{0,24},{1,7},{2,26},{3,5},{4,28},{5,3},{6,30},{7,1},{8,16},{9,15},... | collective-permute-start | bytes 344072 | tf_op jit(solution)/shard_map/ppermute | solution.py:31
  25.0 5.9 %collective-permute-start.9 = (bf16[2,28,8,128]{3,2,1,0:T(8,128)(2,1)S(1)}, bf16[2,28,8,128]{3,2,1,0:T(8,128)(2,1)S(1)}, u32[]{:S(2)}, u32[]{:S(2)}) collective-permute-start(bf16[2,28,8,128]{3,2,1,0:T(8,128)(2,1)S(1)} %add_convert_fusion), channel_id=1, source_target_pairs={{0,4},{1,17},{2,6},{3,19},{4,0},{5,21},{6,2},{7,23},{8,12},{9,25},... | collective-permute-start | bytes 344072 | tf_op jit(solution)/shard_map/ppermute | solution.py:31
  27.2 3.8 %collective-permute-start.10 = (bf16[2,28,8,128]{3,2,1,0:T(8,128)(2,1)S(1)}, bf16[2,28,8,128]{3,2,1,0:T(8,128)(2,1)S(1)}, u32[]{:S(2)}, u32[]{:S(2)}) collective-permute-start(bf16[2,28,8,128]{3,2,1,0:T(8,128)(2,1)S(1)} %add_convert_fusion), channel_id=1, source_target_pairs={{0,2},{1,9},{2,0},{3,11},{4,6},{5,13},{6,4},{7,15},{8,10},{9,1},{1... | collective-permute-start | bytes 344072 | tf_op jit(solution)/shard_map/ppermute | solution.py:31
  28.0 5.4 %collective-permute-start.11 = (bf16[2,28,8,128]{3,2,1,0:T(8,128)(2,1)S(1)}, bf16[2,28,8,128]{3,2,1,0:T(8,128)(2,1)S(1)}, u32[]{:S(2)}, u32[]{:S(2)}) collective-permute-start(bf16[2,28,8,128]{3,2,1,0:T(8,128)(2,1)S(1)} %add_convert_fusion), channel_id=1, source_target_pairs={{0,6},{1,25},{2,4},{3,27},{4,2},{5,29},{6,0},{7,31},{8,14},{9,17},... | collective-permute-start | bytes 344072 | tf_op jit(solution)/shard_map/ppermute | solution.py:31
  33.4 4.8 %collective-permute-start.12 = (bf16[8,28,8,128]{3,2,1,0:T(8,128)(2,1)S(1)}, bf16[8,28,8,128]{3,2,1,0:T(8,128)(2,1)S(1)}, u32[]{:S(2)}, u32[]{:S(2)}) collective-permute-start(bf16[8,28,8,128]{3,2,1,0:T(8,128)(2,1)S(1)} %constant_dynamic-update-slice_fusion.mine_ref), channel_id=1, source_target_pairs={{0,1},{1,0},{2,3},{3,2},{4,5},{5,4},{6,7},{7,6},{8,9},{9,8},{10,11... | collective-permute-start | bytes 1376264 | tf_op jit(solution)/shard_map/ppermute | solution.py:31

commit v6 on v5

--- a/solution.py
+++ b/solution.py
@@ -246,7 +246,7 @@
     part = total.shape[0] // 4
     came = [
         swapped(total[offset * part : (offset + 1) * part].astype(jnp.bfloat16), masks_of(0, offset))
-        for offset in (3, 2, 1)
+        for offset in (2, 1, 3)
     ]
     total = total[:part]
     for piece in came:
@@ -254,9 +254,9 @@
     done = beside_split()
     total, done = lax.optimization_barrier((total, done))
     total = lax.reduce_precision(total, 8, 7)
-    third, second, first = (
+    second, first, third = (
         swapped(total.astype(jnp.bfloat16), masks_of(1, offset)).astype(jnp.float32)
-        for offset in (3, 2, 1)
+        for offset in (2, 1, 3)
     )
     total = (total + first) + (second + third)
     count = lax.axis_size("dp") * lax.axis_size("tm")
@@ -267,7 +267,7 @@
     done = beside_exchange(done)
     total = total.astype(jnp.bfloat16)
     total, done = lax.optimization_barrier((total, done))
-    third, second, first = (swapped(total, masks_of(0, offset)) for offset in (3, 2, 1))
+    second, first, third = (swapped(total, masks_of(0, offset)) for offset in (2, 1, 3))
     total = jnp.concatenate([total, first, second, third], axis=0)
     other = swapped(total, (1, 1))
     return pl.pallas_call(

time: 40 us -> 40.5 us (1.012)
    ppermute x11, waiting for transfers between devices: 16 us -> 16.4 us  [swapped(): lax.ppermute(array, AXES, [(i, i ^ masks[i & 1]) for i in range(count)])]
  transfers between devices with their start and end apart: 13 -> 13, of which waited for: 9 -> 10; matrix products, arithmetic and copies ran while one was open for 0% -> 0% of each run, Pallas kernels for 8% -> 8%
where the time goes in v6:
time: 40.5 us; the launch traced here: 40.1 us
  starting transfers between devices  17.1 us (42%)
  waiting for transfers between devices  16.4 us (40%)
  Pallas kernels  5.44 us (13%)
  between operations  0.72 us (2%)
    ppermute x11, waiting for transfers between devices, swapped(): lax.ppermute(array, AXES, [(i, i ^ masks[i & 1]) for i in range(count)])  16.4 us
    ppermute x11, starting transfers between devices, swapped(): lax.ppermute(array, AXES, [(i, i ^ masks[i & 1]) for i in range(count)])  14.4 us
    ppermute x2, starting transfers between devices, passed_round(): lax.ppermute(shard, axis, [(i, (i + by) % size) for i in range(size)])  2.65 us
    pallas_call x1, Pallas kernels, prepare(): pl.pallas_call(functools.partial(prepare_kernel, shape), out_shape=(jax.S...  1.72 us
    pallas_call x1, Pallas kernels, backward(): pl.pallas_call(functools.partial(backward_kernel, shape), out_shape=(jax....  1.3 us
    pallas_call x1, Pallas kernels, summed(): pl.pallas_call(functools.partial(unpack_kernel, scale), out_shape=(jax.Sh...  1.3 us
    pallas_call x1, Pallas kernels, forward(): pl.pallas_call(functools.partial(forward_kernel, shape), out_shape=(jax.S...  1.12 us
  transfers between devices with their start and end apart: 13, of which 10 were waited for; matrix products, arithmetic and copies ran while one was open for 0% of the time, Pallas kernels for 8%

profile of v6, /device:TPU:1, one launch (start us, length us, event | category | flops | bytes accessed | tf_op | source)
XLA Modules:
  0.0 40.1 jit_solution(7489196828494367891)
XLA Ops:
  0.6 2.7 %collective-permute-start = (bf16[256,128]{1,0:T(8,128)(2,1)}, bf16[256,128]{1,0:T(8,128)(2,1)S(1)}, u32[]{:S(2)}, u32[]{:S(2)}) collective-permute-start(bf16[256,128]{1,0:T(8,128)(2,1)} %bitcast.7), channel_id=1, source_target_pairs={{0,1},{1,2},{2,3},{3,0},{4,5},{5,6},{6,7},{7,4},{8,9},{9,10},{10,1... | collective-permute-start | bytes 196616 | tf_op jit(solution)/shard_map/ppermute | solution.py:22
  3.3 1.7 %prepare.1 = (bf16[256,128]{1,0:T(8,128)(2,1)S(1)}, bf16[256,128]{1,0:T(8,128)(2,1)S(1)}, bf16[3,3,3,128,128]{4,3,2,1,0:T(8,128)(2,1)S(1)}, bf16[128,128]{1,0:T(...) custom-call(bf16[256,128]{1,0:T(8,128)(2,1)} %bitcast.8, ...), custom_call_target="tpu_custom_call" | custom-call | flops 167772160 | bytes 1048576 | tf_op jit(solution)/shard_map/prepare/pallas_call | solution.py:293
  5.0 0.0 collective-permute-done.halo_ref
  5.0 1.1 %forward.1 = (f32[8,28,8,128]{3,2,1,0:T(8,128)S(1)}, f32[8,28,8,128]{3,2,1,0:T(8,128)S(1)}, bf16[256,128]{1,0:T(8,128)(2,1)S(1)}, bf16[256,128]{1,0:T(8,128)(2,1)S(1)}) custom-call(s32[1]{0:T(128)} %bitcast.where_ref, bf16[256,128]{1,0:T(8,128)(2,1)S(1)} %collective-permute-done.halo_ref, bf16[256,128]{1,0:T(8,128)(2,1)S(1)} %get-tuple-element.24.grads_ref, ...), custom_call_target="tpu_custom_call" | custom-call | tf_op jit(solution)/shard_map/forward/pallas_call | solution.py:319
  6.2 0.3 collective-permute-start.1
  6.4 2.3 %collective-permute-done.1 = f32[8,28,8,128]{3,2,1,0:T(8,128)S(1)} collective-permute-done((f32[8,28,8,128]{3,2,1,0:T(8,128)S(1)}, f32[8,28,8,128]{3,2,1,0:T(8,128)S(1)}, u32[]{:S(2)}, u32[]{:S(2)}) %collective-permute-start.1) | collective-permute-done | bytes 917536 | tf_op jit(solution)/shard_map/ppermute | solution.py:31
  8.7 0.1 fusion.2
  8.9 2.0 %collective-permute-start.2 = (bf16[2,28,8,128]{3,2,1,0:T(8,128)(2,1)S(1)}, bf16[2,28,8,128]{3,2,1,0:T(8,128)(2,1)S(1)}, u32[]{:S(2)}, u32[]{:S(2)}) collective-permute-start(bf16[2,28,8,128]{3,2,1,0:T(8,128)(2,1)S(1)} %get-tuple-element.46), channel_id=1, source_target_pairs={{0,2},{1,9},{2,0},{3,11},{4,6},{5,13},{6,4},{7,15},{8,10},{9,1},{1... | collective-permute-start | bytes 344072 | tf_op jit(solution)/shard_map/ppermute | solution.py:31
  10.9 2.3 %collective-permute-start.3 = (bf16[2,28,8,128]{3,2,1,0:T(8,128)(2,1)S(1)}, bf16[2,28,8,128]{3,2,1,0:T(8,128)(2,1)S(1)}, u32[]{:S(2)}, u32[]{:S(2)}) collective-permute-start(bf16[2,28,8,128]{3,2,1,0:T(8,128)(2,1)S(1)} %get-tuple-element.48), channel_id=1, source_target_pairs={{0,4},{1,17},{2,6},{3,19},{4,0},{5,21},{6,2},{7,23},{8,12},{9,25},... | collective-permute-start | bytes 344072 | tf_op jit(solution)/shard_map/ppermute | solution.py:31
  13.2 0.0 collective-permute-start.4
  13.2 0.0 collective-permute-start.5
  13.2 0.2 collective-permute-done.2
  13.4 3.3 %collective-permute-done.3 = bf16[2,28,8,128]{3,2,1,0:T(8,128)(2,1)S(1)} collective-permute-done((bf16[2,28,8,128]{3,2,1,0:T(8,128)(2,1)S(1)}, bf16[2,28,8,128]{3,2,1,0:T(8,128)(2,1)S(1)}, u32[]{:S(2)}, u32[]{:S(2)}) %collective-permute-start.3) | collective-permute-done | bytes 114720 | tf_op jit(solution)/shard_map/ppermute | solution.py:31
  16.6 2.1 %collective-permute-done.4 = bf16[2,28,8,128]{3,2,1,0:T(8,128)(2,1)S(1)} collective-permute-done((bf16[2,28,8,128]{3,2,1,0:T(8,128)(2,1)S(1)}, bf16[2,28,8,128]{3,2,1,0:T(8,128)(2,1)S(1)}, u32[]{:S(2)}, u32[]{:S(2)}) %collective-permute-start.4) | collective-permute-done | bytes 114720 | tf_op jit(solution)/shard_map/ppermute | solution.py:31
  18.7 0.1 fusion.1
  18.8 0.0 collective-permute-done.5.next_ref
  18.8 1.3 %collective-permute-start.6 = (bf16[2,28,8,128]{3,2,1,0:T(8,128)(2,1)S(1)}, bf16[2,28,8,128]{3,2,1,0:T(8,128)(2,1)S(1)}, u32[]{:S(2)}, u32[]{:S(2)}) collective-permute-start(bf16[2,28,8,128]{3,2,1,0:T(8,128)(2,1)S(1)} %reduce-precision_convert_fusion), channel_id=1, source_target_pairs={{0,16},{1,5},{2,18},{3,7},{4,20},{5,1},{6,22},{7,3},{8,24},{9,13},... | collective-permute-start | bytes 344072 | tf_op jit(solution)/shard_map/ppermute | solution.py:31
  20.1 1.2 %collective-permute-start.7 = (bf16[2,28,8,128]{3,2,1,0:T(8,128)(2,1)S(1)}, bf16[2,28,8,128]{3,2,1,0:T(8,128)(2,1)S(1)}, u32[]{:S(2)}, u32[]{:S(2)}) collective-permute-start(bf16[2,28,8,128]{3,2,1,0:T(8,128)(2,1)S(1)} %reduce-precision_convert_fusion), channel_id=1, source_target_pairs={{0,8},{1,3},{2,10},{3,1},{4,12},{5,7},{6,14},{7,5},{8,0},{9,11},{1... | collective-permute-start | bytes 344072 | tf_op jit(solution)/shard_map/ppermute | solution.py:31
  21.4 0.2 collective-permute-start.8
  21.5 1.3 %backward.1 = (bf16[256,128]{1,0:T(8,128)(2,1)}, bf16[256,128]{1,0:T(8,128)(2,1)}) custom-call(s32[1]{0:T(128)} %bitcast.where_ref, bf16[256,128]{1,0:T(8,128)(2,1)S(1)} %get-tuple-element.31.pre_grad_ref, bf16[256,128]{1,0:T(8,128)(2,1)S(1)} %collective-permute-done.5.next_ref, bf16[256,128]{1,0:T(8,128)(2,1)S(1)} %get-tuple-element.34.hidden_ref, ...), custom_call_target="tpu_custom_call" | custom-call | flops 234881024 | bytes 1048576 | tf_op jit(solution)/shard_map/backward/pallas_call | solution.py:339
  22.9 0.0 collective-permute-done.6
  22.9 1.2 %collective-permute-done.7 = bf16[2,28,8,128]{3,2,1,0:T(8,128)(2,1)S(1)} collective-permute-done((bf16[2,28,8,128]{3,2,1,0:T(8,128)(2,1)S(1)}, bf16[2,28,8,128]{3,2,1,0:T(8,128)(2,1)S(1)}, u32[]{:S(2)}, u32[]{:S(2)}) %collective-permute-start.7) | collective-permute-done | bytes 114720 | tf_op jit(solution)/shard_map/ppermute | solution.py:31
  24.1 1.8 %collective-permute-done.8 = bf16[2,28,8,128]{3,2,1,0:T(8,128)(2,1)S(1)} collective-permute-done((bf16[2,28,8,128]{3,2,1,0:T(8,128)(2,1)S(1)}, bf16[2,28,8,128]{3,2,1,0:T(8,128)(2,1)S(1)}, u32[]{:S(2)}, u32[]{:S(2)}) %collective-permute-start.8) | collective-permute-done | bytes 114720 | tf_op jit(solution)/shard_map/ppermute | solution.py:31
  25.9 0.1 add_convert_fusion
  26.0 1.8 %collective-permute-start.9 = (bf16[2,28,8,128]{3,2,1,0:T(8,128)(2,1)S(1)}, bf16[2,28,8,128]{3,2,1,0:T(8,128)(2,1)S(1)}, u32[]{:S(2)}, u32[]{:S(2)}) collective-permute-start(bf16[2,28,8,128]{3,2,1,0:T(8,128)(2,1)S(1)} %add_convert_fusion), channel_id=1, source_target_pairs={{0,4},{1,17},{2,6},{3,19},{4,0},{5,21},{6,2},{7,23},{8,12},{9,25},... | collective-permute-start | bytes 344072 | tf_op jit(solution)/shard_map/ppermute | solution.py:31
  27.8 0.4 %collective-permute-start.10 = (bf16[2,28,8,128]{3,2,1,0:T(8,128)(2,1)S(1)}, bf16[2,28,8,128]{3,2,1,0:T(8,128)(2,1)S(1)}, u32[]{:S(2)}, u32[]{:S(2)}) collective-permute-start(bf16[2,28,8,128]{3,2,1,0:T(8,128)(2,1)S(1)} %add_convert_fusion), channel_id=1, source_target_pairs={{0,2},{1,9},{2,0},{3,11},{4,6},{5,13},{6,4},{7,15},{8,10},{9,1},{1... | collective-permute-start | bytes 344072 | tf_op jit(solution)/shard_map/ppermute | solution.py:31
  28.2 1.4 %collective-permute-start.11 = (bf16[2,28,8,128]{3,2,1,0:T(8,128)(2,1)S(1)}, bf16[2,28,8,128]{3,2,1,0:T(8,128)(2,1)S(1)}, u32[]{:S(2)}, u32[]{:S(2)}) collective-permute-start(bf16[2,28,8,128]{3,2,1,0:T(8,128)(2,1)S(1)} %add_convert_fusion), channel_id=1, source_target_pairs={{0,6},{1,25},{2,4},{3,27},{4,2},{5,29},{6,0},{7,31},{8,14},{9,17},... | collective-permute-start | bytes 344072 | tf_op jit(solution)/shard_map/ppermute | solution.py:31
  29.6 2.3 %collective-permute-done.9 = bf16[2,28,8,128]{3,2,1,0:T(8,128)(2,1)S(1)} collective-permute-done((bf16[2,28,8,128]{3,2,1,0:T(8,128)(2,1)S(1)}, bf16[2,28,8,128]{3,2,1,0:T(8,128)(2,1)S(1)}, u32[]{:S(2)}, u32[]{:S(2)}) %collective-permute-start.9) | collective-permute-done | bytes 114720 | tf_op jit(solution)/shard_map/ppermute | solution.py:31
  32.0 0.2 collective-permute-done.10
  32.2 1.6 %collective-permute-done.11 = bf16[2,28,8,128]{3,2,1,0:T(8,128)(2,1)S(1)} collective-permute-done((bf16[2,28,8,128]{3,2,1,0:T(8,128)(2,1)S(1)}, bf16[2,28,8,128]{3,2,1,0:T(8,128)(2,1)S(1)}, u32[]{:S(2)}, u32[]{:S(2)}) %collective-permute-start.11) | collective-permute-done | bytes 114720 | tf_op jit(solution)/shard_map/ppermute | solution.py:31
  33.8 3.5 %collective-permute-start.12 = (bf16[8,28,8,128]{3,2,1,0:T(8,128)(2,1)S(1)}, bf16[8,28,8,128]{3,2,1,0:T(8,128)(2,1)S(1)}, u32[]{:S(2)}, u32[]{:S(2)}) collective-permute-start(bf16[8,28,8,128]{3,2,1,0:T(8,128)(2,1)S(1)} %constant_dynamic-update-slice_fusion.mine_ref), channel_id=1, source_target_pairs={{0,1},{1,0},{2,3},{3,2},{4,5},{5,4},{6,7},{7,6},{8,9},{9,8},{10,11... | collective-permute-start | bytes 1376264 | tf_op jit(solution)/shard_map/ppermute | solution.py:31
  37.3 1.4 %collective-permute-done.12.other_ref = bf16[8,28,8,128]{3,2,1,0:T(8,128)(2,1)S(1)} collective-permute-done((bf16[8,28,8,128]{3,2,1,0:T(8,128)(2,1)S(1)}, bf16[8,28,8,128]{3,2,1,0:T(8,128)(2,1)S(1)}, u32[]{:S(2)}, u32[]{:S(2)}) %collective-permute-start.12) | collective-permute-done | bytes 458784 | tf_op jit(solution)/shard_map/ppermute | solution.py:31
  38.8 1.3 %unpack.1 = (f32[27,128,128]{2,1,0:T(8,128)}, f32[128,128]{1,0:T(8,128)}) custom-call(s32[1]{0:T(128)} %bitcast.where_ref, bf16[8,28,8,128]{3,2,1,0:T(8,128)(2,1)S(1)} %constant_dynamic-update-slice_fusion.mine_ref, bf16[8,28,8,128]{3,2,1,0:T(8,128)(2,1)S(1)} %collective-permute-done.12.other_ref), custom_call_target="tpu_custom_call" | custom-call | tf_op jit(solution)/shard_map/unpack/pallas_call | solution.py:273
  (6 shorter events, 0.1 us)
Async XLA Ops:
  0.6 4.4 %collective-permute-start = (bf16[256,128]{1,0:T(8,128)(2,1)}, bf16[256,128]{1,0:T(8,128)(2,1)S(1)}, u32[]{:S(2)}, u32[]{:S(2)}) collective-permute-start(bf16[256,128]{1,0:T(8,128)(2,1)} %bitcast.7), channel_id=1, source_target_pairs={{0,1},{1,2},{2,3},{3,0},{4,5},{5,6},{6,7},{7,4},{8,9},{9,10},{10,1... | collective-permute-start | bytes 196616 | tf_op jit(solution)/shard_map/ppermute | solution.py:22
  6.2 2.5 %collective-permute-start.1 = (f32[8,28,8,128]{3,2,1,0:T(8,128)S(1)}, f32[8,28,8,128]{3,2,1,0:T(8,128)S(1)}, u32[]{:S(2)}, u32[]{:S(2)}) collective-permute-start(f32[8,28,8,128]{3,2,1,0:T(8,128)S(1)} %get-tuple-element.30), channel_id=1, source_target_pairs={{0,1},{1,0},{2,3},{3,2},{4,5},{5,4},{6,7},{7,6},{8,9},{9,8},{10,11... | collective-permute-start | bytes 2752520 | tf_op jit(solution)/shard_map/ppermute | solution.py:31
  8.9 4.5 %collective-permute-start.2 = (bf16[2,28,8,128]{3,2,1,0:T(8,128)(2,1)S(1)}, bf16[2,28,8,128]{3,2,1,0:T(8,128)(2,1)S(1)}, u32[]{:S(2)}, u32[]{:S(2)}) collective-permute-start(bf16[2,28,8,128]{3,2,1,0:T(8,128)(2,1)S(1)} %get-tuple-element.46), channel_id=1, source_target_pairs={{0,2},{1,9},{2,0},{3,11},{4,6},{5,13},{6,4},{7,15},{8,10},{9,1},{1... | collective-permute-start | bytes 344072 | tf_op jit(solution)/shard_map/ppermute | solution.py:31
  10.9 5.8 %collective-permute-start.3 = (bf16[2,28,8,128]{3,2,1,0:T(8,128)(2,1)S(1)}, bf16[2,28,8,128]{3,2,1,0:T(8,128)(2,1)S(1)}, u32[]{:S(2)}, u32[]{:S(2)}) collective-permute-start(bf16[2,28,8,128]{3,2,1,0:T(8,128)(2,1)S(1)} %get-tuple-element.48), channel_id=1, source_target_pairs={{0,4},{1,17},{2,6},{3,19},{4,0},{5,21},{6,2},{7,23},{8,12},{9,25},... | collective-permute-start | bytes 344072 | tf_op jit(solution)/shard_map/ppermute | solution.py:31
  13.2 5.5 %collective-permute-start.4 = (bf16[2,28,8,128]{3,2,1,0:T(8,128)(2,1)S(1)}, bf16[2,28,8,128]{3,2,1,0:T(8,128)(2,1)S(1)}, u32[]{:S(2)}, u32[]{:S(2)}) collective-permute-start(bf16[2,28,8,128]{3,2,1,0:T(8,128)(2,1)S(1)} %get-tuple-element.47), channel_id=1, source_target_pairs={{0,6},{1,25},{2,4},{3,27},{4,2},{5,29},{6,0},{7,31},{8,14},{9,17},... | collective-permute-start | bytes 344072 | tf_op jit(solution)/shard_map/ppermute | solution.py:31
  13.2 5.6 %collective-permute-start.5 = (bf16[256,128]{1,0:T(8,128)(2,1)S(1)}, bf16[256,128]{1,0:T(8,128)(2,1)S(1)}, u32[]{:S(2)}, u32[]{:S(2)}) collective-permute-start(bf16[256,128]{1,0:T(8,128)(2,1)S(1)} %get-tuple-element.31.pre_grad_ref), channel_id=1, source_target_pairs={{0,3},{1,0},{2,1},{3,2},{4,7},{5,4},{6,5},{7,6},{8,11},{9,8},{10,9... | collective-permute-start | bytes 196616 | tf_op jit(solution)/shard_map/ppermute | solution.py:22
  18.8 4.0 %collective-permute-start.6 = (bf16[2,28,8,128]{3,2,1,0:T(8,128)(2,1)S(1)}, bf16[2,28,8,128]{3,2,1,0:T(8,128)(2,1)S(1)}, u32[]{:S(2)}, u32[]{:S(2)}) collective-permute-start(bf16[2,28,8,128]{3,2,1,0:T(8,128)(2,1)S(1)} %reduce-precision_convert_fusion), channel_id=1, source_target_pairs={{0,16},{1,5},{2,18},{3,7},{4,20},{5,1},{6,22},{7,3},{8,24},{9,13},... | collective-permute-start | bytes 344072 | tf_op jit(solution)/shard_map/ppermute | solution.py:31
  20.1 3.9 %collective-permute-start.7 = (bf16[2,28,8,128]{3,2,1,0:T(8,128)(2,1)S(1)}, bf16[2,28,8,128]{3,2,1,0:T(8,128)(2,1)S(1)}, u32[]{:S(2)}, u32[]{:S(2)}) collective-permute-start(bf16[2,28,8,128]{3,2,1,0:T(8,128)(2,1)S(1)} %reduce-precision_convert_fusion), channel_id=1, source_target_pairs={{0,8},{1,3},{2,10},{3,1},{4,12},{5,7},{6,14},{7,5},{8,0},{9,11},{1... | collective-permute-start | bytes 344072 | tf_op jit(solution)/shard_map/ppermute | solution.py:31
  21.4 4.5 %collective-permute-start.8 = (bf16[2,28,8,128]{3,2,1,0:T(8,128)(2,1)S(1)}, bf16[2,28,8,128]{3,2,1,0:T(8,128)(2,1)S(1)}, u32[]{:S(2)}, u32[]{:S(2)}) collective-permute-start(bf16[2,28,8,128]{3,2,1,0:T(8,128)(2,1)S(1)} %reduce-precision_convert_fusion), channel_id=1, source_target_pairs={{0,24},{1,7},{2,26},{3,5},{4,28},{5,3},{6,30},{7,1},{8,16},{9,15},... | collective-permute-start | bytes 344072 | tf_op jit(solution)/shard_map/ppermute | solution.py:31
  26.0 5.9 %collective-permute-start.9 = (bf16[2,28,8,128]{3,2,1,0:T(8,128)(2,1)S(1)}, bf16[2,28,8,128]{3,2,1,0:T(8,128)(2,1)S(1)}, u32[]{:S(2)}, u32[]{:S(2)}) collective-permute-start(bf16[2,28,8,128]{3,2,1,0:T(8,128)(2,1)S(1)} %add_convert_fusion), channel_id=1, source_target_pairs={{0,4},{1,17},{2,6},{3,19},{4,0},{5,21},{6,2},{7,23},{8,12},{9,25},... | collective-permute-start | bytes 344072 | tf_op jit(solution)/shard_map/ppermute | solution.py:31
  27.8 4.4 %collective-permute-start.10 = (bf16[2,28,8,128]{3,2,1,0:T(8,128)(2,1)S(1)}, bf16[2,28,8,128]{3,2,1,0:T(8,128)(2,1)S(1)}, u32[]{:S(2)}, u32[]{:S(2)}) collective-permute-start(bf16[2,28,8,128]{3,2,1,0:T(8,128)(2,1)S(1)} %add_convert_fusion), channel_id=1, source_target_pairs={{0,2},{1,9},{2,0},{3,11},{4,6},{5,13},{6,4},{7,15},{8,10},{9,1},{1... | collective-permute-start | bytes 344072 | tf_op jit(solution)/shard_map/ppermute | solution.py:31
  28.2 5.5 %collective-permute-start.11 = (bf16[2,28,8,128]{3,2,1,0:T(8,128)(2,1)S(1)}, bf16[2,28,8,128]{3,2,1,0:T(8,128)(2,1)S(1)}, u32[]{:S(2)}, u32[]{:S(2)}) collective-permute-start(bf16[2,28,8,128]{3,2,1,0:T(8,128)(2,1)S(1)} %add_convert_fusion), channel_id=1, source_target_pairs={{0,6},{1,25},{2,4},{3,27},{4,2},{5,29},{6,0},{7,31},{8,14},{9,17},... | collective-permute-start | bytes 344072 | tf_op jit(solution)/shard_map/ppermute | solution.py:31
  33.8 5.0 %collective-permute-start.12 = (bf16[8,28,8,128]{3,2,1,0:T(8,128)(2,1)S(1)}, bf16[8,28,8,128]{3,2,1,0:T(8,128)(2,1)S(1)}, u32[]{:S(2)}, u32[]{:S(2)}) collective-permute-start(bf16[8,28,8,128]{3,2,1,0:T(8,128)(2,1)S(1)} %constant_dynamic-update-slice_fusion.mine_ref), channel_id=1, source_target_pairs={{0,1},{1,0},{2,3},{3,2},{4,5},{5,4},{6,7},{7,6},{8,9},{9,8},{10,11... | collective-permute-start | bytes 1376264 | tf_op jit(solution)/shard_map/ppermute | solution.py:31

commit v7 on v5

--- a/solution.py
+++ b/solution.py
@@ -10,7 +10,6 @@
 
 AXES = ("dp", "tm")
 PAIRS = (((1, 2), (3, 4)), ((3, 4), (1, 2)))
-UNPACK_CHUNK = 7
 LIMIT = pltpu.CompilerParams(vmem_limit_bytes=16 * 1024 * 1024)
 SCALAR = pl.BlockSpec(memory_space=pltpu.SMEM)
 VECTOR = pl.BlockSpec(memory_space=pltpu.VMEM)
@@ -38,7 +37,7 @@
 
 
 def halves_of(me):
-    first, second = (4 * ((me >> split[0]) & 1) + 2 * ((me >> split[1]) & 1) for split, _ in PAIRS)
+    first, second = (2 * ((me >> split[0]) & 1) + ((me >> split[1]) & 1) for split, _ in PAIRS)
     core = me & 1
     return jnp.where(core == 0, first, second), jnp.where(core == 0, second, first)
 
@@ -153,11 +152,13 @@
     mine, other = halves_of(me)
 
     def put(tap, value):
-        for block in range(8):
-            even = value[16 * block : 16 * block + 8]
-            odd = value[16 * block + 8 : 16 * block + 16]
-            keep_ref[block ^ mine, tap] = jnp.where(core == 0, even, odd)
-            send_ref[block ^ other, tap] = jnp.where(core == 0, odd, even)
+        block_rows = keep_ref.shape[2]
+        for block in range(4):
+            start = block * block_rows
+            low = value[start : start + block_rows]
+            high = value[chans // 2 + start : chans // 2 + start + block_rows]
+            keep_ref[block ^ mine, tap] = jnp.where(core == 0, low, high)
+            send_ref[block ^ other, tap] = jnp.where(core == 0, high, low)
 
     put(27, dot(hidden, grads, (0, 0)))
     grad_rows = jnp.concatenate(
@@ -210,38 +211,62 @@
     ).astype(jnp.bfloat16)
 
 
-def unpack_kernel(scale, where_ref, mine_ref, other_ref, kern_ref, proj_ref, out_ref, sems):
+def unpack_kernel(scale, offsets, where_ref, *refs):
+    count = len(offsets)
+    pieces = refs[: 2 * count]
+    kern_ref, proj_ref, out_ref, sems = refs[-4:]
     me = where_ref[0] >> 2
     core = me & 1
-    mine, other = halves_of(me)
-    taps = kern_ref.shape[0]
+    halves = tuple(zip((core, 1 - core), halves_of(me)))
+    taps, chans, _ = kern_ref.shape
+    block_rows = out_ref.shape[2]
     copies = []
-    for first in range(0, taps + 1, UNPACK_CHUNK):
-        last = min(first + UNPACK_CHUNK, taps + 1)
-        for block in range(8):
-            mine_rows = pl.ds(pl.multiple_of(16 * block + 8 * core, 8), 8)
-            other_rows = pl.ds(pl.multiple_of(16 * block + 8 * (1 - core), 8), 8)
-            out_ref[first:last, mine_rows, :] = (
-                mine_ref[block ^ mine, first:last].astype(jnp.float32) * scale
-            )
-            out_ref[first:last, other_rows, :] = (
-                other_ref[block ^ other, first:last].astype(jnp.float32) * scale
-            )
-        inside = min(last, taps)
-        copies.append(
+    for place, piece_ref in enumerate(pieces):
+        half, flip = halves[place % 2]
+        block = offsets[place // 2] ^ flip
+        out_ref[place] = piece_ref[0].astype(jnp.float32) * scale
+        rows = pl.ds(
+            pl.multiple_of(half * (chans // 2) + block * block_rows, block_rows), block_rows
+        )
+        copies += [
             pltpu.make_async_copy(
-                out_ref.at[first:inside], kern_ref.at[first:inside], sems.at[len(copies)]
-            )
-        )
+                out_ref.at[place, :taps], kern_ref.at[:, rows, :], sems.at[2 * place]
+            ),
+            pltpu.make_async_copy(out_ref.at[place, taps], proj_ref.at[rows, :], sems.at[2 * place + 1]),
+        ]
+        copies[-2].start()
         copies[-1].start()
-    copies.append(pltpu.make_async_copy(out_ref.at[taps], proj_ref, sems.at[len(copies)]))
-    copies[-1].start()
     for copy in copies:
         copy.wait()
 
 
+def unpack(where, pieces, offsets, scale, sofar=()):
+    given = [piece for offset in offsets for piece in pieces[offset]]
+    _, taps, block_rows, chans = given[0].shape
+    return pl.pallas_call(
+        functools.partial(unpack_kernel, scale, offsets),
+        out_shape=(
+            jax.ShapeDtypeStruct((taps - 1, chans, chans), jnp.float32),
+            jax.ShapeDtypeStruct((chans, chans), jnp.float32),
+        ),
+        in_specs=[SCALAR] + [VECTOR] * len(given) + [OUTSIDE] * len(sofar),
+        out_specs=(OUTSIDE, OUTSIDE),
+        scratch_shapes=[
+            pltpu.VMEM((len(given), taps, block_rows, chans), jnp.float32),
+            pltpu.SemaphoreType.DMA((2 * len(given),)),
+        ],
+        input_output_aliases={1 + len(given) + i: i for i in range(len(sofar))},
+        compiler_params=LIMIT,
+        cost_estimate=pl.CostEstimate(
+            flops=taps * block_rows * chans * len(given),
+            bytes_accessed=6 * taps * block_rows * chans * len(given),
+            transcendentals=0,
+        ),
+        name="unpack",
+    )(where, *given, *sofar)
+
+
 def summed(where, keep, send, scale, beside_split, beside_exchange):
-    taps, chans = keep.shape[1] - 1, keep.shape[3]
     total = keep + swapped(send, (1, 1))
     part = total.shape[0] // 4
     came = [
@@ -267,24 +292,11 @@
     done = beside_exchange(done)
     total = total.astype(jnp.bfloat16)
     total, done = lax.optimization_barrier((total, done))
-    third, second, first = (swapped(total, masks_of(0, offset)) for offset in (3, 2, 1))
-    total = jnp.concatenate([total, first, second, third], axis=0)
-    other = swapped(total, (1, 1))
-    return pl.pallas_call(
-        functools.partial(unpack_kernel, scale),
-        out_shape=(
-            jax.ShapeDtypeStruct((taps, chans, chans), jnp.float32),
-            jax.ShapeDtypeStruct((chans, chans), jnp.float32),
-        ),
-        in_specs=[SCALAR, VECTOR, VECTOR],
-        out_specs=(OUTSIDE, OUTSIDE),
-        scratch_shapes=[
-            pltpu.VMEM((taps + 1, chans, chans), jnp.float32),
-            pltpu.SemaphoreType.DMA((pl.cdiv(taps + 1, UNPACK_CHUNK) + 1,)),
-        ],
-        compiler_params=LIMIT,
-        name="unpack",
-    )(where, total, other), done
+    mine = [total] + [swapped(total, masks_of(0, offset)) for offset in (1, 2, 3)]
+    pieces = [(piece, swapped(piece, (1, 1))) for piece in mine[:3]]
+    sofar = unpack(where, pieces, (0, 1, 2), scale)
+    pieces.append((mine[3], swapped(mine[3], (1, 1))))
+    return unpack(where, pieces, (3,), scale, sofar), done
 
 
 def prepare(shape, frames, grads, conv_kernel, proj_weight):
@@ -315,7 +327,7 @@
 def forward(shape, where, halo, grads, conv_kernel, own, sums, hidden_grad):
     n_frames, height, width, chans = shape
     rows = n_frames * height * width
-    half = (8, 28, 8, chans)
+    half = (4, 28, chans // 8, chans)
     return pl.pallas_call(
         functools.partial(forward_kernel, shape),
         out_shape=(

time: 40 us -> 38.9 us (0.972)
  waiting for transfers between devices: 16 us -> 9.86 us
  starting transfers between devices: 17 us -> 21.7 us
  Pallas kernels: 5.44 us -> 6.14 us
    ppermute x11 -> x14, waiting for transfers between devices: 16 us -> 9.86 us  [swapped(): lax.ppermute(array, AXES, [(i, i ^ masks[i & 1]) for i in range(count)])]
    ppermute x11 -> x14, starting transfers between devices: 14.3 us -> 19 us  [swapped(): lax.ppermute(array, AXES, [(i, i ^ masks[i & 1]) for i in range(count)])]
    pallas_call x1 -> x2, Pallas kernels: 1.3 us -> 2.02 us  [unpack(): pl.pallas_call(functools.partial(unpack_kernel, scale, offsets), out_shap...]
  transfers between devices with their start and end apart: 13 -> 16, of which waited for: 9 -> 5; matrix products, arithmetic and copies ran while one was open for 0% -> 0% of each run, Pallas kernels for 8% -> 11%
where the time goes in v7:
time: 38.9 us; the launch traced here: 38.7 us
  starting transfers between devices  21.7 us (56%)
  waiting for transfers between devices  9.86 us (25%)
  Pallas kernels  6.14 us (16%)
  between operations  0.73 us (2%)
    ppermute x14, starting transfers between devices, swapped(): lax.ppermute(array, AXES, [(i, i ^ masks[i & 1]) for i in range(count)])  19 us
    ppermute x14, waiting for transfers between devices, swapped(): lax.ppermute(array, AXES, [(i, i ^ masks[i & 1]) for i in range(count)])  9.86 us
    ppermute x2, starting transfers between devices, passed_round(): lax.ppermute(shard, axis, [(i, (i + by) % size) for i in range(size)])  2.65 us
    pallas_call x2, Pallas kernels, unpack(): pl.pallas_call(functools.partial(unpack_kernel, scale, offsets), out_shap...  2.02 us
    pallas_call x1, Pallas kernels, prepare(): pl.pallas_call(functools.partial(prepare_kernel, shape), out_shape=(jax.S...  1.72 us
    pallas_call x1, Pallas kernels, backward(): pl.pallas_call(functools.partial(backward_kernel, shape), out_shape=(jax....  1.3 us
    pallas_call x1, Pallas kernels, forward(): pl.pallas_call(functools.partial(forward_kernel, shape), out_shape=(jax.S...  1.09 us
  transfers between devices with their start and end apart: 16, of which 5 were waited for; matrix products, arithmetic and copies ran while one was open for 0% of the time, Pallas kernels for 11%

profile of v7, /device:TPU:1, one launch (start us, length us, event | category | flops | bytes accessed | tf_op | source)
XLA Modules:
  0.0 38.7 jit_solution(10187303429218241032)
XLA Ops:
  0.6 2.7 %collective-permute-start = (bf16[256,128]{1,0:T(8,128)(2,1)}, bf16[256,128]{1,0:T(8,128)(2,1)S(1)}, u32[]{:S(2)}, u32[]{:S(2)}) collective-permute-start(bf16[256,128]{1,0:T(8,128)(2,1)} %bitcast.8), channel_id=1, source_target_pairs={{0,1},{1,2},{2,3},{3,0},{4,5},{5,6},{6,7},{7,4},{8,9},{9,10},{10,1... | collective-permute-start | bytes 196616 | tf_op jit(solution)/shard_map/ppermute | solution.py:21
  3.3 1.7 %prepare.1 = (bf16[256,128]{1,0:T(8,128)(2,1)S(1)}, bf16[256,128]{1,0:T(8,128)(2,1)S(1)}, bf16[3,3,3,128,128]{4,3,2,1,0:T(8,128)(2,1)S(1)}, bf16[128,128]{1,0:T(...) custom-call(bf16[256,128]{1,0:T(8,128)(2,1)} %bitcast.9, ...), custom_call_target="tpu_custom_call" | custom-call | flops 167772160 | bytes 1048576 | tf_op jit(solution)/shard_map/prepare/pallas_call | solution.py:305
  5.0 0.0 collective-permute-done.halo_ref
  5.0 1.1 %forward.1 = (f32[4,28,16,128]{3,2,1,0:T(8,128)S(1)}, f32[4,28,16,128]{3,2,1,0:T(8,128)S(1)}, bf16[256,128]{1,0:T(8,128)(2,1)S(1)}, bf16[256,128]{1,0:T(8,128)(2,1)S(1)}) custom-call(s32[1]{0:T(128)} %bitcast.where_ref, bf16[256,128]{1,0:T(8,128)(2,1)S(1)} %collective-permute-done.halo_ref, bf16[256,128]{1,0:T(8,128)(2,1)S(1)} %get-tuple-element.26.grads_ref, ...), custom_call_target="tpu_custom_call" | custom-call | tf_op jit(solution)/shard_map/forward/pallas_call | solution.py:331
  6.1 0.3 collective-permute-start.1
  6.4 2.3 %collective-permute-done.1 = f32[4,28,16,128]{3,2,1,0:T(8,128)S(1)} collective-permute-done((f32[4,28,16,128]{3,2,1,0:T(8,128)S(1)}, f32[4,28,16,128]{3,2,1,0:T(8,128)S(1)}, u32[]{:S(2)}, u32[]{:S(2)}) %collective-permute-start.1) | collective-permute-done | bytes 917536 | tf_op jit(solution)/shard_map/ppermute | solution.py:30
  8.7 0.2 fusion.2
  8.9 4.0 %collective-permute-start.2 = (bf16[1,28,16,128]{3,2,1,0:T(8,128)(2,1)S(1)}, bf16[1,28,16,128]{3,2,1,0:T(8,128)(2,1)S(1)}, u32[]{:S(2)}, u32[]{:S(2)}) collective-permute-start(bf16[1,28,16,128]{3,2,1,0:T(8,128)(2,1)S(1)} %get-tuple-element.50), channel_id=1, source_target_pairs={{0,6},{1,25},{2,4},{3,27},{4,2},{5,29},{6,0},{7,31},{8,14},{9,17},... | collective-permute-start | bytes 344072 | tf_op jit(solution)/shard_map/ppermute | solution.py:30
  12.9 0.0 collective-permute-start.3
  12.9 0.4 collective-permute-start.4
  13.3 0.0 collective-permute-start.5
  13.3 1.9 %collective-permute-done.2 = bf16[1,28,16,128]{3,2,1,0:T(8,128)(2,1)S(1)} collective-permute-done((bf16[1,28,16,128]{3,2,1,0:T(8,128)(2,1)S(1)}, bf16[1,28,16,128]{3,2,1,0:T(8,128)(2,1)S(1)}, u32[]{:S(2)}, u32[]{:S(2)}) %collective-permute-start.2) | collective-permute-done | bytes 114720 | tf_op jit(solution)/shard_map/ppermute | solution.py:30
  15.2 2.6 %collective-permute-done.3 = bf16[1,28,16,128]{3,2,1,0:T(8,128)(2,1)S(1)} collective-permute-done((bf16[1,28,16,128]{3,2,1,0:T(8,128)(2,1)S(1)}, bf16[1,28,16,128]{3,2,1,0:T(8,128)(2,1)S(1)}, u32[]{:S(2)}, u32[]{:S(2)}) %collective-permute-start.3) | collective-permute-done | bytes 114720 | tf_op jit(solution)/shard_map/ppermute | solution.py:30
  17.8 0.0 collective-permute-done.4
  17.8 0.1 fusion.1
  17.8 0.0 collective-permute-done.5.next_ref
  17.9 1.3 %collective-permute-start.6 = (bf16[1,28,16,128]{3,2,1,0:T(8,128)(2,1)S(1)}, bf16[1,28,16,128]{3,2,1,0:T(8,128)(2,1)S(1)}, u32[]{:S(2)}, u32[]{:S(2)}) collective-permute-start(bf16[1,28,16,128]{3,2,1,0:T(8,128)(2,1)S(1)} %reduce-precision_convert_fusion), channel_id=1, source_target_pairs={{0,16},{1,5},{2,18},{3,7},{4,20},{5,1},{6,22},{7,3},{8,24},{9,13},... | collective-permute-start | bytes 344072 | tf_op jit(solution)/shard_map/ppermute | solution.py:30
  19.2 1.2 %collective-permute-start.7 = (bf16[1,28,16,128]{3,2,1,0:T(8,128)(2,1)S(1)}, bf16[1,28,16,128]{3,2,1,0:T(8,128)(2,1)S(1)}, u32[]{:S(2)}, u32[]{:S(2)}) collective-permute-start(bf16[1,28,16,128]{3,2,1,0:T(8,128)(2,1)S(1)} %reduce-precision_convert_fusion), channel_id=1, source_target_pairs={{0,8},{1,3},{2,10},{3,1},{4,12},{5,7},{6,14},{7,5},{8,0},{9,11},{1... | collective-permute-start | bytes 344072 | tf_op jit(solution)/shard_map/ppermute | solution.py:30
  20.4 0.2 collective-permute-start.8
  20.6 1.3 %backward.1 = (bf16[256,128]{1,0:T(8,128)(2,1)}, bf16[256,128]{1,0:T(8,128)(2,1)}) custom-call(s32[1]{0:T(128)} %bitcast.where_ref, bf16[256,128]{1,0:T(8,128)(2,1)S(1)} %get-tuple-element.33.pre_grad_ref, bf16[256,128]{1,0:T(8,128)(2,1)S(1)} %collective-permute-done.5.next_ref, bf16[256,128]{1,0:T(8,128)(2,1)S(1)} %get-tuple-element.36.hidden_ref, ...), custom_call_target="tpu_custom_call" | custom-call | flops 234881024 | bytes 1048576 | tf_op jit(solution)/shard_map/backward/pallas_call | solution.py:351
  21.9 0.0 collective-permute-done.6
  21.9 1.2 %collective-permute-done.7 = bf16[1,28,16,128]{3,2,1,0:T(8,128)(2,1)S(1)} collective-permute-done((bf16[1,28,16,128]{3,2,1,0:T(8,128)(2,1)S(1)}, bf16[1,28,16,128]{3,2,1,0:T(8,128)(2,1)S(1)}, u32[]{:S(2)}, u32[]{:S(2)}) %collective-permute-start.7) | collective-permute-done | bytes 114720 | tf_op jit(solution)/shard_map/ppermute | solution.py:30
  23.1 1.8 %collective-permute-done.8 = bf16[1,28,16,128]{3,2,1,0:T(8,128)(2,1)S(1)} collective-permute-done((bf16[1,28,16,128]{3,2,1,0:T(8,128)(2,1)S(1)}, bf16[1,28,16,128]{3,2,1,0:T(8,128)(2,1)S(1)}, u32[]{:S(2)}, u32[]{:S(2)}) %collective-permute-start.8) | collective-permute-done | bytes 114720 | tf_op jit(solution)/shard_map/ppermute | solution.py:30
  25.0 0.1 add_convert_fusion.refs_0_
  25.0 2.2 %collective-permute-start.12 = (bf16[1,28,16,128]{3,2,1,0:T(8,128)(2,1)S(1)}, bf16[1,28,16,128]{3,2,1,0:T(8,128)(2,1)S(1)}, u32[]{:S(2)}, u32[]{:S(2)}) collective-permute-start(bf16[1,28,16,128]{3,2,1,0:T(8,128)(2,1)S(1)} %add_convert_fusion.refs_0_), channel_id=1, source_target_pairs={{0,4},{1,17},{2,6},{3,19},{4,0},{5,21},{6,2},{7,23},{8,12},{9,25},... | collective-permute-start | bytes 344072 | tf_op jit(solution)/shard_map/ppermute | solution.py:30
  27.2 0.7 %collective-permute-start.14 = (bf16[1,28,16,128]{3,2,1,0:T(8,128)(2,1)S(1)}, bf16[1,28,16,128]{3,2,1,0:T(8,128)(2,1)S(1)}, u32[]{:S(2)}, u32[]{:S(2)}) collective-permute-start(bf16[1,28,16,128]{3,2,1,0:T(8,128)(2,1)S(1)} %add_convert_fusion.refs_0_), channel_id=1, source_target_pairs={{0,2},{1,9},{2,0},{3,11},{4,6},{5,13},{6,4},{7,15},{8,10},{9,1},{1... | collective-permute-start | bytes 344072 | tf_op jit(solution)/shard_map/ppermute | solution.py:30
  28.0 0.7 %collective-permute-start.9 = (bf16[1,28,16,128]{3,2,1,0:T(8,128)(2,1)S(1)}, bf16[1,28,16,128]{3,2,1,0:T(8,128)(2,1)S(1)}, u32[]{:S(2)}, u32[]{:S(2)}) collective-permute-start(bf16[1,28,16,128]{3,2,1,0:T(8,128)(2,1)S(1)} %add_convert_fusion.refs_0_), channel_id=1, source_target_pairs={{0,6},{1,25},{2,4},{3,27},{4,2},{5,29},{6,0},{7,31},{8,14},{9,17},... | collective-permute-start | bytes 344072 | tf_op jit(solution)/shard_map/ppermute | solution.py:30
  28.7 3.6 %collective-permute-start.11 = (bf16[1,28,16,128]{3,2,1,0:T(8,128)(2,1)S(1)}, bf16[1,28,16,128]{3,2,1,0:T(8,128)(2,1)S(1)}, u32[]{:S(2)}, u32[]{:S(2)}) collective-permute-start(bf16[1,28,16,128]{3,2,1,0:T(8,128)(2,1)S(1)} %add_convert_fusion.refs_0_), channel_id=1, source_target_pairs={{0,1},{1,0},{2,3},{3,2},{4,5},{5,4},{6,7},{7,6},{8,9},{9,8},{10,11... | collective-permute-start | bytes 344072 | tf_op jit(solution)/shard_map/ppermute | solution.py:30
  32.3 0.0 collective-permute-done.12.refs_2_
  32.3 1.3 %collective-permute-start.13 = (bf16[1,28,16,128]{3,2,1,0:T(8,128)(2,1)S(1)}, bf16[1,28,16,128]{3,2,1,0:T(8,128)(2,1)S(1)}, u32[]{:S(2)}, u32[]{:S(2)}) collective-permute-start(bf16[1,28,16,128]{3,2,1,0:T(8,128)(2,1)S(1)} %collective-permute-done.12.refs_2_), channel_id=1, source_target_pairs={{0,1},{1,0},{2,3},{3,2},{4,5},{5,4},{6,7},{7,6},{8,9},{9,8},{10,11... | collective-permute-start | bytes 344072 | tf_op jit(solution)/shard_map/ppermute | solution.py:30
  33.6 0.0 collective-permute-done.14.refs_4_
  33.6 0.7 %collective-permute-start.15 = (bf16[1,28,16,128]{3,2,1,0:T(8,128)(2,1)S(1)}, bf16[1,28,16,128]{3,2,1,0:T(8,128)(2,1)S(1)}, u32[]{:S(2)}, u32[]{:S(2)}) collective-permute-start(bf16[1,28,16,128]{3,2,1,0:T(8,128)(2,1)S(1)} %collective-permute-done.14.refs_4_), channel_id=1, source_target_pairs={{0,1},{1,0},{2,3},{3,2},{4,5},{5,4},{6,7},{7,6},{8,9},{9,8},{10,11... | collective-permute-start | bytes 344072 | tf_op jit(solution)/shard_map/ppermute | solution.py:30
  34.3 0.0 collective-permute-done.9.refs_0_
  34.3 2.4 %collective-permute-start.10 = (bf16[1,28,16,128]{3,2,1,0:T(8,128)(2,1)S(1)}, bf16[1,28,16,128]{3,2,1,0:T(8,128)(2,1)S(1)}, u32[]{:S(2)}, u32[]{:S(2)}) collective-permute-start(bf16[1,28,16,128]{3,2,1,0:T(8,128)(2,1)S(1)} %collective-permute-done.9.refs_0_), channel_id=1, source_target_pairs={{0,1},{1,0},{2,3},{3,2},{4,5},{5,4},{6,7},{7,6},{8,9},{9,8},{10,11... | collective-permute-start | bytes 344072 | tf_op jit(solution)/shard_map/ppermute | solution.py:30
  36.7 0.0 collective-permute-done.11.refs_1_
  36.7 0.0 collective-permute-done.13.refs_3_
  36.7 0.0 collective-permute-done.15.refs_5_
  36.7 1.2 %unpack.2 = (f32[27,128,128]{2,1,0:T(8,128)}, f32[128,128]{1,0:T(8,128)}) custom-call(s32[1]{0:T(128)} %bitcast.where_ref, bf16[1,28,16,128]{3,2,1,0:T(8,128)(2,1)S(1)} %add_convert_fusion.refs_0_, bf16[1,28,16,128]{3,2,1,0:T(8,128)(2,1)S(1)} %collective-permute-done.11.refs_1_, bf16[1,28,16,128]{3,2,1,0:T(8,128)(2,1)S(1)} %collective-permute-done.12.refs_2_, ...), custom_call_target="tpu_custom_call" | custom-call | flops 344064 | bytes 2064384 | tf_op jit(solution)/shard_map/unpack/pallas_call | solution.py:246
  37.9 0.0 collective-permute-done.10.refs_1_
  37.9 0.8 %unpack.3 = (f32[27,128,128]{2,1,0:T(8,128)}, f32[128,128]{1,0:T(8,128)}) custom-call(s32[1]{0:T(128)} %bitcast.where_ref, bf16[1,28,16,128]{3,2,1,0:T(8,128)(2,1)S(1)} %collective-permute-done.9.refs_0_, bf16[1,28,16,128]{3,2,1,0:T(8,128)(2,1)S(1)} %collective-permute-done.10.refs_1_, ...), custom_call_target="tpu_custom_call", output_to_operand_aliasing={{0}: (3, {}), {1}: (4, {})} | custom-call | flops 114688 | bytes 688128 | tf_op jit(solution)/shard_map/unpack/pallas_call | solution.py:246
  (2 shorter events, 0.0 us)
Async XLA Ops:
  0.6 4.4 %collective-permute-start = (bf16[256,128]{1,0:T(8,128)(2,1)}, bf16[256,128]{1,0:T(8,128)(2,1)S(1)}, u32[]{:S(2)}, u32[]{:S(2)}) collective-permute-start(bf16[256,128]{1,0:T(8,128)(2,1)} %bitcast.8), channel_id=1, source_target_pairs={{0,1},{1,2},{2,3},{3,0},{4,5},{5,6},{6,7},{7,4},{8,9},{9,10},{10,1... | collective-permute-start | bytes 196616 | tf_op jit(solution)/shard_map/ppermute | solution.py:21
  6.1 2.5 %collective-permute-start.1 = (f32[4,28,16,128]{3,2,1,0:T(8,128)S(1)}, f32[4,28,16,128]{3,2,1,0:T(8,128)S(1)}, u32[]{:S(2)}, u32[]{:S(2)}) collective-permute-start(f32[4,28,16,128]{3,2,1,0:T(8,128)S(1)} %get-tuple-element.32), channel_id=1, source_target_pairs={{0,1},{1,0},{2,3},{3,2},{4,5},{5,4},{6,7},{7,6},{8,9},{9,8},{10,11... | collective-permute-start | bytes 2752520 | tf_op jit(solution)/shard_map/ppermute | solution.py:30
  8.9 6.3 %collective-permute-start.2 = (bf16[1,28,16,128]{3,2,1,0:T(8,128)(2,1)S(1)}, bf16[1,28,16,128]{3,2,1,0:T(8,128)(2,1)S(1)}, u32[]{:S(2)}, u32[]{:S(2)}) collective-permute-start(bf16[1,28,16,128]{3,2,1,0:T(8,128)(2,1)S(1)} %get-tuple-element.50), channel_id=1, source_target_pairs={{0,6},{1,25},{2,4},{3,27},{4,2},{5,29},{6,0},{7,31},{8,14},{9,17},... | collective-permute-start | bytes 344072 | tf_op jit(solution)/shard_map/ppermute | solution.py:30
  12.9 4.9 %collective-permute-start.3 = (bf16[1,28,16,128]{3,2,1,0:T(8,128)(2,1)S(1)}, bf16[1,28,16,128]{3,2,1,0:T(8,128)(2,1)S(1)}, u32[]{:S(2)}, u32[]{:S(2)}) collective-permute-start(bf16[1,28,16,128]{3,2,1,0:T(8,128)(2,1)S(1)} %get-tuple-element.52), channel_id=1, source_target_pairs={{0,2},{1,9},{2,0},{3,11},{4,6},{5,13},{6,4},{7,15},{8,10},{9,1},{1... | collective-permute-start | bytes 344072 | tf_op jit(solution)/shard_map/ppermute | solution.py:30
  12.9 4.9 %collective-permute-start.4 = (bf16[1,28,16,128]{3,2,1,0:T(8,128)(2,1)S(1)}, bf16[1,28,16,128]{3,2,1,0:T(8,128)(2,1)S(1)}, u32[]{:S(2)}, u32[]{:S(2)}) collective-permute-start(bf16[1,28,16,128]{3,2,1,0:T(8,128)(2,1)S(1)} %get-tuple-element.51), channel_id=1, source_target_pairs={{0,4},{1,17},{2,6},{3,19},{4,0},{5,21},{6,2},{7,23},{8,12},{9,25},... | collective-permute-start | bytes 344072 | tf_op jit(solution)/shard_map/ppermute | solution.py:30
  13.3 4.6 %collective-permute-start.5 = (bf16[256,128]{1,0:T(8,128)(2,1)S(1)}, bf16[256,128]{1,0:T(8,128)(2,1)S(1)}, u32[]{:S(2)}, u32[]{:S(2)}) collective-permute-start(bf16[256,128]{1,0:T(8,128)(2,1)S(1)} %get-tuple-element.33.pre_grad_ref), channel_id=1, source_target_pairs={{0,3},{1,0},{2,1},{3,2},{4,7},{5,4},{6,5},{7,6},{8,11},{9,8},{10,9... | collective-permute-start | bytes 196616 | tf_op jit(solution)/shard_map/ppermute | solution.py:21
  17.9 4.0 %collective-permute-start.6 = (bf16[1,28,16,128]{3,2,1,0:T(8,128)(2,1)S(1)}, bf16[1,28,16,128]{3,2,1,0:T(8,128)(2,1)S(1)}, u32[]{:S(2)}, u32[]{:S(2)}) collective-permute-start(bf16[1,28,16,128]{3,2,1,0:T(8,128)(2,1)S(1)} %reduce-precision_convert_fusion), channel_id=1, source_target_pairs={{0,16},{1,5},{2,18},{3,7},{4,20},{5,1},{6,22},{7,3},{8,24},{9,13},... | collective-permute-start | bytes 344072 | tf_op jit(solution)/shard_map/ppermute | solution.py:30
  19.2 3.9 %collective-permute-start.7 = (bf16[1,28,16,128]{3,2,1,0:T(8,128)(2,1)S(1)}, bf16[1,28,16,128]{3,2,1,0:T(8,128)(2,1)S(1)}, u32[]{:S(2)}, u32[]{:S(2)}) collective-permute-start(bf16[1,28,16,128]{3,2,1,0:T(8,128)(2,1)S(1)} %reduce-precision_convert_fusion), channel_id=1, source_target_pairs={{0,8},{1,3},{2,10},{3,1},{4,12},{5,7},{6,14},{7,5},{8,0},{9,11},{1... | collective-permute-start | bytes 344072 | tf_op jit(solution)/shard_map/ppermute | solution.py:30
  20.4 4.5 %collective-permute-start.8 = (bf16[1,28,16,128]{3,2,1,0:T(8,128)(2,1)S(1)}, bf16[1,28,16,128]{3,2,1,0:T(8,128)(2,1)S(1)}, u32[]{:S(2)}, u32[]{:S(2)}) collective-permute-start(bf16[1,28,16,128]{3,2,1,0:T(8,128)(2,1)S(1)} %reduce-precision_convert_fusion), channel_id=1, source_target_pairs={{0,24},{1,7},{2,26},{3,5},{4,28},{5,3},{6,30},{7,1},{8,16},{9,15},... | collective-permute-start | bytes 344072 | tf_op jit(solution)/shard_map/ppermute | solution.py:30
  25.0 7.2 %collective-permute-start.12 = (bf16[1,28,16,128]{3,2,1,0:T(8,128)(2,1)S(1)}, bf16[1,28,16,128]{3,2,1,0:T(8,128)(2,1)S(1)}, u32[]{:S(2)}, u32[]{:S(2)}) collective-permute-start(bf16[1,28,16,128]{3,2,1,0:T(8,128)(2,1)S(1)} %add_convert_fusion.refs_0_), channel_id=1, source_target_pairs={{0,4},{1,17},{2,6},{3,19},{4,0},{5,21},{6,2},{7,23},{8,12},{9,25},... | collective-permute-start | bytes 344072 | tf_op jit(solution)/shard_map/ppermute | solution.py:30
  27.2 6.4 %collective-permute-start.14 = (bf16[1,28,16,128]{3,2,1,0:T(8,128)(2,1)S(1)}, bf16[1,28,16,128]{3,2,1,0:T(8,128)(2,1)S(1)}, u32[]{:S(2)}, u32[]{:S(2)}) collective-permute-start(bf16[1,28,16,128]{3,2,1,0:T(8,128)(2,1)S(1)} %add_convert_fusion.refs_0_), channel_id=1, source_target_pairs={{0,2},{1,9},{2,0},{3,11},{4,6},{5,13},{6,4},{7,15},{8,10},{9,1},{1... | collective-permute-start | bytes 344072 | tf_op jit(solution)/shard_map/ppermute | solution.py:30
  28.0 6.3 %collective-permute-start.9 = (bf16[1,28,16,128]{3,2,1,0:T(8,128)(2,1)S(1)}, bf16[1,28,16,128]{3,2,1,0:T(8,128)(2,1)S(1)}, u32[]{:S(2)}, u32[]{:S(2)}) collective-permute-start(bf16[1,28,16,128]{3,2,1,0:T(8,128)(2,1)S(1)} %add_convert_fusion.refs_0_), channel_id=1, source_target_pairs={{0,6},{1,25},{2,4},{3,27},{4,2},{5,29},{6,0},{7,31},{8,14},{9,17},... | collective-permute-start | bytes 344072 | tf_op jit(solution)/shard_map/ppermute | solution.py:30
  28.7 8.0 %collective-permute-start.11 = (bf16[1,28,16,128]{3,2,1,0:T(8,128)(2,1)S(1)}, bf16[1,28,16,128]{3,2,1,0:T(8,128)(2,1)S(1)}, u32[]{:S(2)}, u32[]{:S(2)}) collective-permute-start(bf16[1,28,16,128]{3,2,1,0:T(8,128)(2,1)S(1)} %add_convert_fusion.refs_0_), channel_id=1, source_target_pairs={{0,1},{1,0},{2,3},{3,2},{4,5},{5,4},{6,7},{7,6},{8,9},{9,8},{10,11... | collective-permute-start | bytes 344072 | tf_op jit(solution)/shard_map/ppermute | solution.py:30
  32.3 4.4 %collective-permute-start.13 = (bf16[1,28,16,128]{3,2,1,0:T(8,128)(2,1)S(1)}, bf16[1,28,16,128]{3,2,1,0:T(8,128)(2,1)S(1)}, u32[]{:S(2)}, u32[]{:S(2)}) collective-permute-start(bf16[1,28,16,128]{3,2,1,0:T(8,128)(2,1)S(1)} %collective-permute-done.12.refs_2_), channel_id=1, source_target_pairs={{0,1},{1,0},{2,3},{3,2},{4,5},{5,4},{6,7},{7,6},{8,9},{9,8},{10,11... | collective-permute-start | bytes 344072 | tf_op jit(solution)/shard_map/ppermute | solution.py:30
  33.6 3.1 %collective-permute-start.15 = (bf16[1,28,16,128]{3,2,1,0:T(8,128)(2,1)S(1)}, bf16[1,28,16,128]{3,2,1,0:T(8,128)(2,1)S(1)}, u32[]{:S(2)}, u32[]{:S(2)}) collective-permute-start(bf16[1,28,16,128]{3,2,1,0:T(8,128)(2,1)S(1)} %collective-permute-done.14.refs_4_), channel_id=1, source_target_pairs={{0,1},{1,0},{2,3},{3,2},{4,5},{5,4},{6,7},{7,6},{8,9},{9,8},{10,11... | collective-permute-start | bytes 344072 | tf_op jit(solution)/shard_map/ppermute | solution.py:30
  34.3 3.6 %collective-permute-start.10 = (bf16[1,28,16,128]{3,2,1,0:T(8,128)(2,1)S(1)}, bf16[1,28,16,128]{3,2,1,0:T(8,128)(2,1)S(1)}, u32[]{:S(2)}, u32[]{:S(2)}) collective-permute-start(bf16[1,28,16,128]{3,2,1,0:T(8,128)(2,1)S(1)} %collective-permute-done.9.refs_0_), channel_id=1, source_target_pairs={{0,1},{1,0},{2,3},{3,2},{4,5},{5,4},{6,7},{7,6},{8,9},{9,8},{10,11... | collective-permute-start | bytes 344072 | tf_op jit(solution)/shard_map/ppermute | solution.py:30

commit v8 on v7

--- a/solution.py
+++ b/solution.py
@@ -92,50 +92,83 @@
 
 
 def prepare_kernel(
-    shape, frames_hbm, grads_hbm, kern_hbm, proj_hbm,
-    frames_ref, grads_ref, kern_ref, proj_ref, wide_ref, sums_ref, hidden_grad_ref, sems,
+    width, frames_hbm, grads_hbm, kern_hbm, proj_hbm,
+    frames_ref, grads_ref, kern_ref, proj_ref, wide_ref, sems,
 ):
-    _, height, width, chans = shape
-    map_rows = height * width
-    rows = shape[0] * map_rows
-    pairs = [(frames_hbm, frames_ref)]
-    pairs += [(kern_hbm.at[tau], kern_ref.at[tau]) for tau in (2, 1, 0)]
-    pairs += [(proj_hbm, proj_ref), (grads_hbm, grads_ref)]
+    pairs = (
+        (frames_hbm, frames_ref), (grads_hbm, grads_ref), (kern_hbm, kern_ref), (proj_hbm, proj_ref)
+    )
     copies = [pltpu.make_async_copy(*pair, sems.at[i]) for i, pair in enumerate(pairs)]
     for copy in copies:
         copy.start()
     copies[0].wait()
     spread(frames_ref[...], width, wide_ref)
-    for place, tau in enumerate((2, 1, 0)):
-        copies[1 + place].wait()
-        skip = place * map_rows
-        if place == 0:
-            sums_ref[...] = dot(wide_ref[...], weights_of(kern_ref, tau), (1, 0))
-        elif skip < rows:
-            sums_ref[skip:] += dot(wide_ref[: rows - skip], weights_of(kern_ref, tau), (1, 0))
-    copies[4].wait()
-    copies[5].wait()
-    hidden_grad_ref[...] = dot(grads_ref[...], proj_ref[...], (1, 1))
-
-
-def forward_kernel(
-    shape, where_ref, halo_ref, grads_ref, kern_ref, own_ref, sums_ref, hidden_grad_ref,
-    keep_ref, send_ref, hidden_ref, pre_grad_ref, wide_ref,
+    for copy in copies[1:]:
+        copy.wait()
+
+
+def join_kernel(
+    shape, where_ref, own_ref, grads_ref, partner_ref, partner_grads_ref, kern_ref, proj_ref,
+    wide_ref, pair_grads_ref, sums_ref, hidden_grad_ref,
 ):
     _, height, width, chans = shape
     map_rows = height * width
     rows = shape[0] * map_rows
-    spread_unless((where_ref[0] & 2) != 0, halo_ref, width, wide_ref)
-    term = dot(wide_ref[...], weights_of(kern_ref, 0), (1, 0))
-    early = dot(wide_ref[map_rows:], weights_of(kern_ref, 1), (1, 0))
-    head = jnp.concatenate([term[:map_rows] + early, term[map_rows:]], axis=0)
+    head = 2 * map_rows
+    core = (where_ref[0] >> 2) & 1
+
+    def part(start, index):
+        return pl.ds(pl.multiple_of(start + index * rows, map_rows), rows)
+
+    wide_ref[part(head, core)] = own_ref[...]
+    spread(partner_ref[...], width, wide_ref.at[part(head, 1 - core)])
+    pair_grads_ref[part(0, core)] = grads_ref[...]
+    pair_grads_ref[part(0, 1 - core)] = partner_grads_ref[...]
+    hidden_grad_ref[...] = dot(pair_grads_ref[...], proj_ref[...], (1, 1))
+    sums_ref[...] = dot(wide_ref[head:], weights_of(kern_ref, 2), (1, 0))
+    for tau in (1, 0):
+        skip = (2 - tau) * map_rows
+        sums_ref[skip:] += dot(
+            wide_ref[head : head + 2 * rows - skip], weights_of(kern_ref, tau), (1, 0)
+        )
+
+
+def forward_kernel(
+    shape, where_ref, first_halo_ref, second_halo_ref, grads_ref, kern_ref, _, sums_ref,
+    hidden_grad_ref, keep_ref, send_ref, hidden_ref, pre_grad_ref, wide_ref,
+):
+    _, height, width, chans = shape
+    map_rows = height * width
+    rows = shape[0] * map_rows
+    head = 2 * map_rows
+    me = where_ref[0] >> 2
+    core = me & 1
+    outside = (where_ref[0] & 2) != 0
+    halo_ref = wide_ref.at[:head]
+
+    @pl.when(outside)
+    def _():
+        halo_ref[...] = jnp.zeros(halo_ref.shape, halo_ref.dtype)
+
+    @pl.when(jnp.logical_not(outside) & (core == 0))
+    def _():
+        spread(first_halo_ref[...], width, halo_ref)
+
+    @pl.when(jnp.logical_not(outside) & (core == 1))
+    def _():
+        spread(second_halo_ref[...], width, halo_ref)
+
+    late = dot(halo_ref[...], weights_of(kern_ref, 0), (1, 0))
+    early = dot(halo_ref[map_rows:], weights_of(kern_ref, 1), (1, 0))
     sums = sums_ref[...]
-    if rows > 2 * map_rows:
-        sums = jnp.concatenate(
-            [sums[: 2 * map_rows] + head, sums[2 * map_rows :]], axis=0
-        )
-    else:
-        sums = sums + head
+    sums = jnp.concatenate(
+        [
+            sums[:map_rows] + (late[:map_rows] + early),
+            sums[map_rows:head] + late[map_rows:],
+            sums[head:],
+        ],
+        axis=0,
+    )
     pre = (
         moved_rows(sums[:, :chans], map_rows, width, 1)
         + sums[:, chans : 2 * chans]
@@ -143,24 +176,18 @@
     )
     sig = jax.nn.sigmoid(pre)
     hidden = (pre * sig).astype(jnp.bfloat16)
-    grads = grads_ref[...]
     pre_grad = (hidden_grad_ref[...] * sig * (1.0 + pre * (1.0 - sig))).astype(jnp.bfloat16)
-    hidden_ref[...] = hidden
-    pre_grad_ref[...] = pre_grad
-    me = where_ref[0] >> 2
-    core = me & 1
-    mine, other = halves_of(me)
-
-    def put(tap, value):
+    hidden_ref[...] = jnp.where(core == 0, hidden[:rows], hidden[rows:])
+    pre_grad_ref[...] = jnp.where(core == 0, pre_grad[:rows], pre_grad[rows:])
+    flip = halves_of(me)[0]
+
+    def put(place, value):
         block_rows = keep_ref.shape[2]
         for block in range(4):
-            start = block * block_rows
-            low = value[start : start + block_rows]
-            high = value[chans // 2 + start : chans // 2 + start + block_rows]
-            keep_ref[block ^ mine, tap] = jnp.where(core == 0, low, high)
-            send_ref[block ^ other, tap] = jnp.where(core == 0, high, low)
-
-    put(27, dot(hidden, grads, (0, 0)))
+            rows_of = value[block * block_rows : (block + 1) * block_rows]
+            keep_ref[block ^ flip, place] = rows_of
+            send_ref[block ^ flip, place] = rows_of.astype(send_ref.dtype)
+
     grad_rows = jnp.concatenate(
         [
             moved_rows(pre_grad, map_rows, width, -1),
@@ -169,18 +196,19 @@
         ],
         axis=1,
     )
-    for tau in range(3):
-        skip = (2 - tau) * map_rows
-        part = dot(own_ref[: rows - skip], grad_rows[skip:], (0, 0)) if skip < rows else None
-        if skip:
-            term = dot(wide_ref[tau * map_rows :], grad_rows[:skip], (0, 0))
-            part = term if part is None else part + term
-        for row in range(3):
-            for col in range(3):
-                put(
-                    tau * 9 + row * 3 + col,
-                    part[col * chans : (col + 1) * chans, row * chans : (row + 1) * chans],
-                )
+
+    def tap(sums, row, col):
+        return sums[col * chans : (col + 1) * chans, row * chans : (row + 1) * chans]
+
+    outer = pl.ds(pl.multiple_of(core * head, map_rows), 2 * rows)
+    sums = dot(wide_ref[outer], grad_rows, (0, 0))
+    for place in range(9):
+        put(place, tap(sums, place // 3, place % 3))
+    sums = dot(wide_ref[map_rows : map_rows + 2 * rows], grad_rows, (0, 0))
+    middle = [tap(sums, place // 3, place % 3) for place in range(9)]
+    middle.append(dot(hidden, grads_ref[...], (0, 0)))
+    for place in range(5):
+        put(9 + place, jnp.where(core == 0, middle[place], middle[5 + place]))
 
 
 def backward_kernel(
@@ -212,54 +240,59 @@
 
 
 def unpack_kernel(scale, offsets, where_ref, *refs):
-    count = len(offsets)
-    pieces = refs[: 2 * count]
+    pieces = refs[: 2 * len(offsets)]
     kern_ref, proj_ref, out_ref, sems = refs[-4:]
     me = where_ref[0] >> 2
     core = me & 1
     halves = tuple(zip((core, 1 - core), halves_of(me)))
-    taps, chans, _ = kern_ref.shape
     block_rows = out_ref.shape[2]
     copies = []
     for place, piece_ref in enumerate(pieces):
         half, flip = halves[place % 2]
         block = offsets[place // 2] ^ flip
         out_ref[place] = piece_ref[0].astype(jnp.float32) * scale
-        rows = pl.ds(
-            pl.multiple_of(half * (chans // 2) + block * block_rows, block_rows), block_rows
-        )
-        copies += [
-            pltpu.make_async_copy(
-                out_ref.at[place, :taps], kern_ref.at[:, rows, :], sems.at[2 * place]
-            ),
-            pltpu.make_async_copy(out_ref.at[place, taps], proj_ref.at[rows, :], sems.at[2 * place + 1]),
-        ]
-        copies[-2].start()
-        copies[-1].start()
-    for copy in copies:
-        copy.wait()
+        rows = pl.ds(pl.multiple_of(block * block_rows, block_rows), block_rows)
+        piece = out_ref.at[place]
+        for start, target, wanted in (
+            (piece.at[:9], kern_ref.at[pl.ds(18 * half, 9), rows, :], None),
+            (piece.at[9:13], kern_ref.at[pl.ds(9 + 5 * half, 4), rows, :], None),
+            (piece.at[13], kern_ref.at[13, rows, :], 0),
+            (piece.at[13], proj_ref.at[rows, :], 1),
+        ):
+            copy = pltpu.make_async_copy(start, target, sems.at[len(copies)])
+            copies.append((copy, None if wanted is None else half == wanted))
+            do(copies[-1][1], copy.start)
+    for copy, wanted in copies:
+        do(wanted, copy.wait)
+
+
+def do(wanted, action):
+    if wanted is None:
+        action()
+    else:
+        pl.when(wanted)(action)
 
 
 def unpack(where, pieces, offsets, scale, sofar=()):
     given = [piece for offset in offsets for piece in pieces[offset]]
-    _, taps, block_rows, chans = given[0].shape
+    _, places, block_rows, chans = given[0].shape
     return pl.pallas_call(
         functools.partial(unpack_kernel, scale, offsets),
         out_shape=(
-            jax.ShapeDtypeStruct((taps - 1, chans, chans), jnp.float32),
+            jax.ShapeDtypeStruct((2 * places - 1, chans, chans), jnp.float32),
             jax.ShapeDtypeStruct((chans, chans), jnp.float32),
         ),
         in_specs=[SCALAR] + [VECTOR] * len(given) + [OUTSIDE] * len(sofar),
         out_specs=(OUTSIDE, OUTSIDE),
         scratch_shapes=[
-            pltpu.VMEM((len(given), taps, block_rows, chans), jnp.float32),
-            pltpu.SemaphoreType.DMA((2 * len(given),)),
+            pltpu.VMEM((len(given), places, block_rows, chans), jnp.float32),
+            pltpu.SemaphoreType.DMA((4 * len(given),)),
         ],
         input_output_aliases={1 + len(given) + i: i for i in range(len(sofar))},
         compiler_params=LIMIT,
         cost_estimate=pl.CostEstimate(
-            flops=taps * block_rows * chans * len(given),
-            bytes_accessed=6 * taps * block_rows * chans * len(given),
+            flops=places * block_rows * chans * len(given),
+            bytes_accessed=6 * places * block_rows * chans * len(given),
             transcendentals=0,
         ),
         name="unpack",
@@ -267,14 +300,9 @@
 
 
 def summed(where, keep, send, scale, beside_split, beside_exchange):
-    total = keep + swapped(send, (1, 1))
-    part = total.shape[0] // 4
-    came = [
-        swapped(total[offset * part : (offset + 1) * part].astype(jnp.bfloat16), masks_of(0, offset))
-        for offset in (3, 2, 1)
-    ]
-    total = total[:part]
-    for piece in came:
+    total = keep[:1]
+    for offset in (3, 2, 1):
+        piece = swapped(send[offset : offset + 1], masks_of(0, offset))
         total = total + piece.astype(jnp.float32)
     done = beside_split()
     total, done = lax.optimization_barrier((total, done))
@@ -299,49 +327,65 @@
     return unpack(where, pieces, (3,), scale, sofar), done
 
 
-def prepare(shape, frames, grads, conv_kernel, proj_weight):
+def prepare(width, frames, grads, conv_kernel, proj_weight):
+    given = (frames, grads, conv_kernel, proj_weight)
+    rows, chans = frames.shape
+    return pl.pallas_call(
+        functools.partial(prepare_kernel, width),
+        out_shape=(
+            *(jax.ShapeDtypeStruct(x.shape, x.dtype) for x in given),
+            jax.ShapeDtypeStruct((rows, 3 * chans), jnp.bfloat16),
+        ),
+        in_specs=[OUTSIDE] * 4,
+        out_specs=(VECTOR,) * 5,
+        scratch_shapes=[pltpu.SemaphoreType.DMA((4,))],
+        compiler_params=LIMIT,
+        cost_estimate=pl.CostEstimate(flops=rows * chans, bytes_accessed=2 << 20, transcendentals=0),
+        name="prepare",
+    )(*(pltpu.with_memory_space_constraint(x, pltpu.HBM) for x in given))
+
+
+def join(shape, where, own, grads, partner, partner_grads, conv_kernel, proj_weight):
     n_frames, height, width, chans = shape
     rows = n_frames * height * width
+    head = 2 * height * width
     return pl.pallas_call(
-        functools.partial(prepare_kernel, shape),
+        functools.partial(join_kernel, shape),
         out_shape=(
-            jax.ShapeDtypeStruct(frames.shape, frames.dtype),
-            jax.ShapeDtypeStruct(grads.shape, grads.dtype),
-            jax.ShapeDtypeStruct(conv_kernel.shape, conv_kernel.dtype),
-            jax.ShapeDtypeStruct(proj_weight.shape, proj_weight.dtype),
-            jax.ShapeDtypeStruct((rows, 3 * chans), jnp.bfloat16),
-            jax.ShapeDtypeStruct((rows, 3 * chans), jnp.float32),
-            jax.ShapeDtypeStruct((rows, chans), jnp.float32),
-        ),
-        in_specs=[OUTSIDE] * 4,
-        out_specs=(VECTOR,) * 7,
-        scratch_shapes=[pltpu.SemaphoreType.DMA((6,))],
+            jax.ShapeDtypeStruct((head + 2 * rows, 3 * chans), jnp.bfloat16),
+            jax.ShapeDtypeStruct((2 * rows, chans), jnp.bfloat16),
+            jax.ShapeDtypeStruct((2 * rows, 3 * chans), jnp.float32),
+            jax.ShapeDtypeStruct((2 * rows, chans), jnp.float32),
+        ),
+        in_specs=[SCALAR] + [VECTOR] * 6,
+        out_specs=(VECTOR,) * 4,
         compiler_params=LIMIT,
         cost_estimate=pl.CostEstimate(
-            flops=2 * rows * 20 * chans * chans, bytes_accessed=1 << 20, transcendentals=0
-        ),
-        name="prepare",
-    )(*(pltpu.with_memory_space_constraint(x, pltpu.HBM) for x in (frames, grads, conv_kernel, proj_weight)))
-
-
-def forward(shape, where, halo, grads, conv_kernel, own, sums, hidden_grad):
+            flops=2 * rows * 40 * chans * chans, bytes_accessed=2 << 20, transcendentals=0
+        ),
+        name="join",
+    )(where, own, grads, partner, partner_grads, conv_kernel, proj_weight)
+
+
+def forward(shape, where, first_halo, second_halo, grads, conv_kernel, wide, sums, hidden_grad):
     n_frames, height, width, chans = shape
     rows = n_frames * height * width
-    half = (4, 28, chans // 8, chans)
+    half = (4, 14, chans // 4, chans)
     return pl.pallas_call(
         functools.partial(forward_kernel, shape),
         out_shape=(
             jax.ShapeDtypeStruct(half, jnp.float32),
-            jax.ShapeDtypeStruct(half, jnp.float32),
+            jax.ShapeDtypeStruct(half, jnp.bfloat16),
             jax.ShapeDtypeStruct((rows, chans), jnp.bfloat16),
             jax.ShapeDtypeStruct((rows, chans), jnp.bfloat16),
-        ),
-        in_specs=[SCALAR] + [VECTOR] * 6,
-        out_specs=(VECTOR,) * 4,
-        scratch_shapes=[pltpu.VMEM((2 * height * width, 3 * chans), jnp.bfloat16)],
+            jax.ShapeDtypeStruct(wide.shape, wide.dtype),
+        ),
+        in_specs=[SCALAR] + [VECTOR] * 7,
+        out_specs=(VECTOR,) * 5,
+        input_output_aliases={5: 4},
         compiler_params=LIMIT,
         name="forward",
-    )(where, halo, grads, conv_kernel, own, sums, hidden_grad)
+    )(where, first_halo, second_halo, grads, conv_kernel, wide, sums, hidden_grad)[:4]
 
 
 def backward(shape, where, pre_grad, following, hidden, frames, grads, conv_kernel, proj_weight):
@@ -368,15 +412,22 @@
     frames = clip_frames.reshape(rows, chans)
     grads = out_grad.reshape(rows, chans)
     block = lax.axis_index("tm")
-    first = (block == 0).astype(jnp.int32)
+    first = (block < 2).astype(jnp.int32)
     last = (block == lax.axis_size("tm") - 1).astype(jnp.int32)
     where = (4 * device_number() + 2 * first + last).astype(jnp.int32).reshape(1)
-    halo = passed_round(frames[rows - halo_rows :], "tm", 1)
-    frames, grads, conv_kernel, proj_weight, own, sums, hidden_grad = prepare(
-        shape, frames, grads, conv_kernel, proj_weight
+    tail = frames[rows - halo_rows :]
+    first_halo = passed_round(tail, "tm", 1)
+    second_halo = passed_round(tail, "tm", 2)
+    partner = swapped(frames, (1, 1))
+    partner_grads = swapped(grads, (1, 1))
+    frames, grads, conv_kernel, proj_weight, own = prepare(
+        width, frames, grads, conv_kernel, proj_weight
+    )
+    wide, pair_grads, sums, hidden_grad = join(
+        shape, where, own, grads, partner, partner_grads, conv_kernel, proj_weight
     )
     keep, send, hidden, pre_grad = forward(
-        shape, where, halo, grads, conv_kernel, own, sums, hidden_grad
+        shape, where, first_halo, second_halo, pair_grads, conv_kernel, wide, sums, hidden_grad
     )
     total_pixels = lax.axis_size("dp") * lax.axis_size("tm") * rows
     (kernel_grad, proj_grad), (mixed, input_grad) = summed(

time: 38.9 us -> 37.2 us (0.956)
  waiting for transfers between devices: 9.86 us -> 6.68 us
  starting transfers between devices: 21.7 us -> 22.9 us
  Pallas kernels: 6.14 us -> 6.55 us
    ppermute x14 -> x15, waiting for transfers between devices: 9.86 us -> 5.85 us  [swapped(): lax.ppermute(array, AXES, [(i, i ^ masks[i & 1]) for i in range(count)])]
    ppermute x2 -> x3, starting transfers between devices: 2.65 us -> 4.02 us  [passed_round(): lax.ppermute(shard, axis, [(i, (i + by) % size) for i in range(size)])]
    ppermute x2 -> x3, waiting for transfers between devices: 0.01 us -> 0.83 us  [passed_round(): lax.ppermute(shard, axis, [(i, (i + by) % size) for i in range(size)])]
    pallas_call x1 -> x2, Pallas kernels: 1.72 us -> 2.07 us  [the longest x1 1.28 us: prepare(): pl.pallas_call(functools.partial(prepare_kernel, width), out_shape=(*(jax...]
    ppermute x14 -> x15, starting transfers between devices: 19 us -> 18.8 us  [swapped(): lax.ppermute(array, AXES, [(i, i ^ masks[i & 1]) for i in range(count)])]
  transfers between devices with their start and end apart: 16 -> 18, of which waited for: 5 -> 7; matrix products, arithmetic and copies ran while one was open for 0% -> 0% of each run, Pallas kernels for 11% -> 13%
where the time goes in v8:
time: 37.2 us; the launch traced here: 37 us
  starting transfers between devices  22.9 us (62%)
  waiting for transfers between devices  6.68 us (18%)
  Pallas kernels  6.55 us (18%)
  between operations  0.75 us (2%)
    ppermute x15, starting transfers between devices, swapped(): lax.ppermute(array, AXES, [(i, i ^ masks[i & 1]) for i in range(count)])  18.8 us
    ppermute x15, waiting for transfers between devices, swapped(): lax.ppermute(array, AXES, [(i, i ^ masks[i & 1]) for i in range(count)])  5.85 us
    ppermute x3, starting transfers between devices, passed_round(): lax.ppermute(shard, axis, [(i, (i + by) % size) for i in range(size)])  4.02 us
    pallas_call x2, Pallas kernels, unpack(): pl.pallas_call(functools.partial(unpack_kernel, scale, offsets), out_shap...  2.14 us
    pallas_call x1, Pallas kernels, backward(): pl.pallas_call(functools.partial(backward_kernel, shape), out_shape=(jax....  1.29 us
    pallas_call x1, Pallas kernels, prepare(): pl.pallas_call(functools.partial(prepare_kernel, width), out_shape=(*(jax...  1.28 us
    pallas_call x1, Pallas kernels, forward(): pl.pallas_call(functools.partial(forward_kernel, shape), out_shape=(jax.S...  1.05 us
    ppermute x3, waiting for transfers between devices, passed_round(): lax.ppermute(shard, axis, [(i, (i + by) % size) for i in range(size)])  0.83 us
  transfers between devices with their start and end apart: 18, of which 7 were waited for; matrix products, arithmetic and copies ran while one was open for 0% of the time, Pallas kernels for 13%

profile of v8, /device:TPU:1, one launch (start us, length us, event | category | flops | bytes accessed | tf_op | source)
XLA Modules:
  0.0 37.0 jit_solution(662624417631438583)
XLA Ops:
  0.6 0.1 collective-permute-start.2
  0.8 0.5 %collective-permute-start.3 = (bf16[256,128]{1,0:T(8,128)(2,1)}, bf16[256,128]{1,0:T(8,128)(2,1)S(1)}, u32[]{:S(2)}, u32[]{:S(2)}) collective-permute-start(bf16[256,128]{1,0:T(8,128)(2,1)} %bitcast.7), channel_id=1, source_target_pairs={{0,1},{1,0},{2,3},{3,2},{4,5},{5,4},{6,7},{7,6},{8,9},{9,8},{10,11... | collective-permute-start | bytes 196616 | tf_op jit(solution)/shard_map/ppermute | solution.py:30
  1.2 2.3 %collective-permute-start.1 = (bf16[256,128]{1,0:T(8,128)(2,1)}, bf16[256,128]{1,0:T(8,128)(2,1)S(1)}, u32[]{:S(2)}, u32[]{:S(2)}) collective-permute-start(bf16[256,128]{1,0:T(8,128)(2,1)} %bitcast.10), channel_id=1, source_target_pairs={{0,2},{1,3},{2,0},{3,1},{4,6},{5,7},{6,4},{7,5},{8,10},{9,11},{10,... | collective-permute-start | bytes 196616 | tf_op jit(solution)/shard_map/ppermute | solution.py:21
  3.5 0.4 collective-permute-start
  3.8 1.3 %prepare.1 = (bf16[256,128]{1,0:T(8,128)(2,1)S(1)}, bf16[256,128]{1,0:T(8,128)(2,1)S(1)}, bf16[3,3,3,128,128]{4,3,2,1,0:T(8,128)(2,1)S(1)}, bf16[128,128]{1,0:T(8,128)(2,1)S(1)}, bf16[256,384]{1,0:T(8,128)(2,1)S(1)}) custom-call(bf16[256,128]{1,0:T(8,128)(2,1)} %bitcast.12, bf16[256,128]{1,0:T(8,128)(2,1)} %bitcast.8, bf16[3,3,3,128,128]{4,3,2,1,0:T(8,128)(2,1)} %kern_hbm.1, ...), custom_call_target="tpu_custom_call" | custom-call | flops 32768 | bytes 2097152 | tf_op jit(solution)/shard_map/prepare/pallas_call | solution.py:333
  5.1 0.0 collective-permute-done.2.partner_ref
  5.2 0.0 collective-permute-done.3.partner_grads_ref
  5.2 0.8 %join.1 = (bf16[768,384]{1,0:T(8,128)(2,1)S(1)}, bf16[512,128]{1,0:T(8,128)(2,1)S(1)}, f32[512,384]{1,0:T(8,128)S(1)}, f32[512,128]{1,0:T(8,128)S(1)}) custom-call(s32[1]{0:T(128)} %bitcast.where_ref, bf16[256,384]{1,0:T(8,128)(2,1)S(1)} %get-tuple-element.28.own_ref, bf16[256,128]{1,0:T(8,128)(2,1)S(1)} %get-tuple-element.29.grads_ref, ...), custom_call_target="tpu_custom_call" | custom-call | flops 335544320 | bytes 2097152 | tf_op jit(solution)/shard_map/join/pallas_call | solution.py:352
  6.0 0.0 collective-permute-done.1.second_halo_ref
  6.0 0.3 collective-permute-done.first_halo_ref
  6.2 1.0 %forward.1 = (f32[4,14,32,128]{3,2,1,0:T(8,128)S(1)}, bf16[4,14,32,128]{3,2,1,0:T(8,128)(2,1)S(1)}, bf16[256,128]{1,0:T(8,128)(2,1)S(1)}, bf16[256,128]{1,0:T(8,128)(2,1)S(1)}, bf16[768,384]{1,0:T(8,128)(2,1)S(1)}) custom-call(s32[1]{0:T(128)} %bitcast.where_ref, ...), custom_call_target="tpu_custom_call", output_to_operand_aliasing={{4}: (5, {})} | custom-call | tf_op jit(solution)/shard_map/forward/pallas_call | solution.py:374
  7.3 3.7 %collective-permute-start.4 = (bf16[1,14,32,128]{3,2,1,0:T(8,128)(2,1)S(1)}, bf16[1,14,32,128]{3,2,1,0:T(8,128)(2,1)S(1)}, u32[]{:S(2)}, u32[]{:S(2)}) collective-permute-start(bf16[1,14,32,128]{3,2,1,0:T(8,128)(2,1)S(1)} %get-tuple-element.52), channel_id=1, source_target_pairs={{0,6},{1,25},{2,4},{3,27},{4,2},{5,29},{6,0},{7,31},{8,14},{9,17},... | collective-permute-start | bytes 344072 | tf_op jit(solution)/shard_map/ppermute | solution.py:30
  11.0 0.0 collective-permute-start.6
  11.0 0.4 collective-permute-start.5
  11.4 1.4 %collective-permute-start.7 = (bf16[256,128]{1,0:T(8,128)(2,1)S(1)}, bf16[256,128]{1,0:T(8,128)(2,1)S(1)}, u32[]{:S(2)}, u32[]{:S(2)}) collective-permute-start(bf16[256,128]{1,0:T(8,128)(2,1)S(1)} %get-tuple-element.38.pre_grad_ref), channel_id=1, source_target_pairs={{0,3},{1,0},{2,1},{3,2},{4,7},{5,4},{6,5},{7,6},{8,11},{9,8},{10,9... | collective-permute-start | bytes 196616 | tf_op jit(solution)/shard_map/ppermute | solution.py:21
  12.8 0.5 %collective-permute-done.4 = bf16[1,14,32,128]{3,2,1,0:T(8,128)(2,1)S(1)} collective-permute-done((bf16[1,14,32,128]{3,2,1,0:T(8,128)(2,1)S(1)}, bf16[1,14,32,128]{3,2,1,0:T(8,128)(2,1)S(1)}, u32[]{:S(2)}, u32[]{:S(2)}) %collective-permute-start.4) | collective-permute-done | bytes 114720 | tf_op jit(solution)/shard_map/ppermute | solution.py:30
  13.3 2.7 %collective-permute-done.6 = bf16[1,14,32,128]{3,2,1,0:T(8,128)(2,1)S(1)} collective-permute-done((bf16[1,14,32,128]{3,2,1,0:T(8,128)(2,1)S(1)}, bf16[1,14,32,128]{3,2,1,0:T(8,128)(2,1)S(1)}, u32[]{:S(2)}, u32[]{:S(2)}) %collective-permute-start.6) | collective-permute-done | bytes 114720 | tf_op jit(solution)/shard_map/ppermute | solution.py:30
  16.0 0.0 collective-permute-done.5
  16.0 0.1 convert_add_fusion
  16.1 0.6 %collective-permute-done.7.next_ref = bf16[256,128]{1,0:T(8,128)(2,1)S(1)} collective-permute-done((bf16[256,128]{1,0:T(8,128)(2,1)S(1)}, bf16[256,128]{1,0:T(8,128)(2,1)S(1)}, u32[]{:S(2)}, u32[]{:S(2)}) %collective-permute-start.7) | collective-permute-done | bytes 65568 | tf_op jit(solution)/shard_map/ppermute | solution.py:21
  16.7 1.7 %collective-permute-start.10 = (bf16[1,14,32,128]{3,2,1,0:T(8,128)(2,1)S(1)}, bf16[1,14,32,128]{3,2,1,0:T(8,128)(2,1)S(1)}, u32[]{:S(2)}, u32[]{:S(2)}) collective-permute-start(bf16[1,14,32,128]{3,2,1,0:T(8,128)(2,1)S(1)} %reduce-precision_convert_fusion), channel_id=1, source_target_pairs={{0,24},{1,7},{2,26},{3,5},{4,28},{5,3},{6,30},{7,1},{8,16},{9,15},... | collective-permute-start | bytes 344072 | tf_op jit(solution)/shard_map/ppermute | solution.py:30
  18.4 0.9 %collective-permute-start.9 = (bf16[1,14,32,128]{3,2,1,0:T(8,128)(2,1)S(1)}, bf16[1,14,32,128]{3,2,1,0:T(8,128)(2,1)S(1)}, u32[]{:S(2)}, u32[]{:S(2)}) collective-permute-start(bf16[1,14,32,128]{3,2,1,0:T(8,128)(2,1)S(1)} %reduce-precision_convert_fusion), channel_id=1, source_target_pairs={{0,8},{1,3},{2,10},{3,1},{4,12},{5,7},{6,14},{7,5},{8,0},{9,11},{1... | collective-permute-start | bytes 344072 | tf_op jit(solution)/shard_map/ppermute | solution.py:30
  19.3 0.1 collective-permute-start.8
  19.4 1.3 %backward.1 = (bf16[256,128]{1,0:T(8,128)(2,1)}, bf16[256,128]{1,0:T(8,128)(2,1)}) custom-call(s32[1]{0:T(128)} %bitcast.where_ref, bf16[256,128]{1,0:T(8,128)(2,1)S(1)} %get-tuple-element.38.pre_grad_ref, bf16[256,128]{1,0:T(8,128)(2,1)S(1)} %collective-permute-done.7.next_ref, bf16[256,128]{1,0:T(8,128)(2,1)S(1)} %get-tuple-element.41.hidden_ref, ...), custom_call_target="tpu_custom_call" | custom-call | flops 234881024 | bytes 1048576 | tf_op jit(solution)/shard_map/backward/pallas_call | solution.py:395
  20.7 0.6 %collective-permute-done.10 = bf16[1,14,32,128]{3,2,1,0:T(8,128)(2,1)S(1)} collective-permute-done((bf16[1,14,32,128]{3,2,1,0:T(8,128)(2,1)S(1)}, bf16[1,14,32,128]{3,2,1,0:T(8,128)(2,1)S(1)}, u32[]{:S(2)}, u32[]{:S(2)}) %collective-permute-start.10) | collective-permute-done | bytes 114720 | tf_op jit(solution)/shard_map/ppermute | solution.py:30
  21.3 1.7 %collective-permute-done.9 = bf16[1,14,32,128]{3,2,1,0:T(8,128)(2,1)S(1)} collective-permute-done((bf16[1,14,32,128]{3,2,1,0:T(8,128)(2,1)S(1)}, bf16[1,14,32,128]{3,2,1,0:T(8,128)(2,1)S(1)}, u32[]{:S(2)}, u32[]{:S(2)}) %collective-permute-start.9) | collective-permute-done | bytes 114720 | tf_op jit(solution)/shard_map/ppermute | solution.py:30
  23.0 0.0 collective-permute-done.8
  23.0 0.1 add_convert_fusion.refs_0_
  23.1 1.3 %collective-permute-start.16 = (bf16[1,14,32,128]{3,2,1,0:T(8,128)(2,1)S(1)}, bf16[1,14,32,128]{3,2,1,0:T(8,128)(2,1)S(1)}, u32[]{:S(2)}, u32[]{:S(2)}) collective-permute-start(bf16[1,14,32,128]{3,2,1,0:T(8,128)(2,1)S(1)} %add_convert_fusion.refs_0_), channel_id=1, source_target_pairs={{0,2},{1,9},{2,0},{3,11},{4,6},{5,13},{6,4},{7,15},{8,10},{9,1},{1... | collective-permute-start | bytes 344072 | tf_op jit(solution)/shard_map/ppermute | solution.py:30
  24.4 2.6 %collective-permute-start.14 = (bf16[1,14,32,128]{3,2,1,0:T(8,128)(2,1)S(1)}, bf16[1,14,32,128]{3,2,1,0:T(8,128)(2,1)S(1)}, u32[]{:S(2)}, u32[]{:S(2)}) collective-permute-start(bf16[1,14,32,128]{3,2,1,0:T(8,128)(2,1)S(1)} %add_convert_fusion.refs_0_), channel_id=1, source_target_pairs={{0,4},{1,17},{2,6},{3,19},{4,0},{5,21},{6,2},{7,23},{8,12},{9,25},... | collective-permute-start | bytes 344072 | tf_op jit(solution)/shard_map/ppermute | solution.py:30
  27.0 0.0 collective-permute-start.11
  27.0 3.4 %collective-permute-start.13 = (bf16[1,14,32,128]{3,2,1,0:T(8,128)(2,1)S(1)}, bf16[1,14,32,128]{3,2,1,0:T(8,128)(2,1)S(1)}, u32[]{:S(2)}, u32[]{:S(2)}) collective-permute-start(bf16[1,14,32,128]{3,2,1,0:T(8,128)(2,1)S(1)} %add_convert_fusion.refs_0_), channel_id=1, source_target_pairs={{0,1},{1,0},{2,3},{3,2},{4,5},{5,4},{6,7},{7,6},{8,9},{9,8},{10,11... | collective-permute-start | bytes 344072 | tf_op jit(solution)/shard_map/ppermute | solution.py:30
  30.4 0.0 collective-permute-done.16.refs_4_
  30.4 1.3 %collective-permute-start.17 = (bf16[1,14,32,128]{3,2,1,0:T(8,128)(2,1)S(1)}, bf16[1,14,32,128]{3,2,1,0:T(8,128)(2,1)S(1)}, u32[]{:S(2)}, u32[]{:S(2)}) collective-permute-start(bf16[1,14,32,128]{3,2,1,0:T(8,128)(2,1)S(1)} %collective-permute-done.16.refs_4_), channel_id=1, source_target_pairs={{0,1},{1,0},{2,3},{3,2},{4,5},{5,4},{6,7},{7,6},{8,9},{9,8},{10,11... | collective-permute-start | bytes 344072 | tf_op jit(solution)/shard_map/ppermute | solution.py:30
  31.7 0.0 collective-permute-done.14.refs_2_
  31.7 0.7 %collective-permute-start.15 = (bf16[1,14,32,128]{3,2,1,0:T(8,128)(2,1)S(1)}, bf16[1,14,32,128]{3,2,1,0:T(8,128)(2,1)S(1)}, u32[]{:S(2)}, u32[]{:S(2)}) collective-permute-start(bf16[1,14,32,128]{3,2,1,0:T(8,128)(2,1)S(1)} %collective-permute-done.14.refs_2_), channel_id=1, source_target_pairs={{0,1},{1,0},{2,3},{3,2},{4,5},{5,4},{6,7},{7,6},{8,9},{9,8},{10,11... | collective-permute-start | bytes 344072 | tf_op jit(solution)/shard_map/ppermute | solution.py:30
  32.3 0.2 collective-permute-done.11.refs_0_
  32.5 2.3 %collective-permute-start.12 = (bf16[1,14,32,128]{3,2,1,0:T(8,128)(2,1)S(1)}, bf16[1,14,32,128]{3,2,1,0:T(8,128)(2,1)S(1)}, u32[]{:S(2)}, u32[]{:S(2)}) collective-permute-start(bf16[1,14,32,128]{3,2,1,0:T(8,128)(2,1)S(1)} %collective-permute-done.11.refs_0_), channel_id=1, source_target_pairs={{0,1},{1,0},{2,3},{3,2},{4,5},{5,4},{6,7},{7,6},{8,9},{9,8},{10,11... | collective-permute-start | bytes 344072 | tf_op jit(solution)/shard_map/ppermute | solution.py:30
  34.8 0.0 collective-permute-done.13.refs_1_
  34.8 0.0 collective-permute-done.17.refs_5_
  34.8 0.0 collective-permute-done.15.refs_3_
  34.9 1.3 %unpack.2 = (f32[27,128,128]{2,1,0:T(8,128)}, f32[128,128]{1,0:T(8,128)}) custom-call(s32[1]{0:T(128)} %bitcast.where_ref, bf16[1,14,32,128]{3,2,1,0:T(8,128)(2,1)S(1)} %add_convert_fusion.refs_0_, bf16[1,14,32,128]{3,2,1,0:T(8,128)(2,1)S(1)} %collective-permute-done.13.refs_1_, bf16[1,14,32,128]{3,2,1,0:T(8,128)(2,1)S(1)} %collective-permute-done.14.refs_2_, ...), custom_call_target="tpu_custom_call" | custom-call | flops 344064 | bytes 2064384 | tf_op jit(solution)/shard_map/unpack/pallas_call | solution.py:279
  36.2 0.0 collective-permute-done.12.refs_1_
  36.2 0.9 %unpack.3 = (f32[27,128,128]{2,1,0:T(8,128)}, f32[128,128]{1,0:T(8,128)}) custom-call(s32[1]{0:T(128)} %bitcast.where_ref, bf16[1,14,32,128]{3,2,1,0:T(8,128)(2,1)S(1)} %collective-permute-done.11.refs_0_, bf16[1,14,32,128]{3,2,1,0:T(8,128)(2,1)S(1)} %collective-permute-done.12.refs_1_, ...), custom_call_target="tpu_custom_call", output_to_operand_aliasing={{0}: (3, {}), {1}: (4, {})} | custom-call | flops 114688 | bytes 688128 | tf_op jit(solution)/shard_map/unpack/pallas_call | solution.py:279
  (2 shorter events, 0.0 us)
Async XLA Ops:
  0.6 4.5 %collective-permute-start.2 = (bf16[256,128]{1,0:T(8,128)(2,1)}, bf16[256,128]{1,0:T(8,128)(2,1)S(1)}, u32[]{:S(2)}, u32[]{:S(2)}) collective-permute-start(bf16[256,128]{1,0:T(8,128)(2,1)} %bitcast.9), channel_id=1, source_target_pairs={{0,1},{1,0},{2,3},{3,2},{4,5},{5,4},{6,7},{7,6},{8,9},{9,8},{10,11... | collective-permute-start | bytes 196616 | tf_op jit(solution)/shard_map/ppermute | solution.py:30
  0.8 4.4 %collective-permute-start.3 = (bf16[256,128]{1,0:T(8,128)(2,1)}, bf16[256,128]{1,0:T(8,128)(2,1)S(1)}, u32[]{:S(2)}, u32[]{:S(2)}) collective-permute-start(bf16[256,128]{1,0:T(8,128)(2,1)} %bitcast.7), channel_id=1, source_target_pairs={{0,1},{1,0},{2,3},{3,2},{4,5},{5,4},{6,7},{7,6},{8,9},{9,8},{10,11... | collective-permute-start | bytes 196616 | tf_op jit(solution)/shard_map/ppermute | solution.py:30
  1.2 4.8 %collective-permute-start.1 = (bf16[256,128]{1,0:T(8,128)(2,1)}, bf16[256,128]{1,0:T(8,128)(2,1)S(1)}, u32[]{:S(2)}, u32[]{:S(2)}) collective-permute-start(bf16[256,128]{1,0:T(8,128)(2,1)} %bitcast.10), channel_id=1, source_target_pairs={{0,2},{1,3},{2,0},{3,1},{4,6},{5,7},{6,4},{7,5},{8,10},{9,11},{10,... | collective-permute-start | bytes 196616 | tf_op jit(solution)/shard_map/ppermute | solution.py:21
  3.5 2.8 %collective-permute-start = (bf16[256,128]{1,0:T(8,128)(2,1)}, bf16[256,128]{1,0:T(8,128)(2,1)S(1)}, u32[]{:S(2)}, u32[]{:S(2)}) collective-permute-start(bf16[256,128]{1,0:T(8,128)(2,1)} %bitcast.11), channel_id=1, source_target_pairs={{0,1},{1,2},{2,3},{3,0},{4,5},{5,6},{6,7},{7,4},{8,9},{9,10},{10,1... | collective-permute-start | bytes 196616 | tf_op jit(solution)/shard_map/ppermute | solution.py:21
  7.3 6.0 %collective-permute-start.4 = (bf16[1,14,32,128]{3,2,1,0:T(8,128)(2,1)S(1)}, bf16[1,14,32,128]{3,2,1,0:T(8,128)(2,1)S(1)}, u32[]{:S(2)}, u32[]{:S(2)}) collective-permute-start(bf16[1,14,32,128]{3,2,1,0:T(8,128)(2,1)S(1)} %get-tuple-element.52), channel_id=1, source_target_pairs={{0,6},{1,25},{2,4},{3,27},{4,2},{5,29},{6,0},{7,31},{8,14},{9,17},... | collective-permute-start | bytes 344072 | tf_op jit(solution)/shard_map/ppermute | solution.py:30
  11.0 5.0 %collective-permute-start.6 = (bf16[1,14,32,128]{3,2,1,0:T(8,128)(2,1)S(1)}, bf16[1,14,32,128]{3,2,1,0:T(8,128)(2,1)S(1)}, u32[]{:S(2)}, u32[]{:S(2)}) collective-permute-start(bf16[1,14,32,128]{3,2,1,0:T(8,128)(2,1)S(1)} %get-tuple-element.53), channel_id=1, source_target_pairs={{0,4},{1,17},{2,6},{3,19},{4,0},{5,21},{6,2},{7,23},{8,12},{9,25},... | collective-permute-start | bytes 344072 | tf_op jit(solution)/shard_map/ppermute | solution.py:30
  11.0 5.0 %collective-permute-start.5 = (bf16[1,14,32,128]{3,2,1,0:T(8,128)(2,1)S(1)}, bf16[1,14,32,128]{3,2,1,0:T(8,128)(2,1)S(1)}, u32[]{:S(2)}, u32[]{:S(2)}) collective-permute-start(bf16[1,14,32,128]{3,2,1,0:T(8,128)(2,1)S(1)} %get-tuple-element.54), channel_id=1, source_target_pairs={{0,2},{1,9},{2,0},{3,11},{4,6},{5,13},{6,4},{7,15},{8,10},{9,1},{1... | collective-permute-start | bytes 344072 | tf_op jit(solution)/shard_map/ppermute | solution.py:30
  11.4 5.3 %collective-permute-start.7 = (bf16[256,128]{1,0:T(8,128)(2,1)S(1)}, bf16[256,128]{1,0:T(8,128)(2,1)S(1)}, u32[]{:S(2)}, u32[]{:S(2)}) collective-permute-start(bf16[256,128]{1,0:T(8,128)(2,1)S(1)} %get-tuple-element.38.pre_grad_ref), channel_id=1, source_target_pairs={{0,3},{1,0},{2,1},{3,2},{4,7},{5,4},{6,5},{7,6},{8,11},{9,8},{10,9... | collective-permute-start | bytes 196616 | tf_op jit(solution)/shard_map/ppermute | solution.py:21
  16.7 4.6 %collective-permute-start.10 = (bf16[1,14,32,128]{3,2,1,0:T(8,128)(2,1)S(1)}, bf16[1,14,32,128]{3,2,1,0:T(8,128)(2,1)S(1)}, u32[]{:S(2)}, u32[]{:S(2)}) collective-permute-start(bf16[1,14,32,128]{3,2,1,0:T(8,128)(2,1)S(1)} %reduce-precision_convert_fusion), channel_id=1, source_target_pairs={{0,24},{1,7},{2,26},{3,5},{4,28},{5,3},{6,30},{7,1},{8,16},{9,15},... | collective-permute-start | bytes 344072 | tf_op jit(solution)/shard_map/ppermute | solution.py:30
  18.4 4.6 %collective-permute-start.9 = (bf16[1,14,32,128]{3,2,1,0:T(8,128)(2,1)S(1)}, bf16[1,14,32,128]{3,2,1,0:T(8,128)(2,1)S(1)}, u32[]{:S(2)}, u32[]{:S(2)}) collective-permute-start(bf16[1,14,32,128]{3,2,1,0:T(8,128)(2,1)S(1)} %reduce-precision_convert_fusion), channel_id=1, source_target_pairs={{0,8},{1,3},{2,10},{3,1},{4,12},{5,7},{6,14},{7,5},{8,0},{9,11},{1... | collective-permute-start | bytes 344072 | tf_op jit(solution)/shard_map/ppermute | solution.py:30
  19.3 3.7 %collective-permute-start.8 = (bf16[1,14,32,128]{3,2,1,0:T(8,128)(2,1)S(1)}, bf16[1,14,32,128]{3,2,1,0:T(8,128)(2,1)S(1)}, u32[]{:S(2)}, u32[]{:S(2)}) collective-permute-start(bf16[1,14,32,128]{3,2,1,0:T(8,128)(2,1)S(1)} %reduce-precision_convert_fusion), channel_id=1, source_target_pairs={{0,16},{1,5},{2,18},{3,7},{4,20},{5,1},{6,22},{7,3},{8,24},{9,13},... | collective-permute-start | bytes 344072 | tf_op jit(solution)/shard_map/ppermute | solution.py:30
  23.1 7.3 %collective-permute-start.16 = (bf16[1,14,32,128]{3,2,1,0:T(8,128)(2,1)S(1)}, bf16[1,14,32,128]{3,2,1,0:T(8,128)(2,1)S(1)}, u32[]{:S(2)}, u32[]{:S(2)}) collective-permute-start(bf16[1,14,32,128]{3,2,1,0:T(8,128)(2,1)S(1)} %add_convert_fusion.refs_0_), channel_id=1, source_target_pairs={{0,2},{1,9},{2,0},{3,11},{4,6},{5,13},{6,4},{7,15},{8,10},{9,1},{1... | collective-permute-start | bytes 344072 | tf_op jit(solution)/shard_map/ppermute | solution.py:30
  24.4 7.3 %collective-permute-start.14 = (bf16[1,14,32,128]{3,2,1,0:T(8,128)(2,1)S(1)}, bf16[1,14,32,128]{3,2,1,0:T(8,128)(2,1)S(1)}, u32[]{:S(2)}, u32[]{:S(2)}) collective-permute-start(bf16[1,14,32,128]{3,2,1,0:T(8,128)(2,1)S(1)} %add_convert_fusion.refs_0_), channel_id=1, source_target_pairs={{0,4},{1,17},{2,6},{3,19},{4,0},{5,21},{6,2},{7,23},{8,12},{9,25},... | collective-permute-start | bytes 344072 | tf_op jit(solution)/shard_map/ppermute | solution.py:30
  27.0 5.5 %collective-permute-start.11 = (bf16[1,14,32,128]{3,2,1,0:T(8,128)(2,1)S(1)}, bf16[1,14,32,128]{3,2,1,0:T(8,128)(2,1)S(1)}, u32[]{:S(2)}, u32[]{:S(2)}) collective-permute-start(bf16[1,14,32,128]{3,2,1,0:T(8,128)(2,1)S(1)} %add_convert_fusion.refs_0_), channel_id=1, source_target_pairs={{0,6},{1,25},{2,4},{3,27},{4,2},{5,29},{6,0},{7,31},{8,14},{9,17},... | collective-permute-start | bytes 344072 | tf_op jit(solution)/shard_map/ppermute | solution.py:30
  27.0 7.8 %collective-permute-start.13 = (bf16[1,14,32,128]{3,2,1,0:T(8,128)(2,1)S(1)}, bf16[1,14,32,128]{3,2,1,0:T(8,128)(2,1)S(1)}, u32[]{:S(2)}, u32[]{:S(2)}) collective-permute-start(bf16[1,14,32,128]{3,2,1,0:T(8,128)(2,1)S(1)} %add_convert_fusion.refs_0_), channel_id=1, source_target_pairs={{0,1},{1,0},{2,3},{3,2},{4,5},{5,4},{6,7},{7,6},{8,9},{9,8},{10,11... | collective-permute-start | bytes 344072 | tf_op jit(solution)/shard_map/ppermute | solution.py:30
  30.4 4.5 %collective-permute-start.17 = (bf16[1,14,32,128]{3,2,1,0:T(8,128)(2,1)S(1)}, bf16[1,14,32,128]{3,2,1,0:T(8,128)(2,1)S(1)}, u32[]{:S(2)}, u32[]{:S(2)}) collective-permute-start(bf16[1,14,32,128]{3,2,1,0:T(8,128)(2,1)S(1)} %collective-permute-done.16.refs_4_), channel_id=1, source_target_pairs={{0,1},{1,0},{2,3},{3,2},{4,5},{5,4},{6,7},{7,6},{8,9},{9,8},{10,11... | collective-permute-start | bytes 344072 | tf_op jit(solution)/shard_map/ppermute | solution.py:30
  31.7 3.2 %collective-permute-start.15 = (bf16[1,14,32,128]{3,2,1,0:T(8,128)(2,1)S(1)}, bf16[1,14,32,128]{3,2,1,0:T(8,128)(2,1)S(1)}, u32[]{:S(2)}, u32[]{:S(2)}) collective-permute-start(bf16[1,14,32,128]{3,2,1,0:T(8,128)(2,1)S(1)} %collective-permute-done.14.refs_2_), channel_id=1, source_target_pairs={{0,1},{1,0},{2,3},{3,2},{4,5},{5,4},{6,7},{7,6},{8,9},{9,8},{10,11... | collective-permute-start | bytes 344072 | tf_op jit(solution)/shard_map/ppermute | solution.py:30
  32.5 3.6 %collective-permute-start.12 = (bf16[1,14,32,128]{3,2,1,0:T(8,128)(2,1)S(1)}, bf16[1,14,32,128]{3,2,1,0:T(8,128)(2,1)S(1)}, u32[]{:S(2)}, u32[]{:S(2)}) collective-permute-start(bf16[1,14,32,128]{3,2,1,0:T(8,128)(2,1)S(1)} %collective-permute-done.11.refs_0_), channel_id=1, source_target_pairs={{0,1},{1,0},{2,3},{3,2},{4,5},{5,4},{6,7},{7,6},{8,9},{9,8},{10,11... | collective-permute-start | bytes 344072 | tf_op jit(solution)/shard_map/ppermute | solution.py:30

commit v9 on v8

--- a/solution.py
+++ b/solution.py
@@ -19,6 +19,16 @@
 def passed_round(shard, axis, by):
     size = lax.axis_size(axis)
     return lax.ppermute(shard, axis, [(i, (i + by) % size) for i in range(size)])
+
+
+def passed_to_last_core(shard):
+    clips, blocks = lax.axis_size("dp"), lax.axis_size("tm")
+    pairs = [
+        (clip * blocks + i, clip * blocks + (i + 2) % blocks if i & 1 else (clip ^ 1) * blocks + i)
+        for clip in range(clips)
+        for i in range(blocks)
+    ]
+    return lax.ppermute(shard, AXES, pairs)
 
 
 def device_number():
@@ -134,7 +144,7 @@
 
 
 def forward_kernel(
-    shape, where_ref, first_halo_ref, second_halo_ref, grads_ref, kern_ref, _, sums_ref,
+    shape, where_ref, second_halo_ref, first_halo_ref, grads_ref, kern_ref, _, sums_ref,
     hidden_grad_ref, keep_ref, send_ref, hidden_ref, pre_grad_ref, wide_ref,
 ):
     _, height, width, chans = shape
@@ -385,7 +395,7 @@
         input_output_aliases={5: 4},
         compiler_params=LIMIT,
         name="forward",
-    )(where, first_halo, second_halo, grads, conv_kernel, wide, sums, hidden_grad)[:4]
+    )(where, second_halo, first_halo, grads, conv_kernel, wide, sums, hidden_grad)[:4]
 
 
 def backward(shape, where, pre_grad, following, hidden, frames, grads, conv_kernel, proj_weight):
@@ -417,7 +427,7 @@
     where = (4 * device_number() + 2 * first + last).astype(jnp.int32).reshape(1)
     tail = frames[rows - halo_rows :]
     first_halo = passed_round(tail, "tm", 1)
-    second_halo = passed_round(tail, "tm", 2)
+    second_halo = passed_to_last_core(tail)
     partner = swapped(frames, (1, 1))
     partner_grads = swapped(grads, (1, 1))
     frames, grads, conv_kernel, proj_weight, own = prepare(

time: 37.2 us -> 36.2 us (0.973)
  starting transfers between devices: 22.9 us -> 20 us
  waiting for transfers between devices: 6.68 us -> 8.56 us
    ppermute x15, waiting for transfers between devices: 5.85 us -> 7.37 us  [swapped(): lax.ppermute(array, AXES, [(i, i ^ masks[i & 1]) for i in range(count)])]
    ppermute x15, starting transfers between devices: 18.8 us -> 17.4 us  [swapped(): lax.ppermute(array, AXES, [(i, i ^ masks[i & 1]) for i in range(count)])]
    ppermute x3 -> x2, starting transfers between devices: 4.02 us -> 2.6 us  [passed_round(): lax.ppermute(shard, axis, [(i, (i + by) % size) for i in range(size)])]
    ppermute x0 -> x1, waiting for transfers between devices: none -> 1.19 us  [passed_to_last_core(): return lax.ppermute(shard, AXES, pairs)]
    ppermute x3 -> x2, waiting for transfers between devices: 0.83 us -> 0.01 us  [passed_round(): lax.ppermute(shard, axis, [(i, (i + by) % size) for i in range(size)])]
where the time goes in v9:
time: 36.2 us; the launch traced here: 36 us
  starting transfers between devices  20 us (55%)
  waiting for transfers between devices  8.56 us (24%)
  Pallas kernels  6.55 us (18%)
  between operations  0.76 us (2%)
    ppermute x15, starting transfers between devices, swapped(): lax.ppermute(array, AXES, [(i, i ^ masks[i & 1]) for i in range(count)])  17.4 us
    ppermute x15, waiting for transfers between devices, swapped(): lax.ppermute(array, AXES, [(i, i ^ masks[i & 1]) for i in range(count)])  7.37 us
    ppermute x2, starting transfers between devices, passed_round(): lax.ppermute(shard, axis, [(i, (i + by) % size) for i in range(size)])  2.6 us
    pallas_call x2, Pallas kernels, unpack(): pl.pallas_call(functools.partial(unpack_kernel, scale, offsets), out_shap...  2.14 us
    pallas_call x1, Pallas kernels, backward(): pl.pallas_call(functools.partial(backward_kernel, shape), out_shape=(jax....  1.29 us
    pallas_call x1, Pallas kernels, prepare(): pl.pallas_call(functools.partial(prepare_kernel, width), out_shape=(*(jax...  1.28 us
    ppermute x1, waiting for transfers between devices, passed_to_last_core(): return lax.ppermute(shard, AXES, pairs)  1.19 us
    pallas_call x1, Pallas kernels, forward(): pl.pallas_call(functools.partial(forward_kernel, shape), out_shape=(jax.S...  1.05 us
  transfers between devices with their start and end apart: 18, of which 7 were waited for; matrix products, arithmetic and copies ran while one was open for 0% of the time, Pallas kernels for 13%

profile of v9, /device:TPU:1, one launch (start us, length us, event | category | flops | bytes accessed | tf_op | source)
XLA Modules:
  0.0 36.0 jit_solution(1982725818918172643)
XLA Ops:
  0.6 0.1 collective-permute-start.2
  0.8 0.5 %collective-permute-start.3 = (bf16[256,128]{1,0:T(8,128)(2,1)}, bf16[256,128]{1,0:T(8,128)(2,1)S(1)}, u32[]{:S(2)}, u32[]{:S(2)}) collective-permute-start(bf16[256,128]{1,0:T(8,128)(2,1)} %bitcast.7), channel_id=1, source_target_pairs={{0,1},{1,0},{2,3},{3,2},{4,5},{5,4},{6,7},{7,6},{8,9},{9,8},{10,11... | collective-permute-start | bytes 196616 | tf_op jit(solution)/shard_map/ppermute | solution.py:40
  1.2 2.6 %collective-permute-start.1 = (bf16[256,128]{1,0:T(8,128)(2,1)}, bf16[256,128]{1,0:T(8,128)(2,1)S(1)}, u32[]{:S(2)}, u32[]{:S(2)}) collective-permute-start(bf16[256,128]{1,0:T(8,128)(2,1)} %bitcast.10), channel_id=1, source_target_pairs={{0,1},{1,2},{2,3},{3,0},{4,5},{5,6},{6,7},{7,4},{8,9},{9,10},{10,1... | collective-permute-start | bytes 196616 | tf_op jit(solution)/shard_map/ppermute | solution.py:21
  3.8 0.0 collective-permute-start
  3.8 1.3 %prepare.1 = (bf16[256,128]{1,0:T(8,128)(2,1)S(1)}, bf16[256,128]{1,0:T(8,128)(2,1)S(1)}, bf16[3,3,3,128,128]{4,3,2,1,0:T(8,128)(2,1)S(1)}, bf16[128,128]{1,0:T(8,128)(2,1)S(1)}, bf16[256,384]{1,0:T(8,128)(2,1)S(1)}) custom-call(bf16[256,128]{1,0:T(8,128)(2,1)} %bitcast.12, bf16[256,128]{1,0:T(8,128)(2,1)} %bitcast.8, bf16[3,3,3,128,128]{4,3,2,1,0:T(8,128)(2,1)} %kern_hbm.1, ...), custom_call_target="tpu_custom_call" | custom-call | flops 32768 | bytes 2097152 | tf_op jit(solution)/shard_map/prepare/pallas_call | solution.py:343
  5.1 0.0 collective-permute-done.2.partner_ref
  5.1 0.0 collective-permute-done.3.partner_grads_ref
  5.1 0.8 %join.1 = (bf16[768,384]{1,0:T(8,128)(2,1)S(1)}, bf16[512,128]{1,0:T(8,128)(2,1)S(1)}, f32[512,384]{1,0:T(8,128)S(1)}, f32[512,128]{1,0:T(8,128)S(1)}) custom-call(s32[1]{0:T(128)} %bitcast.where_ref, bf16[256,384]{1,0:T(8,128)(2,1)S(1)} %get-tuple-element.28.own_ref, bf16[256,128]{1,0:T(8,128)(2,1)S(1)} %get-tuple-element.29.grads_ref, ...), custom_call_target="tpu_custom_call" | custom-call | flops 335544320 | bytes 2097152 | tf_op jit(solution)/shard_map/join/pallas_call | solution.py:362
  5.9 0.0 collective-permute-done.1.first_halo_ref
  5.9 1.2 %collective-permute-done.second_halo_ref = bf16[256,128]{1,0:T(8,128)(2,1)S(1)} collective-permute-done((bf16[256,128]{1,0:T(8,128)(2,1)}, bf16[256,128]{1,0:T(8,128)(2,1)S(1)}, u32[]{:S(2)}, u32[]{:S(2)}) %collective-permute-start) | collective-permute-done | bytes 65568 | tf_op jit(solution)/shard_map/ppermute | solution.py:31
  7.1 1.1 %forward.1 = (f32[4,14,32,128]{3,2,1,0:T(8,128)S(1)}, bf16[4,14,32,128]{3,2,1,0:T(8,128)(2,1)S(1)}, bf16[256,128]{1,0:T(8,128)(2,1)S(1)}, bf16[256,128]{1,0:T(8,128)(2,1)S(1)}, bf16[768,384]{1,0:T(8,128)(2,1)S(1)}) custom-call(s32[1]{0:T(128)} %bitcast.where_ref, ...), custom_call_target="tpu_custom_call", output_to_operand_aliasing={{4}: (5, {})} | custom-call | tf_op jit(solution)/shard_map/forward/pallas_call | solution.py:384
  8.2 3.4 %collective-permute-start.4 = (bf16[1,14,32,128]{3,2,1,0:T(8,128)(2,1)S(1)}, bf16[1,14,32,128]{3,2,1,0:T(8,128)(2,1)S(1)}, u32[]{:S(2)}, u32[]{:S(2)}) collective-permute-start(bf16[1,14,32,128]{3,2,1,0:T(8,128)(2,1)S(1)} %get-tuple-element.52), channel_id=1, source_target_pairs={{0,6},{1,25},{2,4},{3,27},{4,2},{5,29},{6,0},{7,31},{8,14},{9,17},... | collective-permute-start | bytes 344072 | tf_op jit(solution)/shard_map/ppermute | solution.py:40
  11.6 0.0 collective-permute-start.6
  11.6 0.4 collective-permute-start.5
  12.0 0.0 collective-permute-start.7
  12.0 1.9 %collective-permute-done.4 = bf16[1,14,32,128]{3,2,1,0:T(8,128)(2,1)S(1)} collective-permute-done((bf16[1,14,32,128]{3,2,1,0:T(8,128)(2,1)S(1)}, bf16[1,14,32,128]{3,2,1,0:T(8,128)(2,1)S(1)}, u32[]{:S(2)}, u32[]{:S(2)}) %collective-permute-start.4) | collective-permute-done | bytes 114720 | tf_op jit(solution)/shard_map/ppermute | solution.py:40
  13.9 2.7 %collective-permute-done.6 = bf16[1,14,32,128]{3,2,1,0:T(8,128)(2,1)S(1)} collective-permute-done((bf16[1,14,32,128]{3,2,1,0:T(8,128)(2,1)S(1)}, bf16[1,14,32,128]{3,2,1,0:T(8,128)(2,1)S(1)}, u32[]{:S(2)}, u32[]{:S(2)}) %collective-permute-start.6) | collective-permute-done | bytes 114720 | tf_op jit(solution)/shard_map/ppermute | solution.py:40
  16.6 0.0 collective-permute-done.5
  16.6 0.1 convert_add_fusion
  16.7 0.0 collective-permute-done.7.next_ref
  16.7 2.0 %collective-permute-start.10 = (bf16[1,14,32,128]{3,2,1,0:T(8,128)(2,1)S(1)}, bf16[1,14,32,128]{3,2,1,0:T(8,128)(2,1)S(1)}, u32[]{:S(2)}, u32[]{:S(2)}) collective-permute-start(bf16[1,14,32,128]{3,2,1,0:T(8,128)(2,1)S(1)} %reduce-precision_convert_fusion), channel_id=1, source_target_pairs={{0,24},{1,7},{2,26},{3,5},{4,28},{5,3},{6,30},{7,1},{8,16},{9,15},... | collective-permute-start | bytes 344072 | tf_op jit(solution)/shard_map/ppermute | solution.py:40
  18.7 0.5 %collective-permute-start.9 = (bf16[1,14,32,128]{3,2,1,0:T(8,128)(2,1)S(1)}, bf16[1,14,32,128]{3,2,1,0:T(8,128)(2,1)S(1)}, u32[]{:S(2)}, u32[]{:S(2)}) collective-permute-start(bf16[1,14,32,128]{3,2,1,0:T(8,128)(2,1)S(1)} %reduce-precision_convert_fusion), channel_id=1, source_target_pairs={{0,8},{1,3},{2,10},{3,1},{4,12},{5,7},{6,14},{7,5},{8,0},{9,11},{1... | collective-permute-start | bytes 344072 | tf_op jit(solution)/shard_map/ppermute | solution.py:40
  19.2 0.2 collective-permute-start.8
  19.4 1.3 %backward.1 = (bf16[256,128]{1,0:T(8,128)(2,1)}, bf16[256,128]{1,0:T(8,128)(2,1)}) custom-call(s32[1]{0:T(128)} %bitcast.where_ref, bf16[256,128]{1,0:T(8,128)(2,1)S(1)} %get-tuple-element.38.pre_grad_ref, bf16[256,128]{1,0:T(8,128)(2,1)S(1)} %collective-permute-done.7.next_ref, bf16[256,128]{1,0:T(8,128)(2,1)S(1)} %get-tuple-element.41.hidden_ref, ...), custom_call_target="tpu_custom_call" | custom-call | flops 234881024 | bytes 1048576 | tf_op jit(solution)/shard_map/backward/pallas_call | solution.py:405
  20.7 0.9 %collective-permute-done.10 = bf16[1,14,32,128]{3,2,1,0:T(8,128)(2,1)S(1)} collective-permute-done((bf16[1,14,32,128]{3,2,1,0:T(8,128)(2,1)S(1)}, bf16[1,14,32,128]{3,2,1,0:T(8,128)(2,1)S(1)}, u32[]{:S(2)}, u32[]{:S(2)}) %collective-permute-start.10) | collective-permute-done | bytes 114720 | tf_op jit(solution)/shard_map/ppermute | solution.py:40
  21.6 1.0 %collective-permute-done.9 = bf16[1,14,32,128]{3,2,1,0:T(8,128)(2,1)S(1)} collective-permute-done((bf16[1,14,32,128]{3,2,1,0:T(8,128)(2,1)S(1)}, bf16[1,14,32,128]{3,2,1,0:T(8,128)(2,1)S(1)}, u32[]{:S(2)}, u32[]{:S(2)}) %collective-permute-start.9) | collective-permute-done | bytes 114720 | tf_op jit(solution)/shard_map/ppermute | solution.py:40
  22.6 0.5 %collective-permute-done.8 = bf16[1,14,32,128]{3,2,1,0:T(8,128)(2,1)S(1)} collective-permute-done((bf16[1,14,32,128]{3,2,1,0:T(8,128)(2,1)S(1)}, bf16[1,14,32,128]{3,2,1,0:T(8,128)(2,1)S(1)}, u32[]{:S(2)}, u32[]{:S(2)}) %collective-permute-start.8) | collective-permute-done | bytes 114720 | tf_op jit(solution)/shard_map/ppermute | solution.py:40
  23.2 0.1 add_convert_fusion.refs_0_
  23.2 1.2 %collective-permute-start.16 = (bf16[1,14,32,128]{3,2,1,0:T(8,128)(2,1)S(1)}, bf16[1,14,32,128]{3,2,1,0:T(8,128)(2,1)S(1)}, u32[]{:S(2)}, u32[]{:S(2)}) collective-permute-start(bf16[1,14,32,128]{3,2,1,0:T(8,128)(2,1)S(1)} %add_convert_fusion.refs_0_), channel_id=1, source_target_pairs={{0,2},{1,9},{2,0},{3,11},{4,6},{5,13},{6,4},{7,15},{8,10},{9,1},{1... | collective-permute-start | bytes 344072 | tf_op jit(solution)/shard_map/ppermute | solution.py:40
  24.4 2.0 %collective-permute-start.14 = (bf16[1,14,32,128]{3,2,1,0:T(8,128)(2,1)S(1)}, bf16[1,14,32,128]{3,2,1,0:T(8,128)(2,1)S(1)}, u32[]{:S(2)}, u32[]{:S(2)}) collective-permute-start(bf16[1,14,32,128]{3,2,1,0:T(8,128)(2,1)S(1)} %add_convert_fusion.refs_0_), channel_id=1, source_target_pairs={{0,4},{1,17},{2,6},{3,19},{4,0},{5,21},{6,2},{7,23},{8,12},{9,25},... | collective-permute-start | bytes 344072 | tf_op jit(solution)/shard_map/ppermute | solution.py:40
  26.4 0.4 %collective-permute-start.11 = (bf16[1,14,32,128]{3,2,1,0:T(8,128)(2,1)S(1)}, bf16[1,14,32,128]{3,2,1,0:T(8,128)(2,1)S(1)}, u32[]{:S(2)}, u32[]{:S(2)}) collective-permute-start(bf16[1,14,32,128]{3,2,1,0:T(8,128)(2,1)S(1)} %add_convert_fusion.refs_0_), channel_id=1, source_target_pairs={{0,6},{1,25},{2,4},{3,27},{4,2},{5,29},{6,0},{7,31},{8,14},{9,17},... | collective-permute-start | bytes 344072 | tf_op jit(solution)/shard_map/ppermute | solution.py:40
  26.8 2.8 %collective-permute-start.13 = (bf16[1,14,32,128]{3,2,1,0:T(8,128)(2,1)S(1)}, bf16[1,14,32,128]{3,2,1,0:T(8,128)(2,1)S(1)}, u32[]{:S(2)}, u32[]{:S(2)}) collective-permute-start(bf16[1,14,32,128]{3,2,1,0:T(8,128)(2,1)S(1)} %add_convert_fusion.refs_0_), channel_id=1, source_target_pairs={{0,1},{1,0},{2,3},{3,2},{4,5},{5,4},{6,7},{7,6},{8,9},{9,8},{10,11... | collective-permute-start | bytes 344072 | tf_op jit(solution)/shard_map/ppermute | solution.py:40
  29.6 0.0 collective-permute-done.16.refs_4_
  29.6 1.3 %collective-permute-start.17 = (bf16[1,14,32,128]{3,2,1,0:T(8,128)(2,1)S(1)}, bf16[1,14,32,128]{3,2,1,0:T(8,128)(2,1)S(1)}, u32[]{:S(2)}, u32[]{:S(2)}) collective-permute-start(bf16[1,14,32,128]{3,2,1,0:T(8,128)(2,1)S(1)} %collective-permute-done.16.refs_4_), channel_id=1, source_target_pairs={{0,1},{1,0},{2,3},{3,2},{4,5},{5,4},{6,7},{7,6},{8,9},{9,8},{10,11... | collective-permute-start | bytes 344072 | tf_op jit(solution)/shard_map/ppermute | solution.py:40
  30.9 0.0 collective-permute-done.14.refs_2_
  30.9 0.8 %collective-permute-start.15 = (bf16[1,14,32,128]{3,2,1,0:T(8,128)(2,1)S(1)}, bf16[1,14,32,128]{3,2,1,0:T(8,128)(2,1)S(1)}, u32[]{:S(2)}, u32[]{:S(2)}) collective-permute-start(bf16[1,14,32,128]{3,2,1,0:T(8,128)(2,1)S(1)} %collective-permute-done.14.refs_2_), channel_id=1, source_target_pairs={{0,1},{1,0},{2,3},{3,2},{4,5},{5,4},{6,7},{7,6},{8,9},{9,8},{10,11... | collective-permute-start | bytes 344072 | tf_op jit(solution)/shard_map/ppermute | solution.py:40
  31.7 0.3 collective-permute-done.11.refs_0_
  31.9 1.9 %collective-permute-start.12 = (bf16[1,14,32,128]{3,2,1,0:T(8,128)(2,1)S(1)}, bf16[1,14,32,128]{3,2,1,0:T(8,128)(2,1)S(1)}, u32[]{:S(2)}, u32[]{:S(2)}) collective-permute-start(bf16[1,14,32,128]{3,2,1,0:T(8,128)(2,1)S(1)} %collective-permute-done.11.refs_0_), channel_id=1, source_target_pairs={{0,1},{1,0},{2,3},{3,2},{4,5},{5,4},{6,7},{7,6},{8,9},{9,8},{10,11... | collective-permute-start | bytes 344072 | tf_op jit(solution)/shard_map/ppermute | solution.py:40
  33.8 0.0 collective-permute-done.13.refs_1_
  33.8 0.0 collective-permute-done.17.refs_5_
  33.9 0.0 collective-permute-done.15.refs_3_
  33.9 1.3 %unpack.2 = (f32[27,128,128]{2,1,0:T(8,128)}, f32[128,128]{1,0:T(8,128)}) custom-call(s32[1]{0:T(128)} %bitcast.where_ref, bf16[1,14,32,128]{3,2,1,0:T(8,128)(2,1)S(1)} %add_convert_fusion.refs_0_, bf16[1,14,32,128]{3,2,1,0:T(8,128)(2,1)S(1)} %collective-permute-done.13.refs_1_, bf16[1,14,32,128]{3,2,1,0:T(8,128)(2,1)S(1)} %collective-permute-done.14.refs_2_, ...), custom_call_target="tpu_custom_call" | custom-call | flops 344064 | bytes 2064384 | tf_op jit(solution)/shard_map/unpack/pallas_call | solution.py:289
  35.2 0.0 collective-permute-done.12.refs_1_
  35.2 0.9 %unpack.3 = (f32[27,128,128]{2,1,0:T(8,128)}, f32[128,128]{1,0:T(8,128)}) custom-call(s32[1]{0:T(128)} %bitcast.where_ref, bf16[1,14,32,128]{3,2,1,0:T(8,128)(2,1)S(1)} %collective-permute-done.11.refs_0_, bf16[1,14,32,128]{3,2,1,0:T(8,128)(2,1)S(1)} %collective-permute-done.12.refs_1_, ...), custom_call_target="tpu_custom_call", output_to_operand_aliasing={{0}: (3, {}), {1}: (4, {})} | custom-call | flops 114688 | bytes 688128 | tf_op jit(solution)/shard_map/unpack/pallas_call | solution.py:289
  (2 shorter events, 0.0 us)
Async XLA Ops:
  0.6 4.5 %collective-permute-start.2 = (bf16[256,128]{1,0:T(8,128)(2,1)}, bf16[256,128]{1,0:T(8,128)(2,1)S(1)}, u32[]{:S(2)}, u32[]{:S(2)}) collective-permute-start(bf16[256,128]{1,0:T(8,128)(2,1)} %bitcast.9), channel_id=1, source_target_pairs={{0,1},{1,0},{2,3},{3,2},{4,5},{5,4},{6,7},{7,6},{8,9},{9,8},{10,11... | collective-permute-start | bytes 196616 | tf_op jit(solution)/shard_map/ppermute | solution.py:40
  0.8 4.4 %collective-permute-start.3 = (bf16[256,128]{1,0:T(8,128)(2,1)}, bf16[256,128]{1,0:T(8,128)(2,1)S(1)}, u32[]{:S(2)}, u32[]{:S(2)}) collective-permute-start(bf16[256,128]{1,0:T(8,128)(2,1)} %bitcast.7), channel_id=1, source_target_pairs={{0,1},{1,0},{2,3},{3,2},{4,5},{5,4},{6,7},{7,6},{8,9},{9,8},{10,11... | collective-permute-start | bytes 196616 | tf_op jit(solution)/shard_map/ppermute | solution.py:40
  1.2 4.7 %collective-permute-start.1 = (bf16[256,128]{1,0:T(8,128)(2,1)}, bf16[256,128]{1,0:T(8,128)(2,1)S(1)}, u32[]{:S(2)}, u32[]{:S(2)}) collective-permute-start(bf16[256,128]{1,0:T(8,128)(2,1)} %bitcast.10), channel_id=1, source_target_pairs={{0,1},{1,2},{2,3},{3,0},{4,5},{5,6},{6,7},{7,4},{8,9},{9,10},{10,1... | collective-permute-start | bytes 196616 | tf_op jit(solution)/shard_map/ppermute | solution.py:21
  3.8 3.3 %collective-permute-start = (bf16[256,128]{1,0:T(8,128)(2,1)}, bf16[256,128]{1,0:T(8,128)(2,1)S(1)}, u32[]{:S(2)}, u32[]{:S(2)}) collective-permute-start(bf16[256,128]{1,0:T(8,128)(2,1)} %bitcast.11), channel_id=1, source_target_pairs={{0,4},{1,3},{2,6},{3,1},{4,0},{5,7},{6,2},{7,5},{8,12},{9,11},{10,... | collective-permute-start | bytes 196616 | tf_op jit(solution)/shard_map/ppermute | solution.py:31
  8.2 5.7 %collective-permute-start.4 = (bf16[1,14,32,128]{3,2,1,0:T(8,128)(2,1)S(1)}, bf16[1,14,32,128]{3,2,1,0:T(8,128)(2,1)S(1)}, u32[]{:S(2)}, u32[]{:S(2)}) collective-permute-start(bf16[1,14,32,128]{3,2,1,0:T(8,128)(2,1)S(1)} %get-tuple-element.52), channel_id=1, source_target_pairs={{0,6},{1,25},{2,4},{3,27},{4,2},{5,29},{6,0},{7,31},{8,14},{9,17},... | collective-permute-start | bytes 344072 | tf_op jit(solution)/shard_map/ppermute | solution.py:40
  11.6 5.0 %collective-permute-start.6 = (bf16[1,14,32,128]{3,2,1,0:T(8,128)(2,1)S(1)}, bf16[1,14,32,128]{3,2,1,0:T(8,128)(2,1)S(1)}, u32[]{:S(2)}, u32[]{:S(2)}) collective-permute-start(bf16[1,14,32,128]{3,2,1,0:T(8,128)(2,1)S(1)} %get-tuple-element.53), channel_id=1, source_target_pairs={{0,4},{1,17},{2,6},{3,19},{4,0},{5,21},{6,2},{7,23},{8,12},{9,25},... | collective-permute-start | bytes 344072 | tf_op jit(solution)/shard_map/ppermute | solution.py:40
  11.6 5.0 %collective-permute-start.5 = (bf16[1,14,32,128]{3,2,1,0:T(8,128)(2,1)S(1)}, bf16[1,14,32,128]{3,2,1,0:T(8,128)(2,1)S(1)}, u32[]{:S(2)}, u32[]{:S(2)}) collective-permute-start(bf16[1,14,32,128]{3,2,1,0:T(8,128)(2,1)S(1)} %get-tuple-element.54), channel_id=1, source_target_pairs={{0,2},{1,9},{2,0},{3,11},{4,6},{5,13},{6,4},{7,15},{8,10},{9,1},{1... | collective-permute-start | bytes 344072 | tf_op jit(solution)/shard_map/ppermute | solution.py:40
  12.0 4.7 %collective-permute-start.7 = (bf16[256,128]{1,0:T(8,128)(2,1)S(1)}, bf16[256,128]{1,0:T(8,128)(2,1)S(1)}, u32[]{:S(2)}, u32[]{:S(2)}) collective-permute-start(bf16[256,128]{1,0:T(8,128)(2,1)S(1)} %get-tuple-element.38.pre_grad_ref), channel_id=1, source_target_pairs={{0,3},{1,0},{2,1},{3,2},{4,7},{5,4},{6,5},{7,6},{8,11},{9,8},{10,9... | collective-permute-start | bytes 196616 | tf_op jit(solution)/shard_map/ppermute | solution.py:21
  16.7 4.9 %collective-permute-start.10 = (bf16[1,14,32,128]{3,2,1,0:T(8,128)(2,1)S(1)}, bf16[1,14,32,128]{3,2,1,0:T(8,128)(2,1)S(1)}, u32[]{:S(2)}, u32[]{:S(2)}) collective-permute-start(bf16[1,14,32,128]{3,2,1,0:T(8,128)(2,1)S(1)} %reduce-precision_convert_fusion), channel_id=1, source_target_pairs={{0,24},{1,7},{2,26},{3,5},{4,28},{5,3},{6,30},{7,1},{8,16},{9,15},... | collective-permute-start | bytes 344072 | tf_op jit(solution)/shard_map/ppermute | solution.py:40
  18.7 3.9 %collective-permute-start.9 = (bf16[1,14,32,128]{3,2,1,0:T(8,128)(2,1)S(1)}, bf16[1,14,32,128]{3,2,1,0:T(8,128)(2,1)S(1)}, u32[]{:S(2)}, u32[]{:S(2)}) collective-permute-start(bf16[1,14,32,128]{3,2,1,0:T(8,128)(2,1)S(1)} %reduce-precision_convert_fusion), channel_id=1, source_target_pairs={{0,8},{1,3},{2,10},{3,1},{4,12},{5,7},{6,14},{7,5},{8,0},{9,11},{1... | collective-permute-start | bytes 344072 | tf_op jit(solution)/shard_map/ppermute | solution.py:40
  19.2 3.9 %collective-permute-start.8 = (bf16[1,14,32,128]{3,2,1,0:T(8,128)(2,1)S(1)}, bf16[1,14,32,128]{3,2,1,0:T(8,128)(2,1)S(1)}, u32[]{:S(2)}, u32[]{:S(2)}) collective-permute-start(bf16[1,14,32,128]{3,2,1,0:T(8,128)(2,1)S(1)} %reduce-precision_convert_fusion), channel_id=1, source_target_pairs={{0,16},{1,5},{2,18},{3,7},{4,20},{5,1},{6,22},{7,3},{8,24},{9,13},... | collective-permute-start | bytes 344072 | tf_op jit(solution)/shard_map/ppermute | solution.py:40
  23.2 6.4 %collective-permute-start.16 = (bf16[1,14,32,128]{3,2,1,0:T(8,128)(2,1)S(1)}, bf16[1,14,32,128]{3,2,1,0:T(8,128)(2,1)S(1)}, u32[]{:S(2)}, u32[]{:S(2)}) collective-permute-start(bf16[1,14,32,128]{3,2,1,0:T(8,128)(2,1)S(1)} %add_convert_fusion.refs_0_), channel_id=1, source_target_pairs={{0,2},{1,9},{2,0},{3,11},{4,6},{5,13},{6,4},{7,15},{8,10},{9,1},{1... | collective-permute-start | bytes 344072 | tf_op jit(solution)/shard_map/ppermute | solution.py:40
  24.4 6.5 %collective-permute-start.14 = (bf16[1,14,32,128]{3,2,1,0:T(8,128)(2,1)S(1)}, bf16[1,14,32,128]{3,2,1,0:T(8,128)(2,1)S(1)}, u32[]{:S(2)}, u32[]{:S(2)}) collective-permute-start(bf16[1,14,32,128]{3,2,1,0:T(8,128)(2,1)S(1)} %add_convert_fusion.refs_0_), channel_id=1, source_target_pairs={{0,4},{1,17},{2,6},{3,19},{4,0},{5,21},{6,2},{7,23},{8,12},{9,25},... | collective-permute-start | bytes 344072 | tf_op jit(solution)/shard_map/ppermute | solution.py:40
  26.4 5.5 %collective-permute-start.11 = (bf16[1,14,32,128]{3,2,1,0:T(8,128)(2,1)S(1)}, bf16[1,14,32,128]{3,2,1,0:T(8,128)(2,1)S(1)}, u32[]{:S(2)}, u32[]{:S(2)}) collective-permute-start(bf16[1,14,32,128]{3,2,1,0:T(8,128)(2,1)S(1)} %add_convert_fusion.refs_0_), channel_id=1, source_target_pairs={{0,6},{1,25},{2,4},{3,27},{4,2},{5,29},{6,0},{7,31},{8,14},{9,17},... | collective-permute-start | bytes 344072 | tf_op jit(solution)/shard_map/ppermute | solution.py:40
  26.8 7.0 %collective-permute-start.13 = (bf16[1,14,32,128]{3,2,1,0:T(8,128)(2,1)S(1)}, bf16[1,14,32,128]{3,2,1,0:T(8,128)(2,1)S(1)}, u32[]{:S(2)}, u32[]{:S(2)}) collective-permute-start(bf16[1,14,32,128]{3,2,1,0:T(8,128)(2,1)S(1)} %add_convert_fusion.refs_0_), channel_id=1, source_target_pairs={{0,1},{1,0},{2,3},{3,2},{4,5},{5,4},{6,7},{7,6},{8,9},{9,8},{10,11... | collective-permute-start | bytes 344072 | tf_op jit(solution)/shard_map/ppermute | solution.py:40
  29.6 4.2 %collective-permute-start.17 = (bf16[1,14,32,128]{3,2,1,0:T(8,128)(2,1)S(1)}, bf16[1,14,32,128]{3,2,1,0:T(8,128)(2,1)S(1)}, u32[]{:S(2)}, u32[]{:S(2)}) collective-permute-start(bf16[1,14,32,128]{3,2,1,0:T(8,128)(2,1)S(1)} %collective-permute-done.16.refs_4_), channel_id=1, source_target_pairs={{0,1},{1,0},{2,3},{3,2},{4,5},{5,4},{6,7},{7,6},{8,9},{9,8},{10,11... | collective-permute-start | bytes 344072 | tf_op jit(solution)/shard_map/ppermute | solution.py:40
  30.9 2.9 %collective-permute-start.15 = (bf16[1,14,32,128]{3,2,1,0:T(8,128)(2,1)S(1)}, bf16[1,14,32,128]{3,2,1,0:T(8,128)(2,1)S(1)}, u32[]{:S(2)}, u32[]{:S(2)}) collective-permute-start(bf16[1,14,32,128]{3,2,1,0:T(8,128)(2,1)S(1)} %collective-permute-done.14.refs_2_), channel_id=1, source_target_pairs={{0,1},{1,0},{2,3},{3,2},{4,5},{5,4},{6,7},{7,6},{8,9},{9,8},{10,11... | collective-permute-start | bytes 344072 | tf_op jit(solution)/shard_map/ppermute | solution.py:40
  31.9 3.2 %collective-permute-start.12 = (bf16[1,14,32,128]{3,2,1,0:T(8,128)(2,1)S(1)}, bf16[1,14,32,128]{3,2,1,0:T(8,128)(2,1)S(1)}, u32[]{:S(2)}, u32[]{:S(2)}) collective-permute-start(bf16[1,14,32,128]{3,2,1,0:T(8,128)(2,1)S(1)} %collective-permute-done.11.refs_0_), channel_id=1, source_target_pairs={{0,1},{1,0},{2,3},{3,2},{4,5},{5,4},{6,7},{7,6},{8,9},{9,8},{10,11... | collective-permute-start | bytes 344072 | tf_op jit(solution)/shard_map/ppermute | solution.py:40

commit v10 on v9

--- a/solution.py
+++ b/solution.py
@@ -309,13 +309,13 @@
     )(where, *given, *sofar)
 
 
-def summed(where, keep, send, scale, beside_split, beside_exchange):
+def summed(where, keep, send, scale, pre_grad, start_next, finish):
     total = keep[:1]
     for offset in (3, 2, 1):
         piece = swapped(send[offset : offset + 1], masks_of(0, offset))
         total = total + piece.astype(jnp.float32)
-    done = beside_split()
-    total, done = lax.optimization_barrier((total, done))
+    total, pre_grad = lax.optimization_barrier((total, pre_grad))
+    next_halo = start_next(pre_grad)
     total = lax.reduce_precision(total, 8, 7)
     third, second, first = (
         swapped(total.astype(jnp.bfloat16), masks_of(1, offset)).astype(jnp.float32)
@@ -327,10 +327,11 @@
     while mask < count:
         total = total + swapped(total, (mask, mask))
         mask *= 2
-    done = beside_exchange(done)
     total = total.astype(jnp.bfloat16)
-    total, done = lax.optimization_barrier((total, done))
+    total, next_halo = lax.optimization_barrier((total, next_halo))
     mine = [total] + [swapped(total, masks_of(0, offset)) for offset in (1, 2, 3)]
+    done = finish(pre_grad, next_halo)
+    mine[1], done = lax.optimization_barrier((mine[1], done))
     pieces = [(piece, swapped(piece, (1, 1))) for piece in mine[:3]]
     sofar = unpack(where, pieces, (0, 1, 2), scale)
     pieces.append((mine[3], swapped(mine[3], (1, 1))))
@@ -445,9 +446,10 @@
         keep,
         send,
         1.0 / math.sqrt(total_pixels),
-        lambda: passed_round(pre_grad[:halo_rows], "tm", -1),
-        lambda following: backward(
-            shape, where, pre_grad, following, hidden, frames, grads, conv_kernel, proj_weight
+        pre_grad,
+        lambda grads_here: passed_round(grads_here[:halo_rows], "tm", -1),
+        lambda grads_here, following: backward(
+            shape, where, grads_here, following, hidden, frames, grads, conv_kernel, proj_weight
         ),
     )
     return (

time: 36.2 us -> 36.2 us (level)
    ppermute x15, starting transfers between devices: 17.4 us -> 16 us  [swapped(): lax.ppermute(array, AXES, [(i, i ^ masks[i & 1]) for i in range(count)])]
    ppermute x2, starting transfers between devices: 2.6 us -> 3.9 us  [passed_round(): lax.ppermute(shard, axis, [(i, (i + by) % size) for i in range(size)])]
    ppermute x2, waiting for transfers between devices: 0.01 us -> 0.4 us  [passed_round(): lax.ppermute(shard, axis, [(i, (i + by) % size) for i in range(size)])]
where the time goes in v10:
time: 36.2 us; the launch traced here: 36 us
  starting transfers between devices  19.9 us (55%)
  waiting for transfers between devices  8.68 us (24%)
  Pallas kernels  6.56 us (18%)
  between operations  0.75 us (2%)
    ppermute x15, starting transfers between devices, swapped(): lax.ppermute(array, AXES, [(i, i ^ masks[i & 1]) for i in range(count)])  16 us
    ppermute x15, waiting for transfers between devices, swapped(): lax.ppermute(array, AXES, [(i, i ^ masks[i & 1]) for i in range(count)])  7.09 us
    ppermute x2, starting transfers between devices, passed_round(): lax.ppermute(shard, axis, [(i, (i + by) % size) for i in range(size)])  3.9 us
    pallas_call x2, Pallas kernels, unpack(): pl.pallas_call(functools.partial(unpack_kernel, scale, offsets), out_shap...  2.14 us
    pallas_call x1, Pallas kernels, backward(): pl.pallas_call(functools.partial(backward_kernel, shape), out_shape=(jax....  1.29 us
    pallas_call x1, Pallas kernels, prepare(): pl.pallas_call(functools.partial(prepare_kernel, width), out_shape=(*(jax...  1.28 us
    ppermute x1, waiting for transfers between devices, passed_to_last_core(): return lax.ppermute(shard, AXES, pairs)  1.19 us
    pallas_call x1, Pallas kernels, forward(): pl.pallas_call(functools.partial(forward_kernel, shape), out_shape=(jax.S...  1.05 us
  transfers between devices with their start and end apart: 18, of which 7 were waited for; matrix products, arithmetic and copies ran while one was open for 0% of the time, Pallas kernels for 13%

profile of v10, /device:TPU:1, one launch (start us, length us, event | category | flops | bytes accessed | tf_op | source)
XLA Modules:
  0.0 36.0 jit_solution(5367232217182348275)
XLA Ops:
  0.6 0.1 collective-permute-start.2
  0.8 0.5 %collective-permute-start.3 = (bf16[256,128]{1,0:T(8,128)(2,1)}, bf16[256,128]{1,0:T(8,128)(2,1)S(1)}, u32[]{:S(2)}, u32[]{:S(2)}) collective-permute-start(bf16[256,128]{1,0:T(8,128)(2,1)} %bitcast.7), channel_id=1, source_target_pairs={{0,1},{1,0},{2,3},{3,2},{4,5},{5,4},{6,7},{7,6},{8,9},{9,8},{10,11... | collective-permute-start | bytes 196616 | tf_op jit(solution)/shard_map/ppermute | solution.py:40
  1.2 2.6 %collective-permute-start.1 = (bf16[256,128]{1,0:T(8,128)(2,1)}, bf16[256,128]{1,0:T(8,128)(2,1)S(1)}, u32[]{:S(2)}, u32[]{:S(2)}) collective-permute-start(bf16[256,128]{1,0:T(8,128)(2,1)} %bitcast.10), channel_id=1, source_target_pairs={{0,1},{1,2},{2,3},{3,0},{4,5},{5,6},{6,7},{7,4},{8,9},{9,10},{10,1... | collective-permute-start | bytes 196616 | tf_op jit(solution)/shard_map/ppermute | solution.py:21
  3.8 0.0 collective-permute-start
  3.8 1.3 %prepare.1 = (bf16[256,128]{1,0:T(8,128)(2,1)S(1)}, bf16[256,128]{1,0:T(8,128)(2,1)S(1)}, bf16[3,3,3,128,128]{4,3,2,1,0:T(8,128)(2,1)S(1)}, bf16[128,128]{1,0:T(8,128)(2,1)S(1)}, bf16[256,384]{1,0:T(8,128)(2,1)S(1)}) custom-call(bf16[256,128]{1,0:T(8,128)(2,1)} %bitcast.12, bf16[256,128]{1,0:T(8,128)(2,1)} %bitcast.8, bf16[3,3,3,128,128]{4,3,2,1,0:T(8,128)(2,1)} %kern_hbm.1, ...), custom_call_target="tpu_custom_call" | custom-call | flops 32768 | bytes 2097152 | tf_op jit(solution)/shard_map/prepare/pallas_call | solution.py:344
  5.1 0.0 collective-permute-done.2.partner_ref
  5.1 0.0 collective-permute-done.3.partner_grads_ref
  5.1 0.8 %join.1 = (bf16[768,384]{1,0:T(8,128)(2,1)S(1)}, bf16[512,128]{1,0:T(8,128)(2,1)S(1)}, f32[512,384]{1,0:T(8,128)S(1)}, f32[512,128]{1,0:T(8,128)S(1)}) custom-call(s32[1]{0:T(128)} %bitcast.where_ref, bf16[256,384]{1,0:T(8,128)(2,1)S(1)} %get-tuple-element.30.own_ref, bf16[256,128]{1,0:T(8,128)(2,1)S(1)} %get-tuple-element.31.grads_ref, ...), custom_call_target="tpu_custom_call" | custom-call | flops 335544320 | bytes 2097152 | tf_op jit(solution)/shard_map/join/pallas_call | solution.py:363
  5.9 0.0 collective-permute-done.1.first_halo_ref
  5.9 1.2 %collective-permute-done.second_halo_ref = bf16[256,128]{1,0:T(8,128)(2,1)S(1)} collective-permute-done((bf16[256,128]{1,0:T(8,128)(2,1)}, bf16[256,128]{1,0:T(8,128)(2,1)S(1)}, u32[]{:S(2)}, u32[]{:S(2)}) %collective-permute-start) | collective-permute-done | bytes 65568 | tf_op jit(solution)/shard_map/ppermute | solution.py:31
  7.1 1.1 %forward.1 = (f32[4,14,32,128]{3,2,1,0:T(8,128)S(1)}, bf16[4,14,32,128]{3,2,1,0:T(8,128)(2,1)S(1)}, bf16[256,128]{1,0:T(8,128)(2,1)S(1)}, bf16[256,128]{1,0:T(8,128)(2,1)S(1)}, bf16[768,384]{1,0:T(8,128)(2,1)S(1)}) custom-call(s32[1]{0:T(128)} %bitcast.where_ref, ...), custom_call_target="tpu_custom_call", output_to_operand_aliasing={{4}: (5, {})} | custom-call | tf_op jit(solution)/shard_map/forward/pallas_call | solution.py:385
  8.2 3.4 %collective-permute-start.4 = (bf16[1,14,32,128]{3,2,1,0:T(8,128)(2,1)S(1)}, bf16[1,14,32,128]{3,2,1,0:T(8,128)(2,1)S(1)}, u32[]{:S(2)}, u32[]{:S(2)}) collective-permute-start(bf16[1,14,32,128]{3,2,1,0:T(8,128)(2,1)S(1)} %get-tuple-element.56), channel_id=1, source_target_pairs={{0,6},{1,25},{2,4},{3,27},{4,2},{5,29},{6,0},{7,31},{8,14},{9,17},... | collective-permute-start | bytes 344072 | tf_op jit(solution)/shard_map/ppermute | solution.py:40
  11.6 0.0 collective-permute-start.6
  11.6 0.4 collective-permute-start.5
  12.0 1.9 %collective-permute-done.4 = bf16[1,14,32,128]{3,2,1,0:T(8,128)(2,1)S(1)} collective-permute-done((bf16[1,14,32,128]{3,2,1,0:T(8,128)(2,1)S(1)}, bf16[1,14,32,128]{3,2,1,0:T(8,128)(2,1)S(1)}, u32[]{:S(2)}, u32[]{:S(2)}) %collective-permute-start.4) | collective-permute-done | bytes 114720 | tf_op jit(solution)/shard_map/ppermute | solution.py:40
  13.9 2.7 %collective-permute-done.6 = bf16[1,14,32,128]{3,2,1,0:T(8,128)(2,1)S(1)} collective-permute-done((bf16[1,14,32,128]{3,2,1,0:T(8,128)(2,1)S(1)}, bf16[1,14,32,128]{3,2,1,0:T(8,128)(2,1)S(1)}, u32[]{:S(2)}, u32[]{:S(2)}) %collective-permute-start.6) | collective-permute-done | bytes 114720 | tf_op jit(solution)/shard_map/ppermute | solution.py:40
  16.6 0.0 collective-permute-done.5
  16.6 0.1 convert_add_fusion
  16.7 2.0 %collective-permute-start.9 = (bf16[1,14,32,128]{3,2,1,0:T(8,128)(2,1)S(1)}, bf16[1,14,32,128]{3,2,1,0:T(8,128)(2,1)S(1)}, u32[]{:S(2)}, u32[]{:S(2)}) collective-permute-start(bf16[1,14,32,128]{3,2,1,0:T(8,128)(2,1)S(1)} %reduce-precision_convert_fusion), channel_id=1, source_target_pairs={{0,24},{1,7},{2,26},{3,5},{4,28},{5,3},{6,30},{7,1},{8,16},{9,15},... | collective-permute-start | bytes 344072 | tf_op jit(solution)/shard_map/ppermute | solution.py:40
  18.7 0.5 %collective-permute-start.8 = (bf16[1,14,32,128]{3,2,1,0:T(8,128)(2,1)S(1)}, bf16[1,14,32,128]{3,2,1,0:T(8,128)(2,1)S(1)}, u32[]{:S(2)}, u32[]{:S(2)}) collective-permute-start(bf16[1,14,32,128]{3,2,1,0:T(8,128)(2,1)S(1)} %reduce-precision_convert_fusion), channel_id=1, source_target_pairs={{0,8},{1,3},{2,10},{3,1},{4,12},{5,7},{6,14},{7,5},{8,0},{9,11},{1... | collective-permute-start | bytes 344072 | tf_op jit(solution)/shard_map/ppermute | solution.py:40
  19.2 0.2 collective-permute-start.7
  19.4 1.3 %collective-permute-start.10 = (bf16[256,128]{1,0:T(8,128)(2,1)S(1)}, bf16[256,128]{1,0:T(8,128)(2,1)S(1)}, u32[]{:S(2)}, u32[]{:S(2)}) collective-permute-start(bf16[256,128]{1,0:T(8,128)(2,1)S(1)} %get-tuple-element.42.pre_grad_ref), channel_id=1, source_target_pairs={{0,3},{1,0},{2,1},{3,2},{4,7},{5,4},{6,5},{7,6},{8,11},{9,8},{10,9... | collective-permute-start | bytes 196616 | tf_op jit(solution)/shard_map/ppermute | solution.py:21
  20.7 0.9 %collective-permute-done.9 = bf16[1,14,32,128]{3,2,1,0:T(8,128)(2,1)S(1)} collective-permute-done((bf16[1,14,32,128]{3,2,1,0:T(8,128)(2,1)S(1)}, bf16[1,14,32,128]{3,2,1,0:T(8,128)(2,1)S(1)}, u32[]{:S(2)}, u32[]{:S(2)}) %collective-permute-start.9) | collective-permute-done | bytes 114720 | tf_op jit(solution)/shard_map/ppermute | solution.py:40
  21.6 1.1 %collective-permute-done.8 = bf16[1,14,32,128]{3,2,1,0:T(8,128)(2,1)S(1)} collective-permute-done((bf16[1,14,32,128]{3,2,1,0:T(8,128)(2,1)S(1)}, bf16[1,14,32,128]{3,2,1,0:T(8,128)(2,1)S(1)}, u32[]{:S(2)}, u32[]{:S(2)}) %collective-permute-start.8) | collective-permute-done | bytes 114720 | tf_op jit(solution)/shard_map/ppermute | solution.py:40
  22.7 0.4 %collective-permute-done.7 = bf16[1,14,32,128]{3,2,1,0:T(8,128)(2,1)S(1)} collective-permute-done((bf16[1,14,32,128]{3,2,1,0:T(8,128)(2,1)S(1)}, bf16[1,14,32,128]{3,2,1,0:T(8,128)(2,1)S(1)}, u32[]{:S(2)}, u32[]{:S(2)}) %collective-permute-start.7) | collective-permute-done | bytes 114720 | tf_op jit(solution)/shard_map/ppermute | solution.py:40
  23.1 0.1 add_convert_fusion.refs_0_
  23.2 0.4 %collective-permute-done.10.next_ref = bf16[256,128]{1,0:T(8,128)(2,1)S(1)} collective-permute-done((bf16[256,128]{1,0:T(8,128)(2,1)S(1)}, bf16[256,128]{1,0:T(8,128)(2,1)S(1)}, u32[]{:S(2)}, u32[]{:S(2)}) %collective-permute-start.10) | collective-permute-done | bytes 65568 | tf_op jit(solution)/shard_map/ppermute | solution.py:21
  23.6 1.3 %collective-permute-start.11 = (bf16[1,14,32,128]{3,2,1,0:T(8,128)(2,1)S(1)}, bf16[1,14,32,128]{3,2,1,0:T(8,128)(2,1)S(1)}, u32[]{:S(2)}, u32[]{:S(2)}) collective-permute-start(bf16[1,14,32,128]{3,2,1,0:T(8,128)(2,1)S(1)} %add_convert_fusion.refs_0_), channel_id=1, source_target_pairs={{0,4},{1,17},{2,6},{3,19},{4,0},{5,21},{6,2},{7,23},{8,12},{9,25},... | collective-permute-start | bytes 344072 | tf_op jit(solution)/shard_map/ppermute | solution.py:40
  24.9 2.0 %collective-permute-start.16 = (bf16[1,14,32,128]{3,2,1,0:T(8,128)(2,1)S(1)}, bf16[1,14,32,128]{3,2,1,0:T(8,128)(2,1)S(1)}, u32[]{:S(2)}, u32[]{:S(2)}) collective-permute-start(bf16[1,14,32,128]{3,2,1,0:T(8,128)(2,1)S(1)} %add_convert_fusion.refs_0_), channel_id=1, source_target_pairs={{0,2},{1,9},{2,0},{3,11},{4,6},{5,13},{6,4},{7,15},{8,10},{9,1},{1... | collective-permute-start | bytes 344072 | tf_op jit(solution)/shard_map/ppermute | solution.py:40
  27.0 0.2 collective-permute-start.12
  27.2 2.4 %collective-permute-start.14 = (bf16[1,14,32,128]{3,2,1,0:T(8,128)(2,1)S(1)}, bf16[1,14,32,128]{3,2,1,0:T(8,128)(2,1)S(1)}, u32[]{:S(2)}, u32[]{:S(2)}) collective-permute-start(bf16[1,14,32,128]{3,2,1,0:T(8,128)(2,1)S(1)} %add_convert_fusion.refs_0_), channel_id=1, source_target_pairs={{0,1},{1,0},{2,3},{3,2},{4,5},{5,4},{6,7},{7,6},{8,9},{9,8},{10,11... | collective-permute-start | bytes 344072 | tf_op jit(solution)/shard_map/ppermute | solution.py:40
  29.6 1.3 %backward.1 = (bf16[256,128]{1,0:T(8,128)(2,1)}, bf16[256,128]{1,0:T(8,128)(2,1)}) custom-call(s32[1]{0:T(128)} %bitcast.where_ref, bf16[256,128]{1,0:T(8,128)(2,1)S(1)} %get-tuple-element.42.pre_grad_ref, bf16[256,128]{1,0:T(8,128)(2,1)S(1)} %collective-permute-done.10.next_ref, bf16[256,128]{1,0:T(8,128)(2,1)S(1)} %get-tuple-element.45.hidden_ref, ...), custom_call_target="tpu_custom_call" | custom-call | flops 234881024 | bytes 1048576 | tf_op jit(solution)/shard_map/backward/pallas_call | solution.py:406
  30.9 0.0 collective-permute-done.11.refs_2_
  30.9 0.0 collective-permute-done.16.refs_4_
  30.9 1.5 %collective-permute-start.17 = (bf16[1,14,32,128]{3,2,1,0:T(8,128)(2,1)S(1)}, bf16[1,14,32,128]{3,2,1,0:T(8,128)(2,1)S(1)}, u32[]{:S(2)}, u32[]{:S(2)}) collective-permute-start(bf16[1,14,32,128]{3,2,1,0:T(8,128)(2,1)S(1)} %collective-permute-done.16.refs_4_), channel_id=1, source_target_pairs={{0,1},{1,0},{2,3},{3,2},{4,5},{5,4},{6,7},{7,6},{8,9},{9,8},{10,11... | collective-permute-start | bytes 344072 | tf_op jit(solution)/shard_map/ppermute | solution.py:40
  32.4 0.0 collective-permute-start.15
  32.4 0.0 collective-permute-done.12.refs_0_
  32.4 1.4 %collective-permute-start.13 = (bf16[1,14,32,128]{3,2,1,0:T(8,128)(2,1)S(1)}, bf16[1,14,32,128]{3,2,1,0:T(8,128)(2,1)S(1)}, u32[]{:S(2)}, u32[]{:S(2)}) collective-permute-start(bf16[1,14,32,128]{3,2,1,0:T(8,128)(2,1)S(1)} %collective-permute-done.12.refs_0_), channel_id=1, source_target_pairs={{0,1},{1,0},{2,3},{3,2},{4,5},{5,4},{6,7},{7,6},{8,9},{9,8},{10,11... | collective-permute-start | bytes 344072 | tf_op jit(solution)/shard_map/ppermute | solution.py:40
  33.8 0.0 collective-permute-done.14.refs_1_
  33.8 0.0 collective-permute-done.17.refs_5_
  33.8 0.0 collective-permute-done.15.refs_3_
  33.9 1.3 %unpack.2 = (f32[27,128,128]{2,1,0:T(8,128)}, f32[128,128]{1,0:T(8,128)}) custom-call(s32[1]{0:T(128)} %bitcast.where_ref, bf16[1,14,32,128]{3,2,1,0:T(8,128)(2,1)S(1)} %add_convert_fusion.refs_0_, bf16[1,14,32,128]{3,2,1,0:T(8,128)(2,1)S(1)} %collective-permute-done.14.refs_1_, bf16[1,14,32,128]{3,2,1,0:T(8,128)(2,1)S(1)} %collective-permute-done.11.refs_2_, ...), custom_call_target="tpu_custom_call" | custom-call | flops 344064 | bytes 2064384 | tf_op jit(solution)/shard_map/unpack/pallas_call | solution.py:289
  35.2 0.0 collective-permute-done.13.refs_1_
  35.2 0.9 %unpack.3 = (f32[27,128,128]{2,1,0:T(8,128)}, f32[128,128]{1,0:T(8,128)}) custom-call(s32[1]{0:T(128)} %bitcast.where_ref, bf16[1,14,32,128]{3,2,1,0:T(8,128)(2,1)S(1)} %collective-permute-done.12.refs_0_, bf16[1,14,32,128]{3,2,1,0:T(8,128)(2,1)S(1)} %collective-permute-done.13.refs_1_, ...), custom_call_target="tpu_custom_call", output_to_operand_aliasing={{0}: (3, {}), {1}: (4, {})} | custom-call | flops 114688 | bytes 688128 | tf_op jit(solution)/shard_map/unpack/pallas_call | solution.py:289
  (2 shorter events, 0.0 us)
Async XLA Ops:
  0.6 4.5 %collective-permute-start.2 = (bf16[256,128]{1,0:T(8,128)(2,1)}, bf16[256,128]{1,0:T(8,128)(2,1)S(1)}, u32[]{:S(2)}, u32[]{:S(2)}) collective-permute-start(bf16[256,128]{1,0:T(8,128)(2,1)} %bitcast.9), channel_id=1, source_target_pairs={{0,1},{1,0},{2,3},{3,2},{4,5},{5,4},{6,7},{7,6},{8,9},{9,8},{10,11... | collective-permute-start | bytes 196616 | tf_op jit(solution)/shard_map/ppermute | solution.py:40
  0.8 4.4 %collective-permute-start.3 = (bf16[256,128]{1,0:T(8,128)(2,1)}, bf16[256,128]{1,0:T(8,128)(2,1)S(1)}, u32[]{:S(2)}, u32[]{:S(2)}) collective-permute-start(bf16[256,128]{1,0:T(8,128)(2,1)} %bitcast.7), channel_id=1, source_target_pairs={{0,1},{1,0},{2,3},{3,2},{4,5},{5,4},{6,7},{7,6},{8,9},{9,8},{10,11... | collective-permute-start | bytes 196616 | tf_op jit(solution)/shard_map/ppermute | solution.py:40
  1.2 4.7 %collective-permute-start.1 = (bf16[256,128]{1,0:T(8,128)(2,1)}, bf16[256,128]{1,0:T(8,128)(2,1)S(1)}, u32[]{:S(2)}, u32[]{:S(2)}) collective-permute-start(bf16[256,128]{1,0:T(8,128)(2,1)} %bitcast.10), channel_id=1, source_target_pairs={{0,1},{1,2},{2,3},{3,0},{4,5},{5,6},{6,7},{7,4},{8,9},{9,10},{10,1... | collective-permute-start | bytes 196616 | tf_op jit(solution)/shard_map/ppermute | solution.py:21
  3.8 3.3 %collective-permute-start = (bf16[256,128]{1,0:T(8,128)(2,1)}, bf16[256,128]{1,0:T(8,128)(2,1)S(1)}, u32[]{:S(2)}, u32[]{:S(2)}) collective-permute-start(bf16[256,128]{1,0:T(8,128)(2,1)} %bitcast.11), channel_id=1, source_target_pairs={{0,4},{1,3},{2,6},{3,1},{4,0},{5,7},{6,2},{7,5},{8,12},{9,11},{10,... | collective-permute-start | bytes 196616 | tf_op jit(solution)/shard_map/ppermute | solution.py:31
  8.2 5.7 %collective-permute-start.4 = (bf16[1,14,32,128]{3,2,1,0:T(8,128)(2,1)S(1)}, bf16[1,14,32,128]{3,2,1,0:T(8,128)(2,1)S(1)}, u32[]{:S(2)}, u32[]{:S(2)}) collective-permute-start(bf16[1,14,32,128]{3,2,1,0:T(8,128)(2,1)S(1)} %get-tuple-element.56), channel_id=1, source_target_pairs={{0,6},{1,25},{2,4},{3,27},{4,2},{5,29},{6,0},{7,31},{8,14},{9,17},... | collective-permute-start | bytes 344072 | tf_op jit(solution)/shard_map/ppermute | solution.py:40
  11.6 5.0 %collective-permute-start.6 = (bf16[1,14,32,128]{3,2,1,0:T(8,128)(2,1)S(1)}, bf16[1,14,32,128]{3,2,1,0:T(8,128)(2,1)S(1)}, u32[]{:S(2)}, u32[]{:S(2)}) collective-permute-start(bf16[1,14,32,128]{3,2,1,0:T(8,128)(2,1)S(1)} %get-tuple-element.57), channel_id=1, source_target_pairs={{0,4},{1,17},{2,6},{3,19},{4,0},{5,21},{6,2},{7,23},{8,12},{9,25},... | collective-permute-start | bytes 344072 | tf_op jit(solution)/shard_map/ppermute | solution.py:40
  11.6 5.0 %collective-permute-start.5 = (bf16[1,14,32,128]{3,2,1,0:T(8,128)(2,1)S(1)}, bf16[1,14,32,128]{3,2,1,0:T(8,128)(2,1)S(1)}, u32[]{:S(2)}, u32[]{:S(2)}) collective-permute-start(bf16[1,14,32,128]{3,2,1,0:T(8,128)(2,1)S(1)} %get-tuple-element.58), channel_id=1, source_target_pairs={{0,2},{1,9},{2,0},{3,11},{4,6},{5,13},{6,4},{7,15},{8,10},{9,1},{1... | collective-permute-start | bytes 344072 | tf_op jit(solution)/shard_map/ppermute | solution.py:40
  16.7 4.9 %collective-permute-start.9 = (bf16[1,14,32,128]{3,2,1,0:T(8,128)(2,1)S(1)}, bf16[1,14,32,128]{3,2,1,0:T(8,128)(2,1)S(1)}, u32[]{:S(2)}, u32[]{:S(2)}) collective-permute-start(bf16[1,14,32,128]{3,2,1,0:T(8,128)(2,1)S(1)} %reduce-precision_convert_fusion), channel_id=1, source_target_pairs={{0,24},{1,7},{2,26},{3,5},{4,28},{5,3},{6,30},{7,1},{8,16},{9,15},... | collective-permute-start | bytes 344072 | tf_op jit(solution)/shard_map/ppermute | solution.py:40
  18.7 4.0 %collective-permute-start.8 = (bf16[1,14,32,128]{3,2,1,0:T(8,128)(2,1)S(1)}, bf16[1,14,32,128]{3,2,1,0:T(8,128)(2,1)S(1)}, u32[]{:S(2)}, u32[]{:S(2)}) collective-permute-start(bf16[1,14,32,128]{3,2,1,0:T(8,128)(2,1)S(1)} %reduce-precision_convert_fusion), channel_id=1, source_target_pairs={{0,8},{1,3},{2,10},{3,1},{4,12},{5,7},{6,14},{7,5},{8,0},{9,11},{1... | collective-permute-start | bytes 344072 | tf_op jit(solution)/shard_map/ppermute | solution.py:40
  19.2 3.9 %collective-permute-start.7 = (bf16[1,14,32,128]{3,2,1,0:T(8,128)(2,1)S(1)}, bf16[1,14,32,128]{3,2,1,0:T(8,128)(2,1)S(1)}, u32[]{:S(2)}, u32[]{:S(2)}) collective-permute-start(bf16[1,14,32,128]{3,2,1,0:T(8,128)(2,1)S(1)} %reduce-precision_convert_fusion), channel_id=1, source_target_pairs={{0,16},{1,5},{2,18},{3,7},{4,20},{5,1},{6,22},{7,3},{8,24},{9,13},... | collective-permute-start | bytes 344072 | tf_op jit(solution)/shard_map/ppermute | solution.py:40
  19.4 4.2 %collective-permute-start.10 = (bf16[256,128]{1,0:T(8,128)(2,1)S(1)}, bf16[256,128]{1,0:T(8,128)(2,1)S(1)}, u32[]{:S(2)}, u32[]{:S(2)}) collective-permute-start(bf16[256,128]{1,0:T(8,128)(2,1)S(1)} %get-tuple-element.42.pre_grad_ref), channel_id=1, source_target_pairs={{0,3},{1,0},{2,1},{3,2},{4,7},{5,4},{6,5},{7,6},{8,11},{9,8},{10,9... | collective-permute-start | bytes 196616 | tf_op jit(solution)/shard_map/ppermute | solution.py:21
  23.6 7.3 %collective-permute-start.11 = (bf16[1,14,32,128]{3,2,1,0:T(8,128)(2,1)S(1)}, bf16[1,14,32,128]{3,2,1,0:T(8,128)(2,1)S(1)}, u32[]{:S(2)}, u32[]{:S(2)}) collective-permute-start(bf16[1,14,32,128]{3,2,1,0:T(8,128)(2,1)S(1)} %add_convert_fusion.refs_0_), channel_id=1, source_target_pairs={{0,4},{1,17},{2,6},{3,19},{4,0},{5,21},{6,2},{7,23},{8,12},{9,25},... | collective-permute-start | bytes 344072 | tf_op jit(solution)/shard_map/ppermute | solution.py:40
  24.9 6.0 %collective-permute-start.16 = (bf16[1,14,32,128]{3,2,1,0:T(8,128)(2,1)S(1)}, bf16[1,14,32,128]{3,2,1,0:T(8,128)(2,1)S(1)}, u32[]{:S(2)}, u32[]{:S(2)}) collective-permute-start(bf16[1,14,32,128]{3,2,1,0:T(8,128)(2,1)S(1)} %add_convert_fusion.refs_0_), channel_id=1, source_target_pairs={{0,2},{1,9},{2,0},{3,11},{4,6},{5,13},{6,4},{7,15},{8,10},{9,1},{1... | collective-permute-start | bytes 344072 | tf_op jit(solution)/shard_map/ppermute | solution.py:40
  27.0 5.5 %collective-permute-start.12 = (bf16[1,14,32,128]{3,2,1,0:T(8,128)(2,1)S(1)}, bf16[1,14,32,128]{3,2,1,0:T(8,128)(2,1)S(1)}, u32[]{:S(2)}, u32[]{:S(2)}) collective-permute-start(bf16[1,14,32,128]{3,2,1,0:T(8,128)(2,1)S(1)} %add_convert_fusion.refs_0_), channel_id=1, source_target_pairs={{0,6},{1,25},{2,4},{3,27},{4,2},{5,29},{6,0},{7,31},{8,14},{9,17},... | collective-permute-start | bytes 344072 | tf_op jit(solution)/shard_map/ppermute | solution.py:40
  27.2 6.7 %collective-permute-start.14 = (bf16[1,14,32,128]{3,2,1,0:T(8,128)(2,1)S(1)}, bf16[1,14,32,128]{3,2,1,0:T(8,128)(2,1)S(1)}, u32[]{:S(2)}, u32[]{:S(2)}) collective-permute-start(bf16[1,14,32,128]{3,2,1,0:T(8,128)(2,1)S(1)} %add_convert_fusion.refs_0_), channel_id=1, source_target_pairs={{0,1},{1,0},{2,3},{3,2},{4,5},{5,4},{6,7},{7,6},{8,9},{9,8},{10,11... | collective-permute-start | bytes 344072 | tf_op jit(solution)/shard_map/ppermute | solution.py:40
  30.9 2.9 %collective-permute-start.17 = (bf16[1,14,32,128]{3,2,1,0:T(8,128)(2,1)S(1)}, bf16[1,14,32,128]{3,2,1,0:T(8,128)(2,1)S(1)}, u32[]{:S(2)}, u32[]{:S(2)}) collective-permute-start(bf16[1,14,32,128]{3,2,1,0:T(8,128)(2,1)S(1)} %collective-permute-done.16.refs_4_), channel_id=1, source_target_pairs={{0,1},{1,0},{2,3},{3,2},{4,5},{5,4},{6,7},{7,6},{8,9},{9,8},{10,11... | collective-permute-start | bytes 344072 | tf_op jit(solution)/shard_map/ppermute | solution.py:40
  32.4 1.4 %collective-permute-start.15 = (bf16[1,14,32,128]{3,2,1,0:T(8,128)(2,1)S(1)}, bf16[1,14,32,128]{3,2,1,0:T(8,128)(2,1)S(1)}, u32[]{:S(2)}, u32[]{:S(2)}) collective-permute-start(bf16[1,14,32,128]{3,2,1,0:T(8,128)(2,1)S(1)} %collective-permute-done.11.refs_2_), channel_id=1, source_target_pairs={{0,1},{1,0},{2,3},{3,2},{4,5},{5,4},{6,7},{7,6},{8,9},{9,8},{10,11... | collective-permute-start | bytes 344072 | tf_op jit(solution)/shard_map/ppermute | solution.py:40
  32.4 2.7 %collective-permute-start.13 = (bf16[1,14,32,128]{3,2,1,0:T(8,128)(2,1)S(1)}, bf16[1,14,32,128]{3,2,1,0:T(8,128)(2,1)S(1)}, u32[]{:S(2)}, u32[]{:S(2)}) collective-permute-start(bf16[1,14,32,128]{3,2,1,0:T(8,128)(2,1)S(1)} %collective-permute-done.12.refs_0_), channel_id=1, source_target_pairs={{0,1},{1,0},{2,3},{3,2},{4,5},{5,4},{6,7},{7,6},{8,9},{9,8},{10,11... | collective-permute-start | bytes 344072 | tf_op jit(solution)/shard_map/ppermute | solution.py:40

commit v11 on v9

--- a/solution.py
+++ b/solution.py
@@ -119,7 +119,7 @@
 
 def join_kernel(
     shape, where_ref, own_ref, grads_ref, partner_ref, partner_grads_ref, kern_ref, proj_ref,
-    wide_ref, pair_grads_ref, sums_ref, hidden_grad_ref,
+    turned_ref, pair_grads_ref, sums_ref, hidden_grad_ref, wide_ref,
 ):
     _, height, width, chans = shape
     map_rows = height * width
@@ -130,22 +130,21 @@
     def part(start, index):
         return pl.ds(pl.multiple_of(start + index * rows, map_rows), rows)
 
-    wide_ref[part(head, core)] = own_ref[...]
-    spread(partner_ref[...], width, wide_ref.at[part(head, 1 - core)])
+    wide_ref[part(0, core)] = own_ref[...]
+    spread(partner_ref[...], width, wide_ref.at[part(0, 1 - core)])
     pair_grads_ref[part(0, core)] = grads_ref[...]
     pair_grads_ref[part(0, 1 - core)] = partner_grads_ref[...]
     hidden_grad_ref[...] = dot(pair_grads_ref[...], proj_ref[...], (1, 1))
-    sums_ref[...] = dot(wide_ref[head:], weights_of(kern_ref, 2), (1, 0))
+    sums_ref[...] = dot(wide_ref[...], weights_of(kern_ref, 2), (1, 0))
     for tau in (1, 0):
         skip = (2 - tau) * map_rows
-        sums_ref[skip:] += dot(
-            wide_ref[head : head + 2 * rows - skip], weights_of(kern_ref, tau), (1, 0)
-        )
+        sums_ref[skip:] += dot(wide_ref[: 2 * rows - skip], weights_of(kern_ref, tau), (1, 0))
+    turned_ref[:, head:] = wide_ref[...].T
 
 
 def forward_kernel(
     shape, where_ref, second_halo_ref, first_halo_ref, grads_ref, kern_ref, _, sums_ref,
-    hidden_grad_ref, keep_ref, send_ref, hidden_ref, pre_grad_ref, wide_ref,
+    hidden_grad_ref, keep_ref, send_ref, hidden_ref, pre_grad_ref, turned_ref, halo_ref,
 ):
     _, height, width, chans = shape
     map_rows = height * width
@@ -154,7 +153,6 @@
     me = where_ref[0] >> 2
     core = me & 1
     outside = (where_ref[0] & 2) != 0
-    halo_ref = wide_ref.at[:head]
 
     @pl.when(outside)
     def _():
@@ -168,6 +166,7 @@
     def _():
         spread(second_halo_ref[...], width, halo_ref)
 
+    turned_ref[:, :head] = halo_ref[...].T
     late = dot(halo_ref[...], weights_of(kern_ref, 0), (1, 0))
     early = dot(halo_ref[map_rows:], weights_of(kern_ref, 1), (1, 0))
     sums = sums_ref[...]
@@ -211,14 +210,17 @@
         return sums[col * chans : (col + 1) * chans, row * chans : (row + 1) * chans]
 
     outer = pl.ds(pl.multiple_of(core * head, map_rows), 2 * rows)
-    sums = dot(wide_ref[outer], grad_rows, (0, 0))
+    sums = dot(turned_ref[:, outer], grad_rows, (1, 0))
     for place in range(9):
-        put(place, tap(sums, place // 3, place % 3))
-    sums = dot(wide_ref[map_rows : map_rows + 2 * rows], grad_rows, (0, 0))
+        put(place + 4 * core, tap(sums, place // 3, place % 3))
+    sums = dot(turned_ref[:, map_rows : map_rows + 2 * rows], grad_rows, (1, 0))
     middle = [tap(sums, place // 3, place % 3) for place in range(9)]
     middle.append(dot(hidden, grads_ref[...], (0, 0)))
     for place in range(5):
-        put(9 + place, jnp.where(core == 0, middle[place], middle[5 + place]))
+        put(
+            13 if place == 4 else jnp.where(core == 0, 9 + place, place),
+            jnp.where(core == 0, middle[place], middle[5 + place]),
+        )
 
 
 def backward_kernel(
@@ -264,8 +266,7 @@
         rows = pl.ds(pl.multiple_of(block * block_rows, block_rows), block_rows)
         piece = out_ref.at[place]
         for start, target, wanted in (
-            (piece.at[:9], kern_ref.at[pl.ds(18 * half, 9), rows, :], None),
-            (piece.at[9:13], kern_ref.at[pl.ds(9 + 5 * half, 4), rows, :], None),
+            (piece.at[:13], kern_ref.at[pl.ds(14 * half, 13), rows, :], None),
             (piece.at[13], kern_ref.at[13, rows, :], 0),
             (piece.at[13], proj_ref.at[rows, :], 1),
         ):
@@ -296,7 +297,7 @@
         out_specs=(OUTSIDE, OUTSIDE),
         scratch_shapes=[
             pltpu.VMEM((len(given), places, block_rows, chans), jnp.float32),
-            pltpu.SemaphoreType.DMA((4 * len(given),)),
+            pltpu.SemaphoreType.DMA((3 * len(given),)),
         ],
         input_output_aliases={1 + len(given) + i: i for i in range(len(sofar))},
         compiler_params=LIMIT,
@@ -362,13 +363,14 @@
     return pl.pallas_call(
         functools.partial(join_kernel, shape),
         out_shape=(
-            jax.ShapeDtypeStruct((head + 2 * rows, 3 * chans), jnp.bfloat16),
+            jax.ShapeDtypeStruct((3 * chans, head + 2 * rows), jnp.bfloat16),
             jax.ShapeDtypeStruct((2 * rows, chans), jnp.bfloat16),
             jax.ShapeDtypeStruct((2 * rows, 3 * chans), jnp.float32),
             jax.ShapeDtypeStruct((2 * rows, chans), jnp.float32),
         ),
         in_specs=[SCALAR] + [VECTOR] * 6,
         out_specs=(VECTOR,) * 4,
+        scratch_shapes=[pltpu.VMEM((2 * rows, 3 * chans), jnp.bfloat16)],
         compiler_params=LIMIT,
         cost_estimate=pl.CostEstimate(
             flops=2 * rows * 40 * chans * chans, bytes_accessed=2 << 20, transcendentals=0
@@ -392,6 +394,7 @@
         ),
         in_specs=[SCALAR] + [VECTOR] * 7,
         out_specs=(VECTOR,) * 5,
+        scratch_shapes=[pltpu.VMEM((2 * height * width, 3 * chans), jnp.bfloat16)],
         input_output_aliases={5: 4},
         compiler_params=LIMIT,
         name="forward",

time: 36.2 us -> 36.1 us (level)
  no operation moved by 1% of the time
where the time goes in v11:
time: 36.1 us; the launch traced here: 35.9 us
  starting transfers between devices  20 us (55%)
  waiting for transfers between devices  8.56 us (24%)
  Pallas kernels  6.48 us (18%)
  between operations  0.76 us (2%)
    ppermute x15, starting transfers between devices, swapped(): lax.ppermute(array, AXES, [(i, i ^ masks[i & 1]) for i in range(count)])  17.4 us
    ppermute x15, waiting for transfers between devices, swapped(): lax.ppermute(array, AXES, [(i, i ^ masks[i & 1]) for i in range(count)])  7.36 us
    ppermute x2, starting transfers between devices, passed_round(): lax.ppermute(shard, axis, [(i, (i + by) % size) for i in range(size)])  2.6 us
    pallas_call x2, Pallas kernels, unpack(): pl.pallas_call(functools.partial(unpack_kernel, scale, offsets), out_shap...  2.08 us
    pallas_call x1, Pallas kernels, backward(): pl.pallas_call(functools.partial(backward_kernel, shape), out_shape=(jax....  1.29 us
    pallas_call x1, Pallas kernels, prepare(): pl.pallas_call(functools.partial(prepare_kernel, width), out_shape=(*(jax...  1.28 us
    ppermute x1, waiting for transfers between devices, passed_to_last_core(): return lax.ppermute(shard, AXES, pairs)  1.19 us
    pallas_call x1, Pallas kernels, forward(): pl.pallas_call(functools.partial(forward_kernel, shape), out_shape=(jax.S...  1.03 us
  transfers between devices with their start and end apart: 18, of which 7 were waited for; matrix products, arithmetic and copies ran while one was open for 0% of the time, Pallas kernels for 13%

profile of v11, /device:TPU:1, one launch (start us, length us, event | category | flops | bytes accessed | tf_op | source)
XLA Modules:
  0.0 35.9 jit_solution(6799457670440466495)
XLA Ops:
  0.6 0.1 collective-permute-start.2
  0.8 0.5 %collective-permute-start.3 = (bf16[256,128]{1,0:T(8,128)(2,1)}, bf16[256,128]{1,0:T(8,128)(2,1)S(1)}, u32[]{:S(2)}, u32[]{:S(2)}) collective-permute-start(bf16[256,128]{1,0:T(8,128)(2,1)} %bitcast.7), channel_id=1, source_target_pairs={{0,1},{1,0},{2,3},{3,2},{4,5},{5,4},{6,7},{7,6},{8,9},{9,8},{10,11... | collective-permute-start | bytes 196616 | tf_op jit(solution)/shard_map/ppermute | solution.py:40
  1.2 2.6 %collective-permute-start.1 = (bf16[256,128]{1,0:T(8,128)(2,1)}, bf16[256,128]{1,0:T(8,128)(2,1)S(1)}, u32[]{:S(2)}, u32[]{:S(2)}) collective-permute-start(bf16[256,128]{1,0:T(8,128)(2,1)} %bitcast.10), channel_id=1, source_target_pairs={{0,1},{1,2},{2,3},{3,0},{4,5},{5,6},{6,7},{7,4},{8,9},{9,10},{10,1... | collective-permute-start | bytes 196616 | tf_op jit(solution)/shard_map/ppermute | solution.py:21
  3.8 0.0 collective-permute-start
  3.8 1.3 %prepare.1 = (bf16[256,128]{1,0:T(8,128)(2,1)S(1)}, bf16[256,128]{1,0:T(8,128)(2,1)S(1)}, bf16[3,3,3,128,128]{4,3,2,1,0:T(8,128)(2,1)S(1)}, bf16[128,128]{1,0:T(8,128)(2,1)S(1)}, bf16[256,384]{1,0:T(8,128)(2,1)S(1)}) custom-call(bf16[256,128]{1,0:T(8,128)(2,1)} %bitcast.12, bf16[256,128]{1,0:T(8,128)(2,1)} %bitcast.8, bf16[3,3,3,128,128]{4,3,2,1,0:T(8,128)(2,1)} %kern_hbm.1, ...), custom_call_target="tpu_custom_call" | custom-call | flops 32768 | bytes 2097152 | tf_op jit(solution)/shard_map/prepare/pallas_call | solution.py:344
  5.1 0.0 collective-permute-done.2.partner_ref
  5.1 0.0 collective-permute-done.3.partner_grads_ref
  5.1 0.8 %join.1 = (bf16[384,768]{1,0:T(8,128)(2,1)S(1)}, bf16[512,128]{1,0:T(8,128)(2,1)S(1)}, f32[512,384]{1,0:T(8,128)S(1)}, f32[512,128]{1,0:T(8,128)S(1)}) custom-call(s32[1]{0:T(128)} %bitcast.where_ref, bf16[256,384]{1,0:T(8,128)(2,1)S(1)} %get-tuple-element.28.own_ref, bf16[256,128]{1,0:T(8,128)(2,1)S(1)} %get-tuple-element.29.grads_ref, ...), custom_call_target="tpu_custom_call" | custom-call | flops 335544320 | bytes 2097152 | tf_op jit(solution)/shard_map/join/pallas_call | solution.py:363
  5.9 0.0 collective-permute-done.1.first_halo_ref
  5.9 1.2 %collective-permute-done.second_halo_ref = bf16[256,128]{1,0:T(8,128)(2,1)S(1)} collective-permute-done((bf16[256,128]{1,0:T(8,128)(2,1)}, bf16[256,128]{1,0:T(8,128)(2,1)S(1)}, u32[]{:S(2)}, u32[]{:S(2)}) %collective-permute-start) | collective-permute-done | bytes 65568 | tf_op jit(solution)/shard_map/ppermute | solution.py:31
  7.1 1.0 %forward.1 = (f32[4,14,32,128]{3,2,1,0:T(8,128)S(1)}, bf16[4,14,32,128]{3,2,1,0:T(8,128)(2,1)S(1)}, bf16[256,128]{1,0:T(8,128)(2,1)S(1)}, bf16[256,128]{1,0:T(8,128)(2,1)S(1)}, bf16[384,768]{1,0:T(8,128)(2,1)S(1)}) custom-call(s32[1]{0:T(128)} %bitcast.where_ref, ...), custom_call_target="tpu_custom_call", output_to_operand_aliasing={{4}: (5, {})} | custom-call | tf_op jit(solution)/shard_map/forward/pallas_call | solution.py:386
  8.2 3.4 %collective-permute-start.4 = (bf16[1,14,32,128]{3,2,1,0:T(8,128)(2,1)S(1)}, bf16[1,14,32,128]{3,2,1,0:T(8,128)(2,1)S(1)}, u32[]{:S(2)}, u32[]{:S(2)}) collective-permute-start(bf16[1,14,32,128]{3,2,1,0:T(8,128)(2,1)S(1)} %get-tuple-element.52), channel_id=1, source_target_pairs={{0,6},{1,25},{2,4},{3,27},{4,2},{5,29},{6,0},{7,31},{8,14},{9,17},... | collective-permute-start | bytes 344072 | tf_op jit(solution)/shard_map/ppermute | solution.py:40
  11.6 0.0 collective-permute-start.6
  11.6 0.4 %collective-permute-start.5 = (bf16[1,14,32,128]{3,2,1,0:T(8,128)(2,1)S(1)}, bf16[1,14,32,128]{3,2,1,0:T(8,128)(2,1)S(1)}, u32[]{:S(2)}, u32[]{:S(2)}) collective-permute-start(bf16[1,14,32,128]{3,2,1,0:T(8,128)(2,1)S(1)} %get-tuple-element.54), channel_id=1, source_target_pairs={{0,2},{1,9},{2,0},{3,11},{4,6},{5,13},{6,4},{7,15},{8,10},{9,1},{1... | collective-permute-start | bytes 344072 | tf_op jit(solution)/shard_map/ppermute | solution.py:40
  12.0 0.0 collective-permute-start.7
  12.0 1.9 %collective-permute-done.4 = bf16[1,14,32,128]{3,2,1,0:T(8,128)(2,1)S(1)} collective-permute-done((bf16[1,14,32,128]{3,2,1,0:T(8,128)(2,1)S(1)}, bf16[1,14,32,128]{3,2,1,0:T(8,128)(2,1)S(1)}, u32[]{:S(2)}, u32[]{:S(2)}) %collective-permute-start.4) | collective-permute-done | bytes 114720 | tf_op jit(solution)/shard_map/ppermute | solution.py:40
  13.9 2.7 %collective-permute-done.6 = bf16[1,14,32,128]{3,2,1,0:T(8,128)(2,1)S(1)} collective-permute-done((bf16[1,14,32,128]{3,2,1,0:T(8,128)(2,1)S(1)}, bf16[1,14,32,128]{3,2,1,0:T(8,128)(2,1)S(1)}, u32[]{:S(2)}, u32[]{:S(2)}) %collective-permute-start.6) | collective-permute-done | bytes 114720 | tf_op jit(solution)/shard_map/ppermute | solution.py:40
  16.6 0.0 collective-permute-done.5
  16.6 0.1 convert_add_fusion
  16.7 0.0 collective-permute-done.7.next_ref
  16.7 2.0 %collective-permute-start.10 = (bf16[1,14,32,128]{3,2,1,0:T(8,128)(2,1)S(1)}, bf16[1,14,32,128]{3,2,1,0:T(8,128)(2,1)S(1)}, u32[]{:S(2)}, u32[]{:S(2)}) collective-permute-start(bf16[1,14,32,128]{3,2,1,0:T(8,128)(2,1)S(1)} %reduce-precision_convert_fusion), channel_id=1, source_target_pairs={{0,24},{1,7},{2,26},{3,5},{4,28},{5,3},{6,30},{7,1},{8,16},{9,15},... | collective-permute-start | bytes 344072 | tf_op jit(solution)/shard_map/ppermute | solution.py:40
  18.7 0.5 %collective-permute-start.9 = (bf16[1,14,32,128]{3,2,1,0:T(8,128)(2,1)S(1)}, bf16[1,14,32,128]{3,2,1,0:T(8,128)(2,1)S(1)}, u32[]{:S(2)}, u32[]{:S(2)}) collective-permute-start(bf16[1,14,32,128]{3,2,1,0:T(8,128)(2,1)S(1)} %reduce-precision_convert_fusion), channel_id=1, source_target_pairs={{0,8},{1,3},{2,10},{3,1},{4,12},{5,7},{6,14},{7,5},{8,0},{9,11},{1... | collective-permute-start | bytes 344072 | tf_op jit(solution)/shard_map/ppermute | solution.py:40
  19.2 0.2 collective-permute-start.8
  19.4 1.3 %backward.1 = (bf16[256,128]{1,0:T(8,128)(2,1)}, bf16[256,128]{1,0:T(8,128)(2,1)}) custom-call(s32[1]{0:T(128)} %bitcast.where_ref, bf16[256,128]{1,0:T(8,128)(2,1)S(1)} %get-tuple-element.38.pre_grad_ref, bf16[256,128]{1,0:T(8,128)(2,1)S(1)} %collective-permute-done.7.next_ref, bf16[256,128]{1,0:T(8,128)(2,1)S(1)} %get-tuple-element.41.hidden_ref, ...), custom_call_target="tpu_custom_call" | custom-call | flops 234881024 | bytes 1048576 | tf_op jit(solution)/shard_map/backward/pallas_call | solution.py:408
  20.7 0.9 %collective-permute-done.10 = bf16[1,14,32,128]{3,2,1,0:T(8,128)(2,1)S(1)} collective-permute-done((bf16[1,14,32,128]{3,2,1,0:T(8,128)(2,1)S(1)}, bf16[1,14,32,128]{3,2,1,0:T(8,128)(2,1)S(1)}, u32[]{:S(2)}, u32[]{:S(2)}) %collective-permute-start.10) | collective-permute-done | bytes 114720 | tf_op jit(solution)/shard_map/ppermute | solution.py:40
  21.6 1.0 %collective-permute-done.9 = bf16[1,14,32,128]{3,2,1,0:T(8,128)(2,1)S(1)} collective-permute-done((bf16[1,14,32,128]{3,2,1,0:T(8,128)(2,1)S(1)}, bf16[1,14,32,128]{3,2,1,0:T(8,128)(2,1)S(1)}, u32[]{:S(2)}, u32[]{:S(2)}) %collective-permute-start.9) | collective-permute-done | bytes 114720 | tf_op jit(solution)/shard_map/ppermute | solution.py:40
  22.6 0.5 %collective-permute-done.8 = bf16[1,14,32,128]{3,2,1,0:T(8,128)(2,1)S(1)} collective-permute-done((bf16[1,14,32,128]{3,2,1,0:T(8,128)(2,1)S(1)}, bf16[1,14,32,128]{3,2,1,0:T(8,128)(2,1)S(1)}, u32[]{:S(2)}, u32[]{:S(2)}) %collective-permute-start.8) | collective-permute-done | bytes 114720 | tf_op jit(solution)/shard_map/ppermute | solution.py:40
  23.1 0.1 add_convert_fusion.refs_0_
  23.2 1.2 %collective-permute-start.16 = (bf16[1,14,32,128]{3,2,1,0:T(8,128)(2,1)S(1)}, bf16[1,14,32,128]{3,2,1,0:T(8,128)(2,1)S(1)}, u32[]{:S(2)}, u32[]{:S(2)}) collective-permute-start(bf16[1,14,32,128]{3,2,1,0:T(8,128)(2,1)S(1)} %add_convert_fusion.refs_0_), channel_id=1, source_target_pairs={{0,2},{1,9},{2,0},{3,11},{4,6},{5,13},{6,4},{7,15},{8,10},{9,1},{1... | collective-permute-start | bytes 344072 | tf_op jit(solution)/shard_map/ppermute | solution.py:40
  24.4 2.0 %collective-permute-start.14 = (bf16[1,14,32,128]{3,2,1,0:T(8,128)(2,1)S(1)}, bf16[1,14,32,128]{3,2,1,0:T(8,128)(2,1)S(1)}, u32[]{:S(2)}, u32[]{:S(2)}) collective-permute-start(bf16[1,14,32,128]{3,2,1,0:T(8,128)(2,1)S(1)} %add_convert_fusion.refs_0_), channel_id=1, source_target_pairs={{0,4},{1,17},{2,6},{3,19},{4,0},{5,21},{6,2},{7,23},{8,12},{9,25},... | collective-permute-start | bytes 344072 | tf_op jit(solution)/shard_map/ppermute | solution.py:40
  26.4 0.4 %collective-permute-start.11 = (bf16[1,14,32,128]{3,2,1,0:T(8,128)(2,1)S(1)}, bf16[1,14,32,128]{3,2,1,0:T(8,128)(2,1)S(1)}, u32[]{:S(2)}, u32[]{:S(2)}) collective-permute-start(bf16[1,14,32,128]{3,2,1,0:T(8,128)(2,1)S(1)} %add_convert_fusion.refs_0_), channel_id=1, source_target_pairs={{0,6},{1,25},{2,4},{3,27},{4,2},{5,29},{6,0},{7,31},{8,14},{9,17},... | collective-permute-start | bytes 344072 | tf_op jit(solution)/shard_map/ppermute | solution.py:40
  26.8 2.8 %collective-permute-start.13 = (bf16[1,14,32,128]{3,2,1,0:T(8,128)(2,1)S(1)}, bf16[1,14,32,128]{3,2,1,0:T(8,128)(2,1)S(1)}, u32[]{:S(2)}, u32[]{:S(2)}) collective-permute-start(bf16[1,14,32,128]{3,2,1,0:T(8,128)(2,1)S(1)} %add_convert_fusion.refs_0_), channel_id=1, source_target_pairs={{0,1},{1,0},{2,3},{3,2},{4,5},{5,4},{6,7},{7,6},{8,9},{9,8},{10,11... | collective-permute-start | bytes 344072 | tf_op jit(solution)/shard_map/ppermute | solution.py:40
  29.6 0.0 collective-permute-done.16.refs_4_
  29.6 1.3 %collective-permute-start.17 = (bf16[1,14,32,128]{3,2,1,0:T(8,128)(2,1)S(1)}, bf16[1,14,32,128]{3,2,1,0:T(8,128)(2,1)S(1)}, u32[]{:S(2)}, u32[]{:S(2)}) collective-permute-start(bf16[1,14,32,128]{3,2,1,0:T(8,128)(2,1)S(1)} %collective-permute-done.16.refs_4_), channel_id=1, source_target_pairs={{0,1},{1,0},{2,3},{3,2},{4,5},{5,4},{6,7},{7,6},{8,9},{9,8},{10,11... | collective-permute-start | bytes 344072 | tf_op jit(solution)/shard_map/ppermute | solution.py:40
  30.9 0.0 collective-permute-done.14.refs_2_
  30.9 0.8 %collective-permute-start.15 = (bf16[1,14,32,128]{3,2,1,0:T(8,128)(2,1)S(1)}, bf16[1,14,32,128]{3,2,1,0:T(8,128)(2,1)S(1)}, u32[]{:S(2)}, u32[]{:S(2)}) collective-permute-start(bf16[1,14,32,128]{3,2,1,0:T(8,128)(2,1)S(1)} %collective-permute-done.14.refs_2_), channel_id=1, source_target_pairs={{0,1},{1,0},{2,3},{3,2},{4,5},{5,4},{6,7},{7,6},{8,9},{9,8},{10,11... | collective-permute-start | bytes 344072 | tf_op jit(solution)/shard_map/ppermute | solution.py:40
  31.7 0.3 collective-permute-done.11.refs_0_
  31.9 1.9 %collective-permute-start.12 = (bf16[1,14,32,128]{3,2,1,0:T(8,128)(2,1)S(1)}, bf16[1,14,32,128]{3,2,1,0:T(8,128)(2,1)S(1)}, u32[]{:S(2)}, u32[]{:S(2)}) collective-permute-start(bf16[1,14,32,128]{3,2,1,0:T(8,128)(2,1)S(1)} %collective-permute-done.11.refs_0_), channel_id=1, source_target_pairs={{0,1},{1,0},{2,3},{3,2},{4,5},{5,4},{6,7},{7,6},{8,9},{9,8},{10,11... | collective-permute-start | bytes 344072 | tf_op jit(solution)/shard_map/ppermute | solution.py:40
  33.8 0.0 collective-permute-done.13.refs_1_
  33.8 0.0 collective-permute-done.17.refs_5_
  33.8 0.0 collective-permute-done.15.refs_3_
  33.8 1.2 %unpack.2 = (f32[27,128,128]{2,1,0:T(8,128)}, f32[128,128]{1,0:T(8,128)}) custom-call(s32[1]{0:T(128)} %bitcast.where_ref, bf16[1,14,32,128]{3,2,1,0:T(8,128)(2,1)S(1)} %add_convert_fusion.refs_0_, bf16[1,14,32,128]{3,2,1,0:T(8,128)(2,1)S(1)} %collective-permute-done.13.refs_1_, bf16[1,14,32,128]{3,2,1,0:T(8,128)(2,1)S(1)} %collective-permute-done.14.refs_2_, ...), custom_call_target="tpu_custom_call" | custom-call | flops 344064 | bytes 2064384 | tf_op jit(solution)/shard_map/unpack/pallas_call | solution.py:290
  35.1 0.0 collective-permute-done.12.refs_1_
  35.1 0.8 %unpack.3 = (f32[27,128,128]{2,1,0:T(8,128)}, f32[128,128]{1,0:T(8,128)}) custom-call(s32[1]{0:T(128)} %bitcast.where_ref, bf16[1,14,32,128]{3,2,1,0:T(8,128)(2,1)S(1)} %collective-permute-done.11.refs_0_, bf16[1,14,32,128]{3,2,1,0:T(8,128)(2,1)S(1)} %collective-permute-done.12.refs_1_, ...), custom_call_target="tpu_custom_call", output_to_operand_aliasing={{0}: (3, {}), {1}: (4, {})} | custom-call | flops 114688 | bytes 688128 | tf_op jit(solution)/shard_map/unpack/pallas_call | solution.py:290
  (2 shorter events, 0.0 us)
Async XLA Ops:
  0.6 4.5 %collective-permute-start.2 = (bf16[256,128]{1,0:T(8,128)(2,1)}, bf16[256,128]{1,0:T(8,128)(2,1)S(1)}, u32[]{:S(2)}, u32[]{:S(2)}) collective-permute-start(bf16[256,128]{1,0:T(8,128)(2,1)} %bitcast.9), channel_id=1, source_target_pairs={{0,1},{1,0},{2,3},{3,2},{4,5},{5,4},{6,7},{7,6},{8,9},{9,8},{10,11... | collective-permute-start | bytes 196616 | tf_op jit(solution)/shard_map/ppermute | solution.py:40
  0.8 4.4 %collective-permute-start.3 = (bf16[256,128]{1,0:T(8,128)(2,1)}, bf16[256,128]{1,0:T(8,128)(2,1)S(1)}, u32[]{:S(2)}, u32[]{:S(2)}) collective-permute-start(bf16[256,128]{1,0:T(8,128)(2,1)} %bitcast.7), channel_id=1, source_target_pairs={{0,1},{1,0},{2,3},{3,2},{4,5},{5,4},{6,7},{7,6},{8,9},{9,8},{10,11... | collective-permute-start | bytes 196616 | tf_op jit(solution)/shard_map/ppermute | solution.py:40
  1.2 4.7 %collective-permute-start.1 = (bf16[256,128]{1,0:T(8,128)(2,1)}, bf16[256,128]{1,0:T(8,128)(2,1)S(1)}, u32[]{:S(2)}, u32[]{:S(2)}) collective-permute-start(bf16[256,128]{1,0:T(8,128)(2,1)} %bitcast.10), channel_id=1, source_target_pairs={{0,1},{1,2},{2,3},{3,0},{4,5},{5,6},{6,7},{7,4},{8,9},{9,10},{10,1... | collective-permute-start | bytes 196616 | tf_op jit(solution)/shard_map/ppermute | solution.py:21
  3.8 3.3 %collective-permute-start = (bf16[256,128]{1,0:T(8,128)(2,1)}, bf16[256,128]{1,0:T(8,128)(2,1)S(1)}, u32[]{:S(2)}, u32[]{:S(2)}) collective-permute-start(bf16[256,128]{1,0:T(8,128)(2,1)} %bitcast.11), channel_id=1, source_target_pairs={{0,4},{1,3},{2,6},{3,1},{4,0},{5,7},{6,2},{7,5},{8,12},{9,11},{10,... | collective-permute-start | bytes 196616 | tf_op jit(solution)/shard_map/ppermute | solution.py:31
  8.2 5.7 %collective-permute-start.4 = (bf16[1,14,32,128]{3,2,1,0:T(8,128)(2,1)S(1)}, bf16[1,14,32,128]{3,2,1,0:T(8,128)(2,1)S(1)}, u32[]{:S(2)}, u32[]{:S(2)}) collective-permute-start(bf16[1,14,32,128]{3,2,1,0:T(8,128)(2,1)S(1)} %get-tuple-element.52), channel_id=1, source_target_pairs={{0,6},{1,25},{2,4},{3,27},{4,2},{5,29},{6,0},{7,31},{8,14},{9,17},... | collective-permute-start | bytes 344072 | tf_op jit(solution)/shard_map/ppermute | solution.py:40
  11.6 5.0 %collective-permute-start.6 = (bf16[1,14,32,128]{3,2,1,0:T(8,128)(2,1)S(1)}, bf16[1,14,32,128]{3,2,1,0:T(8,128)(2,1)S(1)}, u32[]{:S(2)}, u32[]{:S(2)}) collective-permute-start(bf16[1,14,32,128]{3,2,1,0:T(8,128)(2,1)S(1)} %get-tuple-element.53), channel_id=1, source_target_pairs={{0,4},{1,17},{2,6},{3,19},{4,0},{5,21},{6,2},{7,23},{8,12},{9,25},... | collective-permute-start | bytes 344072 | tf_op jit(solution)/shard_map/ppermute | solution.py:40
  11.6 5.0 %collective-permute-start.5 = (bf16[1,14,32,128]{3,2,1,0:T(8,128)(2,1)S(1)}, bf16[1,14,32,128]{3,2,1,0:T(8,128)(2,1)S(1)}, u32[]{:S(2)}, u32[]{:S(2)}) collective-permute-start(bf16[1,14,32,128]{3,2,1,0:T(8,128)(2,1)S(1)} %get-tuple-element.54), channel_id=1, source_target_pairs={{0,2},{1,9},{2,0},{3,11},{4,6},{5,13},{6,4},{7,15},{8,10},{9,1},{1... | collective-permute-start | bytes 344072 | tf_op jit(solution)/shard_map/ppermute | solution.py:40
  12.0 4.7 %collective-permute-start.7 = (bf16[256,128]{1,0:T(8,128)(2,1)S(1)}, bf16[256,128]{1,0:T(8,128)(2,1)S(1)}, u32[]{:S(2)}, u32[]{:S(2)}) collective-permute-start(bf16[256,128]{1,0:T(8,128)(2,1)S(1)} %get-tuple-element.38.pre_grad_ref), channel_id=1, source_target_pairs={{0,3},{1,0},{2,1},{3,2},{4,7},{5,4},{6,5},{7,6},{8,11},{9,8},{10,9... | collective-permute-start | bytes 196616 | tf_op jit(solution)/shard_map/ppermute | solution.py:21
  16.7 4.9 %collective-permute-start.10 = (bf16[1,14,32,128]{3,2,1,0:T(8,128)(2,1)S(1)}, bf16[1,14,32,128]{3,2,1,0:T(8,128)(2,1)S(1)}, u32[]{:S(2)}, u32[]{:S(2)}) collective-permute-start(bf16[1,14,32,128]{3,2,1,0:T(8,128)(2,1)S(1)} %reduce-precision_convert_fusion), channel_id=1, source_target_pairs={{0,24},{1,7},{2,26},{3,5},{4,28},{5,3},{6,30},{7,1},{8,16},{9,15},... | collective-permute-start | bytes 344072 | tf_op jit(solution)/shard_map/ppermute | solution.py:40
  18.7 3.9 %collective-permute-start.9 = (bf16[1,14,32,128]{3,2,1,0:T(8,128)(2,1)S(1)}, bf16[1,14,32,128]{3,2,1,0:T(8,128)(2,1)S(1)}, u32[]{:S(2)}, u32[]{:S(2)}) collective-permute-start(bf16[1,14,32,128]{3,2,1,0:T(8,128)(2,1)S(1)} %reduce-precision_convert_fusion), channel_id=1, source_target_pairs={{0,8},{1,3},{2,10},{3,1},{4,12},{5,7},{6,14},{7,5},{8,0},{9,11},{1... | collective-permute-start | bytes 344072 | tf_op jit(solution)/shard_map/ppermute | solution.py:40
  19.2 3.9 %collective-permute-start.8 = (bf16[1,14,32,128]{3,2,1,0:T(8,128)(2,1)S(1)}, bf16[1,14,32,128]{3,2,1,0:T(8,128)(2,1)S(1)}, u32[]{:S(2)}, u32[]{:S(2)}) collective-permute-start(bf16[1,14,32,128]{3,2,1,0:T(8,128)(2,1)S(1)} %reduce-precision_convert_fusion), channel_id=1, source_target_pairs={{0,16},{1,5},{2,18},{3,7},{4,20},{5,1},{6,22},{7,3},{8,24},{9,13},... | collective-permute-start | bytes 344072 | tf_op jit(solution)/shard_map/ppermute | solution.py:40
  23.2 6.4 %collective-permute-start.16 = (bf16[1,14,32,128]{3,2,1,0:T(8,128)(2,1)S(1)}, bf16[1,14,32,128]{3,2,1,0:T(8,128)(2,1)S(1)}, u32[]{:S(2)}, u32[]{:S(2)}) collective-permute-start(bf16[1,14,32,128]{3,2,1,0:T(8,128)(2,1)S(1)} %add_convert_fusion.refs_0_), channel_id=1, source_target_pairs={{0,2},{1,9},{2,0},{3,11},{4,6},{5,13},{6,4},{7,15},{8,10},{9,1},{1... | collective-permute-start | bytes 344072 | tf_op jit(solution)/shard_map/ppermute | solution.py:40
  24.4 6.5 %collective-permute-start.14 = (bf16[1,14,32,128]{3,2,1,0:T(8,128)(2,1)S(1)}, bf16[1,14,32,128]{3,2,1,0:T(8,128)(2,1)S(1)}, u32[]{:S(2)}, u32[]{:S(2)}) collective-permute-start(bf16[1,14,32,128]{3,2,1,0:T(8,128)(2,1)S(1)} %add_convert_fusion.refs_0_), channel_id=1, source_target_pairs={{0,4},{1,17},{2,6},{3,19},{4,0},{5,21},{6,2},{7,23},{8,12},{9,25},... | collective-permute-start | bytes 344072 | tf_op jit(solution)/shard_map/ppermute | solution.py:40
  26.4 5.5 %collective-permute-start.11 = (bf16[1,14,32,128]{3,2,1,0:T(8,128)(2,1)S(1)}, bf16[1,14,32,128]{3,2,1,0:T(8,128)(2,1)S(1)}, u32[]{:S(2)}, u32[]{:S(2)}) collective-permute-start(bf16[1,14,32,128]{3,2,1,0:T(8,128)(2,1)S(1)} %add_convert_fusion.refs_0_), channel_id=1, source_target_pairs={{0,6},{1,25},{2,4},{3,27},{4,2},{5,29},{6,0},{7,31},{8,14},{9,17},... | collective-permute-start | bytes 344072 | tf_op jit(solution)/shard_map/ppermute | solution.py:40
  26.8 7.0 %collective-permute-start.13 = (bf16[1,14,32,128]{3,2,1,0:T(8,128)(2,1)S(1)}, bf16[1,14,32,128]{3,2,1,0:T(8,128)(2,1)S(1)}, u32[]{:S(2)}, u32[]{:S(2)}) collective-permute-start(bf16[1,14,32,128]{3,2,1,0:T(8,128)(2,1)S(1)} %add_convert_fusion.refs_0_), channel_id=1, source_target_pairs={{0,1},{1,0},{2,3},{3,2},{4,5},{5,4},{6,7},{7,6},{8,9},{9,8},{10,11... | collective-permute-start | bytes 344072 | tf_op jit(solution)/shard_map/ppermute | solution.py:40
  29.6 4.2 %collective-permute-start.17 = (bf16[1,14,32,128]{3,2,1,0:T(8,128)(2,1)S(1)}, bf16[1,14,32,128]{3,2,1,0:T(8,128)(2,1)S(1)}, u32[]{:S(2)}, u32[]{:S(2)}) collective-permute-start(bf16[1,14,32,128]{3,2,1,0:T(8,128)(2,1)S(1)} %collective-permute-done.16.refs_4_), channel_id=1, source_target_pairs={{0,1},{1,0},{2,3},{3,2},{4,5},{5,4},{6,7},{7,6},{8,9},{9,8},{10,11... | collective-permute-start | bytes 344072 | tf_op jit(solution)/shard_map/ppermute | solution.py:40
  30.9 2.9 %collective-permute-start.15 = (bf16[1,14,32,128]{3,2,1,0:T(8,128)(2,1)S(1)}, bf16[1,14,32,128]{3,2,1,0:T(8,128)(2,1)S(1)}, u32[]{:S(2)}, u32[]{:S(2)}) collective-permute-start(bf16[1,14,32,128]{3,2,1,0:T(8,128)(2,1)S(1)} %collective-permute-done.14.refs_2_), channel_id=1, source_target_pairs={{0,1},{1,0},{2,3},{3,2},{4,5},{5,4},{6,7},{7,6},{8,9},{9,8},{10,11... | collective-permute-start | bytes 344072 | tf_op jit(solution)/shard_map/ppermute | solution.py:40
  31.9 3.2 %collective-permute-start.12 = (bf16[1,14,32,128]{3,2,1,0:T(8,128)(2,1)S(1)}, bf16[1,14,32,128]{3,2,1,0:T(8,128)(2,1)S(1)}, u32[]{:S(2)}, u32[]{:S(2)}) collective-permute-start(bf16[1,14,32,128]{3,2,1,0:T(8,128)(2,1)S(1)} %collective-permute-done.11.refs_0_), channel_id=1, source_target_pairs={{0,1},{1,0},{2,3},{3,2},{4,5},{5,4},{6,7},{7,6},{8,9},{9,8},{10,11... | collective-permute-start | bytes 344072 | tf_op jit(solution)/shard_map/ppermute | solution.py:40

commit v12 on v11

--- a/solution.py
+++ b/solution.py
@@ -310,13 +310,13 @@
     )(where, *given, *sofar)
 
 
-def summed(where, keep, send, scale, beside_split, beside_exchange):
+def summed(where, keep, send, scale, pre_grad, start_next, finish):
     total = keep[:1]
     for offset in (3, 2, 1):
         piece = swapped(send[offset : offset + 1], masks_of(0, offset))
         total = total + piece.astype(jnp.float32)
-    done = beside_split()
-    total, done = lax.optimization_barrier((total, done))
+    total, pre_grad = lax.optimization_barrier((total, pre_grad))
+    next_halo = start_next(pre_grad)
     total = lax.reduce_precision(total, 8, 7)
     third, second, first = (
         swapped(total.astype(jnp.bfloat16), masks_of(1, offset)).astype(jnp.float32)
@@ -328,10 +328,11 @@
     while mask < count:
         total = total + swapped(total, (mask, mask))
         mask *= 2
-    done = beside_exchange(done)
     total = total.astype(jnp.bfloat16)
-    total, done = lax.optimization_barrier((total, done))
+    total, next_halo = lax.optimization_barrier((total, next_halo))
     mine = [total] + [swapped(total, masks_of(0, offset)) for offset in (1, 2, 3)]
+    done = finish(pre_grad, next_halo)
+    mine[1], done = lax.optimization_barrier((mine[1], done))
     pieces = [(piece, swapped(piece, (1, 1))) for piece in mine[:3]]
     sofar = unpack(where, pieces, (0, 1, 2), scale)
     pieces.append((mine[3], swapped(mine[3], (1, 1))))
@@ -448,9 +449,10 @@
         keep,
         send,
         1.0 / math.sqrt(total_pixels),
-        lambda: passed_round(pre_grad[:halo_rows], "tm", -1),
-        lambda following: backward(
-            shape, where, pre_grad, following, hidden, frames, grads, conv_kernel, proj_weight
+        pre_grad,
+        lambda grads_here: passed_round(grads_here[:halo_rows], "tm", -1),
+        lambda grads_here, following: backward(
+            shape, where, grads_here, following, hidden, frames, grads, conv_kernel, proj_weight
         ),
     )
     return (

time: 36.1 us -> 36.1 us (level)
    ppermute x15, starting transfers between devices: 17.4 us -> 16 us  [swapped(): lax.ppermute(array, AXES, [(i, i ^ masks[i & 1]) for i in range(count)])]
    ppermute x2, starting transfers between devices: 2.6 us -> 3.9 us  [passed_round(): lax.ppermute(shard, axis, [(i, (i + by) % size) for i in range(size)])]
    ppermute x2, waiting for transfers between devices: 0.01 us -> 0.4 us  [passed_round(): lax.ppermute(shard, axis, [(i, (i + by) % size) for i in range(size)])]
where the time goes in v12:
time: 36.1 us; the launch traced here: 35.9 us
  starting transfers between devices  19.9 us (55%)
  waiting for transfers between devices  8.69 us (24%)
  Pallas kernels  6.47 us (18%)
  between operations  0.75 us (2%)
    ppermute x15, starting transfers between devices, swapped(): lax.ppermute(array, AXES, [(i, i ^ masks[i & 1]) for i in range(count)])  16 us
    ppermute x15, waiting for transfers between devices, swapped(): lax.ppermute(array, AXES, [(i, i ^ masks[i & 1]) for i in range(count)])  7.1 us
    ppermute x2, starting transfers between devices, passed_round(): lax.ppermute(shard, axis, [(i, (i + by) % size) for i in range(size)])  3.9 us
    pallas_call x2, Pallas kernels, unpack(): pl.pallas_call(functools.partial(unpack_kernel, scale, offsets), out_shap...  2.08 us
    pallas_call x1, Pallas kernels, backward(): pl.pallas_call(functools.partial(backward_kernel, shape), out_shape=(jax....  1.29 us
    pallas_call x1, Pallas kernels, prepare(): pl.pallas_call(functools.partial(prepare_kernel, width), out_shape=(*(jax...  1.28 us
    ppermute x1, waiting for transfers between devices, passed_to_last_core(): return lax.ppermute(shard, AXES, pairs)  1.19 us
    pallas_call x1, Pallas kernels, forward(): pl.pallas_call(functools.partial(forward_kernel, shape), out_shape=(jax.S...  1.03 us
  transfers between devices with their start and end apart: 18, of which 7 were waited for; matrix products, arithmetic and copies ran while one was open for 0% of the time, Pallas kernels for 13%

profile of v12, /device:TPU:1, one launch (start us, length us, event | category | flops | bytes accessed | tf_op | source)
XLA Modules:
  0.0 35.9 jit_solution(8228402674819307995)
XLA Ops:
  0.6 0.1 collective-permute-start.2
  0.8 0.5 %collective-permute-start.3 = (bf16[256,128]{1,0:T(8,128)(2,1)}, bf16[256,128]{1,0:T(8,128)(2,1)S(1)}, u32[]{:S(2)}, u32[]{:S(2)}) collective-permute-start(bf16[256,128]{1,0:T(8,128)(2,1)} %bitcast.7), channel_id=1, source_target_pairs={{0,1},{1,0},{2,3},{3,2},{4,5},{5,4},{6,7},{7,6},{8,9},{9,8},{10,11... | collective-permute-start | bytes 196616 | tf_op jit(solution)/shard_map/ppermute | solution.py:40
  1.2 2.6 %collective-permute-start.1 = (bf16[256,128]{1,0:T(8,128)(2,1)}, bf16[256,128]{1,0:T(8,128)(2,1)S(1)}, u32[]{:S(2)}, u32[]{:S(2)}) collective-permute-start(bf16[256,128]{1,0:T(8,128)(2,1)} %bitcast.10), channel_id=1, source_target_pairs={{0,1},{1,2},{2,3},{3,0},{4,5},{5,6},{6,7},{7,4},{8,9},{9,10},{10,1... | collective-permute-start | bytes 196616 | tf_op jit(solution)/shard_map/ppermute | solution.py:21
  3.8 0.0 collective-permute-start
  3.8 1.3 %prepare.1 = (bf16[256,128]{1,0:T(8,128)(2,1)S(1)}, bf16[256,128]{1,0:T(8,128)(2,1)S(1)}, bf16[3,3,3,128,128]{4,3,2,1,0:T(8,128)(2,1)S(1)}, bf16[128,128]{1,0:T(8,128)(2,1)S(1)}, bf16[256,384]{1,0:T(8,128)(2,1)S(1)}) custom-call(bf16[256,128]{1,0:T(8,128)(2,1)} %bitcast.12, bf16[256,128]{1,0:T(8,128)(2,1)} %bitcast.8, bf16[3,3,3,128,128]{4,3,2,1,0:T(8,128)(2,1)} %kern_hbm.1, ...), custom_call_target="tpu_custom_call" | custom-call | flops 32768 | bytes 2097152 | tf_op jit(solution)/shard_map/prepare/pallas_call | solution.py:345
  5.1 0.0 collective-permute-done.2.partner_ref
  5.1 0.0 collective-permute-done.3.partner_grads_ref
  5.1 0.8 %join.1 = (bf16[384,768]{1,0:T(8,128)(2,1)S(1)}, bf16[512,128]{1,0:T(8,128)(2,1)S(1)}, f32[512,384]{1,0:T(8,128)S(1)}, f32[512,128]{1,0:T(8,128)S(1)}) custom-call(s32[1]{0:T(128)} %bitcast.where_ref, bf16[256,384]{1,0:T(8,128)(2,1)S(1)} %get-tuple-element.30.own_ref, bf16[256,128]{1,0:T(8,128)(2,1)S(1)} %get-tuple-element.31.grads_ref, ...), custom_call_target="tpu_custom_call" | custom-call | flops 335544320 | bytes 2097152 | tf_op jit(solution)/shard_map/join/pallas_call | solution.py:364
  5.9 0.0 collective-permute-done.1.first_halo_ref
  5.9 1.2 %collective-permute-done.second_halo_ref = bf16[256,128]{1,0:T(8,128)(2,1)S(1)} collective-permute-done((bf16[256,128]{1,0:T(8,128)(2,1)}, bf16[256,128]{1,0:T(8,128)(2,1)S(1)}, u32[]{:S(2)}, u32[]{:S(2)}) %collective-permute-start) | collective-permute-done | bytes 65568 | tf_op jit(solution)/shard_map/ppermute | solution.py:31
  7.1 1.0 %forward.1 = (f32[4,14,32,128]{3,2,1,0:T(8,128)S(1)}, bf16[4,14,32,128]{3,2,1,0:T(8,128)(2,1)S(1)}, bf16[256,128]{1,0:T(8,128)(2,1)S(1)}, bf16[256,128]{1,0:T(8,128)(2,1)S(1)}, bf16[384,768]{1,0:T(8,128)(2,1)S(1)}) custom-call(s32[1]{0:T(128)} %bitcast.where_ref, ...), custom_call_target="tpu_custom_call", output_to_operand_aliasing={{4}: (5, {})} | custom-call | tf_op jit(solution)/shard_map/forward/pallas_call | solution.py:387
  8.2 3.4 %collective-permute-start.4 = (bf16[1,14,32,128]{3,2,1,0:T(8,128)(2,1)S(1)}, bf16[1,14,32,128]{3,2,1,0:T(8,128)(2,1)S(1)}, u32[]{:S(2)}, u32[]{:S(2)}) collective-permute-start(bf16[1,14,32,128]{3,2,1,0:T(8,128)(2,1)S(1)} %get-tuple-element.56), channel_id=1, source_target_pairs={{0,6},{1,25},{2,4},{3,27},{4,2},{5,29},{6,0},{7,31},{8,14},{9,17},... | collective-permute-start | bytes 344072 | tf_op jit(solution)/shard_map/ppermute | solution.py:40
  11.6 0.0 collective-permute-start.6
  11.6 0.4 %collective-permute-start.5 = (bf16[1,14,32,128]{3,2,1,0:T(8,128)(2,1)S(1)}, bf16[1,14,32,128]{3,2,1,0:T(8,128)(2,1)S(1)}, u32[]{:S(2)}, u32[]{:S(2)}) collective-permute-start(bf16[1,14,32,128]{3,2,1,0:T(8,128)(2,1)S(1)} %get-tuple-element.58), channel_id=1, source_target_pairs={{0,2},{1,9},{2,0},{3,11},{4,6},{5,13},{6,4},{7,15},{8,10},{9,1},{1... | collective-permute-start | bytes 344072 | tf_op jit(solution)/shard_map/ppermute | solution.py:40
  12.0 1.9 %collective-permute-done.4 = bf16[1,14,32,128]{3,2,1,0:T(8,128)(2,1)S(1)} collective-permute-done((bf16[1,14,32,128]{3,2,1,0:T(8,128)(2,1)S(1)}, bf16[1,14,32,128]{3,2,1,0:T(8,128)(2,1)S(1)}, u32[]{:S(2)}, u32[]{:S(2)}) %collective-permute-start.4) | collective-permute-done | bytes 114720 | tf_op jit(solution)/shard_map/ppermute | solution.py:40
  13.9 2.7 %collective-permute-done.6 = bf16[1,14,32,128]{3,2,1,0:T(8,128)(2,1)S(1)} collective-permute-done((bf16[1,14,32,128]{3,2,1,0:T(8,128)(2,1)S(1)}, bf16[1,14,32,128]{3,2,1,0:T(8,128)(2,1)S(1)}, u32[]{:S(2)}, u32[]{:S(2)}) %collective-permute-start.6) | collective-permute-done | bytes 114720 | tf_op jit(solution)/shard_map/ppermute | solution.py:40
  16.6 0.0 collective-permute-done.5
  16.6 0.1 convert_add_fusion
  16.7 2.0 %collective-permute-start.9 = (bf16[1,14,32,128]{3,2,1,0:T(8,128)(2,1)S(1)}, bf16[1,14,32,128]{3,2,1,0:T(8,128)(2,1)S(1)}, u32[]{:S(2)}, u32[]{:S(2)}) collective-permute-start(bf16[1,14,32,128]{3,2,1,0:T(8,128)(2,1)S(1)} %reduce-precision_convert_fusion), channel_id=1, source_target_pairs={{0,24},{1,7},{2,26},{3,5},{4,28},{5,3},{6,30},{7,1},{8,16},{9,15},... | collective-permute-start | bytes 344072 | tf_op jit(solution)/shard_map/ppermute | solution.py:40
  18.7 0.5 %collective-permute-start.8 = (bf16[1,14,32,128]{3,2,1,0:T(8,128)(2,1)S(1)}, bf16[1,14,32,128]{3,2,1,0:T(8,128)(2,1)S(1)}, u32[]{:S(2)}, u32[]{:S(2)}) collective-permute-start(bf16[1,14,32,128]{3,2,1,0:T(8,128)(2,1)S(1)} %reduce-precision_convert_fusion), channel_id=1, source_target_pairs={{0,8},{1,3},{2,10},{3,1},{4,12},{5,7},{6,14},{7,5},{8,0},{9,11},{1... | collective-permute-start | bytes 344072 | tf_op jit(solution)/shard_map/ppermute | solution.py:40
  19.2 0.2 collective-permute-start.7
  19.4 1.3 %collective-permute-start.10 = (bf16[256,128]{1,0:T(8,128)(2,1)S(1)}, bf16[256,128]{1,0:T(8,128)(2,1)S(1)}, u32[]{:S(2)}, u32[]{:S(2)}) collective-permute-start(bf16[256,128]{1,0:T(8,128)(2,1)S(1)} %get-tuple-element.42.pre_grad_ref), channel_id=1, source_target_pairs={{0,3},{1,0},{2,1},{3,2},{4,7},{5,4},{6,5},{7,6},{8,11},{9,8},{10,9... | collective-permute-start | bytes 196616 | tf_op jit(solution)/shard_map/ppermute | solution.py:21
  20.7 0.9 %collective-permute-done.9 = bf16[1,14,32,128]{3,2,1,0:T(8,128)(2,1)S(1)} collective-permute-done((bf16[1,14,32,128]{3,2,1,0:T(8,128)(2,1)S(1)}, bf16[1,14,32,128]{3,2,1,0:T(8,128)(2,1)S(1)}, u32[]{:S(2)}, u32[]{:S(2)}) %collective-permute-start.9) | collective-permute-done | bytes 114720 | tf_op jit(solution)/shard_map/ppermute | solution.py:40
  21.6 1.1 %collective-permute-done.8 = bf16[1,14,32,128]{3,2,1,0:T(8,128)(2,1)S(1)} collective-permute-done((bf16[1,14,32,128]{3,2,1,0:T(8,128)(2,1)S(1)}, bf16[1,14,32,128]{3,2,1,0:T(8,128)(2,1)S(1)}, u32[]{:S(2)}, u32[]{:S(2)}) %collective-permute-start.8) | collective-permute-done | bytes 114720 | tf_op jit(solution)/shard_map/ppermute | solution.py:40
  22.7 0.4 %collective-permute-done.7 = bf16[1,14,32,128]{3,2,1,0:T(8,128)(2,1)S(1)} collective-permute-done((bf16[1,14,32,128]{3,2,1,0:T(8,128)(2,1)S(1)}, bf16[1,14,32,128]{3,2,1,0:T(8,128)(2,1)S(1)}, u32[]{:S(2)}, u32[]{:S(2)}) %collective-permute-start.7) | collective-permute-done | bytes 114720 | tf_op jit(solution)/shard_map/ppermute | solution.py:40
  23.1 0.1 add_convert_fusion.refs_0_
  23.2 0.4 %collective-permute-done.10.next_ref = bf16[256,128]{1,0:T(8,128)(2,1)S(1)} collective-permute-done((bf16[256,128]{1,0:T(8,128)(2,1)S(1)}, bf16[256,128]{1,0:T(8,128)(2,1)S(1)}, u32[]{:S(2)}, u32[]{:S(2)}) %collective-permute-start.10) | collective-permute-done | bytes 65568 | tf_op jit(solution)/shard_map/ppermute | solution.py:21
  23.6 1.3 %collective-permute-start.11 = (bf16[1,14,32,128]{3,2,1,0:T(8,128)(2,1)S(1)}, bf16[1,14,32,128]{3,2,1,0:T(8,128)(2,1)S(1)}, u32[]{:S(2)}, u32[]{:S(2)}) collective-permute-start(bf16[1,14,32,128]{3,2,1,0:T(8,128)(2,1)S(1)} %add_convert_fusion.refs_0_), channel_id=1, source_target_pairs={{0,4},{1,17},{2,6},{3,19},{4,0},{5,21},{6,2},{7,23},{8,12},{9,25},... | collective-permute-start | bytes 344072 | tf_op jit(solution)/shard_map/ppermute | solution.py:40
  24.9 2.0 %collective-permute-start.16 = (bf16[1,14,32,128]{3,2,1,0:T(8,128)(2,1)S(1)}, bf16[1,14,32,128]{3,2,1,0:T(8,128)(2,1)S(1)}, u32[]{:S(2)}, u32[]{:S(2)}) collective-permute-start(bf16[1,14,32,128]{3,2,1,0:T(8,128)(2,1)S(1)} %add_convert_fusion.refs_0_), channel_id=1, source_target_pairs={{0,2},{1,9},{2,0},{3,11},{4,6},{5,13},{6,4},{7,15},{8,10},{9,1},{1... | collective-permute-start | bytes 344072 | tf_op jit(solution)/shard_map/ppermute | solution.py:40
  26.9 0.2 collective-permute-start.12
  27.1 2.4 %collective-permute-start.14 = (bf16[1,14,32,128]{3,2,1,0:T(8,128)(2,1)S(1)}, bf16[1,14,32,128]{3,2,1,0:T(8,128)(2,1)S(1)}, u32[]{:S(2)}, u32[]{:S(2)}) collective-permute-start(bf16[1,14,32,128]{3,2,1,0:T(8,128)(2,1)S(1)} %add_convert_fusion.refs_0_), channel_id=1, source_target_pairs={{0,1},{1,0},{2,3},{3,2},{4,5},{5,4},{6,7},{7,6},{8,9},{9,8},{10,11... | collective-permute-start | bytes 344072 | tf_op jit(solution)/shard_map/ppermute | solution.py:40
  29.6 1.3 %backward.1 = (bf16[256,128]{1,0:T(8,128)(2,1)}, bf16[256,128]{1,0:T(8,128)(2,1)}) custom-call(s32[1]{0:T(128)} %bitcast.where_ref, bf16[256,128]{1,0:T(8,128)(2,1)S(1)} %get-tuple-element.42.pre_grad_ref, bf16[256,128]{1,0:T(8,128)(2,1)S(1)} %collective-permute-done.10.next_ref, bf16[256,128]{1,0:T(8,128)(2,1)S(1)} %get-tuple-element.45.hidden_ref, ...), custom_call_target="tpu_custom_call" | custom-call | flops 234881024 | bytes 1048576 | tf_op jit(solution)/shard_map/backward/pallas_call | solution.py:409
  30.9 0.0 collective-permute-done.11.refs_2_
  30.9 0.0 collective-permute-done.16.refs_4_
  30.9 1.5 %collective-permute-start.17 = (bf16[1,14,32,128]{3,2,1,0:T(8,128)(2,1)S(1)}, bf16[1,14,32,128]{3,2,1,0:T(8,128)(2,1)S(1)}, u32[]{:S(2)}, u32[]{:S(2)}) collective-permute-start(bf16[1,14,32,128]{3,2,1,0:T(8,128)(2,1)S(1)} %collective-permute-done.16.refs_4_), channel_id=1, source_target_pairs={{0,1},{1,0},{2,3},{3,2},{4,5},{5,4},{6,7},{7,6},{8,9},{9,8},{10,11... | collective-permute-start | bytes 344072 | tf_op jit(solution)/shard_map/ppermute | solution.py:40
  32.4 0.0 collective-permute-start.15
  32.4 0.0 collective-permute-done.12.refs_0_
  32.4 1.4 %collective-permute-start.13 = (bf16[1,14,32,128]{3,2,1,0:T(8,128)(2,1)S(1)}, bf16[1,14,32,128]{3,2,1,0:T(8,128)(2,1)S(1)}, u32[]{:S(2)}, u32[]{:S(2)}) collective-permute-start(bf16[1,14,32,128]{3,2,1,0:T(8,128)(2,1)S(1)} %collective-permute-done.12.refs_0_), channel_id=1, source_target_pairs={{0,1},{1,0},{2,3},{3,2},{4,5},{5,4},{6,7},{7,6},{8,9},{9,8},{10,11... | collective-permute-start | bytes 344072 | tf_op jit(solution)/shard_map/ppermute | solution.py:40
  33.8 0.0 collective-permute-done.14.refs_1_
  33.8 0.0 collective-permute-done.17.refs_5_
  33.8 0.0 collective-permute-done.15.refs_3_
  33.8 1.2 %unpack.2 = (f32[27,128,128]{2,1,0:T(8,128)}, f32[128,128]{1,0:T(8,128)}) custom-call(s32[1]{0:T(128)} %bitcast.where_ref, bf16[1,14,32,128]{3,2,1,0:T(8,128)(2,1)S(1)} %add_convert_fusion.refs_0_, bf16[1,14,32,128]{3,2,1,0:T(8,128)(2,1)S(1)} %collective-permute-done.14.refs_1_, bf16[1,14,32,128]{3,2,1,0:T(8,128)(2,1)S(1)} %collective-permute-done.11.refs_2_, ...), custom_call_target="tpu_custom_call" | custom-call | flops 344064 | bytes 2064384 | tf_op jit(solution)/shard_map/unpack/pallas_call | solution.py:290
  35.1 0.0 collective-permute-done.13.refs_1_
  35.1 0.8 %unpack.3 = (f32[27,128,128]{2,1,0:T(8,128)}, f32[128,128]{1,0:T(8,128)}) custom-call(s32[1]{0:T(128)} %bitcast.where_ref, bf16[1,14,32,128]{3,2,1,0:T(8,128)(2,1)S(1)} %collective-permute-done.12.refs_0_, bf16[1,14,32,128]{3,2,1,0:T(8,128)(2,1)S(1)} %collective-permute-done.13.refs_1_, ...), custom_call_target="tpu_custom_call", output_to_operand_aliasing={{0}: (3, {}), {1}: (4, {})} | custom-call | flops 114688 | bytes 688128 | tf_op jit(solution)/shard_map/unpack/pallas_call | solution.py:290
  (2 shorter events, 0.0 us)
Async XLA Ops:
  0.6 4.5 %collective-permute-start.2 = (bf16[256,128]{1,0:T(8,128)(2,1)}, bf16[256,128]{1,0:T(8,128)(2,1)S(1)}, u32[]{:S(2)}, u32[]{:S(2)}) collective-permute-start(bf16[256,128]{1,0:T(8,128)(2,1)} %bitcast.9), channel_id=1, source_target_pairs={{0,1},{1,0},{2,3},{3,2},{4,5},{5,4},{6,7},{7,6},{8,9},{9,8},{10,11... | collective-permute-start | bytes 196616 | tf_op jit(solution)/shard_map/ppermute | solution.py:40
  0.8 4.4 %collective-permute-start.3 = (bf16[256,128]{1,0:T(8,128)(2,1)}, bf16[256,128]{1,0:T(8,128)(2,1)S(1)}, u32[]{:S(2)}, u32[]{:S(2)}) collective-permute-start(bf16[256,128]{1,0:T(8,128)(2,1)} %bitcast.7), channel_id=1, source_target_pairs={{0,1},{1,0},{2,3},{3,2},{4,5},{5,4},{6,7},{7,6},{8,9},{9,8},{10,11... | collective-permute-start | bytes 196616 | tf_op jit(solution)/shard_map/ppermute | solution.py:40
  1.2 4.7 %collective-permute-start.1 = (bf16[256,128]{1,0:T(8,128)(2,1)}, bf16[256,128]{1,0:T(8,128)(2,1)S(1)}, u32[]{:S(2)}, u32[]{:S(2)}) collective-permute-start(bf16[256,128]{1,0:T(8,128)(2,1)} %bitcast.10), channel_id=1, source_target_pairs={{0,1},{1,2},{2,3},{3,0},{4,5},{5,6},{6,7},{7,4},{8,9},{9,10},{10,1... | collective-permute-start | bytes 196616 | tf_op jit(solution)/shard_map/ppermute | solution.py:21
  3.8 3.3 %collective-permute-start = (bf16[256,128]{1,0:T(8,128)(2,1)}, bf16[256,128]{1,0:T(8,128)(2,1)S(1)}, u32[]{:S(2)}, u32[]{:S(2)}) collective-permute-start(bf16[256,128]{1,0:T(8,128)(2,1)} %bitcast.11), channel_id=1, source_target_pairs={{0,4},{1,3},{2,6},{3,1},{4,0},{5,7},{6,2},{7,5},{8,12},{9,11},{10,... | collective-permute-start | bytes 196616 | tf_op jit(solution)/shard_map/ppermute | solution.py:31
  8.2 5.7 %collective-permute-start.4 = (bf16[1,14,32,128]{3,2,1,0:T(8,128)(2,1)S(1)}, bf16[1,14,32,128]{3,2,1,0:T(8,128)(2,1)S(1)}, u32[]{:S(2)}, u32[]{:S(2)}) collective-permute-start(bf16[1,14,32,128]{3,2,1,0:T(8,128)(2,1)S(1)} %get-tuple-element.56), channel_id=1, source_target_pairs={{0,6},{1,25},{2,4},{3,27},{4,2},{5,29},{6,0},{7,31},{8,14},{9,17},... | collective-permute-start | bytes 344072 | tf_op jit(solution)/shard_map/ppermute | solution.py:40
  11.6 5.0 %collective-permute-start.6 = (bf16[1,14,32,128]{3,2,1,0:T(8,128)(2,1)S(1)}, bf16[1,14,32,128]{3,2,1,0:T(8,128)(2,1)S(1)}, u32[]{:S(2)}, u32[]{:S(2)}) collective-permute-start(bf16[1,14,32,128]{3,2,1,0:T(8,128)(2,1)S(1)} %get-tuple-element.57), channel_id=1, source_target_pairs={{0,4},{1,17},{2,6},{3,19},{4,0},{5,21},{6,2},{7,23},{8,12},{9,25},... | collective-permute-start | bytes 344072 | tf_op jit(solution)/shard_map/ppermute | solution.py:40
  11.6 5.0 %collective-permute-start.5 = (bf16[1,14,32,128]{3,2,1,0:T(8,128)(2,1)S(1)}, bf16[1,14,32,128]{3,2,1,0:T(8,128)(2,1)S(1)}, u32[]{:S(2)}, u32[]{:S(2)}) collective-permute-start(bf16[1,14,32,128]{3,2,1,0:T(8,128)(2,1)S(1)} %get-tuple-element.58), channel_id=1, source_target_pairs={{0,2},{1,9},{2,0},{3,11},{4,6},{5,13},{6,4},{7,15},{8,10},{9,1},{1... | collective-permute-start | bytes 344072 | tf_op jit(solution)/shard_map/ppermute | solution.py:40
  16.7 4.9 %collective-permute-start.9 = (bf16[1,14,32,128]{3,2,1,0:T(8,128)(2,1)S(1)}, bf16[1,14,32,128]{3,2,1,0:T(8,128)(2,1)S(1)}, u32[]{:S(2)}, u32[]{:S(2)}) collective-permute-start(bf16[1,14,32,128]{3,2,1,0:T(8,128)(2,1)S(1)} %reduce-precision_convert_fusion), channel_id=1, source_target_pairs={{0,24},{1,7},{2,26},{3,5},{4,28},{5,3},{6,30},{7,1},{8,16},{9,15},... | collective-permute-start | bytes 344072 | tf_op jit(solution)/shard_map/ppermute | solution.py:40
  18.7 4.0 %collective-permute-start.8 = (bf16[1,14,32,128]{3,2,1,0:T(8,128)(2,1)S(1)}, bf16[1,14,32,128]{3,2,1,0:T(8,128)(2,1)S(1)}, u32[]{:S(2)}, u32[]{:S(2)}) collective-permute-start(bf16[1,14,32,128]{3,2,1,0:T(8,128)(2,1)S(1)} %reduce-precision_convert_fusion), channel_id=1, source_target_pairs={{0,8},{1,3},{2,10},{3,1},{4,12},{5,7},{6,14},{7,5},{8,0},{9,11},{1... | collective-permute-start | bytes 344072 | tf_op jit(solution)/shard_map/ppermute | solution.py:40
  19.2 3.9 %collective-permute-start.7 = (bf16[1,14,32,128]{3,2,1,0:T(8,128)(2,1)S(1)}, bf16[1,14,32,128]{3,2,1,0:T(8,128)(2,1)S(1)}, u32[]{:S(2)}, u32[]{:S(2)}) collective-permute-start(bf16[1,14,32,128]{3,2,1,0:T(8,128)(2,1)S(1)} %reduce-precision_convert_fusion), channel_id=1, source_target_pairs={{0,16},{1,5},{2,18},{3,7},{4,20},{5,1},{6,22},{7,3},{8,24},{9,13},... | collective-permute-start | bytes 344072 | tf_op jit(solution)/shard_map/ppermute | solution.py:40
  19.4 4.2 %collective-permute-start.10 = (bf16[256,128]{1,0:T(8,128)(2,1)S(1)}, bf16[256,128]{1,0:T(8,128)(2,1)S(1)}, u32[]{:S(2)}, u32[]{:S(2)}) collective-permute-start(bf16[256,128]{1,0:T(8,128)(2,1)S(1)} %get-tuple-element.42.pre_grad_ref), channel_id=1, source_target_pairs={{0,3},{1,0},{2,1},{3,2},{4,7},{5,4},{6,5},{7,6},{8,11},{9,8},{10,9... | collective-permute-start | bytes 196616 | tf_op jit(solution)/shard_map/ppermute | solution.py:21
  23.6 7.3 %collective-permute-start.11 = (bf16[1,14,32,128]{3,2,1,0:T(8,128)(2,1)S(1)}, bf16[1,14,32,128]{3,2,1,0:T(8,128)(2,1)S(1)}, u32[]{:S(2)}, u32[]{:S(2)}) collective-permute-start(bf16[1,14,32,128]{3,2,1,0:T(8,128)(2,1)S(1)} %add_convert_fusion.refs_0_), channel_id=1, source_target_pairs={{0,4},{1,17},{2,6},{3,19},{4,0},{5,21},{6,2},{7,23},{8,12},{9,25},... | collective-permute-start | bytes 344072 | tf_op jit(solution)/shard_map/ppermute | solution.py:40
  24.9 6.0 %collective-permute-start.16 = (bf16[1,14,32,128]{3,2,1,0:T(8,128)(2,1)S(1)}, bf16[1,14,32,128]{3,2,1,0:T(8,128)(2,1)S(1)}, u32[]{:S(2)}, u32[]{:S(2)}) collective-permute-start(bf16[1,14,32,128]{3,2,1,0:T(8,128)(2,1)S(1)} %add_convert_fusion.refs_0_), channel_id=1, source_target_pairs={{0,2},{1,9},{2,0},{3,11},{4,6},{5,13},{6,4},{7,15},{8,10},{9,1},{1... | collective-permute-start | bytes 344072 | tf_op jit(solution)/shard_map/ppermute | solution.py:40
  26.9 5.5 %collective-permute-start.12 = (bf16[1,14,32,128]{3,2,1,0:T(8,128)(2,1)S(1)}, bf16[1,14,32,128]{3,2,1,0:T(8,128)(2,1)S(1)}, u32[]{:S(2)}, u32[]{:S(2)}) collective-permute-start(bf16[1,14,32,128]{3,2,1,0:T(8,128)(2,1)S(1)} %add_convert_fusion.refs_0_), channel_id=1, source_target_pairs={{0,6},{1,25},{2,4},{3,27},{4,2},{5,29},{6,0},{7,31},{8,14},{9,17},... | collective-permute-start | bytes 344072 | tf_op jit(solution)/shard_map/ppermute | solution.py:40
  27.1 6.7 %collective-permute-start.14 = (bf16[1,14,32,128]{3,2,1,0:T(8,128)(2,1)S(1)}, bf16[1,14,32,128]{3,2,1,0:T(8,128)(2,1)S(1)}, u32[]{:S(2)}, u32[]{:S(2)}) collective-permute-start(bf16[1,14,32,128]{3,2,1,0:T(8,128)(2,1)S(1)} %add_convert_fusion.refs_0_), channel_id=1, source_target_pairs={{0,1},{1,0},{2,3},{3,2},{4,5},{5,4},{6,7},{7,6},{8,9},{9,8},{10,11... | collective-permute-start | bytes 344072 | tf_op jit(solution)/shard_map/ppermute | solution.py:40
  30.9 2.9 %collective-permute-start.17 = (bf16[1,14,32,128]{3,2,1,0:T(8,128)(2,1)S(1)}, bf16[1,14,32,128]{3,2,1,0:T(8,128)(2,1)S(1)}, u32[]{:S(2)}, u32[]{:S(2)}) collective-permute-start(bf16[1,14,32,128]{3,2,1,0:T(8,128)(2,1)S(1)} %collective-permute-done.16.refs_4_), channel_id=1, source_target_pairs={{0,1},{1,0},{2,3},{3,2},{4,5},{5,4},{6,7},{7,6},{8,9},{9,8},{10,11... | collective-permute-start | bytes 344072 | tf_op jit(solution)/shard_map/ppermute | solution.py:40
  32.4 1.4 %collective-permute-start.15 = (bf16[1,14,32,128]{3,2,1,0:T(8,128)(2,1)S(1)}, bf16[1,14,32,128]{3,2,1,0:T(8,128)(2,1)S(1)}, u32[]{:S(2)}, u32[]{:S(2)}) collective-permute-start(bf16[1,14,32,128]{3,2,1,0:T(8,128)(2,1)S(1)} %collective-permute-done.11.refs_2_), channel_id=1, source_target_pairs={{0,1},{1,0},{2,3},{3,2},{4,5},{5,4},{6,7},{7,6},{8,9},{9,8},{10,11... | collective-permute-start | bytes 344072 | tf_op jit(solution)/shard_map/ppermute | solution.py:40
  32.4 2.7 %collective-permute-start.13 = (bf16[1,14,32,128]{3,2,1,0:T(8,128)(2,1)S(1)}, bf16[1,14,32,128]{3,2,1,0:T(8,128)(2,1)S(1)}, u32[]{:S(2)}, u32[]{:S(2)}) collective-permute-start(bf16[1,14,32,128]{3,2,1,0:T(8,128)(2,1)S(1)} %collective-permute-done.12.refs_0_), channel_id=1, source_target_pairs={{0,1},{1,0},{2,3},{3,2},{4,5},{5,4},{6,7},{7,6},{8,9},{9,8},{10,11... | collective-permute-start | bytes 344072 | tf_op jit(solution)/shard_map/ppermute | solution.py:40
